TPU v7x, 32 devices: a whole 2x2x4 slice. The times are simulated.
32 devices in a mesh: dp: 8 (over z, y), mp: 4 (over x, core).
Axes of the slice: x: 2, y: 2, z: 4, core: 2. Of those that a mesh axis runs over, the one named last changes fastest.
Arguments:
- tokens: bfloat16 [16384, 1024], P(('dp', 'mp')), may hold values from -6 to 6
- cotangent: bfloat16 [16384, 1024], P(('dp', 'mp')), may hold values from -6 to 6
- lengths: int32 [8, 4], P('dp'), may hold values from 1 to 1024, 2048 in all within a row
- key_mask: int32 [8, 2048], P('dp'), may hold values 0 or 1
- w_query: bfloat16 [1024, 1024], P('dp', 'mp'), may hold values from -0.1875 to 0.1875
- w_key: bfloat16 [1024, 1024], P('dp', 'mp'), may hold values from -0.1875 to 0.1875
- w_value: bfloat16 [1024, 1024], P('dp', 'mp'), may hold values from -0.1875 to 0.1875
- w_out: bfloat16 [1024, 1024], P('mp', 'dp'), may hold values from -0.1875 to 0.1875
- w_up: bfloat16 [1024, 4096], P('dp', 'mp'), may hold values from -0.1875 to 0.1875
- w_gate: bfloat16 [1024, 4096], P('dp', 'mp'), may hold values from -0.1875 to 0.1875
- w_down: bfloat16 [4096, 1024], P('mp', 'dp'), may hold values from -0.09375 to 0.09375
- s_qk: float32 [1024], P(('dp', 'mp')), may hold values from 0.7 to 1.4
- s_up: float32 [4096], P(('dp', 'mp')), may hold values from 0.5 to 1.5
- s_gate: float32 [4096], P(('dp', 'mp')), may hold values from 0.5 to 1.5
- alpha_attn: float32 [1024], P(('dp', 'mp')), may hold values from 0.1 to 0.6
- alpha_mlp: float32 [1024], P(('dp', 'mp')), may hold values from 0.1 to 0.6
Outputs:
- out_tokens: bfloat16 [16384, 1024], P(('dp', 'mp'))
- grad_tokens: float32 [16384, 1024], P(('dp', 'mp'))
- grad_query: float32 [1024, 1024], P('dp', 'mp')
- grad_key: float32 [1024, 1024], P('dp', 'mp')
- grad_value: float32 [1024, 1024], P('dp', 'mp')
- grad_out: float32 [1024, 1024], P('mp', 'dp')
- grad_up: float32 [1024, 4096], P('dp', 'mp')
- grad_gate: float32 [1024, 4096], P('dp', 'mp')
- grad_down: float32 [4096, 1024], P('mp', 'dp')
- grad_sqk: float32 [1024], P(('dp', 'mp'))
- grad_s_up: float32 [4096], P(('dp', 'mp'))
- grad_s_gate: float32 [4096], P(('dp', 'mp'))
- grad_alpha_attn: float32 [1024], P(('dp', 'mp'))
- grad_alpha_mlp: float32 [1024], P(('dp', 'mp'))
- grad_norm: float32 [], replicated
- mean_alphas: float32 [2], replicated
Inputs may be any that keep to these rules, and one draw needn't show every extreme that they name: `lengths`: each row's 4 documents fill its 2048 slots in order; in each row the longest is exactly 1024.
All inputs are finite; a program needn't handle non-finite values. No bound on the sum of `key_mask` on one device may be relied on, other than what follows from the above.
Results may differ from a plain program's by a relative error of at most 0.018.
Values may be sent and summed in bfloat16 or wider, within the bound.
No kernel may reach another device: no remote copies, remote signals or barrier semaphores. Data moves between devices by JAX's collectives and lax.ppermute only.
A program may use at most 256 MiB of HBM per device.

v0:
```python
import jax
import jax.numpy as jnp
from jax import lax
from jax.sharding import PartitionSpec as P

D = 1024
HEADS = 16
FF = 4096


EPS = 1e-06
NEG = -1e30


def rms_rows(tensor):
    factor = lax.rsqrt(jnp.mean(tensor * tensor, axis=-1, keepdims=True) + EPS)
    return (tensor * factor, factor)


def rms_back(incoming, normed, factor):
    return factor * (incoming - normed * jnp.mean(incoming * normed, axis=-1, keepdims=True))


def rotate_half(tensor):
    middle = tensor.shape[-1] // 2
    return jnp.concatenate([-tensor[..., middle:], tensor[..., :middle]], axis=-1)


def rope_tables(positions, length):
    steps_even = jnp.arange(0, length, 2).astype(jnp.float32)
    inverse = jnp.power(jnp.float32(10000.0), -steps_even / length)
    angles = positions.astype(jnp.float32)[:, None] * inverse[None, :]
    angles = jnp.concatenate([angles, angles], axis=-1)
    return (jnp.cos(angles)[:, None, :], jnp.sin(angles)[:, None, :])


def row_layout(length_row, length):
    doc_ends = jnp.cumsum(length_row)
    slot_ids = jnp.arange(length, dtype=jnp.int32)
    passed = (slot_ids[:, None] >= doc_ends[None, :]).astype(jnp.int32)
    documents = jnp.sum(passed, axis=1)
    starts = jnp.sum(passed * length_row[None, :], axis=1)
    return (documents, slot_ids - starts)


def masked_scores(queries, keys_all, documents, mask_row, block_start, block_stop):
    scaling = queries.shape[-1] ** (-0.5)
    scores = (
        jnp.einsum("qhd,khd->hqk", queries, keys_all, preferred_element_type=jnp.float32) * scaling
    )
    query_ids = jnp.arange(block_start, block_stop)
    key_ids = jnp.arange(block_stop)
    allowed = (documents[block_start:block_stop, None] == documents[None, :block_stop]) & (
        key_ids[None, :] <= query_ids[:, None]
    )
    allowed = allowed & (
        (mask_row[None, :block_stop] == 1) | (key_ids[None, :] == query_ids[:, None])
    )
    return jnp.where(allowed[None], scores, NEG)


def attend_row(row_items):
    query_row, key_row, value_row, documents, mask_row = row_items
    length = query_row.shape[0]
    block_len = min(512, length)
    outputs = []
    log_parts = []
    for block_start in range(0, length, block_len):
        block_stop = block_start + block_len
        scores = masked_scores(
            query_row[block_start:block_stop],
            key_row[:block_stop],
            documents,
            mask_row,
            block_start,
            block_stop,
        )
        highest = jnp.max(scores, axis=-1, keepdims=True)
        expo_vals = jnp.exp(scores - highest)
        total_mass = jnp.sum(expo_vals, axis=-1, keepdims=True)
        weights = (expo_vals / total_mass).astype(jnp.bfloat16)
        outputs.append(
            jnp.einsum(
                "hqk,khd->qhd", weights, value_row[:block_stop], preferred_element_type=jnp.float32
            )
        )
        log_parts.append((highest + jnp.log(total_mass))[..., 0])
    return (
        jnp.concatenate(outputs, axis=0).astype(jnp.bfloat16),
        jnp.concatenate(log_parts, axis=1),
    )


def attend_back(row_items):
    query_row, key_row, value_row, grad_row, log_mass, documents, mask_row = row_items
    length = query_row.shape[0]
    block_len = min(512, length)
    scaling = query_row.shape[-1] ** (-0.5)
    grad_queries = []
    grad_keys = jnp.zeros(key_row.shape, jnp.float32)
    grad_values = jnp.zeros(value_row.shape, jnp.float32)
    for block_start in range(0, length, block_len):
        block_stop = block_start + block_len
        scores = masked_scores(
            query_row[block_start:block_stop],
            key_row[:block_stop],
            documents,
            mask_row,
            block_start,
            block_stop,
        )
        probs_full = jnp.exp(scores - log_mass[:, block_start:block_stop, None])
        weights = probs_full.astype(jnp.bfloat16)
        grad_block = grad_row[block_start:block_stop]
        grad_values = grad_values.at[:block_stop].add(
            jnp.einsum("hqk,qhd->khd", weights, grad_block, preferred_element_type=jnp.float32)
        )
        grad_probs = jnp.einsum(
            "qhd,khd->hqk", grad_block, value_row[:block_stop], preferred_element_type=jnp.float32
        )
        grad_scores = (
            probs_full * (grad_probs - jnp.sum(probs_full * grad_probs, axis=-1, keepdims=True))
        ).astype(jnp.bfloat16)
        grad_queries.append(
            jnp.einsum(
                "hqk,khd->qhd",
                grad_scores,
                key_row[:block_stop],
                preferred_element_type=jnp.float32,
            )
            * scaling
        )
        grad_keys = grad_keys.at[:block_stop].add(
            jnp.einsum(
                "hqk,qhd->khd",
                grad_scores,
                query_row[block_start:block_stop],
                preferred_element_type=jnp.float32,
            )
            * scaling
        )
    return (jnp.concatenate(grad_queries, axis=0), grad_keys, grad_values)


def shards(
    tokens,
    cotangent,
    lengths,
    key_mask,
    w_query,
    w_key,
    w_value,
    w_out,
    w_up,
    w_gate,
    w_down,
    s_qk,
    s_up,
    s_gate,
    alpha_attn,
    alpha_mlp,
):
    mp_index = lax.axis_index("mp")
    gathered = (
        lax.all_gather(w_query, "dp", axis=0, tiled=True),
        lax.all_gather(w_key, "dp", axis=0, tiled=True),
        lax.all_gather(w_value, "dp", axis=0, tiled=True),
        lax.all_gather(w_out, "dp", axis=1, tiled=True),
        lax.all_gather(w_up, "dp", axis=0, tiled=True),
        lax.all_gather(w_gate, "dp", axis=0, tiled=True),
        lax.all_gather(w_down, "dp", axis=1, tiled=True),
    )
    full_query, full_key, full_value, full_out, full_up, full_gate, full_down = gathered
    scalars = (
        lax.all_gather(s_qk, ("dp", "mp"), axis=0, tiled=True),
        lax.all_gather(s_up, ("dp", "mp"), axis=0, tiled=True),
        lax.all_gather(s_gate, ("dp", "mp"), axis=0, tiled=True),
        lax.all_gather(alpha_attn, ("dp", "mp"), axis=0, tiled=True),
        lax.all_gather(alpha_mlp, ("dp", "mp"), axis=0, tiled=True),
    )
    head_width = full_query.shape[1]
    hidden_width = full_up.shape[1]
    head_size = D // HEADS
    local_heads = head_width // head_size
    sqk_local = lax.dynamic_slice_in_dim(scalars[0], mp_index * head_width, head_width).reshape(
        local_heads, head_size
    )
    sup_local = lax.dynamic_slice_in_dim(scalars[1], mp_index * hidden_width, hidden_width)
    sgate_local = lax.dynamic_slice_in_dim(scalars[2], mp_index * hidden_width, hidden_width)
    alpha_one = scalars[3]
    alpha_two = scalars[4]
    x_local = tokens.astype(jnp.float32)
    x_full = lax.all_gather(tokens, "mp", axis=0, tiled=True)
    row_total, row_len = key_mask.shape
    total_rows = x_full.shape[0]
    local_rows = tokens.shape[0]
    documents, positions = jax.vmap(lambda one_row: row_layout(one_row, row_len))(lengths)
    cosine, sine_vals = rope_tables(positions.reshape(total_rows), head_size)

    def project(weight):
        raw_proj = jnp.dot(x_full, weight, preferred_element_type=jnp.float32).reshape(
            total_rows, local_heads, head_size
        )
        turned = raw_proj * cosine + rotate_half(raw_proj) * sine_vals
        return rms_rows(turned)

    query_unit, query_factor = project(full_query)
    key_unit, key_factor = project(full_key)
    query_scaled = (query_unit * sqk_local).astype(jnp.bfloat16)
    key_scaled = (key_unit * sqk_local).astype(jnp.bfloat16)
    value_proj = (
        jnp.dot(x_full, full_value, preferred_element_type=jnp.float32)
        .astype(jnp.bfloat16)
        .reshape(total_rows, local_heads, head_size)
    )
    shaped = (row_total, row_len, local_heads, head_size)
    attended, log_mass = lax.map(
        attend_row,
        (
            query_scaled.reshape(shaped),
            key_scaled.reshape(shaped),
            value_proj.reshape(shaped),
            documents,
            key_mask,
        ),
    )
    attended = attended.reshape(total_rows, head_width)
    branch_attn = lax.psum_scatter(
        jnp.dot(
            lax.slice_in_dim(attended, 0, local_rows * lax.axis_size("mp"), axis=0),
            full_out,
            preferred_element_type=jnp.float32,
        ).astype(jnp.bfloat16),
        "mp",
        scatter_dimension=0,
        tiled=True,
    ).astype(jnp.float32)
    h_attn, attn_factor = rms_rows(branch_attn)
    hidden_one, one_factor = rms_rows(x_local + alpha_one * (h_attn - x_local))
    hidden_full = lax.all_gather(hidden_one.astype(jnp.bfloat16), "mp", axis=0, tiled=True)
    up_proj = jnp.dot(hidden_full, full_up, preferred_element_type=jnp.float32)
    gate_proj = jnp.dot(hidden_full, full_gate, preferred_element_type=jnp.float32)
    inner_act = sup_local * up_proj
    outer_act = sgate_local * gate_proj
    sigma_gate = jax.nn.sigmoid(outer_act)
    activation = (inner_act * (outer_act * sigma_gate)).astype(jnp.bfloat16)
    branch_mlp = lax.psum_scatter(
        jnp.dot(
            lax.slice_in_dim(activation, 0, local_rows * lax.axis_size("mp"), axis=0),
            full_down,
            preferred_element_type=jnp.float32,
        ).astype(jnp.bfloat16),
        "mp",
        scatter_dimension=0,
        tiled=True,
    ).astype(jnp.float32)
    h_mlp, mlp_factor = rms_rows(branch_mlp)
    result, two_factor = rms_rows(hidden_one + alpha_two * (h_mlp - hidden_one))
    grad_two = rms_back(cotangent.astype(jnp.float32), result, two_factor)
    grad_hidden = grad_two * (1.0 - alpha_two)
    grad_alpha_two = jnp.sum(grad_two * (h_mlp - hidden_one), axis=0)
    grad_branch = rms_back(grad_two * alpha_two, h_mlp, mlp_factor).astype(jnp.bfloat16)
    grad_branch_full = lax.all_gather(grad_branch, "mp", axis=0, tiled=True)
    grad_activ = jnp.dot(grad_branch_full, full_down.T, preferred_element_type=jnp.float32)
    grad_down_local = jnp.dot(activation.T, grad_branch_full, preferred_element_type=jnp.float32)
    grad_inner = grad_activ * outer_act * sigma_gate
    grad_outer = grad_activ * inner_act * sigma_gate * (1.0 + outer_act * (1.0 - sigma_gate))
    grad_sup_local = jnp.sum(grad_inner * up_proj, axis=0)
    grad_sgate_local = jnp.sum(grad_outer * gate_proj, axis=0)
    grad_up_proj = (grad_inner * sup_local).astype(jnp.bfloat16)
    grad_gate_proj = (grad_outer * sgate_local).astype(jnp.bfloat16)
    grad_up_local = jnp.dot(hidden_full.T, grad_up_proj, preferred_element_type=jnp.float32)
    grad_gate_local = jnp.dot(hidden_full.T, grad_gate_proj, preferred_element_type=jnp.float32)
    up_rows = lax.slice_in_dim(grad_up_proj, 0, local_rows * lax.axis_size("mp"), axis=0)
    gate_rows = lax.slice_in_dim(grad_gate_proj, 0, local_rows * lax.axis_size("mp"), axis=0)
    grad_hidden = grad_hidden + lax.psum_scatter(
        (
            jnp.dot(up_rows, full_up.T, preferred_element_type=jnp.float32)
            + jnp.dot(gate_rows, full_gate.T, preferred_element_type=jnp.float32)
        ).astype(jnp.bfloat16),
        "mp",
        scatter_dimension=0,
        tiled=True,
    ).astype(jnp.float32)
    grad_one = rms_back(grad_hidden, hidden_one, one_factor)
    grad_tokens = grad_one * (1.0 - alpha_one)
    grad_alpha_one = jnp.sum(grad_one * (h_attn - x_local), axis=0)
    grad_attn = rms_back(grad_one * alpha_one, h_attn, attn_factor).astype(jnp.bfloat16)
    grad_attn_full = lax.all_gather(grad_attn, "mp", axis=0, tiled=True)
    grad_attended = jnp.dot(grad_attn_full, full_out.T, preferred_element_type=jnp.float32).astype(
        jnp.bfloat16
    )
    grad_out_local = jnp.dot(attended.T, grad_attn_full, preferred_element_type=jnp.float32)
    grad_query_scaled, grad_key_scaled, grad_value_vals = lax.map(
        attend_back,
        (
            query_scaled.reshape(shaped),
            key_scaled.reshape(shaped),
            value_proj.reshape(shaped),
            grad_attended.reshape(shaped),
            log_mass,
            documents,
            key_mask,
        ),
    )
    heads_shape = (total_rows, local_heads, head_size)
    grad_query_scaled = grad_query_scaled.reshape(heads_shape)
    grad_key_scaled = grad_key_scaled.reshape(heads_shape)
    grad_sqk_local = jnp.sum(
        grad_query_scaled * query_unit + grad_key_scaled * key_unit, axis=0
    ).reshape(head_width)

    def unturn(grad_scaled, unit_vals, factor):
        grad_turned = rms_back(grad_scaled * sqk_local, unit_vals, factor)
        grad_raw = grad_turned * cosine - rotate_half(grad_turned) * sine_vals
        return grad_raw.reshape(total_rows, head_width).astype(jnp.bfloat16)

    grad_query_proj = unturn(grad_query_scaled, query_unit, query_factor)
    grad_key_proj = unturn(grad_key_scaled, key_unit, key_factor)
    grad_value_proj = grad_value_vals.reshape(total_rows, head_width).astype(jnp.bfloat16)
    grad_query_local = jnp.dot(x_full.T, grad_query_proj, preferred_element_type=jnp.float32)
    grad_key_local = jnp.dot(x_full.T, grad_key_proj, preferred_element_type=jnp.float32)
    grad_value_local = jnp.dot(x_full.T, grad_value_proj, preferred_element_type=jnp.float32)
    summed = jnp.dot(grad_query_proj, full_query.T, preferred_element_type=jnp.float32)
    summed = summed + jnp.dot(grad_key_proj, full_key.T, preferred_element_type=jnp.float32)
    grad_tokens = grad_tokens + lax.psum_scatter(
        (
            summed + jnp.dot(grad_value_proj, full_value.T, preferred_element_type=jnp.float32)
        ).astype(jnp.bfloat16),
        "mp",
        scatter_dimension=0,
        tiled=True,
    ).astype(jnp.float32)
    grad_sqk_full = lax.dynamic_update_slice_in_dim(
        jnp.zeros((D,), jnp.float32), grad_sqk_local, mp_index * head_width, 0
    )
    grad_sup_full = lax.dynamic_update_slice_in_dim(
        jnp.zeros((FF,), jnp.float32), grad_sup_local, mp_index * hidden_width, 0
    )
    grad_sgate_full = lax.dynamic_update_slice_in_dim(
        jnp.zeros((FF,), jnp.float32), grad_sgate_local, mp_index * hidden_width, 0
    )
    sharded = (
        lax.psum_scatter(grad_query_local, "dp", scatter_dimension=0, tiled=True),
        lax.psum_scatter(grad_key_local, "dp", scatter_dimension=0, tiled=True),
        lax.psum_scatter(grad_value_local, "dp", scatter_dimension=0, tiled=True),
        lax.psum_scatter(grad_out_local, "dp", scatter_dimension=1, tiled=True),
        lax.psum_scatter(grad_up_local, "dp", scatter_dimension=0, tiled=True),
        lax.psum_scatter(grad_gate_local, "dp", scatter_dimension=0, tiled=True),
        lax.psum_scatter(grad_down_local, "dp", scatter_dimension=1, tiled=True),
        lax.psum_scatter(grad_sqk_full, "dp", scatter_dimension=0, tiled=True),
        lax.psum_scatter(grad_sup_full, "dp", scatter_dimension=0, tiled=True),
        lax.psum_scatter(grad_sgate_full, "dp", scatter_dimension=0, tiled=True),
        lax.psum_scatter(grad_alpha_one, "dp", scatter_dimension=0, tiled=True),
        lax.psum_scatter(grad_alpha_two, "dp", scatter_dimension=0, tiled=True),
    )
    small_parts = (
        lax.psum_scatter(sharded[7], "mp", scatter_dimension=0, tiled=True),
        lax.psum_scatter(sharded[8], "mp", scatter_dimension=0, tiled=True),
        lax.psum_scatter(sharded[9], "mp", scatter_dimension=0, tiled=True),
        lax.psum_scatter(sharded[10], "mp", scatter_dimension=0, tiled=True),
        lax.psum_scatter(sharded[11], "mp", scatter_dimension=0, tiled=True),
    )
    pieces = tuple(sharded[:7]) + tuple(small_parts)
    squares = jnp.float32(0.0)
    for piece in pieces:
        squares = squares + jnp.sum(piece * piece)
    totals = lax.psum((squares, jnp.sum(alpha_attn), jnp.sum(alpha_mlp)), ("dp", "mp"))
    grad_norm = jnp.sqrt(totals[0])
    mean_alphas = jnp.stack([totals[1], totals[2]]) / D
    return (
        result.astype(jnp.bfloat16),
        grad_tokens,
        pieces[0],
        pieces[1],
        pieces[2],
        pieces[3],
        pieces[4],
        pieces[5],
        pieces[6],
        pieces[7],
        pieces[8],
        pieces[9],
        pieces[10],
        pieces[11],
        grad_norm,
        mean_alphas,
    )


def solution(mesh):
    in_specs = (
        P(("dp", "mp"), None),
        P(("dp", "mp"), None),
        P("dp", None),
        P("dp", None),
        P("dp", "mp"),
        P("dp", "mp"),
        P("dp", "mp"),
        P("mp", "dp"),
        P("dp", "mp"),
        P("dp", "mp"),
        P("mp", "dp"),
        P(("dp", "mp")),
        P(("dp", "mp")),
        P(("dp", "mp")),
        P(("dp", "mp")),
        P(("dp", "mp")),
    )
    out_specs = (
        P(("dp", "mp"), None),
        P(("dp", "mp"), None),
        P("dp", "mp"),
        P("dp", "mp"),
        P("dp", "mp"),
        P("mp", "dp"),
        P("dp", "mp"),
        P("dp", "mp"),
        P("mp", "dp"),
        P(("dp", "mp")),
        P(("dp", "mp")),
        P(("dp", "mp")),
        P(("dp", "mp")),
        P(("dp", "mp")),
        P(),
        P(),
    )
    return jax.shard_map(shards, mesh=mesh, in_specs=in_specs, out_specs=out_specs, check_vma=False)
```

profile of v0, /device:TPU:0, one launch (start us, length us, event | category | flops | bytes accessed | tf_op | source)
XLA Modules:
  0.0 1285.8 jit_solution(12886531379956318757)
XLA Ops:
  12.1 42.3 %all-reduce.16 = (f32[1024]{0:T(1024)S(1)}, f32[1024]{0:T(1024)S(1)}, f32[1024]{0:T(1024)S(1)}) all-reduce(f32[1024]{0:T(1024)S(1)} %dynamic-update-slice.29, f32[1024]{0:T(1024)S(1)} %dynamic-update-slice.28, f32[1024]{0:T(1024)S(1)} %dynamic-update-slice.30), channel_id=1, replica_groups=mesh['dp'=8,'mp'=4] {'dp','mp'}, use_global_device_ids=true, to_apply=%add.3 | all-reduce | flops 3072 | bytes 24576
  58.3 33.5 %all_gather.51 = bf16[1024,256]{1,0:T(8,128)(2,1)} all-gather(bf16[128,256]{1,0:T(8,128)(2,1)} %param.40), channel_id=1, replica_groups=mesh['dp'=8,'mp'=4] {'dp'}, dimensions={0}, use_global_device_ids=true | all-gather | bytes 589824 | tf_op jit(solution)/shard_map/all_gather | solution.py:165
  91.8 33.5 %all_gather.53 = bf16[1024,256]{1,0:T(8,128)(2,1)} all-gather(bf16[128,256]{1,0:T(8,128)(2,1)} %param.41), channel_id=1, replica_groups=mesh['dp'=8,'mp'=4] {'dp'}, dimensions={0}, use_global_device_ids=true | all-gather | bytes 589824 | tf_op jit(solution)/shard_map/all_gather | solution.py:166
  125.3 33.6 %all_gather.50 = bf16[1024,256]{1,0:T(8,128)(2,1)} all-gather(bf16[128,256]{1,0:T(8,128)(2,1)S(1)} %copy-done.78), channel_id=1, replica_groups=mesh['dp'=8,'mp'=4] {'dp'}, dimensions={0}, use_global_device_ids=true | all-gather | bytes 589824 | tf_op jit(solution)/shard_map/all_gather | solution.py:167
  158.9 28.1 %all_gather.54 = bf16[256,1024]{1,0:T(8,128)(2,1)} all-gather(bf16[256,128]{1,0:T(8,128)(2,1)S(1)} %copy-done.79), channel_id=1, replica_groups=mesh['dp'=8,'mp'=4] {'dp'}, dimensions={1}, use_global_device_ids=true | all-gather | bytes 589824 | tf_op jit(solution)/shard_map/all_gather | solution.py:168
  188.1 2.6 fusion.112
  192.3 3.8 fusion.18
  198.3 3.7 convolution_convert_fusion.3
  209.0 2.9 multiply_reduce_fusion.14
  217.2 3.0 fusion.133
  220.2 9.1 fusion.132
  236.8 3.4 fusion.104
  240.2 8.2 fusion
  248.4 7.5 fusion.105
  256.0 3.3 convolution_convert_fusion
  260.0 42.8 %reduce-scatter.12.cloned.1.call-done = bf16[512,1024]{1,0:T(8,128)(2,1)} async-done(((bf16[2048,1024]{1,0:T(8,128)(2,1)}), bf16[512,1024]{1,0:T(8,128)(2,1)}) %reduce-scatter.12.cloned.1.call-update) | async-done | bytes 1048592 | tf_op jit(solution)/shard_map/reduce_scatter | solution.py:228
  309.6 40.3 %all-gather = f32[32,1,128]{2,1,0:T(1,128)S(1)} all-gather(f32[1,1,128]{2,1,0:T(1,128)S(1)} %bitcast.245), channel_id=1, replica_groups=mesh['dp'=8,'mp'=4] {'dp','mp'}, dimensions={0}, use_global_device_ids=true | all-gather | bytes 16896 | tf_op jit(solution)/shard_map/all_gather | solution.py:176
  349.9 36.8 %all-gather.1 = f32[32,1,128]{2,1,0:T(1,128)S(1)} all-gather(f32[1,1,128]{2,1,0:T(1,128)S(1)} %bitcast.246), channel_id=1, replica_groups=mesh['dp'=8,'mp'=4] {'dp','mp'}, dimensions={0}, use_global_device_ids=true | all-gather | bytes 16896 | tf_op jit(solution)/shard_map/all_gather | solution.py:177
  386.7 10.7 fusion.138
  397.4 15.7 %multiply_convert_fusion.5 = (bf16[2048,1024]{1,0:T(8,128)(2,1)}, f32[2048,1024]{1,0:T(8,128)}) fusion(f32[2048,1024]{1,0:T(8,128)} %fusion.138, f32[1024]{0:T(1024)S(1)} %dynamic_slice.38, f32[1024]{0:T(1024)S(1)} %dynamic_slice.37, bf16[2048,1024]{1,0:T(8,128)(2,1)} %all-gather.12.cloned.1.call-done, bf16[1024,1024]{1,0:T(8,128)(2,1)} %all-gather.14.cloned.1.call-done), kind=kOutput, calls=%fused_computation.29 | convolution fusion | flops 4311744512 | bytes 27271168 | tf_op jit(solution)/shard_map/dot_general | solution.py:241
  413.1 35.1 %all-gather.18.cloned.1.call-done = bf16[1024,1024]{1,0:T(8,128)(2,1)} async-done(((bf16[1024,128]{1,0:T(8,128)(2,1)}), bf16[1024,1024]{1,0:T(8,128)(2,1)}) %all-gather.18.cloned.1.call-update) | async-done | bytes 2097168 | tf_op jit(solution)/shard_map/all_gather | solution.py:171
  448.1 9.6 convolution_convert_fusion.1
  457.8 42.8 %reduce-scatter.14.cloned.1.call-done = bf16[512,1024]{1,0:T(8,128)(2,1)} async-done(((bf16[2048,1024]{1,0:T(8,128)(2,1)}), bf16[512,1024]{1,0:T(8,128)(2,1)}) %reduce-scatter.14.cloned.1.call-update) | async-done | bytes 1048592 | tf_op jit(solution)/shard_map/reduce_scatter | solution.py:247
  502.2 2.6 multiply_reduce_fusion.11
  504.8 2.9 fusion.65
  509.7 2.6 fusion.63
  512.8 34.0 %all-gather.20.cloned.1.call-done = bf16[2048,1024]{1,0:T(8,128)(2,1)} async-done(((bf16[512,1024]{1,0:T(8,128)(2,1)}), bf16[2048,1024]{1,0:T(8,128)(2,1)}) %all-gather.20.cloned.1.call-update) | async-done | bytes 4194320 | tf_op jit(solution)/shard_map/all_gather | solution.py:263
  546.8 18.2 %multiply_reduce_fusion.2 = (f32[1024]{0:T(1024)}, f32[2048,1024]{1,0:T(8,128)}, f32[1024]{0:T(1024)}, f32[2048,1024]{1,0:T(8,128)}) fusion(f32[2048,1024]{1,0:T(8,128)} %fusion.138, f32[1024]{0:T(1024)S(1)} %dynamic_slice.38, f32[2048,1024]{1,0:T(8,128)} %get-tuple-element.356, f32[1024]{0:T(1024)S(1)} %dynamic_slice.37, ...), kind=kOutput, calls=%fused_computation.17 | convolution fusion | flops 4330616832 | bytes 39862272 | tf_op jit(solution)/shard_map/dot_general | solution.py:264
  565.0 10.4 fusion.84
  575.5 8.6 add_convert_fusion.1
  584.1 44.6 %reduce-scatter.16.cloned.1.call-done = bf16[512,1024]{1,0:T(8,128)(2,1)} async-done(((bf16[2048,1024]{1,0:T(8,128)(2,1)}), bf16[512,1024]{1,0:T(8,128)(2,1)}) %reduce-scatter.16.cloned.1.call-update) | async-done | bytes 1048592 | tf_op jit(solution)/shard_map/reduce_scatter | solution.py:276
  628.7 4.3 multiply_reduce_fusion.6
  633.0 4.1 multiply_reduce_fusion.7
  640.3 10.0 fusion.141
  650.4 11.2 fusion.83
  662.5 11.3 fusion.85
  674.8 3.6 convolution_convert_fusion.2
  681.6 3.6 fusion.101
  685.3 3.0 multiply_reduce_fusion.4
  694.7 6.1 multiply_reduce_fusion.1
  700.8 10.1 multiply_convert_fusion.1
  711.0 2.8 convolution_multiply_fusion.4
  715.0 2.3 fusion.28
  717.4 8.5 multiply_reduce_fusion
  725.9 11.2 multiply_convert_fusion
  737.2 6.6 convolution_multiply_fusion.3
  743.9 5.4 add_reduce_fusion
  758.6 3.2 fusion.98
  764.5 5.2 fusion.95
  769.7 6.0 fusion.40
  775.8 8.0 fusion.52
  784.8 2.3 convolution_bitcast_fusion
  787.2 4.6 fusion.125
  794.7 3.3 add_convert_fusion
  806.1 52.8 %reduce-scatter.28.cloned.1.call-done = f32[128,1024]{1,0:T(8,128)} async-done(((f32[1024,1024]{1,0:T(8,128)}), f32[128,1024]{1,0:T(8,128)}) %reduce-scatter.28.cloned.1.call-update) | async-done | bytes 524304 | tf_op jit(solution)/shard_map/reduce_scatter | solution.py:348
  860.7 90.2 %reduce-scatter.30.cloned.1.call-done = f32[128,1024]{1,0:T(8,128)} async-done(((f32[1024,1024]{1,0:T(8,128)}), f32[128,1024]{1,0:T(8,128)}) %reduce-scatter.30.cloned.1.call-update) | async-done | bytes 524304 | tf_op jit(solution)/shard_map/reduce_scatter | solution.py:349
  953.0 36.7 %all-reduce.17 = (f32[1024]{0:T(1024)S(1)}, f32[4096]{0:T(1024)S(1)}, f32[4096]{0:T(1024)S(1)}, f32[1024]{0:T(1024)S(1)}, f32[1024]{0:T(1024)S(1)}) all-reduce(f32[1024]{0:T(1024)S(1)} %dynamic_update_slice.22, f32[4096]{0:T(1024)S(1)} %dynamic_update_slice.23, ...), channel_id=13, replica_groups=mesh['dp'=8,'mp'=4] {'dp'}, use_global_device_ids=true, to_apply=%region_39.40.clone | all-reduce | flops 11264 | bytes 90112
  990.1 5.9 all-reduce.18
  1002.0 16.1 %reduce-scatter.20.cloned.1.call-done = f32[128,256]{0,1:T(8,128)} async-done(((f32[1024,256]{0,1:T(8,128)}), f32[128,256]{0,1:T(8,128)}) %reduce-scatter.20.cloned.1.call-update) | async-done | bytes 131088 | tf_op jit(solution)/shard_map/reduce_scatter | solution.py:344
  1019.7 65.3 %reduce-scatter.22.cloned.1.call-done = f32[128,256]{0,1:T(8,128)} async-done(((f32[1024,256]{0,1:T(8,128)}), f32[128,256]{0,1:T(8,128)}) %reduce-scatter.22.cloned.1.call-update) | async-done | bytes 131088 | tf_op jit(solution)/shard_map/reduce_scatter | solution.py:345
  1087.7 63.9 %reduce-scatter.24.cloned.1.call-done = f32[128,256]{0,1:T(8,128)} async-done(((f32[1024,256]{0,1:T(8,128)}), f32[128,256]{0,1:T(8,128)}) %reduce-scatter.24.cloned.1.call-update) | async-done | bytes 131088 | tf_op jit(solution)/shard_map/reduce_scatter | solution.py:346
  1153.7 65.2 %reduce-scatter.26.cloned.1.call-done = f32[256,128]{1,0:T(8,128)} async-done(((f32[256,1024]{1,0:T(8,128)}), f32[256,128]{1,0:T(8,128)}) %reduce-scatter.26.cloned.1.call-update) | async-done | bytes 131088 | tf_op jit(solution)/shard_map/reduce_scatter | solution.py:347
  1226.3 40.4 %all-reduce.15 = (f32[]{:T(128)}, f32[1]{0:T(128)}, f32[1]{0:T(128)}) all-reduce(f32[]{:T(128)S(6)} %add.377, f32[1]{0:T(128)} %bitcast.58, f32[1]{0:T(128)} %bitcast.57), channel_id=1, replica_groups=mesh['dp'=8,'mp'=4] {'dp','mp'}, use_global_device_ids=true, to_apply=%region_65.66 | all-reduce | flops 3 | bytes 24 | tf_op jit(solution)/shard_map/psum | solution.py:368
  1274.2 2.9 convert_add_fusion.1
  (408 shorter events, 103.9 us)
Async XLA Ops:
  8.0 117.3 %copy-start.78 = (bf16[128,256]{1,0:T(8,128)(2,1)S(1)}, bf16[128,256]{1,0:T(8,128)(2,1)}, u32[]{:S(2)}) copy-start(bf16[128,256]{1,0:T(8,128)(2,1)} %param.42) | copy-start | bytes 196612
  8.0 150.9 %copy-start.79 = (bf16[256,128]{1,0:T(8,128)(2,1)S(1)}, bf16[256,128]{1,0:T(8,128)(2,1)}, u32[]{:S(2)}) copy-start(bf16[256,128]{1,0:T(8,128)(2,1)} %param.43) | copy-start | bytes 196612
  8.0 190.2 %all-gather.10.cloned.1.call-start = ((), (), s32[]{:S(2)}) async-start(), calls=%async_computation.11 | async-start | bytes 5242880 | tf_op jit(solution)/shard_map/all_gather | solution.py:193
  8.8 294.0 %reduce-scatter.12.cloned.1.call-start = ((), (), s32[]{:S(2)}) async-start(), calls=%async_computation.12 | async-start | bytes 5242880 | tf_op jit(solution)/shard_map/reduce_scatter | solution.py:228
  54.4 582.8 %copy-start.67 = (f32[1024]{0:T(1024)}, f32[1024]{0:T(1024)S(1)}, u32[]{:S(2)}) copy-start(f32[1024]{0:T(1024)S(1)} %get-tuple-element.286) | copy-start | bytes 12292
  54.6 157.3 %copy-start.76 = (f32[4,64]{1,0:T(4,128)}, f32[4,64]{1,0:T(4,128)S(1)}, u32[]{:S(2)}) copy-start(f32[4,64]{1,0:T(4,128)S(1)} %mul.607) | copy-start | bytes 3076
  190.6 17.2 %copy-start.27 = (f32[2048,64]{0,1:T(8,128)}, f32[2048,64]{0,1:T(8,128)S(1)}, u32[]{:S(2)}) copy-start(f32[2048,64]{0,1:T(8,128)S(1)} %get-tuple-element.337) | copy-start | bytes 1572868
  202.0 46.4 %copy-start.23 = (bf16[2048,256]{0,1:T(8,128)(2,1)}, bf16[2048,256]{0,1:T(8,128)(2,1)S(1)}, u32[]{:S(2)}) copy-start(bf16[2048,256]{0,1:T(8,128)(2,1)S(1)} %convolution_convert_fusion.3) | copy-start | bytes 3145732
  202.1 27.8 %copy-start.61 = (bf16[512,256]{0,1:T(8,128)(2,1)}, bf16[512,256]{0,1:T(8,128)(2,1)S(1)}, u32[]{:S(2)}) copy-start(bf16[512,256]{0,1:T(8,128)(2,1)S(1)} %slice.481) | copy-start | bytes 786436
  213.9 6.3 copy-start.14
  215.4 14.5 %copy-start.5 = (f32[4,512,512]{1,2,0:T(8,128)}, f32[4,512,512]{1,2,0:T(8,128)S(1)}, u32[]{:S(2)}) copy-start(f32[4,512,512]{1,2,0:T(8,128)S(1)} %get-tuple-element.354) | copy-start | bytes 12582916
  215.4 14.5 %copy-start.80 = (f32[4,512]{1,0:T(4,128)}, f32[4,512]{1,0:T(4,128)S(1)}, u32[]{:S(2)}) copy-start(f32[4,512]{1,0:T(4,128)S(1)} %get-tuple-element.353) | copy-start | bytes 24580
  217.2 15.5 %copy-start.1 = (f32[4,512,1024]{2,1,0:T(8,128)}, f32[4,512,1024]{2,1,0:T(8,128)S(1)}, u32[]{:S(2)}) copy-start(f32[4,512,1024]{2,1,0:T(8,128)S(1)} %get-tuple-element.352) | copy-start | bytes 25165828
  217.2 15.5 %copy-start.84 = (f32[4,512]{1,0:T(4,128)}, f32[4,512]{1,0:T(4,128)S(1)}, u32[]{:S(2)}) copy-start(f32[4,512]{1,0:T(4,128)S(1)} %get-tuple-element.351) | copy-start | bytes 24580
  220.2 16.5 %copy-start = (f32[4,512,1536]{2,1,0:T(8,128)}, f32[4,512,1536]{2,1,0:T(8,128)S(1)}, u32[]{:S(2)}) copy-start(f32[4,512,1536]{2,1,0:T(8,128)S(1)} %get-tuple-element.350) | copy-start | bytes 37748740
  230.8 25.2 %copy-start.105 = (bf16[4,64,512]{2,1,0:T(8,128)(2,1)}, bf16[4,64,512]{2,1,0:T(8,128)(2,1)S(1)}, u32[]{:S(2)}) copy-start(bf16[4,64,512]{2,1,0:T(8,128)(2,1)S(1)} %fusion.102) | copy-start | bytes 786436
  234.9 21.1 %copy-start.107 = (bf16[4,64,512]{2,1,0:T(8,128)(2,1)}, bf16[4,64,512]{2,1,0:T(8,128)(2,1)S(1)}, u32[]{:S(2)}) copy-start(bf16[4,64,512]{2,1,0:T(8,128)(2,1)S(1)} %fusion.103) | copy-start | bytes 786436
  240.2 15.8 %copy-start.109 = (bf16[4,64,512]{2,1,0:T(8,128)(2,1)}, bf16[4,64,512]{2,1,0:T(8,128)(2,1)S(1)}, u32[]{:S(2)}) copy-start(bf16[4,64,512]{2,1,0:T(8,128)(2,1)S(1)} %fusion.104) | copy-start | bytes 786436
  248.4 7.6 copy-start.64
  259.3 45.1 %copy-start.3 = (bf16[512,1024]{1,0:T(8,128)(2,1)S(1)}, bf16[512,1024]{1,0:T(8,128)(2,1)}, u32[]{:S(2)}) copy-start(bf16[512,1024]{1,0:T(8,128)(2,1)} %param.36) | copy-start | bytes 3145732
  259.4 127.3 %all-gather.16.cloned.1.call-start = ((), (), s32[]{:S(2)}) async-start(), calls=%async_computation.15 | async-start | bytes 2359296 | tf_op jit(solution)/shard_map/all_gather | solution.py:170
  259.9 126.7 %all-gather.12.cloned.1.call-start = ((), (), s32[]{:S(2)}) async-start(), calls=%async_computation.13 | async-start | bytes 5242880 | tf_op jit(solution)/shard_map/all_gather | solution.py:240
  306.5 43.4 %copy-start.96 = (f32[128]{0:T(128)S(1)}, f32[128]{0:T(128)}, u32[]{:S(2)}) copy-start(f32[128]{0:T(128)} %param.49) | copy-start | bytes 1540
  308.2 89.2 %all-gather.14.cloned.1.call-start = ((), (), s32[]{:S(2)}) async-start(), calls=%async_computation.14 | async-start | bytes 2359296 | tf_op jit(solution)/shard_map/all_gather | solution.py:169
  308.8 139.4 %all-gather.18.cloned.1.call-start = ((), (), s32[]{:S(2)}) async-start(), calls=%async_computation.16 | async-start | bytes 2359296 | tf_op jit(solution)/shard_map/all_gather | solution.py:171
  309.5 191.1 %reduce-scatter.14.cloned.1.call-start = ((), (), s32[]{:S(2)}) async-start(), calls=%async_computation.17 | async-start | bytes 5242880 | tf_op jit(solution)/shard_map/reduce_scatter | solution.py:247
  457.7 89.1 %all-gather.20.cloned.1.call-start = ((), (), s32[]{:S(2)}) async-start(), calls=%async_computation.18 | async-start | bytes 5242880 | tf_op jit(solution)/shard_map/all_gather | solution.py:263
  512.4 116.3 %reduce-scatter.16.cloned.1.call-start = ((), (), s32[]{:S(2)}) async-start(), calls=%async_computation.19 | async-start | bytes 5242880 | tf_op jit(solution)/shard_map/reduce_scatter | solution.py:276
  546.8 18.2 %copy-start.102 = (bf16[1024,1024]{1,0:T(8,128)(2,1)S(1)}, bf16[1024,1024]{1,0:T(8,128)(2,1)}, u32[]{:S(2)}) copy-start(bf16[1024,1024]{1,0:T(8,128)(2,1)} %all-gather.14.cloned.1.call-done) | copy-start | bytes 6291460
  565.0 10.4 copy-start.25
  565.0 10.4 copy-start.101
  584.1 90.5 %all-gather.22.cloned.1.call-start = ((), (), s32[]{:S(2)}) async-start(), calls=%async_computation.20 | async-start | bytes 5242880 | tf_op jit(solution)/shard_map/all_gather | solution.py:289
  640.1 164.1 %reduce-scatter.32.cloned.1.call-start = ((), (), s32[]{:S(2)}) async-start(), calls=%async_computation.28 | async-start | bytes 4718592 | tf_op jit(solution)/shard_map/reduce_scatter | solution.py:350
  650.4 208.5 %reduce-scatter.28.cloned.1.call-start = ((), (), s32[]{:S(2)}) async-start(), calls=%async_computation.26 | async-start | bytes 4718592 | tf_op jit(solution)/shard_map/reduce_scatter | solution.py:348
  661.7 289.3 %reduce-scatter.30.cloned.1.call-start = ((), (), s32[]{:S(2)}) async-start(), calls=%async_computation.27 | async-start | bytes 4718592 | tf_op jit(solution)/shard_map/reduce_scatter | solution.py:349
  662.4 17.9 %copy-start.74 = (f32[4,512]{1,0:T(4,128)}, f32[4,512]{1,0:T(4,128)S(1)}, u32[]{:S(2)}) copy-start(f32[4,512]{1,0:T(4,128)S(1)} %log_add_fusion.3) | copy-start | bytes 24580
  662.4 25.8 %copy-start.72 = (f32[4,512]{1,0:T(4,128)}, f32[4,512]{1,0:T(4,128)S(1)}, u32[]{:S(2)}) copy-start(f32[4,512]{1,0:T(4,128)S(1)} %log_add_fusion.2) | copy-start | bytes 24580
  662.5 38.4 %copy-start.70 = (f32[4,512]{1,0:T(4,128)}, f32[4,512]{1,0:T(4,128)S(1)}, u32[]{:S(2)}) copy-start(f32[4,512]{1,0:T(4,128)S(1)} %log_add_fusion.1) | copy-start | bytes 24580
  673.8 344.4 %reduce-scatter.20.cloned.1.call-start = ((), (), s32[]{:S(2)}) async-start(), calls=%async_computation.22 | async-start | bytes 1179648 | tf_op jit(solution)/shard_map/reduce_scatter | solution.py:344
  681.6 6.7 copy-start.19
  688.3 6.3 slice-start.4
  688.3 6.3 slice-start.5
  700.8 16.5 %slice-start = ((s8[16777216]{0:T(1024)(128)(4,1)}), s8[4194304]{0:T(1024)(128)(4,1)S(1)}, s32[]{:S(2)}) async-start(s8[16777216]{0:T(1024)(128)(4,1)} %bitcast.193), calls=%async_computation.29 | async-start | bytes 8388608
  700.8 16.5 %slice-start.1 = ((s8[16777216]{0:T(1024)(128)(4,1)}), s8[4194304]{0:T(1024)(128)(4,1)S(1)}, s32[]{:S(2)}) async-start(s8[16777216]{0:T(1024)(128)(4,1)} %bitcast.193), calls=%async_computation.30 | async-start | bytes 8388608
  700.8 16.5 %slice-start.2 = ((s8[16777216]{0:T(1024)(128)(4,1)}), s8[4194304]{0:T(1024)(128)(4,1)S(1)}, s32[]{:S(2)}) async-start(s8[16777216]{0:T(1024)(128)(4,1)} %bitcast.193), calls=%async_computation.31 | async-start | bytes 8388608
  711.0 6.4 slice-start.3
  717.3 8.5 copy-start.16
  725.9 17.9 %copy-start.9 = (f32[2048,4,64]{0,2,1:T(8,128)S(1)}, f32[2048,4,64]{0,2,1:T(8,128)}, u32[]{:S(2)}) copy-start(f32[2048,4,64]{0,2,1:T(8,128)} %copy-done.8) | copy-start | bytes 6291460
  725.9 17.9 %copy-start.11 = (f32[2048,4,64]{0,2,1:T(8,128)S(1)}, f32[2048,4,64]{0,2,1:T(8,128)}, u32[]{:S(2)}) copy-start(f32[2048,4,64]{0,2,1:T(8,128)} %copy-done.10) | copy-start | bytes 6291460
  725.9 17.9 %copy-start.58 = (f32[2048,4]{0,1:T(4,128)S(1)}, f32[2048,4]{0,1:T(4,128)}, u32[]{:S(2)}) copy-start(f32[2048,4]{0,1:T(4,128)} %copy-done.57) | copy-start | bytes 98308
  737.1 6.7 copy-start.4
  737.1 6.7 copy-start.29
  737.1 6.7 copy-start.30
  737.2 6.7 copy-start.31
  737.2 6.7 copy-start.77
  758.6 326.4 %reduce-scatter.22.cloned.1.call-start = ((), (), s32[]{:S(2)}) async-start(), calls=%async_computation.23 | async-start | bytes 1179648 | tf_op jit(solution)/shard_map/reduce_scatter | solution.py:345
  764.5 387.0 %reduce-scatter.24.cloned.1.call-start = ((), (), s32[]{:S(2)}) async-start(), calls=%async_computation.24 | async-start | bytes 1179648 | tf_op jit(solution)/shard_map/reduce_scatter | solution.py:346
  775.8 9.0 copy-start.100
  787.1 431.8 %reduce-scatter.26.cloned.1.call-start = ((), (), s32[]{:S(2)}) async-start(), calls=%async_computation.25 | async-start | bytes 1179648 | tf_op jit(solution)/shard_map/reduce_scatter | solution.py:347
  791.9 482.3 %reduce-scatter.18.cloned.1.call-start = ((), (), s32[]{:S(2)}) async-start(), calls=%async_computation.21 | async-start | bytes 5242880 | tf_op jit(solution)/shard_map/reduce_scatter | solution.py:326
  798.0 154.8 %copy-start.92 = (f32[4,64]{1,0:T(4,128)S(1)}, f32[4,64]{1,0:T(4,128)}, u32[]{:S(2)}) copy-start(f32[4,64]{1,0:T(4,128)} %get-tuple-element.273) | copy-start | bytes 3076
  798.0 155.0 %copy-start.88 = (f32[1024]{0:T(1024)S(1)}, f32[1024]{0:T(1024)}, u32[]{:S(2)}) copy-start(f32[1024]{0:T(1024)} %get-tuple-element.278) | copy-start | bytes 12292
  798.0 155.0 %copy-start.89 = (f32[1024]{0:T(1024)S(1)}, f32[1024]{0:T(1024)}, u32[]{:S(2)}) copy-start(f32[1024]{0:T(1024)} %get-tuple-element.276) | copy-start | bytes 12292
  798.0 476.2 %copy-start.18 = (f32[512,1024]{1,0:T(8,128)S(1)}, f32[512,1024]{1,0:T(8,128)}, u32[]{:S(2)}) copy-start(f32[512,1024]{1,0:T(8,128)} %copy-done.17) | copy-start | bytes 6291460
  (77 other events, 204.9 us)
Sparse Core Ops, SparseCore 0:
  10.4 37.4 all-gather.9
  259.5 43.2 reduce-scatter.11
  457.9 42.6 reduce-scatter.13
  584.2 44.4 reduce-scatter.15
Sparse Core Ops, SparseCore 1:
  262.2 47.9 all-gather.15
  312.3 32.9 all-gather.11
  347.4 49.3 all-gather.13
  399.0 49.0 all-gather.17
  512.5 34.3 all-gather.19
  640.2 34.3 all-gather.21
  679.1 88.2 reduce-scatter.31
  771.4 87.5 reduce-scatter.27
  863.4 87.5 reduce-scatter.29
  954.4 63.7 reduce-scatter.19
  1021.8 63.1 reduce-scatter.21
  1088.4 63.1 reduce-scatter.23
  1155.8 63.1 reduce-scatter.25
  1221.5 43.8 reduce-scatter.17
where the time goes:
time: 1290 us
  waiting for transfers between devices  556 us (43%)
  blocking collectives  331 us (26%)
  matrix products  232 us (18%)
  other arithmetic  111 us (9%)
  between operations  29.6 us (2%)
  local copies, waits for them, and re-layouts  24.4 us (2%)
    reduce_scatter x1, waiting for transfers between devices, shards(): lax.psum_scatter(grad_gate_local, 'dp', scatter_dimension=0, tiled=True)  90.2 us
    unnamed x3, blocking collectives  84.9 us
    reduce_scatter x1, waiting for transfers between devices, shards(): lax.psum_scatter(grad_key_local, 'dp', scatter_dimension=0, tiled=True)  65.3 us
    reduce_scatter x1, waiting for transfers between devices, shards(): lax.psum_scatter(grad_out_local, 'dp', scatter_dimension=1, tiled=True)  65.2 us
    reduce_scatter x1, waiting for transfers between devices, shards(): lax.psum_scatter(grad_value_local, 'dp', scatter_dimension=0, tiled=True)  63.9 us
    reduce_scatter x1, waiting for transfers between devices, shards(): lax.psum_scatter(grad_up_local, 'dp', scatter_dimension=0, tiled=True)  52.8 us
    reduce_scatter x1, waiting for transfers between devices, shards(): lax.psum_scatter((jnp.dot(up_rows, full_up.T, preferred_element_type=jnp....  44.6 us
    reduce_scatter x1, waiting for transfers between devices, shards(): lax.psum_scatter(jnp.dot(lax.slice_in_dim(attended, 0, local_rows * lax.a...  42.8 us
  transfers between devices with their start and end apart: 18, of which 12 were waited for; matrix products, arithmetic and copies ran while one was open for 18% of the time, Pallas kernels for 0%

commit v1 on v0

v1 whole, which is shorter than its diff:
```python
import functools

import jax
import jax.numpy as jnp
from jax import lax
from jax.experimental import pallas as pl
from jax.experimental.pallas import tpu as pltpu
from jax.sharding import PartitionSpec as P

D = 1024
HEADS = 16
HEAD = D // HEADS
EPS = 1e-06
BLOCK = 256
F32 = jnp.float32
BF16 = jnp.bfloat16


def rms_rows(tensor):
    factor = lax.rsqrt(jnp.mean(tensor * tensor, axis=-1, keepdims=True) + EPS)
    return (tensor * factor, factor)


def rms_back(incoming, normed, factor):
    return factor * (incoming - normed * jnp.mean(incoming * normed, axis=-1, keepdims=True))


def dot(left, right, left_dim=1, right_dim=0):
    return lax.dot_general(
        left, right, (((left_dim,), (right_dim,)), ((), ())), preferred_element_type=F32
    )


def swap(array, axis, bit):
    size = lax.axis_size(axis)
    return lax.ppermute(array, axis, [(i, i ^ bit) for i in range(size)])


def from_z(array, step):
    return lax.ppermute(
        array, "dp", [(((z + step) % 4) * 2 + y, z * 2 + y) for z in range(4) for y in range(2)]
    )


def to_z(array, step):
    return lax.ppermute(
        array, "dp", [(z * 2 + y, ((z + step) % 4) * 2 + y) for z in range(4) for y in range(2)]
    )


def gather(weight, axis, after):
    if lax.axis_size("dp") != 8:
        return lax.all_gather(weight, "dp", axis=axis, tiled=True), ()
    if after:
        weight = lax.optimization_barrier((weight,) + tuple(after))[0]
    parts = [from_z(weight, step) for step in (1, 2, 3)]
    half = jnp.concatenate([weight] + parts, axis=axis)
    other = swap(half, "dp", 1)
    return jnp.concatenate([half, other], axis=axis), tuple(parts)


def scatter(grad, axis):
    if lax.axis_size("dp") != 8:
        return lax.psum_scatter(grad.astype(F32), "dp", scatter_dimension=axis, tiled=True)
    size = grad.shape[axis] // 8
    mine = lax.slice_in_dim(grad, 0, 4 * size, axis=axis)
    theirs = lax.slice_in_dim(grad, 4 * size, 8 * size, axis=axis)
    half = mine.astype(F32) + swap(theirs.astype(BF16), "dp", 1).astype(F32)
    total = lax.slice_in_dim(half, 0, size, axis=axis)
    for step in (1, 2, 3):
        part = lax.slice_in_dim(half, step * size, (step + 1) * size, axis=axis)
        total = total + to_z(part.astype(BF16), step).astype(F32)
    return total


def reduce_pair(remote, local):
    rows = local.shape[0] // 2
    for_x = remote[:rows].astype(F32) + swap(remote[rows:].astype(BF16), "mp", 1).astype(F32)
    from_x = swap(for_x.astype(BF16), "mp", 2)
    mine = local[:rows].astype(F32) + swap(local[rows:].astype(BF16), "mp", 1).astype(F32)
    return mine + from_x.astype(F32)


def spread(own):
    local = jnp.concatenate([own, swap(own, "mp", 1)], axis=0)
    over_x = swap(own, "mp", 2)
    remote = jnp.concatenate([over_x, swap(over_x, "mp", 1)], axis=0)
    return local, remote


def pick_cols(array, table):
    rows, cols = array.shape

    def body(table_ref, in_ref, out_ref):
        out_ref[...] = in_ref[...]

    return pl.pallas_call(
        body,
        out_shape=jax.ShapeDtypeStruct(array.shape, array.dtype),
        grid_spec=pltpu.PrefetchScalarGridSpec(
            num_scalar_prefetch=1,
            grid=(8,),
            in_specs=[pl.BlockSpec((rows, cols // 8), lambda i, t: (0, t[i]))],
            out_specs=pl.BlockSpec((rows, cols // 8), lambda i, t: (0, i)),
        ),
        cost_estimate=pl.CostEstimate(
            flops=0, bytes_accessed=2 * array.size * array.dtype.itemsize, transcendentals=0
        ),
        name="pick_cols",
    )(table, array)


def rotate_half(tensor):
    width = tensor.shape[-1]
    lane = lax.broadcasted_iota(jnp.int32, tensor.shape, 1)
    ahead = pltpu.roll(tensor, width - HEAD // 2, 1)
    behind = pltpu.roll(tensor, HEAD // 2, 1)
    return jnp.where((lane & (HEAD - 1)) < HEAD // 2, -ahead, behind)


def head_mean(tensor):
    width = tensor.shape[-1]
    row = lax.broadcasted_iota(jnp.int32, (width, width), 0) // HEAD
    col = lax.broadcasted_iota(jnp.int32, (width, width), 1) // HEAD
    ones = jnp.where(row == col, 1.0 / HEAD, 0.0).astype(F32)
    return jnp.dot(tensor, ones, precision=lax.Precision.HIGHEST, preferred_element_type=F32)


def wide(table):
    return jnp.concatenate([table, table], axis=1)


def project_body(m_ref, x_ref, wq_ref, wk_ref, wv_ref, cos_ref, sin_ref, sqk_ref, *refs):
    q_ref, k_ref, v_ref, qr_ref, kr_ref = refs[-5:]
    rows = x_ref[...]
    cosine, sine = wide(cos_ref[...]), wide(sin_ref[...])
    scale = sqk_ref[0:1, :]
    for weight_ref, out_ref, rot_ref in ((wq_ref, q_ref, qr_ref), (wk_ref, k_ref, kr_ref)):
        raw = jnp.dot(rows, weight_ref[...], preferred_element_type=F32)
        turned = raw * cosine + rotate_half(raw) * sine
        rot_ref[...] = turned
        unit = turned * lax.rsqrt(head_mean(turned * turned) + EPS)
        out_ref[...] = (unit * scale).astype(BF16)
    v_ref[...] = jnp.dot(rows, wv_ref[...], preferred_element_type=F32).astype(BF16)


def project(place, x_rows, weights, cosine, sine, sqk, previous, first):
    rows, width = x_rows.shape[0], weights[0].shape[1]
    total = cosine.shape[0]
    per = total // 4 // BLOCK

    def row_block(i, m):
        return ((m[0] ^ (first + i // per)) * per + i % per, 0)

    any_spec = pl.BlockSpec(memory_space=pl.ANY)
    whole = pl.BlockSpec((x_rows.shape[1], width), lambda i, m: (0, 0))
    table = pl.BlockSpec((BLOCK, cosine.shape[1]), row_block)
    out = pl.BlockSpec((BLOCK, width), row_block)
    shapes = [jax.ShapeDtypeStruct((total, width), t) for t in (BF16, BF16, BF16, F32, F32)]
    extra = list(previous) if previous is not None else []
    return pl.pallas_call(
        project_body,
        out_shape=shapes,
        grid_spec=pltpu.PrefetchScalarGridSpec(
            num_scalar_prefetch=1,
            grid=(rows // BLOCK,),
            in_specs=[
                pl.BlockSpec((BLOCK, x_rows.shape[1]), lambda i, m: (i, 0)),
                whole,
                whole,
                whole,
                table,
                table,
                pl.BlockSpec((8, width), lambda i, m: (0, 0)),
            ]
            + [any_spec] * len(extra),
            out_specs=[out] * 5,
        ),
        input_output_aliases={8 + i: i for i in range(len(extra))},
        cost_estimate=pl.CostEstimate(
            flops=6 * rows * D * width, bytes_accessed=8 * rows * D, transcendentals=rows
        ),
        name="project",
    )(place, x_rows, *weights, cosine, sine, sqk, *extra)


def head_lanes(array, head):
    lane = lax.broadcasted_iota(jnp.int32, array.shape, 1)
    return jnp.where(lane // HEAD == head, array, jnp.zeros_like(array))


def stack_heads(array):
    heads = array.shape[1] // HEAD
    return jnp.concatenate([head_lanes(array, h) for h in range(heads)], axis=0)


def doc_start(meta_ref, docs, slots):
    start = jnp.zeros_like(slots)
    end = 0
    for i in range(docs):
        length = meta_ref[1 + i]
        end = end + length
        start = start + jnp.where(slots >= end, length, 0)
    return start


def attend_body(docs, meta_ref, q_ref, k_ref, v_ref, kpos_ref, o_ref, inv_ref, acc_ref, sum_ref):
    step = pl.program_id(0)
    heads = q_ref.shape[1] // HEAD
    base = step * BLOCK
    low = doc_start(meta_ref, docs, base) // BLOCK
    queries = stack_heads(q_ref[...] * jnp.bfloat16(HEAD**-0.5))
    rows = lax.broadcasted_iota(jnp.int32, (BLOCK, BLOCK), 0) + base
    starts = doc_start(meta_ref, docs, rows)
    acc_ref[...] = jnp.zeros_like(acc_ref)
    sum_ref[...] = jnp.zeros_like(sum_ref)

    def visit(block, allowed):
        at = pl.ds(pl.multiple_of(block * BLOCK, BLOCK), BLOCK)
        keys, vals = k_ref[at, :], v_ref[at, :]
        scores = dot(queries, keys, 1, 1)
        total = acc_ref[...]
        for h in range(heads):
            part = slice(h * BLOCK, (h + 1) * BLOCK)
            expo = jnp.where(allowed, jnp.exp(scores[part]), 0.0)
            sum_ref[part, :] += expo[:, :128] + expo[:, 128:]
            total = total + dot(expo.astype(BF16), head_lanes(vals, h))
        acc_ref[...] = total

    def off_diagonal(block, carry):
        at = pl.ds(pl.multiple_of(block * BLOCK, BLOCK), BLOCK)
        visit(block, kpos_ref[0:1, at] >= starts)
        return carry

    lax.fori_loop(low, step, off_diagonal, 0)
    cols = lax.broadcasted_iota(jnp.int32, (BLOCK, BLOCK), 1) + base
    at = pl.ds(pl.multiple_of(base, BLOCK), BLOCK)
    visit(step, ((kpos_ref[0:1, at] >= starts) & (cols <= rows)) | (cols == rows))
    lane = lax.broadcasted_iota(jnp.int32, (BLOCK, q_ref.shape[1]), 1) // HEAD
    inverse = jnp.zeros((BLOCK, q_ref.shape[1]), F32)
    for h in range(heads):
        mass = jnp.sum(sum_ref[h * BLOCK : (h + 1) * BLOCK, :], axis=1, keepdims=True)
        inverse = jnp.where(lane == h, 1.0 / mass, inverse)
    inv_ref[...] = inverse
    o_ref[...] = (acc_ref[...] * inverse).astype(BF16)


def attend(meta, queries, keys, vals, kpos, docs):
    total, width = queries.shape
    per = total // 4 // BLOCK
    heads = width // HEAD
    whole = pl.BlockSpec((total, width), lambda i, m: (0, 0))
    block = pl.BlockSpec((BLOCK, width), lambda i, m: (i, 0))

    def rel(i, m):
        return ((m[0] ^ (i // per)) * per + i % per, 0)

    return pl.pallas_call(
        functools.partial(attend_body, docs),
        out_shape=[
            jax.ShapeDtypeStruct((total, width), BF16),
            jax.ShapeDtypeStruct((total, width), F32),
        ],
        grid_spec=pltpu.PrefetchScalarGridSpec(
            num_scalar_prefetch=1,
            grid=(total // BLOCK,),
            in_specs=[block, whole, whole, pl.BlockSpec((8, total), lambda i, m: (0, 0))],
            out_specs=[pl.BlockSpec((BLOCK, width), rel), block],
            scratch_shapes=[
                pltpu.VMEM((BLOCK, width), F32),
                pltpu.VMEM((heads * BLOCK, 128), F32),
            ],
        ),
        cost_estimate=pl.CostEstimate(
            flops=12_000_000_000, bytes_accessed=8 * total * width, transcendentals=6_000_000
        ),
        name="attend",
    )(meta, queries, keys, vals, kpos)


def finish(grad, turned, cosine, sine, scale):
    factor = lax.rsqrt(head_mean(turned * turned) + EPS)
    unit = turned * factor
    by_scale = jnp.sum(grad * unit, axis=0, keepdims=True)
    scaled = grad * scale
    back = factor * (scaled - unit * head_mean(scaled * unit))
    raw = back * cosine - rotate_half(back) * sine
    return raw.astype(BF16), by_scale


def back_body(
    docs,
    meta_ref,
    q_ref,
    qr_ref,
    o_ref,
    inv_ref,
    do_ref,
    k_ref,
    v_ref,
    kr_ref,
    kpos_ref,
    cos_ref,
    sin_ref,
    sqk_ref,
    gq_ref,
    gk_ref,
    gv_ref,
    gs_ref,
    dq_ref,
    dk_ref,
    dv_ref,
):
    step = pl.program_id(0)
    width = q_ref.shape[1]
    heads = width // HEAD
    per = k_ref.shape[0] // 4 // BLOCK
    base = step * BLOCK
    low = doc_start(meta_ref, docs, base) // BLOCK

    @pl.when(step == 0)
    def _():
        dk_ref[...] = jnp.zeros_like(dk_ref)
        dv_ref[...] = jnp.zeros_like(dv_ref)
        gs_ref[...] = jnp.zeros_like(gs_ref)

    dq_ref[...] = jnp.zeros_like(dq_ref)
    queries = stack_heads(q_ref[...] * jnp.bfloat16(HEAD**-0.5))
    upward = do_ref[...].astype(F32) * inv_ref[...]
    ups = stack_heads(upward.astype(BF16))
    picks = lax.broadcasted_iota(jnp.int32, (8, width), 0)
    lanes = lax.broadcasted_iota(jnp.int32, (8, width), 1) // HEAD
    delta = lax.dot_general(
        jnp.where(picks == lanes, 1.0, 0.0).astype(F32),
        upward * o_ref[...].astype(F32),
        (((1,), (1,)), ((), ())),
        precision=lax.Precision.HIGHEST,
        preferred_element_type=F32,
    )
    cols = lax.broadcasted_iota(jnp.int32, (BLOCK, BLOCK), 1) + base
    starts = doc_start(meta_ref, docs, cols)

    def visit(block, allowed):
        at = pl.ds(pl.multiple_of(block * BLOCK, BLOCK), BLOCK)
        keys, vals = k_ref[at, :], v_ref[at, :]
        scores = dot(keys, queries, 1, 1)
        grads = dot(vals, ups, 1, 1)
        expos, slopes = [], []
        total = dq_ref[...]
        for h in range(heads):
            part = slice(h * BLOCK, (h + 1) * BLOCK)
            expo = jnp.where(allowed, jnp.exp(scores[:, part]), 0.0)
            slope = (expo * (grads[:, part] - delta[h : h + 1, :])).astype(BF16)
            expos.append(expo.astype(BF16))
            slopes.append(slope)
            total = total + dot(slope, head_lanes(keys, h), 0, 0)
        dq_ref[...] = total
        dv_ref[at, :] += dot(jnp.concatenate(expos, axis=1), ups)
        dk_ref[at, :] += dot(jnp.concatenate(slopes, axis=1), queries)

    def key_slots(block):
        at = pl.ds(pl.multiple_of(block * BLOCK, BLOCK), BLOCK)
        return wide(kpos_ref[at, :])

    def off_diagonal(block, carry):
        visit(block, key_slots(block) >= starts)
        return carry

    lax.fori_loop(low, step, off_diagonal, 0)
    rows = lax.broadcasted_iota(jnp.int32, (BLOCK, BLOCK), 0) + base
    visit(step, ((key_slots(step) >= starts) & (rows <= cols)) | (rows == cols))

    scale = sqk_ref[0:1, :]
    here = pl.ds(pl.multiple_of(base, BLOCK), BLOCK)
    raw, by_scale = finish(
        dq_ref[...] * (HEAD**-0.5),
        qr_ref[...],
        wide(cos_ref[here, :]),
        wide(sin_ref[here, :]),
        scale,
    )
    gq_ref[...] = raw
    gs_ref[0:1, :] += by_scale

    @pl.when(step == pl.num_programs(0) - 1)
    def _():
        def one(block, carry):
            at = pl.ds(pl.multiple_of(block * BLOCK, BLOCK), BLOCK)
            slot = (meta_ref[0] ^ (block // per)) * per + block % per
            to = pl.ds(pl.multiple_of(slot * BLOCK, BLOCK), BLOCK)
            raw, by_scale = finish(
                dk_ref[at, :], kr_ref[at, :], wide(cos_ref[at, :]), wide(sin_ref[at, :]), scale
            )
            gk_ref[to, :] = raw
            gs_ref[0:1, :] += by_scale
            gv_ref[to, :] = dv_ref[at, :].astype(BF16)
            return carry

        lax.fori_loop(0, pl.num_programs(0), one, 0)


def attend_back(meta, queries, qrot, out, inverse, grad, keys, vals, krot, kpos, cosine, sine, sqk, docs):
    total, width = queries.shape
    per = total // 4 // BLOCK

    def rel(i, m):
        return ((m[0] ^ (i // per)) * per + i % per, 0)

    whole = pl.BlockSpec((total, width), lambda i, m: (0, 0))
    half = pl.BlockSpec((total, 128), lambda i, m: (0, 0))
    block = pl.BlockSpec((BLOCK, width), lambda i, m: (i, 0))
    moved = pl.BlockSpec((BLOCK, width), rel)
    small = pl.BlockSpec((8, width), lambda i, m: (0, 0))
    return pl.pallas_call(
        functools.partial(back_body, docs),
        out_shape=[jax.ShapeDtypeStruct((total, width), BF16)] * 3
        + [jax.ShapeDtypeStruct((8, width), F32)],
        grid_spec=pltpu.PrefetchScalarGridSpec(
            num_scalar_prefetch=1,
            grid=(total // BLOCK,),
            in_specs=[block, block, moved, block, moved, whole, whole, whole, half, half, half, small],
            out_specs=[moved, whole, whole, small],
            scratch_shapes=[
                pltpu.VMEM((BLOCK, width), F32),
                pltpu.VMEM((total, width), F32),
                pltpu.VMEM((total, width), F32),
            ],
        ),
        cost_estimate=pl.CostEstimate(
            flops=30_000_000_000, bytes_accessed=24 * total * width, transcendentals=6_000_000
        ),
        name="attend_back",
    )(meta, queries, qrot, out, inverse, grad, keys, vals, krot, kpos, cosine, sine, sqk)


def both(own, axis, bit, index):
    other = swap(own, axis, bit)
    stacked = jnp.stack([own, other])
    return jnp.where((index & bit) == 0, stacked, jnp.stack([other, own]))


def gather_small(vectors, d, m):
    s_qk, s_up, s_gate, alpha_attn, alpha_mlp = vectors
    if lax.axis_size("dp") != 8:
        whole = [lax.all_gather(v, ("dp", "mp"), axis=0, tiled=True) for v in vectors]
        cut = [
            lax.dynamic_slice_in_dim(v, m * (v.shape[0] // 4), v.shape[0] // 4) for v in whole[:3]
        ]
        return cut[0], cut[1], cut[2], whole[3], whole[4]
    packed = jnp.concatenate([s_up, s_gate, s_qk, alpha_attn, alpha_mlp, s_qk])
    packed = packed.reshape(3, 128)
    pair = both(packed, "mp", 1, m)
    quad = both(pair, "mp", 2, m).reshape(4, 3, 128)
    near = jnp.stack([quad] + [from_z(quad, step) for step in (1, 2, 3)])
    every = jnp.stack([near, swap(near, "dp", 1)]).reshape(2, 4, 4, 384)
    z, y = d >> 1, d & 1
    mine = lax.dynamic_slice_in_dim(every, (m - z) & 3, 1, axis=1)[:, 0]
    mine = jnp.where(y == 0, mine, mine[::-1])
    return (
        mine[..., 256:288].reshape(-1),
        mine[..., :128].reshape(-1),
        mine[..., 128:256].reshape(-1),
        every[..., 288:320].reshape(-1),
        every[..., 320:352].reshape(-1),
    )


def scatter_small(g_sqk, g_up, g_gate, g_alpha_attn, g_alpha_mlp, d, m):
    if lax.axis_size("dp") != 8:
        def place(part):
            whole = jnp.zeros((part.shape[0] * 4,), F32)
            return lax.dynamic_update_slice_in_dim(whole, part, m * part.shape[0], 0)

        whole = (place(g_sqk), place(g_up), place(g_gate), g_alpha_attn, g_alpha_mlp)
        return tuple(
            lax.psum_scatter(
                lax.psum_scatter(v, "dp", scatter_dimension=0, tiled=True),
                "mp",
                scatter_dimension=0,
                tiled=True,
            )
            for v in whole
        )
    z, y = d >> 1, d & 1
    mine = jnp.concatenate(
        [g_up.reshape(2, 4, 128), g_gate.reshape(2, 4, 128), g_sqk.reshape(2, 4, 32)], axis=-1
    )
    mine = jnp.where(y == 0, mine, mine[::-1])
    slot = lax.broadcasted_iota(jnp.int32, (1, 4, 1, 1), 1)
    mine = jnp.where(slot == ((m - z) & 3), mine[:, None], 0.0)
    total = jnp.concatenate(
        [
            mine,
            g_alpha_attn.reshape(2, 4, 4, 32),
            g_alpha_mlp.reshape(2, 4, 4, 32),
            jnp.zeros((2, 4, 4, 32), F32),
        ],
        axis=-1,
    ).reshape(2, 4, 12, 128)
    total = total + swap(total, "mp", 1)
    total = total + swap(total, "mp", 2)
    half = total[0] + swap(total[1], "dp", 1)
    rest = half[0]
    for step in (1, 2, 3):
        rest = rest + to_z(half[step], step)
    rest = lax.dynamic_slice_in_dim(rest.reshape(4, 384), m, 1, axis=0)[0]
    return rest[256:288], rest[:128], rest[128:256], rest[288:320], rest[320:352]


def sum_everywhere(value):
    if lax.axis_size("dp") != 8:
        return lax.psum(value, ("dp", "mp"))
    value = jnp.broadcast_to(value, (8, 128))
    value = value + swap(value, "mp", 1) + swap(value, "mp", 2) + swap(value, "mp", 3)
    value = value + to_z(value, 1) + to_z(value, 2) + to_z(value, 3)
    value = value + swap(value, "dp", 1)
    return value[0, 0]


def shards(
    tokens,
    cotangent,
    lengths,
    key_mask,
    w_query,
    w_key,
    w_value,
    w_out,
    w_up,
    w_gate,
    w_down,
    s_qk,
    s_up,
    s_gate,
    alpha_attn,
    alpha_mlp,
):
    m = lax.axis_index("mp").astype(jnp.int32)
    d = lax.axis_index("dp").astype(jnp.int32)
    direct = lax.axis_size("dp") == 8
    local = tokens.shape[0]
    row_len = key_mask.shape[1]
    docs = lengths.shape[1]

    if direct:
        slots = jnp.arange(8, dtype=jnp.int32)
        z, y = d >> 1, d & 1
        natural = 2 * ((z + (slots & 3)) & 3) + (y ^ (slots >> 2))
        inverse = ((slots & 1) ^ y) * 4 + (((slots >> 1) - z) & 3)
        tokens = pick_cols(tokens, natural)
        cotangent = pick_cols(cotangent, natural)

    x_near, x_far = spread(tokens)
    full_query, after = gather(w_query, 0, ())
    full_key, after = gather(w_key, 0, after)
    full_value, after = gather(w_value, 0, after)
    full_out, after = gather(w_out, 1, after)
    full_up, after = gather(w_up, 0, after)
    full_gate, after = gather(w_gate, 0, after)
    full_down, after = gather(w_down, 1, after)
    sqk, sup, sgate, alpha_one, alpha_two = gather_small(
        (s_qk, s_up, s_gate, alpha_attn, alpha_mlp), d, m
    )
    sqk = jnp.broadcast_to(sqk[None], (8, sqk.shape[0]))

    place = m.reshape(1)
    meta = jnp.concatenate([place, lengths[0]])
    slot_ids = jnp.arange(row_len, dtype=jnp.int32)
    ends = jnp.cumsum(lengths[0])
    passed = (slot_ids[:, None] >= ends[None, :]).astype(jnp.int32)
    positions = slot_ids - jnp.sum(passed * lengths, axis=1)
    steps_even = jnp.arange(0, HEAD, 2).astype(F32)
    frequencies = jnp.power(jnp.float32(10000.0), -steps_even / HEAD)
    angles = positions.astype(F32)[:, None] * jnp.tile(frequencies, 4)[None, :]
    cosine, sine = jnp.cos(angles), jnp.sin(angles)
    kpos = jnp.where(key_mask[0] == 1, slot_ids, -1)
    kpos_rows = jnp.broadcast_to(kpos[None, :], (8, row_len))
    kpos_cols = jnp.broadcast_to(kpos[:, None], (row_len, 128))

    weights = (full_query, full_key, full_value)
    half = project(place, x_near, weights, cosine, sine, sqk, None, 0)
    queries, keys, vals, qrot, krot = project(place, x_far, weights, cosine, sine, sqk, half, 2)
    attended, inverse_mass = attend(meta, queries, keys, vals, kpos_rows, docs)

    near, far = attended[: 2 * local], attended[2 * local :]
    branch_attn = reduce_pair(dot(far, full_out).astype(BF16), dot(near, full_out))
    x_local = tokens.astype(F32)
    h_attn, attn_factor = rms_rows(branch_attn)
    hidden_one, one_factor = rms_rows(x_local + alpha_one * (h_attn - x_local))
    h_near, h_far = spread(hidden_one.astype(BF16))

    def forward(rows):
        up_proj = dot(rows, full_up)
        gate_proj = dot(rows, full_gate)
        outer = sgate * gate_proj
        active = (sup * up_proj * (outer * jax.nn.sigmoid(outer))).astype(BF16)
        return up_proj, gate_proj, active

    up_near, gate_near, act_near = forward(h_near)
    up_far, gate_far, act_far = forward(h_far)
    branch_mlp = reduce_pair(dot(act_far, full_down).astype(BF16), dot(act_near, full_down))
    h_mlp, mlp_factor = rms_rows(branch_mlp)
    result, two_factor = rms_rows(hidden_one + alpha_two * (h_mlp - hidden_one))
    grad_two = rms_back(cotangent.astype(F32), result, two_factor)
    g_alpha_two = jnp.sum(grad_two * (h_mlp - hidden_one), axis=0)
    grad_branch = rms_back(grad_two * alpha_two, h_mlp, mlp_factor).astype(BF16)
    gm_near, gm_far = spread(grad_branch)

    def backward(rows, up_proj, gate_proj):
        g_act = dot(rows, full_down, 1, 1)
        outer = sgate * gate_proj
        sigma = jax.nn.sigmoid(outer)
        g_inner = g_act * (outer * sigma)
        g_outer = g_act * (sup * up_proj) * (sigma * (1.0 + outer * (1.0 - sigma)))
        by_up = jnp.sum(g_inner * up_proj, axis=0)
        by_gate = jnp.sum(g_outer * gate_proj, axis=0)
        g_up = (g_inner * sup).astype(BF16)
        g_gate = (g_outer * sgate).astype(BF16)
        g_hidden = dot(g_up, full_up, 1, 1) + dot(g_gate, full_gate, 1, 1)
        return g_up, g_gate, g_hidden, by_up, by_gate

    gu_near, gg_near, gh_near, bu_near, bg_near = backward(gm_near, up_near, gate_near)
    gu_far, gg_far, gh_far, bu_far, bg_far = backward(gm_far, up_far, gate_far)
    grad_hidden = grad_two * (1.0 - alpha_two) + reduce_pair(gh_far.astype(BF16), gh_near)
    grad_down = scatter(dot(act_near, gm_near, 0, 0) + dot(act_far, gm_far, 0, 0), 1)
    grad_up = scatter(dot(h_near, gu_near, 0, 0) + dot(h_far, gu_far, 0, 0), 0)
    grad_gate = scatter(dot(h_near, gg_near, 0, 0) + dot(h_far, gg_far, 0, 0), 0)

    grad_one = rms_back(grad_hidden, hidden_one, one_factor)
    g_alpha_one = jnp.sum(grad_one * (h_attn - x_local), axis=0)
    grad_attn = rms_back(grad_one * alpha_one, h_attn, attn_factor).astype(BF16)
    ga_near, ga_far = spread(grad_attn)
    g_att = jnp.concatenate(
        [dot(ga_near, full_out, 1, 1).astype(BF16), dot(ga_far, full_out, 1, 1).astype(BF16)]
    )
    grad_out = scatter(dot(near, ga_near, 0, 0) + dot(far, ga_far, 0, 0), 1)

    g_query, g_key, g_val, g_sqk = attend_back(
        meta, queries, qrot, attended, inverse_mass, g_att, keys, vals, krot, kpos_cols, cosine, sine, sqk, docs
    )

    def to_tokens(rows):
        return (
            dot(g_query[rows], full_query, 1, 1)
            + dot(g_key[rows], full_key, 1, 1)
            + dot(g_val[rows], full_value, 1, 1)
        )

    first, second = slice(0, 2 * local), slice(2 * local, 4 * local)
    grad_tokens = grad_one * (1.0 - alpha_one) + reduce_pair(
        to_tokens(second).astype(BF16), to_tokens(first)
    )

    def by_weight(grad):
        return scatter(dot(x_near, grad[first], 0, 0) + dot(x_far, grad[second], 0, 0), 0)

    small = scatter_small(
        g_sqk[0], bu_near + bu_far, bg_near + bg_far, g_alpha_one, g_alpha_two, d, m
    )
    pieces = (
        by_weight(g_query),
        by_weight(g_key),
        by_weight(g_val),
        grad_out,
        grad_up,
        grad_gate,
        grad_down,
    ) + small
    squares = jnp.float32(0.0)
    for piece in pieces:
        squares = squares + jnp.sum(piece * piece)
    grad_norm = jnp.sqrt(sum_everywhere(squares))
    mean_alphas = jnp.stack([jnp.mean(alpha_one), jnp.mean(alpha_two)])
    result = result.astype(BF16)
    if direct:
        result = pick_cols(result, inverse)
        grad_tokens = pick_cols(grad_tokens, inverse)
    return (result, grad_tokens) + pieces + (grad_norm, mean_alphas)


def solution(mesh):
    both_axes = P(("dp", "mp"))
    rows = P(("dp", "mp"), None)
    in_specs = (
        (rows, rows, P("dp", None), P("dp", None))
        + (P("dp", "mp"),) * 3
        + (P("mp", "dp"),)
        + (P("dp", "mp"),) * 2
        + (P("mp", "dp"),)
        + (both_axes,) * 5
    )
    out_specs = (
        (rows, rows)
        + (P("dp", "mp"),) * 3
        + (P("mp", "dp"),)
        + (P("dp", "mp"),) * 2
        + (P("mp", "dp"),)
        + (both_axes,) * 5
        + (P(), P())
    )
    return jax.shard_map(shards, mesh=mesh, in_specs=in_specs, out_specs=out_specs, check_vma=False)
```

time: 1290 us -> 694 us (0.54)
  blocking collectives: 331 us -> 0 us
  waiting for transfers between devices: 556 us -> 244 us
  matrix products: 232 us -> 102 us
  Pallas kernels: 0 us -> 120 us
  starting transfers between devices: 1.56 us -> 115 us
  other arithmetic: 111 us -> 60.3 us
  between operations: 29.6 us -> 13.8 us
    reduce_scatter x11 -> x0, waiting for transfers between devices: 484 us -> none  [the longest x1 90.2 us: shards(): lax.psum_scatter(grad_gate_local, 'dp', scatter_dimension=0, tiled=True)]
    ppermute x0 -> x99, waiting for transfers between devices: none -> 244 us  [the longest x48 141 us: swap(): return lax.ppermute(array, axis, [(i, i ^ bit) for i in range(size)])]
    all_gather x6 -> x0, blocking collectives: 206 us -> none  [the longest x1 40.3 us: shards(): lax.all_gather(s_up, ('dp', 'mp'), axis=0, tiled=True)]
    dot_general x45 -> x36, matrix products: 232 us -> 102 us  [dot(): lax.dot_general(left, right, (((left_dim,), (right_dim,)), ((), ())), pre...]
    pallas_call x0 -> x8, Pallas kernels: none -> 120 us  [the longest x1 52.1 us: attend_back(): pl.pallas_call(functools.partial(back_body, docs), out_shape=[jax.ShapeDt...]
    ppermute x0 -> x99, starting transfers between devices: none -> 115 us  [the longest x27 51 us: to_z(): lax.ppermute(array, 'dp', [(z * 2 + y, (z + step) % 4 * 2 + y) for z in r...]
    unnamed x3 -> x0, blocking collectives: 84.9 us -> none
    all_gather x7 -> x0, waiting for transfers between devices: 69.8 us -> none  [the longest x1 35.1 us: shards(): lax.all_gather(w_down, 'dp', axis=1, tiled=True)]
  transfers between devices with their start and end apart: 18 -> 99, of which waited for: 12 -> 42; matrix products, arithmetic and copies ran while one was open for 18% -> 18% of each run, Pallas kernels for 0% -> 5%
where the time goes in v1:
time: 694 us; the launch traced here: 685 us
  waiting for transfers between devices  244 us (35%)
  Pallas kernels  120 us (17%)
  starting transfers between devices  115 us (17%)
  matrix products  102 us (15%)
  other arithmetic  60.3 us (9%)
  local copies, waits for them, and re-layouts  30.1 us (4%)
  between operations  13.8 us (2%)
    ppermute x48, waiting for transfers between devices, swap(): return lax.ppermute(array, axis, [(i, i ^ bit) for i in range(size)])  141 us
    dot_general x36, matrix products, dot(): lax.dot_general(left, right, (((left_dim,), (right_dim,)), ((), ())), pre...  102 us
    ppermute x24, waiting for transfers between devices, from_z(): lax.ppermute(array, 'dp', [((z + step) % 4 * 2 + y, z * 2 + y) for z in r...  70.7 us
    pallas_call x1, Pallas kernels, attend_back(): pl.pallas_call(functools.partial(back_body, docs), out_shape=[jax.ShapeDt...  52.1 us
    ppermute x27, starting transfers between devices, to_z(): lax.ppermute(array, 'dp', [(z * 2 + y, (z + step) % 4 * 2 + y) for z in r...  51 us
    ppermute x24, starting transfers between devices, from_z(): lax.ppermute(array, 'dp', [((z + step) % 4 * 2 + y, z * 2 + y) for z in r...  33.8 us
    pallas_call x4, Pallas kernels, pick_cols(): pl.pallas_call(body, out_shape=jax.ShapeDtypeStruct(array.shape, array.dt...  32.3 us
    ppermute x27, waiting for transfers between devices, to_z(): lax.ppermute(array, 'dp', [(z * 2 + y, (z + step) % 4 * 2 + y) for z in r...  32.3 us
  transfers between devices with their start and end apart: 99, of which 42 were waited for; matrix products, arithmetic and copies ran while one was open for 18% of the time, Pallas kernels for 5%

profile of v1, /device:TPU:0, one launch (start us, length us, event | category | flops | bytes accessed | tf_op | source)
XLA Modules:
  0.0 684.8 jit_solution(17345215232462324485)
XLA Ops:
  0.7 5.1 collective-permute-start.8
  9.0 5.6 multiply_sine_fusion
  21.4 2.8 collective-permute-start.2
  24.7 6.0 pick_cols.4
  36.8 3.4 collective-permute-start.12
  42.6 4.5 collective-permute-done.13
  51.4 4.4 collective-permute-done.17
  66.4 3.1 collective-permute-done.11
  71.1 4.1 collective-permute-done.15
  75.2 5.6 collective-permute-done.19
  80.8 2.9 collective-permute-done.24
  83.7 2.5 constant_dynamic-update-slice_fusion.1
  86.1 2.7 pad_maximum_fusion.x_ref
  89.4 8.7 %project.2 = (bf16[2048,256]{1,0:T(8,128)(2,1)}, bf16[2048,256]{1,0:T(8,128)(2,1)}, bf16[2048,256]{1,0:T(8,128)(2,1)}, f32[2048,256]{1,0:T(8,128)}, f32[2048,256]{1,0:T(8,128)}) custom-call(s32[1]{0:T(128)} %bitcast.15.m_ref, bf16[1024,1024]{1,0:T(8,128)(2,1)} %pad_maximum_fusion.x_ref, bf16[1024,256]{1,0:T(8,128)(2,1)} %copy-done.13, ...), custom_call_target="tpu_custom_call" | custom-call | flops 1610612736 | bytes 8388608 | tf_op jit(solution)/shard_map/project/pallas_call | solution.py:161
  100.8 8.5 %project.3 = (bf16[2048,256]{1,0:T(8,128)(2,1)}, bf16[2048,256]{1,0:T(8,128)(2,1)}, bf16[2048,256]{1,0:T(8,128)(2,1)}, f32[2048,256]{1,0:T(8,128)}, f32[2048,256]{1,0:T(8,128)}) custom-call(s32[1]{0:T(128)} %bitcast.15.m_ref, bf16[1024,1024]{1,0:T(8,128)(2,1)} %copy-done.22, ...), custom_call_target="tpu_custom_call", output_to_operand_aliasing={{0}: (8, {}), {1}: (9, {}), {2}: (10, {}), {3}: (11, {}), {... | custom-call | flops 1610612736 | bytes 8388608 | tf_op jit(solution)/shard_map/project/pallas_call | solution.py:161
  110.0 18.0 %attend.1 = (bf16[2048,256]{1,0:T(8,128)(2,1)}, f32[2048,256]{1,0:T(8,128)}) custom-call(s32[5]{0:T(128)} %pad_add_fusion.meta_ref, bf16[2048,256]{1,0:T(8,128)(2,1)} %get-tuple-element.45.q_ref, bf16[2048,256]{1,0:T(8,128)(2,1)} %get-tuple-element.46.k_ref, bf16[2048,256]{1,0:T(8,128)(2,1)} %get-tuple-element.47.v_ref, s32[8,2048]{1,0:T(8,128)} %broadcast_in_dim.71.kpos_ref), custom_call_target="tpu_custom_call" | custom-call | flops 12000000000 | bytes 4194304 | tf_op jit(solution)/shard_map/attend/pallas_call | solution.py:258
  139.5 3.1 collective-permute-done.29
  142.6 18.1 %collective-permute-done.30 = bf16[128,1024]{1,0:T(8,128)(2,1)S(1)} collective-permute-done((bf16[128,1024]{1,0:T(8,128)(2,1)S(1)}, bf16[128,1024]{1,0:T(8,128)(2,1)S(1)}, u32[]{:S(2)}, u32[]{:S(2)}) %collective-permute-start.30) | collective-permute-done | bytes 262176 | tf_op jit(solution)/shard_map/ppermute | solution.py:40
  164.5 4.5 collective-permute-done.33
  169.0 15.9 %collective-permute-done.34 = bf16[128,1024]{1,0:T(8,128)(2,1)S(1)} collective-permute-done((bf16[128,1024]{1,0:T(8,128)(2,1)}, bf16[128,1024]{1,0:T(8,128)(2,1)S(1)}, u32[]{:S(2)}, u32[]{:S(2)}) %collective-permute-start.34) | collective-permute-done | bytes 262176 | tf_op jit(solution)/shard_map/ppermute | solution.py:40
  195.3 14.5 %collective-permute-done.38 = bf16[1024,128]{1,0:T(8,128)(2,1)S(1)} collective-permute-done((bf16[1024,128]{1,0:T(8,128)(2,1)S(1)}, bf16[1024,128]{1,0:T(8,128)(2,1)S(1)}, u32[]{:S(2)}, u32[]{:S(2)}) %collective-permute-start.38) | collective-permute-done | bytes 262176 | tf_op jit(solution)/shard_map/ppermute | solution.py:40
  210.5 6.2 collective-permute-done.42
  216.8 3.4 collective-permute-done.36
  220.2 20.3 %collective-permute-done.40 = bf16[1024,512]{1,0:T(8,128)(2,1)S(1)} collective-permute-done((bf16[1024,512]{1,0:T(8,128)(2,1)S(1)}, bf16[1024,512]{1,0:T(8,128)(2,1)S(1)}, u32[]{:S(2)}, u32[]{:S(2)}) %collective-permute-start.40) | collective-permute-done | bytes 1048608 | tf_op jit(solution)/shard_map/ppermute | solution.py:36
  248.0 6.4 multiply_convert_fusion.5
  262.5 14.1 %pick_cols.6 = bf16[512,1024]{1,0:T(8,128)(2,1)} custom-call(s32[8]{0:T(128)} %xor_add_fusion.table_ref, bf16[512,1024]{1,0:T(8,128)(2,1)} %in_ref.3), custom_call_target="tpu_custom_call" | custom-call | bytes 2097152 | tf_op jit(solution)/shard_map/pick_cols/pallas_call | solution.py:97
  276.8 10.5 %collective-permute-done.45 = bf16[512,1024]{1,0:T(8,128)(2,1)} collective-permute-done((bf16[512,1024]{1,0:T(8,128)(2,1)S(1)}, bf16[512,1024]{1,0:T(8,128)(2,1)}, u32[]{:S(2)}, u32[]{:S(2)}) %collective-permute-start.45) | collective-permute-done | bytes 1048608 | tf_op jit(solution)/shard_map/ppermute | solution.py:36
  287.2 2.7 multiply_reduce_fusion.10
  292.8 3.4 multiply_convert_fusion.7
  299.0 22.2 %collective-permute-done.48 = bf16[512,1024]{1,0:T(8,128)(2,1)} collective-permute-done((bf16[512,1024]{1,0:T(8,128)(2,1)}, bf16[512,1024]{1,0:T(8,128)(2,1)}, u32[]{:S(2)}, u32[]{:S(2)}) %collective-permute-start.48) | collective-permute-done | bytes 1048608 | tf_op jit(solution)/shard_map/ppermute | solution.py:36
  322.6 6.1 fusion.13
  328.6 4.0 fusion.12
  332.7 16.5 %multiply_reduce_fusion.2 = (f32[1024]{0:T(1024)S(1)}, f32[1024]{0:T(1024)S(1)}, f32[1024]{0:T(1024)S(1)}, f32[1024]{0:T(1024)S(1)}, f32[1024,1024]{1,0:T(8,128)...) fusion(f32[1024,1024]{1,0:T(8,128)} %copy-done.76, f32[1024,1024]{1,0:T(8,128)} %copy-done.75, ...), kind=kOutput, calls=%fused_computation.2 | convolution fusion | flops 2187325440 | bytes 37773312 | tf_op jit(solution)/shard_map/dot_general | solution.py:29
  349.3 4.7 fusion.17
  354.0 2.4 add_convert_fusion.1
  359.5 2.4 convolution_add_fusion.3
  363.4 2.5 fusion.70
  365.9 2.9 convolution_add_fusion.2
  369.5 6.6 fusion.15
  376.1 5.9 convolution_add_fusion.1
  385.3 2.4 convolution_add_fusion
  388.9 6.2 collective-permute-done.74
  397.7 19.8 %collective-permute-done.78 = bf16[512,1024]{1,0:T(8,128)(2,1)S(1)} collective-permute-done((bf16[512,1024]{1,0:T(8,128)(2,1)S(1)}, bf16[512,1024]{1,0:T(8,128)(2,1)S(1)}, u32[]{:S(2)}, u32[]{:S(2)}) %collective-permute-start.78) | collective-permute-done | bytes 1048608 | tf_op jit(solution)/shard_map/ppermute | solution.py:36
  420.9 3.7 multiply_reduce_fusion.7
  428.2 10.8 %collective-permute-done.82 = bf16[1024,512]{1,0:T(8,128)(2,1)S(1)} collective-permute-done((bf16[1024,512]{1,0:T(8,128)(2,1)S(1)}, bf16[1024,512]{1,0:T(8,128)(2,1)S(1)}, u32[]{:S(2)}, u32[]{:S(2)}) %collective-permute-start.82) | collective-permute-done | bytes 1048608 | tf_op jit(solution)/shard_map/ppermute | solution.py:36
  444.5 4.6 collective-permute-done.81
  449.1 3.9 collective-permute-start.85
  453.0 12.7 %collective-permute-done.80 = bf16[128,1024]{1,0:T(8,128)(2,1)S(1)} collective-permute-done((bf16[128,1024]{1,0:T(8,128)(2,1)S(1)}, bf16[128,1024]{1,0:T(8,128)(2,1)S(1)}, u32[]{:S(2)}, u32[]{:S(2)}) %collective-permute-start.80) | collective-permute-done | bytes 262176 | tf_op jit(solution)/shard_map/ppermute | solution.py:46
  465.8 11.9 %collective-permute-start.83 = (bf16[1024,128]{1,0:T(8,128)(2,1)S(1)}, bf16[1024,128]{1,0:T(8,128)(2,1)S(1)}, u32[]{:S(2)}, u32[]{:S(2)}) collective-permute-start(bf16[1024,128]{1,0:T(8,128)(2,1)S(1)} %get-tuple-element.126), channel_id=1, source_target_pairs={{0,8},{4,12},{8,16},{12,20},{16,24},{20,28},{24,0},{28,4},{1,9},{5... | collective-permute-start | bytes 786440 | tf_op jit(solution)/shard_map/ppermute | solution.py:46
  479.3 8.4 %collective-permute-done.84 = bf16[1024,128]{1,0:T(8,128)(2,1)S(1)} collective-permute-done((bf16[1024,128]{1,0:T(8,128)(2,1)S(1)}, bf16[1024,128]{1,0:T(8,128)(2,1)S(1)}, u32[]{:S(2)}, u32[]{:S(2)}) %collective-permute-start.84) | collective-permute-done | bytes 262176 | tf_op jit(solution)/shard_map/ppermute | solution.py:46
  491.6 3.0 fusion.10
  499.6 52.1 %attend_back.1 = (bf16[2048,256]{1,0:T(8,128)(2,1)}, bf16[2048,256]{1,0:T(8,128)(2,1)}, bf16[2048,256]{1,0:T(8,128)(2,1)}, f32[8,256]{1,0:T(8,128)}) custom-call(s32[5]{0:T(128)} %pad_add_fusion.meta_ref, bf16[2048,256]{1,0:T(8,128)(2,1)} %get-tuple-element.45.q_ref, f32[2048,256]{1,0:T(8,128)} %get-tuple-element.53.qr_ref, ...), custom_call_target="tpu_custom_call" | custom-call | flops 30000001024 | bytes 12582912 | tf_op jit(solution)/shard_map/attend_back/pallas_call | solution.py:414
  561.7 2.8 fusion.45
  576.3 3.1 collective-permute-done.88
  579.5 4.9 collective-permute-start.90
  595.1 4.9 collective-permute-done.58
  601.2 4.4 collective-permute-done.62
  620.6 4.0 collective-permute-start.69
  629.1 2.9 collective-permute-start.73
  632.3 2.4 collective-permute-start.71
  651.1 4.4 collective-permute-done.94
  665.7 5.9 pick_cols.5
  672.8 4.2 fusion.5.in_ref
  676.9 6.3 pick_cols.7
  (509 shorter events, 194.2 us)
Async XLA Ops:
  0.7 35.7 %collective-permute-start.8 = (bf16[128,256]{1,0:T(8,128)(2,1)}, bf16[128,256]{1,0:T(8,128)(2,1)S(1)}, u32[]{:S(2)}, u32[]{:S(2)}) collective-permute-start(bf16[128,256]{1,0:T(8,128)(2,1)} %param.20), channel_id=1, source_target_pairs={{8,0},{12,4},{16,8},{20,12},{24,16},{28,20},{0,24},{4,28},{9,1},{1... | collective-permute-start | bytes 196616 | tf_op jit(solution)/shard_map/ppermute | solution.py:40
  5.8 30.6 %collective-permute-start.9 = (bf16[128,256]{1,0:T(8,128)(2,1)}, bf16[128,256]{1,0:T(8,128)(2,1)S(1)}, u32[]{:S(2)}, u32[]{:S(2)}) collective-permute-start(bf16[128,256]{1,0:T(8,128)(2,1)} %param.20), channel_id=1, source_target_pairs={{16,0},{20,4},{24,8},{28,12},{0,16},{4,20},{8,24},{12,28},{17,1},{... | collective-permute-start | bytes 196616 | tf_op jit(solution)/shard_map/ppermute | solution.py:40
  18.3 12.4 %collective-permute-start.4 = (f32[4,3,128]{2,0,1:T(4,128)S(1)}, f32[4,3,128]{2,0,1:T(4,128)S(1)}, u32[]{:S(2)}, u32[]{:S(2)}) collective-permute-start(f32[4,3,128]{2,0,1:T(4,128)S(1)} %bitcast.112), channel_id=1, source_target_pairs={{24,0},{28,4},{0,8},{4,12},{8,16},{12,20},{16,24},{20,28},{25,1},{... | collective-permute-start | bytes 18440 | tf_op jit(solution)/shard_map/ppermute | solution.py:40
  19.4 11.4 %collective-permute-start.3 = (f32[4,3,128]{2,0,1:T(4,128)S(1)}, f32[4,3,128]{2,0,1:T(4,128)S(1)}, u32[]{:S(2)}, u32[]{:S(2)}) collective-permute-start(f32[4,3,128]{2,0,1:T(4,128)S(1)} %bitcast.113), channel_id=1, source_target_pairs={{16,0},{20,4},{24,8},{28,12},{0,16},{4,20},{8,24},{12,28},{17,1},{... | collective-permute-start | bytes 18440 | tf_op jit(solution)/shard_map/ppermute | solution.py:40
  21.4 10.9 %collective-permute-start.2 = (f32[4,3,128]{2,0,1:T(4,128)S(1)}, f32[4,3,128]{2,0,1:T(4,128)S(1)}, u32[]{:S(2)}, u32[]{:S(2)}) collective-permute-start(f32[4,3,128]{2,0,1:T(4,128)S(1)} %bitcast.114), channel_id=1, source_target_pairs={{8,0},{12,4},{16,8},{20,12},{24,16},{28,20},{0,24},{4,28},{9,1},{1... | collective-permute-start | bytes 18440 | tf_op jit(solution)/shard_map/ppermute | solution.py:40
  30.7 35.5 %collective-permute-start.6 = (bf16[512,1024]{1,0:T(8,128)(2,1)}, bf16[512,1024]{1,0:T(8,128)(2,1)}, u32[]{:S(2)}, u32[]{:S(2)}) collective-permute-start(bf16[512,1024]{1,0:T(8,128)(2,1)} %pick_cols.4), channel_id=1, source_target_pairs={{0,2},{1,3},{2,0},{3,1},{4,6},{5,7},{6,4},{7,5},{8,10},{9,11},{10,... | collective-permute-start | bytes 3145736 | tf_op jit(solution)/shard_map/ppermute | solution.py:36
  36.2 49.9 %collective-permute-start.20 = (bf16[512,1024]{1,0:T(8,128)(2,1)}, bf16[512,1024]{1,0:T(8,128)(2,1)}, u32[]{:S(2)}, u32[]{:S(2)}) collective-permute-start(bf16[512,1024]{1,0:T(8,128)(2,1)} %pick_cols.4), channel_id=1, source_target_pairs={{0,1},{1,0},{2,3},{3,2},{4,5},{5,4},{6,7},{7,6},{8,9},{9,8},{10,11... | collective-permute-start | bytes 3145736 | tf_op jit(solution)/shard_map/ppermute | solution.py:36
  60.3 9.2 %collective-permute-start.11 = (bf16[512,256]{1,0:T(8,128)(2,1)S(1)}, bf16[512,256]{1,0:T(8,128)(2,1)S(1)}, u32[]{:S(2)}, u32[]{:S(2)}) collective-permute-start(bf16[512,256]{1,0:T(8,128)(2,1)S(1)} %pad_maximum_fusion.14), channel_id=1, source_target_pairs={{0,4},{4,0},{8,12},{12,8},{16,20},{20,16},{24,28},{28,24},{1,5},{5... | collective-permute-start | bytes 786440 | tf_op jit(solution)/shard_map/ppermute | solution.py:36
  64.2 11.0 %collective-permute-start.15 = (bf16[512,256]{1,0:T(8,128)(2,1)S(1)}, bf16[512,256]{1,0:T(8,128)(2,1)S(1)}, u32[]{:S(2)}, u32[]{:S(2)}) collective-permute-start(bf16[512,256]{1,0:T(8,128)(2,1)S(1)} %pad_maximum_fusion.15), channel_id=1, source_target_pairs={{0,4},{4,0},{8,12},{12,8},{16,20},{20,16},{24,28},{28,24},{1,5},{5... | collective-permute-start | bytes 786440 | tf_op jit(solution)/shard_map/ppermute | solution.py:36
  65.7 15.1 %collective-permute-start.19 = (bf16[512,256]{1,0:T(8,128)(2,1)S(1)}, bf16[512,256]{1,0:T(8,128)(2,1)S(1)}, u32[]{:S(2)}, u32[]{:S(2)}) collective-permute-start(bf16[512,256]{1,0:T(8,128)(2,1)S(1)} %pad_maximum_fusion.16), channel_id=1, source_target_pairs={{0,4},{4,0},{8,12},{12,8},{16,20},{20,16},{24,28},{28,24},{1,5},{5... | collective-permute-start | bytes 786440 | tf_op jit(solution)/shard_map/ppermute | solution.py:36
  66.3 31.9 %collective-permute-start.7 = (bf16[512,1024]{1,0:T(8,128)(2,1)}, bf16[512,1024]{1,0:T(8,128)(2,1)}, u32[]{:S(2)}, u32[]{:S(2)}) collective-permute-start(bf16[512,1024]{1,0:T(8,128)(2,1)} %collective-permute-done.6), channel_id=1, source_target_pairs={{0,1},{1,0},{2,3},{3,2},{4,5},{5,4},{6,7},{7,6},{8,9},{9,8},{10,11... | collective-permute-start | bytes 3145736 | tf_op jit(solution)/shard_map/ppermute | solution.py:36
  69.5 14.1 %collective-permute-start.24 = (bf16[256,512]{1,0:T(8,128)(2,1)S(1)}, bf16[256,512]{1,0:T(8,128)(2,1)S(1)}, u32[]{:S(2)}, u32[]{:S(2)}) collective-permute-start(bf16[256,512]{1,0:T(8,128)(2,1)S(1)} %pad_maximum_fusion.17), channel_id=1, source_target_pairs={{0,4},{4,0},{8,12},{12,8},{16,20},{20,16},{24,28},{28,24},{1,5},{5... | collective-permute-start | bytes 786440 | tf_op jit(solution)/shard_map/ppermute | solution.py:36
  130.9 55.6 %collective-permute-start.25 = (bf16[512,1024]{1,0:T(8,128)(2,1)S(1)}, bf16[512,1024]{1,0:T(8,128)(2,1)}, u32[]{:S(2)}, u32[]{:S(2)}) collective-permute-start(bf16[512,1024]{1,0:T(8,128)(2,1)S(1)} %slice.595), channel_id=1, source_target_pairs={{0,1},{1,0},{2,3},{3,2},{4,5},{5,4},{6,7},{7,6},{8,9},{9,8},{10,11... | collective-permute-start | bytes 3145736 | tf_op jit(solution)/shard_map/ppermute | solution.py:36
  133.0 55.7 %collective-permute-start.27 = (bf16[512,1024]{1,0:T(8,128)(2,1)S(1)}, bf16[512,1024]{1,0:T(8,128)(2,1)}, u32[]{:S(2)}, u32[]{:S(2)}) collective-permute-start(bf16[512,1024]{1,0:T(8,128)(2,1)S(1)} %add_convert_fusion.5), channel_id=1, source_target_pairs={{0,2},{1,3},{2,0},{3,1},{4,6},{5,7},{6,4},{7,5},{8,10},{9,11},{10,... | collective-permute-start | bytes 3145736 | tf_op jit(solution)/shard_map/ppermute | solution.py:36
  135.4 25.2 %collective-permute-start.30 = (bf16[128,1024]{1,0:T(8,128)(2,1)S(1)}, bf16[128,1024]{1,0:T(8,128)(2,1)S(1)}, u32[]{:S(2)}, u32[]{:S(2)}) collective-permute-start(bf16[128,1024]{1,0:T(8,128)(2,1)S(1)} %copy-done.41), channel_id=1, source_target_pairs={{16,0},{20,4},{24,8},{28,12},{0,16},{4,20},{8,24},{12,28},{17,1},{... | collective-permute-start | bytes 786440 | tf_op jit(solution)/shard_map/ppermute | solution.py:40
  137.5 23.1 %collective-permute-start.31 = (bf16[128,1024]{1,0:T(8,128)(2,1)S(1)}, bf16[128,1024]{1,0:T(8,128)(2,1)S(1)}, u32[]{:S(2)}, u32[]{:S(2)}) collective-permute-start(bf16[128,1024]{1,0:T(8,128)(2,1)S(1)} %copy-done.41), channel_id=1, source_target_pairs={{24,0},{28,4},{0,8},{4,12},{8,16},{12,20},{16,24},{20,28},{25,1},{... | collective-permute-start | bytes 786440 | tf_op jit(solution)/shard_map/ppermute | solution.py:40
  160.7 24.3 %collective-permute-start.34 = (bf16[128,1024]{1,0:T(8,128)(2,1)}, bf16[128,1024]{1,0:T(8,128)(2,1)S(1)}, u32[]{:S(2)}, u32[]{:S(2)}) collective-permute-start(bf16[128,1024]{1,0:T(8,128)(2,1)} %param.25), channel_id=1, source_target_pairs={{16,0},{20,4},{24,8},{28,12},{0,16},{4,20},{8,24},{12,28},{17,1},{... | collective-permute-start | bytes 786440 | tf_op jit(solution)/shard_map/ppermute | solution.py:40
  161.3 23.7 %collective-permute-start.35 = (bf16[128,1024]{1,0:T(8,128)(2,1)}, bf16[128,1024]{1,0:T(8,128)(2,1)S(1)}, u32[]{:S(2)}, u32[]{:S(2)}) collective-permute-start(bf16[128,1024]{1,0:T(8,128)(2,1)} %param.25), channel_id=1, source_target_pairs={{24,0},{28,4},{0,8},{4,12},{8,16},{12,20},{16,24},{20,28},{25,1},{... | collective-permute-start | bytes 786440 | tf_op jit(solution)/shard_map/ppermute | solution.py:40
  169.0 47.7 %collective-permute-start.32 = (bf16[512,1024]{1,0:T(8,128)(2,1)S(1)}, bf16[512,1024]{1,0:T(8,128)(2,1)S(1)}, u32[]{:S(2)}, u32[]{:S(2)}) collective-permute-start(bf16[512,1024]{1,0:T(8,128)(2,1)S(1)} %pad_maximum_fusion.10), channel_id=1, source_target_pairs={{0,4},{4,0},{8,12},{12,8},{16,20},{20,16},{24,28},{28,24},{1,5},{5... | collective-permute-start | bytes 3145736 | tf_op jit(solution)/shard_map/ppermute | solution.py:36
  185.0 9.0 %collective-permute-start.37 = (bf16[1024,128]{1,0:T(8,128)(2,1)S(1)}, bf16[1024,128]{1,0:T(8,128)(2,1)S(1)}, u32[]{:S(2)}, u32[]{:S(2)}) collective-permute-start(bf16[1024,128]{1,0:T(8,128)(2,1)S(1)} %copy-done.43), channel_id=1, source_target_pairs={{8,0},{12,4},{16,8},{20,12},{24,16},{28,20},{0,24},{4,28},{9,1},{1... | collective-permute-start | bytes 786440 | tf_op jit(solution)/shard_map/ppermute | solution.py:40
  185.0 24.8 %collective-permute-start.38 = (bf16[1024,128]{1,0:T(8,128)(2,1)S(1)}, bf16[1024,128]{1,0:T(8,128)(2,1)S(1)}, u32[]{:S(2)}, u32[]{:S(2)}) collective-permute-start(bf16[1024,128]{1,0:T(8,128)(2,1)S(1)} %copy-done.43), channel_id=1, source_target_pairs={{16,0},{20,4},{24,8},{28,12},{0,16},{4,20},{8,24},{12,28},{17,1},{... | collective-permute-start | bytes 786440 | tf_op jit(solution)/shard_map/ppermute | solution.py:40
  186.5 23.3 %collective-permute-start.39 = (bf16[1024,128]{1,0:T(8,128)(2,1)S(1)}, bf16[1024,128]{1,0:T(8,128)(2,1)S(1)}, u32[]{:S(2)}, u32[]{:S(2)}) collective-permute-start(bf16[1024,128]{1,0:T(8,128)(2,1)S(1)} %copy-done.43), channel_id=1, source_target_pairs={{24,0},{28,4},{0,8},{4,12},{8,16},{12,20},{16,24},{20,28},{25,1},{... | collective-permute-start | bytes 786440 | tf_op jit(solution)/shard_map/ppermute | solution.py:40
  192.4 24.3 %collective-permute-start.42 = (bf16[512,1024]{1,0:T(8,128)(2,1)S(1)}, bf16[512,1024]{1,0:T(8,128)(2,1)S(1)}, u32[]{:S(2)}, u32[]{:S(2)}) collective-permute-start(bf16[512,1024]{1,0:T(8,128)(2,1)S(1)} %multiply_convert_fusion.9), channel_id=1, source_target_pairs={{0,2},{1,3},{2,0},{3,1},{4,6},{5,7},{6,4},{7,5},{8,10},{9,11},{10,... | collective-permute-start | bytes 3145736 | tf_op jit(solution)/shard_map/ppermute | solution.py:36
  194.0 26.2 %collective-permute-start.36 = (bf16[512,1024]{1,0:T(8,128)(2,1)S(1)}, bf16[512,1024]{1,0:T(8,128)(2,1)S(1)}, u32[]{:S(2)}, u32[]{:S(2)}) collective-permute-start(bf16[512,1024]{1,0:T(8,128)(2,1)S(1)} %pad_maximum_fusion.11), channel_id=1, source_target_pairs={{0,4},{4,0},{8,12},{12,8},{16,20},{20,16},{24,28},{28,24},{1,5},{5... | collective-permute-start | bytes 3145736 | tf_op jit(solution)/shard_map/ppermute | solution.py:36
  209.9 30.5 %collective-permute-start.40 = (bf16[1024,512]{1,0:T(8,128)(2,1)S(1)}, bf16[1024,512]{1,0:T(8,128)(2,1)S(1)}, u32[]{:S(2)}, u32[]{:S(2)}) collective-permute-start(bf16[1024,512]{1,0:T(8,128)(2,1)S(1)} %pad_maximum_fusion.12), channel_id=1, source_target_pairs={{0,4},{4,0},{8,12},{12,8},{16,20},{20,16},{24,28},{28,24},{1,5},{5... | collective-permute-start | bytes 3145736 | tf_op jit(solution)/shard_map/ppermute | solution.py:36
  210.1 30.6 %collective-permute-start.28 = (bf16[512,1024]{1,0:T(8,128)(2,1)S(1)}, bf16[512,1024]{1,0:T(8,128)(2,1)S(1)}, u32[]{:S(2)}, u32[]{:S(2)}) collective-permute-start(bf16[512,1024]{1,0:T(8,128)(2,1)S(1)} %multiply_convert_fusion.9), channel_id=1, source_target_pairs={{0,1},{1,0},{2,3},{3,2},{4,5},{5,4},{6,7},{7,6},{8,9},{9,8},{10,11... | collective-permute-start | bytes 3145736 | tf_op jit(solution)/shard_map/ppermute | solution.py:36
  216.7 26.4 %collective-permute-start.43 = (bf16[512,1024]{1,0:T(8,128)(2,1)S(1)}, bf16[512,1024]{1,0:T(8,128)(2,1)S(1)}, u32[]{:S(2)}, u32[]{:S(2)}) collective-permute-start(bf16[512,1024]{1,0:T(8,128)(2,1)S(1)} %collective-permute-done.42), channel_id=1, source_target_pairs={{0,1},{1,0},{2,3},{3,2},{4,5},{5,4},{6,7},{7,6},{8,9},{9,8},{10,11... | collective-permute-start | bytes 3145736 | tf_op jit(solution)/shard_map/ppermute | solution.py:36
  260.5 16.2 %collective-permute-start.41 = (bf16[512,1024]{1,0:T(8,128)(2,1)}, bf16[512,1024]{1,0:T(8,128)(2,1)}, u32[]{:S(2)}, u32[]{:S(2)}) collective-permute-start(bf16[512,1024]{1,0:T(8,128)(2,1)} %slice.594), channel_id=1, source_target_pairs={{0,1},{1,0},{2,3},{3,2},{4,5},{5,4},{6,7},{7,6},{8,9},{9,8},{10,11... | collective-permute-start | bytes 3145736 | tf_op jit(solution)/shard_map/ppermute | solution.py:36
  261.6 25.6 %collective-permute-start.45 = (bf16[512,1024]{1,0:T(8,128)(2,1)S(1)}, bf16[512,1024]{1,0:T(8,128)(2,1)}, u32[]{:S(2)}, u32[]{:S(2)}) collective-permute-start(bf16[512,1024]{1,0:T(8,128)(2,1)S(1)} %add_convert_fusion.4), channel_id=1, source_target_pairs={{0,2},{1,3},{2,0},{3,1},{4,6},{5,7},{6,4},{7,5},{8,10},{9,11},{10,... | collective-permute-start | bytes 3145736 | tf_op jit(solution)/shard_map/ppermute | solution.py:36
  296.2 25.1 %collective-permute-start.48 = (bf16[512,1024]{1,0:T(8,128)(2,1)}, bf16[512,1024]{1,0:T(8,128)(2,1)}, u32[]{:S(2)}, u32[]{:S(2)}) collective-permute-start(bf16[512,1024]{1,0:T(8,128)(2,1)} %multiply_convert_fusion.7), channel_id=1, source_target_pairs={{0,2},{1,3},{2,0},{3,1},{4,6},{5,7},{6,4},{7,5},{8,10},{9,11},{10,... | collective-permute-start | bytes 3145736 | tf_op jit(solution)/shard_map/ppermute | solution.py:36
  297.1 25.4 %collective-permute-start.46 = (bf16[512,1024]{1,0:T(8,128)(2,1)}, bf16[512,1024]{1,0:T(8,128)(2,1)}, u32[]{:S(2)}, u32[]{:S(2)}) collective-permute-start(bf16[512,1024]{1,0:T(8,128)(2,1)} %multiply_convert_fusion.7), channel_id=1, source_target_pairs={{0,1},{1,0},{2,3},{3,2},{4,5},{5,4},{6,7},{7,6},{8,9},{9,8},{10,11... | collective-permute-start | bytes 3145736 | tf_op jit(solution)/shard_map/ppermute | solution.py:36
  321.2 11.4 %collective-permute-start.49 = (bf16[512,1024]{1,0:T(8,128)(2,1)}, bf16[512,1024]{1,0:T(8,128)(2,1)S(1)}, u32[]{:S(2)}, u32[]{:S(2)}) collective-permute-start(bf16[512,1024]{1,0:T(8,128)(2,1)} %collective-permute-done.48), channel_id=1, source_target_pairs={{0,1},{1,0},{2,3},{3,2},{4,5},{5,4},{6,7},{7,6},{8,9},{9,8},{10,11... | collective-permute-start | bytes 3145736 | tf_op jit(solution)/shard_map/ppermute | solution.py:36
  356.5 27.4 %collective-permute-start.50 = (bf16[512,1024]{1,0:T(8,128)(2,1)S(1)}, bf16[512,1024]{1,0:T(8,128)(2,1)S(1)}, u32[]{:S(2)}, u32[]{:S(2)}) collective-permute-start(bf16[512,1024]{1,0:T(8,128)(2,1)S(1)} %slice.410), channel_id=1, source_target_pairs={{0,1},{1,0},{2,3},{3,2},{4,5},{5,4},{6,7},{7,6},{8,9},{9,8},{10,11... | collective-permute-start | bytes 3145736 | tf_op jit(solution)/shard_map/ppermute | solution.py:36
  362.1 56.8 %collective-permute-start.47 = (bf16[512,1024]{1,0:T(8,128)(2,1)S(1)}, bf16[512,1024]{1,0:T(8,128)(2,1)S(1)}, u32[]{:S(2)}, u32[]{:S(2)}) collective-permute-start(bf16[512,1024]{1,0:T(8,128)(2,1)S(1)} %slice.593), channel_id=1, source_target_pairs={{0,1},{1,0},{2,3},{3,2},{4,5},{5,4},{6,7},{7,6},{8,9},{9,8},{10,11... | collective-permute-start | bytes 3145736 | tf_op jit(solution)/shard_map/ppermute | solution.py:36
  369.0 26.1 %collective-permute-start.74 = (bf16[512,1024]{1,0:T(8,128)(2,1)S(1)}, bf16[512,1024]{1,0:T(8,128)(2,1)S(1)}, u32[]{:S(2)}, u32[]{:S(2)}) collective-permute-start(bf16[512,1024]{1,0:T(8,128)(2,1)S(1)} %slice.591), channel_id=1, source_target_pairs={{0,4},{4,0},{8,12},{12,8},{16,20},{20,16},{24,28},{28,24},{1,5},{5... | collective-permute-start | bytes 3145736 | tf_op jit(solution)/shard_map/ppermute | solution.py:36
  382.2 35.3 %collective-permute-start.78 = (bf16[512,1024]{1,0:T(8,128)(2,1)S(1)}, bf16[512,1024]{1,0:T(8,128)(2,1)S(1)}, u32[]{:S(2)}, u32[]{:S(2)}) collective-permute-start(bf16[512,1024]{1,0:T(8,128)(2,1)S(1)} %slice.590), channel_id=1, source_target_pairs={{0,4},{4,0},{8,12},{12,8},{16,20},{20,16},{24,28},{28,24},{1,5},{5... | collective-permute-start | bytes 3145736 | tf_op jit(solution)/shard_map/ppermute | solution.py:36
  384.3 36.6 %collective-permute-start.51 = (bf16[512,1024]{1,0:T(8,128)(2,1)S(1)}, bf16[512,1024]{1,0:T(8,128)(2,1)}, u32[]{:S(2)}, u32[]{:S(2)}) collective-permute-start(bf16[512,1024]{1,0:T(8,128)(2,1)S(1)} %add_convert_fusion.3), channel_id=1, source_target_pairs={{0,2},{1,3},{2,0},{3,1},{4,6},{5,7},{6,4},{7,5},{8,10},{9,11},{10,... | collective-permute-start | bytes 3145736 | tf_op jit(solution)/shard_map/ppermute | solution.py:36
  387.9 51.2 %collective-permute-start.82 = (bf16[1024,512]{1,0:T(8,128)(2,1)S(1)}, bf16[1024,512]{1,0:T(8,128)(2,1)S(1)}, u32[]{:S(2)}, u32[]{:S(2)}) collective-permute-start(bf16[1024,512]{1,0:T(8,128)(2,1)S(1)} %slice.589), channel_id=1, source_target_pairs={{0,4},{4,0},{8,12},{12,8},{16,20},{20,16},{24,28},{28,24},{1,5},{5... | collective-permute-start | bytes 3145736 | tf_op jit(solution)/shard_map/ppermute | solution.py:36
  395.6 44.3 %collective-permute-start.77 = (bf16[128,1024]{1,0:T(8,128)(2,1)S(1)}, bf16[128,1024]{1,0:T(8,128)(2,1)S(1)}, u32[]{:S(2)}, u32[]{:S(2)}) collective-permute-start(bf16[128,1024]{1,0:T(8,128)(2,1)S(1)} %get-tuple-element.133), channel_id=1, source_target_pairs={{0,24},{4,28},{8,0},{12,4},{16,8},{20,12},{24,16},{28,20},{1,25},{... | collective-permute-start | bytes 786440 | tf_op jit(solution)/shard_map/ppermute | solution.py:46
  417.5 24.4 %collective-permute-start.76 = (bf16[128,1024]{1,0:T(8,128)(2,1)S(1)}, bf16[128,1024]{1,0:T(8,128)(2,1)S(1)}, u32[]{:S(2)}, u32[]{:S(2)}) collective-permute-start(bf16[128,1024]{1,0:T(8,128)(2,1)S(1)} %get-tuple-element.134), channel_id=1, source_target_pairs={{0,16},{4,20},{8,24},{12,28},{16,0},{20,4},{24,8},{28,12},{1,17},{... | collective-permute-start | bytes 786440 | tf_op jit(solution)/shard_map/ppermute | solution.py:46
  419.0 23.0 %collective-permute-start.75 = (bf16[128,1024]{1,0:T(8,128)(2,1)S(1)}, bf16[128,1024]{1,0:T(8,128)(2,1)S(1)}, u32[]{:S(2)}, u32[]{:S(2)}) collective-permute-start(bf16[128,1024]{1,0:T(8,128)(2,1)S(1)} %get-tuple-element.132), channel_id=1, source_target_pairs={{0,8},{4,12},{8,16},{12,20},{16,24},{20,28},{24,0},{28,4},{1,9},{5... | collective-permute-start | bytes 786440 | tf_op jit(solution)/shard_map/ppermute | solution.py:46
  427.3 50.4 %collective-permute-start.53 = (bf16[512,1024]{1,0:T(8,128)(2,1)S(1)}, bf16[512,1024]{1,0:T(8,128)(2,1)S(1)}, u32[]{:S(2)}, u32[]{:S(2)}) collective-permute-start(bf16[512,1024]{1,0:T(8,128)(2,1)S(1)} %multiply_convert_fusion.6), channel_id=1, source_target_pairs={{0,2},{1,3},{2,0},{3,1},{4,6},{5,7},{6,4},{7,5},{8,10},{9,11},{10,... | collective-permute-start | bytes 3145736 | tf_op jit(solution)/shard_map/ppermute | solution.py:36
  439.6 49.9 %collective-permute-start.52 = (bf16[512,1024]{1,0:T(8,128)(2,1)S(1)}, bf16[512,1024]{1,0:T(8,128)(2,1)}, u32[]{:S(2)}, u32[]{:S(2)}) collective-permute-start(bf16[512,1024]{1,0:T(8,128)(2,1)S(1)} %multiply_convert_fusion.6), channel_id=1, source_target_pairs={{0,1},{1,0},{2,3},{3,2},{4,5},{5,4},{6,7},{7,6},{8,9},{9,8},{10,11... | collective-permute-start | bytes 3145736 | tf_op jit(solution)/shard_map/ppermute | solution.py:36
  439.8 9.2 %collective-permute-start.81 = (bf16[128,1024]{1,0:T(8,128)(2,1)S(1)}, bf16[128,1024]{1,0:T(8,128)(2,1)S(1)}, u32[]{:S(2)}, u32[]{:S(2)}) collective-permute-start(bf16[128,1024]{1,0:T(8,128)(2,1)S(1)} %get-tuple-element.130), channel_id=1, source_target_pairs={{0,24},{4,28},{8,0},{12,4},{16,8},{20,12},{24,16},{28,20},{1,25},{... | collective-permute-start | bytes 786440 | tf_op jit(solution)/shard_map/ppermute | solution.py:46
  442.0 23.8 %collective-permute-start.80 = (bf16[128,1024]{1,0:T(8,128)(2,1)S(1)}, bf16[128,1024]{1,0:T(8,128)(2,1)S(1)}, u32[]{:S(2)}, u32[]{:S(2)}) collective-permute-start(bf16[128,1024]{1,0:T(8,128)(2,1)S(1)} %get-tuple-element.131), channel_id=1, source_target_pairs={{0,16},{4,20},{8,24},{12,28},{16,0},{20,4},{24,8},{28,12},{1,17},{... | collective-permute-start | bytes 786440 | tf_op jit(solution)/shard_map/ppermute | solution.py:46
  442.0 23.8 %collective-permute-start.79 = (bf16[128,1024]{1,0:T(8,128)(2,1)S(1)}, bf16[128,1024]{1,0:T(8,128)(2,1)S(1)}, u32[]{:S(2)}, u32[]{:S(2)}) collective-permute-start(bf16[128,1024]{1,0:T(8,128)(2,1)S(1)} %get-tuple-element.129), channel_id=1, source_target_pairs={{0,8},{4,12},{8,16},{12,20},{16,24},{20,28},{24,0},{28,4},{1,9},{5... | collective-permute-start | bytes 786440 | tf_op jit(solution)/shard_map/ppermute | solution.py:46
  449.1 30.2 %collective-permute-start.85 = (bf16[1024,128]{1,0:T(8,128)(2,1)S(1)}, bf16[1024,128]{1,0:T(8,128)(2,1)S(1)}, u32[]{:S(2)}, u32[]{:S(2)}) collective-permute-start(bf16[1024,128]{1,0:T(8,128)(2,1)S(1)} %get-tuple-element.127), channel_id=1, source_target_pairs={{0,24},{4,28},{8,0},{12,4},{16,8},{20,12},{24,16},{28,20},{1,25},{... | collective-permute-start | bytes 786440 | tf_op jit(solution)/shard_map/ppermute | solution.py:46
  465.8 21.9 %collective-permute-start.84 = (bf16[1024,128]{1,0:T(8,128)(2,1)S(1)}, bf16[1024,128]{1,0:T(8,128)(2,1)S(1)}, u32[]{:S(2)}, u32[]{:S(2)}) collective-permute-start(bf16[1024,128]{1,0:T(8,128)(2,1)S(1)} %get-tuple-element.128), channel_id=1, source_target_pairs={{0,16},{4,20},{8,24},{12,28},{16,0},{20,4},{24,8},{28,12},{1,17},{... | collective-permute-start | bytes 786440 | tf_op jit(solution)/shard_map/ppermute | solution.py:46
  465.8 21.9 %collective-permute-start.83 = (bf16[1024,128]{1,0:T(8,128)(2,1)S(1)}, bf16[1024,128]{1,0:T(8,128)(2,1)S(1)}, u32[]{:S(2)}, u32[]{:S(2)}) collective-permute-start(bf16[1024,128]{1,0:T(8,128)(2,1)S(1)} %get-tuple-element.126), channel_id=1, source_target_pairs={{0,8},{4,12},{8,16},{12,20},{16,24},{20,28},{24,0},{28,4},{1,9},{5... | collective-permute-start | bytes 786440 | tf_op jit(solution)/shard_map/ppermute | solution.py:46
  477.7 16.9 %collective-permute-start.54 = (bf16[512,1024]{1,0:T(8,128)(2,1)S(1)}, bf16[512,1024]{1,0:T(8,128)(2,1)}, u32[]{:S(2)}, u32[]{:S(2)}) collective-permute-start(bf16[512,1024]{1,0:T(8,128)(2,1)S(1)} %collective-permute-done.53), channel_id=1, source_target_pairs={{0,1},{1,0},{2,3},{3,2},{4,5},{5,4},{6,7},{7,6},{8,9},{9,8},{10,11... | collective-permute-start | bytes 3145736 | tf_op jit(solution)/shard_map/ppermute | solution.py:36
  558.9 78.6 %collective-permute-start.56 = (bf16[512,1024]{1,0:T(8,128)(2,1)}, bf16[512,1024]{1,0:T(8,128)(2,1)}, u32[]{:S(2)}, u32[]{:S(2)}) collective-permute-start(bf16[512,1024]{1,0:T(8,128)(2,1)} %slice.414), channel_id=1, source_target_pairs={{0,1},{1,0},{2,3},{3,2},{4,5},{5,4},{6,7},{7,6},{8,9},{9,8},{10,11... | collective-permute-start | bytes 3145736 | tf_op jit(solution)/shard_map/ppermute | solution.py:36
  560.8 111.9 %collective-permute-start.55 = (bf16[512,1024]{1,0:T(8,128)(2,1)}, bf16[512,1024]{1,0:T(8,128)(2,1)}, u32[]{:S(2)}, u32[]{:S(2)}) collective-permute-start(bf16[512,1024]{1,0:T(8,128)(2,1)} %slice.592), channel_id=1, source_target_pairs={{0,1},{1,0},{2,3},{3,2},{4,5},{5,4},{6,7},{7,6},{8,9},{9,8},{10,11... | collective-permute-start | bytes 3145736 | tf_op jit(solution)/shard_map/ppermute | solution.py:36
  579.5 10.9 %collective-permute-start.91 = (f32[12,128]{1,0:T(8,128)S(1)}, f32[12,128]{1,0:T(8,128)S(1)}, u32[]{:S(2)}, u32[]{:S(2)}) collective-permute-start(f32[12,128]{1,0:T(8,128)S(1)} %get-tuple-element.150), channel_id=1, source_target_pairs={{0,24},{4,28},{8,0},{12,4},{16,8},{20,12},{24,16},{28,20},{1,25},{... | collective-permute-start | bytes 18440 | tf_op jit(solution)/shard_map/ppermute | solution.py:46
  579.5 10.9 %collective-permute-start.90 = (f32[12,128]{1,0:T(8,128)S(1)}, f32[12,128]{1,0:T(8,128)S(1)}, u32[]{:S(2)}, u32[]{:S(2)}) collective-permute-start(f32[12,128]{1,0:T(8,128)S(1)} %get-tuple-element.151), channel_id=1, source_target_pairs={{0,16},{4,20},{8,24},{12,28},{16,0},{20,4},{24,8},{28,12},{1,17},{... | collective-permute-start | bytes 18440 | tf_op jit(solution)/shard_map/ppermute | solution.py:46
  590.4 9.6 %collective-permute-start.58 = (bf16[512,256]{1,0:T(8,128)(2,1)}, bf16[512,256]{1,0:T(8,128)(2,1)}, u32[]{:S(2)}, u32[]{:S(2)}) collective-permute-start(bf16[512,256]{1,0:T(8,128)(2,1)} %slice.599), channel_id=1, source_target_pairs={{0,4},{4,0},{8,12},{12,8},{16,20},{20,16},{24,28},{28,24},{1,5},{5... | collective-permute-start | bytes 786440 | tf_op jit(solution)/shard_map/ppermute | solution.py:36
  590.5 15.2 %collective-permute-start.62 = (bf16[512,256]{1,0:T(8,128)(2,1)}, bf16[512,256]{1,0:T(8,128)(2,1)}, u32[]{:S(2)}, u32[]{:S(2)}) collective-permute-start(bf16[512,256]{1,0:T(8,128)(2,1)} %slice.598), channel_id=1, source_target_pairs={{0,4},{4,0},{8,12},{12,8},{16,20},{20,16},{24,28},{28,24},{1,5},{5... | collective-permute-start | bytes 786440 | tf_op jit(solution)/shard_map/ppermute | solution.py:36
  592.5 17.3 %collective-permute-start.66 = (bf16[512,256]{1,0:T(8,128)(2,1)}, bf16[512,256]{1,0:T(8,128)(2,1)}, u32[]{:S(2)}, u32[]{:S(2)}) collective-permute-start(bf16[512,256]{1,0:T(8,128)(2,1)} %slice.597), channel_id=1, source_target_pairs={{0,4},{4,0},{8,12},{12,8},{16,20},{20,16},{24,28},{28,24},{1,5},{5... | collective-permute-start | bytes 786440 | tf_op jit(solution)/shard_map/ppermute | solution.py:36
  600.0 12.5 %collective-permute-start.70 = (bf16[256,512]{1,0:T(8,128)(2,1)S(1)}, bf16[256,512]{1,0:T(8,128)(2,1)S(1)}, u32[]{:S(2)}, u32[]{:S(2)}) collective-permute-start(bf16[256,512]{1,0:T(8,128)(2,1)S(1)} %slice.596), channel_id=1, source_target_pairs={{0,4},{4,0},{8,12},{12,8},{16,20},{20,16},{24,28},{28,24},{1,5},{5... | collective-permute-start | bytes 786440 | tf_op jit(solution)/shard_map/ppermute | solution.py:36
  605.6 9.6 %collective-permute-start.61 = (bf16[128,256]{1,0:T(8,128)(2,1)S(1)}, bf16[128,256]{1,0:T(8,128)(2,1)S(1)}, u32[]{:S(2)}, u32[]{:S(2)}) collective-permute-start(bf16[128,256]{1,0:T(8,128)(2,1)S(1)} %get-tuple-element.145), channel_id=1, source_target_pairs={{0,24},{4,28},{8,0},{12,4},{16,8},{20,12},{24,16},{28,20},{1,25},{... | collective-permute-start | bytes 196616 | tf_op jit(solution)/shard_map/ppermute | solution.py:46
  620.6 8.4 %collective-permute-start.69 = (bf16[128,256]{1,0:T(8,128)(2,1)S(1)}, bf16[128,256]{1,0:T(8,128)(2,1)S(1)}, u32[]{:S(2)}, u32[]{:S(2)}) collective-permute-start(bf16[128,256]{1,0:T(8,128)(2,1)S(1)} %get-tuple-element.139), channel_id=1, source_target_pairs={{0,24},{4,28},{8,0},{12,4},{16,8},{20,12},{24,16},{28,20},{1,25},{... | collective-permute-start | bytes 196616 | tf_op jit(solution)/shard_map/ppermute | solution.py:46
  629.1 11.6 %collective-permute-start.73 = (bf16[256,128]{1,0:T(8,128)(2,1)S(1)}, bf16[256,128]{1,0:T(8,128)(2,1)S(1)}, u32[]{:S(2)}, u32[]{:S(2)}) collective-permute-start(bf16[256,128]{1,0:T(8,128)(2,1)S(1)} %get-tuple-element.136), channel_id=1, source_target_pairs={{0,24},{4,28},{8,0},{12,4},{16,8},{20,12},{24,16},{28,20},{1,25},{... | collective-permute-start | bytes 196616 | tf_op jit(solution)/shard_map/ppermute | solution.py:46
  632.0 8.7 %collective-permute-start.72 = (bf16[256,128]{1,0:T(8,128)(2,1)S(1)}, bf16[256,128]{1,0:T(8,128)(2,1)S(1)}, u32[]{:S(2)}, u32[]{:S(2)}) collective-permute-start(bf16[256,128]{1,0:T(8,128)(2,1)S(1)} %get-tuple-element.137), channel_id=1, source_target_pairs={{0,16},{4,20},{8,24},{12,28},{16,0},{20,4},{24,8},{28,12},{1,17},{... | collective-permute-start | bytes 196616 | tf_op jit(solution)/shard_map/ppermute | solution.py:46
  632.3 8.4 %collective-permute-start.71 = (bf16[256,128]{1,0:T(8,128)(2,1)S(1)}, bf16[256,128]{1,0:T(8,128)(2,1)S(1)}, u32[]{:S(2)}, u32[]{:S(2)}) collective-permute-start(bf16[256,128]{1,0:T(8,128)(2,1)S(1)} %get-tuple-element.135), channel_id=1, source_target_pairs={{0,8},{4,12},{8,16},{12,20},{16,24},{20,28},{24,0},{28,4},{1,9},{5... | collective-permute-start | bytes 196616 | tf_op jit(solution)/shard_map/ppermute | solution.py:46
  639.2 33.6 %collective-permute-start.57 = (bf16[512,1024]{1,0:T(8,128)(2,1)S(1)}, bf16[512,1024]{1,0:T(8,128)(2,1)}, u32[]{:S(2)}, u32[]{:S(2)}) collective-permute-start(bf16[512,1024]{1,0:T(8,128)(2,1)S(1)} %add_convert_fusion.2), channel_id=1, source_target_pairs={{0,2},{1,3},{2,0},{3,1},{4,6},{5,7},{6,4},{7,5},{8,10},{9,11},{10,... | collective-permute-start | bytes 3145736 | tf_op jit(solution)/shard_map/ppermute | solution.py:36
  (113 other events, 1028.3 us)

commit v2 on v1

v2 whole, which is shorter than its diff:
```python
import functools

import jax
import jax.numpy as jnp
from jax import lax
from jax.experimental import pallas as pl
from jax.experimental.pallas import tpu as pltpu
from jax.sharding import PartitionSpec as P

D = 1024
HEADS = 16
HEAD = D // HEADS
EPS = 1e-06
NEG = -1e30
BLOCK = 256
F32 = jnp.float32
BF16 = jnp.bfloat16


def mean_rows(tensor):
    return jnp.mean(tensor, axis=-1, keepdims=True)


def normed(tensor):
    factor = lax.rsqrt(mean_rows(tensor * tensor) + EPS)
    return tensor * factor, factor


def normed_back(incoming, unit, factor):
    return factor * (incoming - unit * mean_rows(incoming * unit))


def dot(left, right, left_dim=1, right_dim=0):
    return lax.dot_general(
        left, right, (((left_dim,), (right_dim,)), ((), ())), preferred_element_type=F32
    )


RING = (0, 2, 4, 6, 7, 5, 3, 1)


def swap(array, axis, bit):
    size = lax.axis_size(axis)
    return lax.ppermute(array, axis, [(i, i ^ bit) for i in range(size)])


def to_z(array, step):
    return lax.ppermute(
        array, "dp", [(z * 2 + y, ((z + step) % 4) * 2 + y) for z in range(4) for y in range(2)]
    )


def around(array, step):
    return lax.ppermute(array, "dp", [(RING[p], RING[(p + step) % 8]) for p in range(8)])


def gather(shard, before_last=()):
    if lax.axis_size("dp") != 8:
        return lax.all_gather(shard, "dp", axis=0, tiled=True)
    d = lax.axis_index("dp")
    rows, width = shard.shape
    place = jnp.where((d & 1) == 0, d >> 1, 7 - (d >> 1))

    def put(full, part, step):
        q = (place + step) & 7
        index = jnp.where(q < 4, 2 * q, 2 * (7 - q) + 1)
        return lax.dynamic_update_slice(full, part, (index * rows, jnp.int32(0)))

    full = put(jnp.zeros((8 * rows, width), shard.dtype), shard, 0)
    ahead = behind = shard
    for step in (1, 2, 3):
        ahead, behind = around(ahead, 1), around(behind, -1)
        full = put(put(full, ahead, -step), behind, step)
    if before_last:
        ahead = lax.optimization_barrier((ahead,) + tuple(before_last))[0]
    return put(full, around(ahead, 1), 4)


def chip_groups():
    return [
        [d * 4 + 2 * x + core for d in range(lax.axis_size("dp")) for core in range(2)]
        for x in range(2)
    ]


def scatter(grad):
    if lax.axis_size("dp") != 8:
        return lax.psum_scatter(grad.astype(F32), "dp", scatter_dimension=0, tiled=True)
    d = lax.axis_index("dp")
    z, y = d >> 1, d & 1
    rows, width = grad.shape[0] // 8, grad.shape[1]
    grad = grad.reshape(4, 2, rows, width)
    theirs = lax.dynamic_index_in_dim(grad, 1 - y, axis=1, keepdims=False)
    mine = lax.dynamic_index_in_dim(grad, y, axis=1, keepdims=False)
    half = mine.astype(F32) + swap(theirs.astype(BF16), "dp", 1).astype(F32)
    total = lax.dynamic_index_in_dim(half, z, axis=0, keepdims=False)
    for step in (1, 2, 3):
        part = lax.dynamic_index_in_dim(half, (z + step) & 3, axis=0, keepdims=False)
        total = total + to_z(part.astype(BF16), step).astype(F32)
    return total


def to_all(rows):
    return lax.all_to_all(rows, ("dp", "mp"), 0, 0, tiled=True)


def rotate_half(tensor):
    width = tensor.shape[-1]
    lane = lax.broadcasted_iota(jnp.int32, tensor.shape, 1)
    ahead = pltpu.roll(tensor, width - HEAD // 2, 1)
    behind = pltpu.roll(tensor, HEAD // 2, 1)
    return jnp.where((lane & (HEAD - 1)) < HEAD // 2, -ahead, behind)


def head_mean(tensor):
    width = tensor.shape[-1]
    row = lax.broadcasted_iota(jnp.int32, (width, width), 0) // HEAD
    col = lax.broadcasted_iota(jnp.int32, (width, width), 1) // HEAD
    ones = jnp.where(row == col, 1.0 / HEAD, 0.0).astype(BF16)
    high = tensor.astype(BF16)
    rest = (tensor - high.astype(F32)).astype(BF16)
    return dot(high, ones) + dot(rest, ones)


def wide(table):
    return jnp.concatenate([table, table], axis=1)


def project_body(m_ref, x_ref, wq_ref, wk_ref, wv_ref, cos_ref, sin_ref, sqk_ref, *refs):
    q_ref, k_ref, v_ref, qr_ref, kr_ref = refs[-5:]
    rows = x_ref[...]
    cosine, sine = wide(cos_ref[...]), wide(sin_ref[...])
    scale = sqk_ref[0:1, :]
    for weight_ref, out_ref, rot_ref in ((wq_ref, q_ref, qr_ref), (wk_ref, k_ref, kr_ref)):
        raw = jnp.dot(rows, weight_ref[...], preferred_element_type=F32)
        turned = raw * cosine + rotate_half(raw) * sine
        rot_ref[...] = turned
        unit = turned * lax.rsqrt(head_mean(turned * turned) + EPS)
        out_ref[...] = (unit * scale).astype(BF16)
    v_ref[...] = jnp.dot(rows, wv_ref[...], preferred_element_type=F32).astype(BF16)


def project(place, x_rows, weight, cosine, sine, sqk, previous, first):
    rows, width = x_rows.shape[0], weight.shape[1] // 4
    total = cosine.shape[0]
    per = total // 4 // BLOCK

    def row_block(i, m):
        return ((m[0] ^ (first + 2 * (i // per))) * per + i % per, 0)

    any_spec = pl.BlockSpec(memory_space=pl.ANY)

    def column(index):
        return pl.BlockSpec((x_rows.shape[1], width), lambda i, m: (0, index))

    table = pl.BlockSpec((BLOCK, cosine.shape[1]), row_block)
    out = pl.BlockSpec((BLOCK, width), row_block)
    shapes = [jax.ShapeDtypeStruct((total, width), t) for t in (BF16, BF16, BF16, F32, F32)]
    extra = list(previous) if previous is not None else []
    return pl.pallas_call(
        project_body,
        out_shape=shapes,
        grid_spec=pltpu.PrefetchScalarGridSpec(
            num_scalar_prefetch=1,
            grid=(rows // BLOCK,),
            in_specs=[
                pl.BlockSpec((BLOCK, x_rows.shape[1]), lambda i, m: (i, 0)),
                column(0),
                column(1),
                column(2),
                table,
                table,
                pl.BlockSpec((8, width), lambda i, m: (0, 0)),
            ]
            + [any_spec] * len(extra),
            out_specs=[out] * 5,
        ),
        input_output_aliases={8 + i: i for i in range(len(extra))},
        cost_estimate=pl.CostEstimate(
            flops=6 * rows * D * width, bytes_accessed=8 * rows * D, transcendentals=rows
        ),
        name="project",
    )(place, x_rows, weight, weight, weight, cosine, sine, sqk, *extra)


def head_lanes(array, head):
    lane = lax.broadcasted_iota(jnp.int32, array.shape, 1)
    return jnp.where(lane // HEAD == head, array, jnp.zeros_like(array))


def stack_heads(array):
    heads = array.shape[1] // HEAD
    return jnp.concatenate([head_lanes(array, h) for h in range(heads)], axis=0)


def doc_start(meta_ref, docs, slots):
    start = jnp.zeros_like(slots)
    end = 0
    for i in range(docs):
        length = meta_ref[1 + i]
        end = end + length
        start = start + jnp.where(slots >= end, length, 0)
    return start


def slot_place(rel):
    return (rel >> 1) + 2 * (rel & 1)


def block_at(block):
    return pl.ds(pl.multiple_of(block * BLOCK, BLOCK), BLOCK)


def split_heads(source_ref, split_ref):
    def one(block, carry):
        split_ref[block] = stack_heads(source_ref[block_at(block), :])
        return carry

    lax.fori_loop(0, source_ref.shape[0] // BLOCK, one, 0)


def attend_body(docs, meta_ref, q_ref, k_ref, v_ref, kpos_ref, o_ref, inv_ref, acc_ref, sum_ref, vs_ref):
    step = pl.program_id(0)
    heads = q_ref.shape[1] // HEAD
    base = step * BLOCK
    low = doc_start(meta_ref, docs, base) // BLOCK

    @pl.when(step == 0)
    def _():
        split_heads(v_ref, vs_ref)

    scaled = q_ref[...] * jnp.bfloat16(HEAD**-0.5)
    queries = [head_lanes(scaled, h) for h in range(heads)]
    rows = lax.broadcasted_iota(jnp.int32, (BLOCK, BLOCK), 0) + base
    starts = doc_start(meta_ref, docs, rows)
    acc_ref[...] = jnp.zeros_like(acc_ref)
    sum_ref[...] = jnp.zeros_like(sum_ref)

    def visit(block, allowed):
        keys = k_ref[block_at(block), :]
        bias = jnp.where(allowed, 0.0, NEG)
        expos = []
        for h in range(heads):
            expo = jnp.exp(dot(queries[h], keys, 1, 1) + bias)
            sum_ref[h * BLOCK : (h + 1) * BLOCK, :] += expo[:, :128] + expo[:, 128:]
            expos.append(expo.astype(BF16))
        acc_ref[...] += dot(jnp.concatenate(expos, axis=1), vs_ref[block])

    def off_diagonal(block, carry):
        visit(block, kpos_ref[0:1, block_at(block)] >= starts)
        return carry

    lax.fori_loop(low, step, off_diagonal, 0)
    cols = lax.broadcasted_iota(jnp.int32, (BLOCK, BLOCK), 1) + base
    visit(step, ((kpos_ref[0:1, block_at(step)] >= starts) & (cols <= rows)) | (cols == rows))
    lane = lax.broadcasted_iota(jnp.int32, (BLOCK, q_ref.shape[1]), 1) // HEAD
    inverse = jnp.zeros((BLOCK, q_ref.shape[1]), F32)
    for h in range(heads):
        mass = jnp.sum(sum_ref[h * BLOCK : (h + 1) * BLOCK, :], axis=1, keepdims=True)
        inverse = jnp.where(lane == h, 1.0 / mass, inverse)
    inv_ref[...] = inverse
    o_ref[...] = (acc_ref[...] * inverse).astype(BF16)


def attend(meta, queries, keys, vals, kpos, docs):
    total, width = queries.shape
    per = total // 4 // BLOCK
    heads = width // HEAD
    whole = pl.BlockSpec((total, width), lambda i, m: (0, 0))
    block = pl.BlockSpec((BLOCK, width), lambda i, m: (i, 0))

    def rel(i, m):
        return (slot_place(m[0] ^ (i // per)) * per + i % per, 0)

    return pl.pallas_call(
        functools.partial(attend_body, docs),
        out_shape=[
            jax.ShapeDtypeStruct((total, width), BF16),
            jax.ShapeDtypeStruct((total, width), F32),
        ],
        grid_spec=pltpu.PrefetchScalarGridSpec(
            num_scalar_prefetch=1,
            grid=(total // BLOCK,),
            in_specs=[block, whole, whole, pl.BlockSpec((8, total), lambda i, m: (0, 0))],
            out_specs=[pl.BlockSpec((BLOCK, width), rel), block],
            scratch_shapes=[
                pltpu.VMEM((BLOCK, width), F32),
                pltpu.VMEM((heads * BLOCK, 128), F32),
                pltpu.VMEM((total // BLOCK, heads * BLOCK, width), BF16),
            ],
        ),
        cost_estimate=pl.CostEstimate(
            flops=12_000_000_000, bytes_accessed=8 * total * width, transcendentals=6_000_000
        ),
        name="attend",
    )(meta, queries, keys, vals, kpos)


def finish(grad, turned, cosine, sine, scale):
    factor = lax.rsqrt(head_mean(turned * turned) + EPS)
    unit = turned * factor
    by_scale = jnp.sum(grad * unit, axis=0, keepdims=True)
    scaled = grad * scale
    back = factor * (scaled - unit * head_mean(scaled * unit))
    raw = back * cosine - rotate_half(back) * sine
    return raw.astype(BF16), by_scale


def back_body(
    docs,
    meta_ref,
    q_ref,
    qr_ref,
    o_ref,
    inv_ref,
    do_ref,
    k_ref,
    v_ref,
    kr_ref,
    kpos_ref,
    cos_ref,
    sin_ref,
    sqk_ref,
    g_ref,
    gs_ref,
    dq_ref,
    dk_ref,
    dv_ref,
    ks_ref,
):
    step = pl.program_id(0)
    width = q_ref.shape[1]
    heads = width // HEAD
    per = k_ref.shape[0] // 4 // BLOCK
    base = step * BLOCK
    low = doc_start(meta_ref, docs, base) // BLOCK

    @pl.when(step == 0)
    def _():
        dk_ref[...] = jnp.zeros_like(dk_ref)
        dv_ref[...] = jnp.zeros_like(dv_ref)
        gs_ref[...] = jnp.zeros_like(gs_ref)
        split_heads(k_ref, ks_ref)

    dq_ref[...] = jnp.zeros_like(dq_ref)
    scaled = q_ref[...] * jnp.bfloat16(HEAD**-0.5)
    queries = [head_lanes(scaled, h) for h in range(heads)]
    all_queries = jnp.concatenate(queries, axis=0)
    upward = do_ref[...].astype(F32) * inv_ref[...]
    ups = [head_lanes(upward.astype(BF16), h) for h in range(heads)]
    all_ups = jnp.concatenate(ups, axis=0)
    picks = lax.broadcasted_iota(jnp.int32, (8, width), 0)
    lanes = lax.broadcasted_iota(jnp.int32, (8, width), 1) // HEAD
    delta = lax.dot_general(
        jnp.where(picks == lanes, 1.0, 0.0).astype(F32),
        upward * o_ref[...].astype(F32),
        (((1,), (1,)), ((), ())),
        precision=lax.Precision.HIGHEST,
        preferred_element_type=F32,
    )
    cols = lax.broadcasted_iota(jnp.int32, (BLOCK, BLOCK), 1) + base
    starts = doc_start(meta_ref, docs, cols)

    def visit(block, allowed):
        at = block_at(block)
        keys, vals = k_ref[at, :], v_ref[at, :]
        bias = jnp.where(allowed, 0.0, NEG)
        expos, slopes = [], []
        for h in range(heads):
            expo = jnp.exp(dot(keys, queries[h], 1, 1) + bias)
            expos.append(expo.astype(BF16))
            slope = expo * (dot(vals, ups[h], 1, 1) - delta[h : h + 1, :])
            slopes.append(slope.astype(BF16))
        dv_ref[at, :] += dot(jnp.concatenate(expos, axis=1), all_ups)
        dk_ref[at, :] += dot(jnp.concatenate(slopes, axis=1), all_queries)
        dq_ref[...] += dot(jnp.concatenate(slopes, axis=0), ks_ref[block], 0, 0)

    def key_slots(block):
        return wide(kpos_ref[block_at(block), :])

    def off_diagonal(block, carry):
        visit(block, key_slots(block) >= starts)
        return carry

    lax.fori_loop(low, step, off_diagonal, 0)
    rows = lax.broadcasted_iota(jnp.int32, (BLOCK, BLOCK), 0) + base
    visit(step, ((key_slots(step) >= starts) & (rows <= cols)) | (rows == cols))

    scale = sqk_ref[0:1, :]
    here = pl.ds(pl.multiple_of(base, BLOCK), BLOCK)
    raw, by_scale = finish(
        dq_ref[...] * (HEAD**-0.5),
        qr_ref[...],
        wide(cos_ref[here, :]),
        wide(sin_ref[here, :]),
        scale,
    )
    slot = slot_place(meta_ref[0] ^ (step // per)) * per + step % per
    g_ref[pl.ds(pl.multiple_of(slot * BLOCK, BLOCK), BLOCK), :width] = raw
    gs_ref[0:1, :] += by_scale

    @pl.when(step == pl.num_programs(0) - 1)
    def _():
        def one(block, carry):
            at = pl.ds(pl.multiple_of(block * BLOCK, BLOCK), BLOCK)
            slot = slot_place(meta_ref[0] ^ (block // per)) * per + block % per
            to = pl.ds(pl.multiple_of(slot * BLOCK, BLOCK), BLOCK)
            raw, by_scale = finish(
                dk_ref[at, :], kr_ref[at, :], wide(cos_ref[at, :]), wide(sin_ref[at, :]), scale
            )
            g_ref[to, width : 2 * width] = raw
            gs_ref[0:1, :] += by_scale
            g_ref[to, 2 * width :] = dv_ref[at, :].astype(BF16)
            return carry

        lax.fori_loop(0, pl.num_programs(0), one, 0)


def attend_back(meta, queries, qrot, out, inverse, grad, keys, vals, krot, kpos, cosine, sine, sqk, docs):
    total, width = queries.shape
    per = total // 4 // BLOCK

    def rel(i, m):
        return (slot_place(m[0] ^ (i // per)) * per + i % per, 0)

    whole = pl.BlockSpec((total, width), lambda i, m: (0, 0))
    half = pl.BlockSpec((total, 128), lambda i, m: (0, 0))
    block = pl.BlockSpec((BLOCK, width), lambda i, m: (i, 0))
    moved = pl.BlockSpec((BLOCK, width), rel)
    small = pl.BlockSpec((8, width), lambda i, m: (0, 0))
    return pl.pallas_call(
        functools.partial(back_body, docs),
        out_shape=[
            jax.ShapeDtypeStruct((total, 3 * width), BF16),
            jax.ShapeDtypeStruct((8, width), F32),
        ],
        grid_spec=pltpu.PrefetchScalarGridSpec(
            num_scalar_prefetch=1,
            grid=(total // BLOCK,),
            in_specs=[block, block, moved, block, moved, whole, whole, whole, half, half, half, small],
            out_specs=[pl.BlockSpec((total, 3 * width), lambda i, m: (0, 0)), small],
            scratch_shapes=[
                pltpu.VMEM((BLOCK, width), F32),
                pltpu.VMEM((total, width), F32),
                pltpu.VMEM((total, width), F32),
                pltpu.VMEM((total // BLOCK, width // HEAD * BLOCK, width), BF16),
            ],
        ),
        cost_estimate=pl.CostEstimate(
            flops=30_000_000_000, bytes_accessed=24 * total * width, transcendentals=6_000_000
        ),
        name="attend_back",
    )(meta, queries, qrot, out, inverse, grad, keys, vals, krot, kpos, cosine, sine, sqk)


TILE = 256


def weight_tile(weight_ref, part, index):
    return weight_ref[:, part, index].reshape(D, TILE)


def weight_spec(weights):
    return pl.BlockSpec(weights.shape[:4] + (TILE,), lambda t: (0, 0, 0, 0, t))


def forward_body(
    h_ref, w_ref, sup_ref, sgate_ref, gate_ref, act_ref, by_up_ref, by_gate_ref, out_ref, acc_ref
):
    t = pl.program_id(0)
    rows = h_ref[...]
    acts = []
    for part in range(2):
        sup, sgate = sup_ref[part, 0:1, :], sgate_ref[part, 0:1, :]
        scaled = sup * dot(rows, weight_tile(w_ref, part, 0))
        gate_proj = dot(rows, weight_tile(w_ref, part, 1))
        outer = sgate * gate_proj
        sigma = jax.nn.sigmoid(outer)
        silu = outer * sigma
        acts.append((scaled * silu).astype(BF16))
        gate_ref[part] = gate_proj.astype(BF16)
        act_ref[part] = acts[part]
        by_up_ref[part] = (sup * silu).astype(BF16)
        by_gate_ref[part] = ((sgate * scaled) * (sigma + silu * (1.0 - sigma))).astype(BF16)
    total = dot(
        jnp.concatenate(acts, axis=1),
        jnp.concatenate([weight_tile(w_ref, part, 2) for part in range(2)], axis=1),
        1,
        1,
    )
    add_up(t, total, acc_ref, out_ref)


def add_up(t, total, acc_ref, out_ref):
    @pl.when(t == 0)
    def _():
        acc_ref[...] = total

    @pl.when((t > 0) & (t < pl.num_programs(0) - 1))
    def _():
        acc_ref[...] += total

    @pl.when(t == pl.num_programs(0) - 1)
    def _():
        out_ref[...] = (acc_ref[...] + total).astype(out_ref.dtype)


def ffn_specs(count):
    whole = pl.BlockSpec((count, D), lambda t: (0, 0))
    tile = pl.BlockSpec((2, count, TILE), lambda t: (0, 0, t))
    scale = pl.BlockSpec((2, 8, TILE), lambda t: (0, 0, t))
    return whole, tile, scale


def ffn_forward(rows, weights, sup, sgate, kind):
    count, hidden = rows.shape[0], sup.shape[2]
    whole, tile, scale = ffn_specs(count)
    return pl.pallas_call(
        forward_body,
        out_shape=[jax.ShapeDtypeStruct((2, count, hidden), BF16)] * 4
        + [jax.ShapeDtypeStruct((count, D), kind)],
        grid=(hidden // TILE,),
        in_specs=[whole, weight_spec(weights), scale, scale],
        out_specs=[tile] * 4 + [whole],
        scratch_shapes=[pltpu.VMEM((count, D), F32)],
        cost_estimate=pl.CostEstimate(
            flops=12 * count * D * hidden,
            bytes_accessed=12 * D * hidden + 12 * count * hidden,
            transcendentals=2 * count * hidden,
        ),
        name="ffn_forward",
    )(rows, weights, sup, sgate)


def backward_body(
    gm_ref, w_ref, gate_ref, act_ref, by_up_ref, by_gate_ref, sup_ref, sgate_ref, gu_ref, gg_ref, bu_ref, bg_ref, out_ref, acc_ref
):
    t = pl.program_id(0)
    rows = gm_ref[...]
    lefts, rights = [], []
    for part in range(2):
        g_act = dot(rows, weight_tile(w_ref, part, 2))
        g_up = (g_act * by_up_ref[part].astype(F32)).astype(BF16)
        g_gate = g_act * by_gate_ref[part].astype(F32)
        up_sum = jnp.sum(g_act * act_ref[part].astype(F32), axis=0, keepdims=True)
        gate_sum = jnp.sum(g_gate * gate_ref[part].astype(F32), axis=0, keepdims=True)
        g_gate = g_gate.astype(BF16)
        bu_ref[part, 0:1, :] = up_sum / sup_ref[part, 0:1, :]
        bg_ref[part, 0:1, :] = gate_sum / sgate_ref[part, 0:1, :]
        gu_ref[part] = g_up
        gg_ref[part] = g_gate
        lefts += [g_up, g_gate]
        rights += [weight_tile(w_ref, part, 0), weight_tile(w_ref, part, 1)]
    total = dot(jnp.concatenate(lefts, axis=1), jnp.concatenate(rights, axis=1), 1, 1)
    add_up(t, total, acc_ref, out_ref)


def ffn_backward(grads, weights, saved, sup, sgate, kind):
    count, hidden = grads.shape[0], sup.shape[2]
    whole, tile, scale = ffn_specs(count)
    return pl.pallas_call(
        backward_body,
        out_shape=[jax.ShapeDtypeStruct((2, count, hidden), BF16)] * 2
        + [jax.ShapeDtypeStruct((2, 8, hidden), F32)] * 2
        + [jax.ShapeDtypeStruct((count, D), kind)],
        grid=(hidden // TILE,),
        in_specs=[whole, weight_spec(weights)] + [tile] * 4 + [scale, scale],
        out_specs=[tile, tile, scale, scale, whole],
        scratch_shapes=[pltpu.VMEM((count, D), F32)],
        cost_estimate=pl.CostEstimate(
            flops=12 * count * D * hidden,
            bytes_accessed=12 * D * hidden + 24 * count * hidden,
            transcendentals=0,
        ),
        name="ffn_backward",
    )(grads, weights, *saved, sup, sgate)


def turn_rows(own_ref, far_ref, turned_ref):
    count = own_ref.shape[0]

    @pl.when(pl.program_id(0) == 0)
    def _():
        turned_ref[:, :count] = own_ref[...].T
        turned_ref[:, count:] = far_ref[...].T


def down_grad_body(m_ref, lo_ref, lr_ref, ro_ref, rr_ref, mine_ref, other_ref, turned_ref):
    turn_rows(lo_ref, lr_ref, turned_ref)
    core = m_ref[0] & 1
    for part, out_ref in ((core, mine_ref), (1 - core, other_ref)):
        right = jnp.concatenate([ro_ref[part], rr_ref[part]], axis=0)
        out_ref[...] = dot(turned_ref[...], right).astype(BF16)


def up_grad_body(m_ref, lo_ref, lr_ref, uo_ref, ur_ref, go_ref, gr_ref, out_ref, turned_ref):
    turn_rows(lo_ref, lr_ref, turned_ref)
    for index, (own_ref, far_ref) in enumerate(((uo_ref, ur_ref), (go_ref, gr_ref))):
        for part in range(2):
            right = jnp.concatenate([own_ref[part], far_ref[part]], axis=0)
            total = dot(turned_ref[...], right).astype(BF16)
            out_ref[:, part, index] = total.reshape(out_ref.shape[0], out_ref.shape[3], TILE)


def weight_grad(body, place, lefts, rights, out_shape, out_specs):
    _, count, hidden = rights[0].shape
    whole = pl.BlockSpec((count, D), lambda t, m: (0, 0))
    tile = pl.BlockSpec((2, count, TILE), lambda t, m: (0, 0, t))
    pairs = len(rights) // 2
    return pl.pallas_call(
        body,
        out_shape=out_shape,
        grid_spec=pltpu.PrefetchScalarGridSpec(
            num_scalar_prefetch=1,
            grid=(hidden // TILE,),
            in_specs=[whole, whole] + [tile] * len(rights),
            out_specs=out_specs,
            scratch_shapes=[pltpu.VMEM((D, 2 * count), BF16)],
        ),
        cost_estimate=pl.CostEstimate(
            flops=8 * pairs * count * D * hidden,
            bytes_accessed=pairs * (4 * D * hidden + 8 * count * hidden),
            transcendentals=0,
        ),
        name="weight_grad",
    )(place, *lefts, *rights)


def own_call(body, name, rows_in, vectors, wholes, outs, sums, flops):
    count = outs[0][0]
    blocks = count // BLOCK

    def rows_spec(width, skip, column):
        return pl.BlockSpec((BLOCK, width), lambda i: (skip // BLOCK + i, column))

    in_specs = [rows_spec(w, s, c) for _, w, s, c in rows_in]
    in_specs += [pl.BlockSpec((8, v.shape[1]), lambda i: (0, 0)) for v in vectors]
    in_specs += [pl.BlockSpec((D, w), lambda i, c=c: (0, c)) for _, w, c in wholes]
    shapes = [jax.ShapeDtypeStruct((count, w), t) for count, w, t in outs]
    shapes += [jax.ShapeDtypeStruct((8, D), F32)] * sums
    out_specs = [pl.BlockSpec((BLOCK, w), lambda i: (i, 0)) for _, w, _ in outs]
    out_specs += [pl.BlockSpec((8, D), lambda i: (0, 0))] * sums
    return pl.pallas_call(
        body,
        out_shape=shapes,
        grid=(blocks,),
        in_specs=in_specs,
        out_specs=out_specs,
        cost_estimate=pl.CostEstimate(
            flops=flops, bytes_accessed=20 * count * D, transcendentals=count
        ),
        name=name,
    )(*[a for a, *_ in rows_in], *vectors, *[a for a, *_ in wholes])


def first_update(branch, x_rows, alpha):
    h_attn, attn_factor = normed(branch)
    hidden, one_factor = normed(x_rows + alpha * (h_attn - x_rows))
    return h_attn, attn_factor, hidden, one_factor


def attn_body(a0, a1, a2, a3, x_ref, alpha_ref, w0, w1, w2, w3, branch_ref, low_ref):
    branch = dot(a0[...], w0[...], 1, 1) + dot(a1[...], w1[...], 1, 1)
    branch = branch + dot(a2[...], w2[...], 1, 1) + dot(a3[...], w3[...], 1, 1)
    branch_ref[...] = branch
    hidden = first_update(branch, x_ref[...].astype(F32), alpha_ref[0:1, :])[2]
    low_ref[...] = hidden.astype(BF16)


def turn_body(own_ref, far_ref, branch_ref, x_ref, cot_ref, one_ref, two_ref, out_ref, gm_ref, keep_ref, sum_ref):
    hidden = first_update(branch_ref[...], x_ref[...].astype(F32), one_ref[0:1, :])[2]
    alpha = two_ref[0:1, :]
    h_mlp, mlp_factor = normed(own_ref[...] + far_ref[...].astype(F32))
    step = h_mlp - hidden
    result, two_factor = normed(hidden + alpha * step)
    out_ref[...] = result.astype(BF16)
    grad_two = normed_back(cot_ref[...].astype(F32), result, two_factor)
    keep_ref[...] = grad_two * (1.0 - alpha)
    gm_ref[...] = normed_back(grad_two * alpha, h_mlp, mlp_factor).astype(BF16)

    @pl.when(pl.program_id(0) == 0)
    def _():
        sum_ref[...] = jnp.zeros_like(sum_ref)

    sum_ref[0:1, :] += jnp.sum(grad_two * step, axis=0, keepdims=True)


def attn_back_body(
    own_ref, far_ref, keep_ref, branch_ref, x_ref, one_ref, w0, w1, w2, w3, ga_ref, gt_ref, o0, o1, o2, o3, sum_ref
):
    x_rows, alpha = x_ref[...].astype(F32), one_ref[0:1, :]
    h_attn, attn_factor, hidden, one_factor = first_update(branch_ref[...], x_rows, alpha)
    incoming = keep_ref[...] + own_ref[...] + far_ref[...].astype(F32)
    grad_one = normed_back(incoming, hidden, one_factor)
    gt_ref[...] = grad_one * (1.0 - alpha)
    grad_attn = normed_back(grad_one * alpha, h_attn, attn_factor).astype(BF16)
    ga_ref[...] = grad_attn
    for weight_ref, out_ref in ((w0, o0), (w1, o1), (w2, o2), (w3, o3)):
        out_ref[...] = dot(grad_attn, weight_ref[...]).astype(BF16)

    @pl.when(pl.program_id(0) == 0)
    def _():
        sum_ref[...] = jnp.zeros_like(sum_ref)

    sum_ref[0:1, :] += jnp.sum(grad_one * (h_attn - x_rows), axis=0, keepdims=True)


def shards(
    tokens,
    cotangent,
    lengths,
    key_mask,
    w_query,
    w_key,
    w_value,
    w_out,
    w_up,
    w_gate,
    w_down,
    s_qk,
    s_up,
    s_gate,
    alpha_attn,
    alpha_mlp,
):
    m = lax.axis_index("mp").astype(jnp.int32)
    devices = lax.axis_size("dp") * lax.axis_size("mp")
    local = tokens.shape[0]
    row_len = key_mask.shape[1]
    docs = lengths.shape[1]
    part = w_up.shape[1]
    width = w_query.shape[1]

    shard = jnp.concatenate([w_up, w_gate, w_down.T], axis=0)
    weights = lax.all_gather(
        shard, ("dp", "mp"), axis=0, tiled=True, axis_index_groups=chip_groups()
    ).reshape(-1, 2, 3, shard.shape[0] // 3, part)
    x_over = swap(tokens, "mp", 2)
    vector = jnp.concatenate([s_up, s_gate, s_qk, alpha_attn, alpha_mlp])[None]
    every = to_all(jnp.broadcast_to(vector, (devices, vector.shape[1])))
    attn = gather(jnp.concatenate([w_query, w_key, w_value, w_out.T], axis=1), (x_over, every))
    cuts, start = [], 0
    for piece in (s_up, s_gate, s_qk, alpha_attn, alpha_mlp):
        cuts.append(every[:, start : start + piece.shape[0]].reshape(-1))
        start += piece.shape[0]
    sup_all, sgate_all, sqk_all, alpha_one, alpha_two = cuts

    def quarter(array, index):
        size = array.shape[0] // 4
        return lax.dynamic_slice_in_dim(array, index * size, size)

    def eight(array):
        return jnp.broadcast_to(array[None], (8, array.shape[0]))

    sqk = eight(quarter(sqk_all, m))
    low = m & 2
    sup = jnp.stack([eight(quarter(sup_all, low)), eight(quarter(sup_all, low + 1))])
    sgate = jnp.stack([eight(quarter(sgate_all, low)), eight(quarter(sgate_all, low + 1))])
    one, two = eight(alpha_one), eight(alpha_two)
    x_first = jnp.concatenate([tokens, x_over], axis=0)
    x_second = swap(x_first, "mp", 1)
    out_mine = attn[:, 3 * width :]
    out_core = swap(out_mine, "mp", 1)
    out_over = swap(out_mine, "mp", 2)
    out_cross = swap(out_over, "mp", 1)
    out_parts = [(w, width, 0) for w in (out_mine, out_core, out_over, out_cross)]

    place = m.reshape(1)
    meta = jnp.concatenate([place, lengths[0]])
    slot_ids = jnp.arange(row_len, dtype=jnp.int32)
    positions, end = slot_ids, 0
    for i in range(docs):
        end = end + lengths[0, i]
        positions = positions - jnp.where(slot_ids >= end, lengths[0, i], 0)
    steps_even = jnp.arange(0, HEAD, 2).astype(F32)
    frequencies = jnp.power(jnp.float32(10000.0), -steps_even / HEAD)
    angles = positions.astype(F32)[:, None] * jnp.tile(frequencies, 4)[None, :]
    cosine, sine = jnp.cos(angles), jnp.sin(angles)
    kpos = jnp.where(key_mask[0] == 1, slot_ids, -1)
    kpos_rows = jnp.broadcast_to(kpos[None, :], (8, row_len))
    kpos_cols = jnp.broadcast_to(kpos[:, None], (row_len, 128))

    half = project(place, x_first, attn, cosine, sine, sqk, None, 0)
    queries, keys, vals, qrot, krot = project(place, x_second, attn, cosine, sine, sqk, half, 1)
    attended, inverse_mass = attend(meta, queries, keys, vals, kpos_rows, docs)
    near = attended[: 2 * local]
    by_core = swap(attended[2 * local :], "mp", 1)
    by_x = swap(jnp.concatenate([near[local:], by_core[local:]]), "mp", 2)
    heads_in = [(near, width, 0, 0), (by_core, width, 0, 0), (by_x, width, 0, 0), (by_x, width, local, 0)]
    branch, h_own = own_call(
        attn_body,
        "attn_out",
        heads_in + [(tokens, D, 0, 0)],
        [one],
        out_parts,
        [(local, D, F32), (local, D, BF16)],
        0,
        2 * local * D * D,
    )

    h_far = swap(h_own, "mp", 2)
    *saved_own, sum_own = ffn_forward(h_own, weights, sup, sgate, F32)
    *saved_far, sum_far = ffn_forward(h_far, weights, sup, sgate, BF16)
    result, gm_own, keep_two, by_two = own_call(
        turn_body,
        "turn",
        [(sum_own, D, 0, 0), (swap(sum_far, "mp", 2), D, 0, 0), (branch, D, 0, 0), (tokens, D, 0, 0), (cotangent, D, 0, 0)],
        [one, two],
        [],
        [(local, D, BF16), (local, D, BF16), (local, D, F32)],
        1,
        60 * local * D,
    )
    gm_far = swap(gm_own, "mp", 2)
    gu_own, gg_own, bu_own, bg_own, gh_own = ffn_backward(gm_own, weights, saved_own, sup, sgate, F32)
    gu_far, gg_far, bu_far, bg_far, gh_far = ffn_backward(gm_far, weights, saved_far, sup, sgate, BF16)
    gh_over = swap(gh_far, "mp", 2)

    down_mine, down_other = weight_grad(
        down_grad_body,
        place,
        (gm_own, gm_far),
        (saved_own[1], saved_far[1]),
        [jax.ShapeDtypeStruct((D, part), BF16)] * 2,
        [pl.BlockSpec((D, TILE), lambda t, m: (0, t))] * 2,
    )
    ups = weights.shape[:2] + (2,) + weights.shape[3:]
    ups = weight_grad(
        up_grad_body,
        place,
        (h_own, h_far),
        (gu_own, gu_far, gg_own, gg_far),
        jax.ShapeDtypeStruct(ups, BF16),
        pl.BlockSpec(ups[:4] + (TILE,), lambda t, m: (0, 0, 0, 0, t)),
    )
    grad_ups = lax.psum_scatter(
        ups.reshape(-1, part), ("dp", "mp"), scatter_dimension=0, tiled=True, axis_index_groups=chip_groups()
    ).astype(F32)
    grad_up, grad_gate = jnp.split(grad_ups, 2, axis=0)
    grad_down = scatter(down_mine.astype(F32) + swap(down_other, "mp", 1).astype(F32)).T

    grad_attn, grad_x, att0, att1, att2, att3, by_one = own_call(
        attn_back_body,
        "attn_back_out",
        [(gh_own, D, 0, 0), (gh_over, D, 0, 0), (keep_two, D, 0, 0), (branch, D, 0, 0), (tokens, D, 0, 0)],
        [one],
        out_parts,
        [(local, D, BF16), (local, D, F32)] + [(local, width, BF16)] * 4,
        1,
        2 * local * D * D,
    )
    back_x = swap(jnp.concatenate([att2, att3]), "mp", 2)
    back_core = swap(jnp.concatenate([att1, back_x[local:]]), "mp", 1)
    g_att = jnp.concatenate([att0, back_x[:local], back_core])
    outs = [dot(grad_attn, a[s : s + local], 0, 0) for a, _, s, _ in heads_in]
    core_out = swap(jnp.concatenate([outs[1], outs[3]], axis=1).astype(BF16), "mp", 1)
    over_out = swap((outs[2] + core_out[:, width:].astype(F32)).astype(BF16), "mp", 2)
    grad_out = scatter(outs[0] + core_out[:, :width].astype(F32) + over_out.astype(F32)).T

    grads, g_sqk = attend_back(
        meta, queries, qrot, attended, inverse_mass, g_att, keys, vals, krot, kpos_cols, cosine, sine, sqk, docs
    )
    g_first, g_second = grads[: 2 * local], grads[2 * local :]
    qkv = attn[:, : 3 * width]
    to_core = swap(dot(g_second, qkv, 1, 1).astype(BF16), "mp", 1)
    partial = dot(g_first, qkv, 1, 1)
    to_x = swap((partial[local:] + to_core[local:].astype(F32)).astype(BF16), "mp", 2)
    grad_tokens = grad_x + partial[:local] + to_core[:local].astype(F32) + to_x.astype(F32)
    grad_qkv = scatter(dot(x_first, g_first, 0, 0) + dot(x_second, g_second, 0, 0))
    g_qkv = [grad_qkv[:, i * width : (i + 1) * width] for i in range(3)]

    def placed(array, index):
        slots = lax.broadcasted_iota(jnp.int32, (4, 1), 0)
        return jnp.where(slots == index, array[None], 0.0)

    def quarters(own, far):
        by = own[:, 0] + far[:, 0]
        return (placed(by[0], m & 2) + placed(by[1], (m & 2) + 1)).reshape(devices, -1)

    rows = [
        quarters(bu_own, bu_far),
        quarters(bg_own, bg_far),
        placed(g_sqk[0], m).reshape(devices, -1),
        by_one[0].reshape(devices, -1),
        by_two[0].reshape(devices, -1),
    ]
    small = jnp.sum(to_all(jnp.concatenate(rows, axis=1)), axis=0)
    cuts, start = [], 0
    for piece in rows:
        cuts.append(small[start : start + piece.shape[1]])
        start += piece.shape[1]
    g_sup, g_sgate, g_sqk, g_alpha_one, g_alpha_two = cuts

    pieces = tuple(g_qkv) + (grad_out, grad_up, grad_gate, grad_down)
    pieces = pieces + (g_sqk, g_sup, g_sgate, g_alpha_one, g_alpha_two)
    squares = jnp.float32(0.0)
    for piece in pieces:
        squares = squares + jnp.sum(piece * piece)
    squares = jnp.sum(to_all(jnp.broadcast_to(squares, (devices, 128))), axis=0)
    grad_norm = jnp.sqrt(squares[0])
    mean_alphas = jnp.stack([jnp.mean(alpha_one), jnp.mean(alpha_two)])
    return (result, grad_tokens) + pieces + (grad_norm, mean_alphas)


def solution(mesh):
    both_axes = P(("dp", "mp"))
    rows = P(("dp", "mp"), None)
    in_specs = (
        (rows, rows, P("dp", None), P("dp", None))
        + (P("dp", "mp"),) * 3
        + (P("mp", "dp"),)
        + (P("dp", "mp"),) * 2
        + (P("mp", "dp"),)
        + (both_axes,) * 5
    )
    out_specs = (
        (rows, rows)
        + (P("dp", "mp"),) * 3
        + (P("mp", "dp"),)
        + (P("dp", "mp"),) * 2
        + (P("mp", "dp"),)
        + (both_axes,) * 5
        + (P(), P())
    )
    return jax.shard_map(shards, mesh=mesh, in_specs=in_specs, out_specs=out_specs, check_vma=False)
```

time: 694 us -> 520 us (0.75)
  waiting for transfers between devices: 244 us -> 116 us
  matrix products: 102 us -> 21.8 us
  Pallas kernels: 120 us -> 171 us
  starting transfers between devices: 115 us -> 82 us
  local copies, waits for them, and re-layouts: 30.1 us -> 55.4 us
  other arithmetic: 60.3 us -> 40.8 us
  between operations: 13.8 us -> 27.7 us
    dot_general x36 -> x8, matrix products: 102 us -> 21.8 us  [dot(): lax.dot_general(left, right, (((left_dim,), (right_dim,)), ((), ())), pre...]
    ppermute x48 -> x21, waiting for transfers between devices: 141 us -> 72.2 us  [swap(): return lax.ppermute(array, axis, [(i, i ^ bit) for i in range(size)])]
    pallas_call x4 -> x9, Pallas kernels: 32.3 us -> 97.9 us  [the longest x2 28.3 us: ffn_backward(): pl.pallas_call(backward_body, out_shape=[jax.ShapeDtypeStruct((2, count,...]
    ppermute x24 -> x7, waiting for transfers between devices: 70.7 us -> 27.6 us  [around(): lax.ppermute(array, 'dp', [(RING[p], RING[(p + step) % 8]) for p in range...]
    ppermute x27 -> x9, starting transfers between devices: 51 us -> 23 us  [to_z(): lax.ppermute(array, 'dp', [(z * 2 + y, (z + step) % 4 * 2 + y) for z in r...]
    ppermute x27 -> x9, waiting for transfers between devices: 32.3 us -> 10.1 us  [to_z(): lax.ppermute(array, 'dp', [(z * 2 + y, (z + step) % 4 * 2 + y) for z in r...]
    ppermute x24 -> x7, starting transfers between devices: 33.8 us -> 15.2 us  [around(): lax.ppermute(array, 'dp', [(RING[p], RING[(p + step) % 8]) for p in range...]
    all_gather x0 -> x1, local copies, waits for them, and re-layouts: none -> 16.7 us  [shards(): lax.all_gather(shard, ('dp', 'mp'), axis=0, tiled=True, axis_index_groups...]
  transfers between devices with their start and end apart: 99 -> 42, of which waited for: 42 -> 17; matrix products, arithmetic and copies ran while one was open for 18% -> 20% of each run, Pallas kernels for 5% -> 27%
where the time goes in v2:
time: 520 us; the launch traced here: 515 us
  Pallas kernels  171 us (33%)
  waiting for transfers between devices  116 us (22%)
  starting transfers between devices  82 us (16%)
  local copies, waits for them, and re-layouts  55.4 us (11%)
  other arithmetic  40.8 us (8%)
  between operations  27.7 us (5%)
  matrix products  21.8 us (4%)
    ppermute x21, waiting for transfers between devices, swap(): return lax.ppermute(array, axis, [(i, i ^ bit) for i in range(size)])  72.2 us
    pallas_call x1, Pallas kernels, attend_back(): pl.pallas_call(functools.partial(back_body, docs), out_shape=[jax.ShapeDt...  38.5 us
    ppermute x21, starting transfers between devices, swap(): return lax.ppermute(array, axis, [(i, i ^ bit) for i in range(size)])  28.6 us
    pallas_call x2, Pallas kernels, ffn_backward(): pl.pallas_call(backward_body, out_shape=[jax.ShapeDtypeStruct((2, count,...  28.3 us
    ppermute x7, waiting for transfers between devices, around(): lax.ppermute(array, 'dp', [(RING[p], RING[(p + step) % 8]) for p in range...  27.6 us
    pallas_call x2, Pallas kernels, ffn_forward(): pl.pallas_call(forward_body, out_shape=[jax.ShapeDtypeStruct((2, count, h...  26.5 us
    ppermute x9, starting transfers between devices, to_z(): lax.ppermute(array, 'dp', [(z * 2 + y, (z + step) % 4 * 2 + y) for z in r...  23 us
    pallas_call x2, Pallas kernels, weight_grad(): pl.pallas_call(body, out_shape=out_shape, grid_spec=pltpu.PrefetchScalarG...  23 us
  transfers between devices with their start and end apart: 42, of which 17 were waited for; matrix products, arithmetic and copies ran while one was open for 20% of the time, Pallas kernels for 27%

profile of v2, /device:TPU:0, one launch (start us, length us, event | category | flops | bytes accessed | tf_op | source)
XLA Modules:
  0.0 514.8 jit_solution(6175078744386547604)
XLA Ops:
  9.6 2.0 pad_maximum_fusion.2
  11.7 3.0 collective-permute-start
  18.6 4.9 all-to-all-start
  26.9 2.6 subtract_convert_fusion
  30.6 7.8 %collective-permute-done = bf16[512,1024]{1,0:T(8,128)(2,1)} collective-permute-done((bf16[512,1024]{1,0:T(8,128)(2,1)S(1)}, bf16[512,1024]{1,0:T(8,128)(2,1)}, u32[]{:S(2)}, u32[]{:S(2)}) %collective-permute-start) | collective-permute-done | bytes 1048608 | tf_op jit(solution)/shard_map/ppermute | solution.py:44
  38.4 2.3 constant_dynamic-update-slice_fusion.8.x_ref
  40.7 5.5 %multiply_sine_fusion = (f32[2048,128]{1,0:T(8,128)}, f32[2048,128]{1,0:T(8,128)}) fusion(f32[128]{0:T(128)S(1)} %mul.171, f32[2048]{0:T(1024)S(1)} %subtract_convert_fusion), kind=kLoop, calls=%fused_computation.11 | loop fusion | flops 262144 | bytes 2105856 | tf_op jit(solution)/shard_map/sin | solution.py:778
  46.2 1.9 collective-permute-start.4
  49.8 8.3 %collective-permute-done.4 = bf16[128,1024]{1,0:T(8,128)(2,1)S(1)} collective-permute-done((bf16[128,1024]{1,0:T(8,128)(2,1)}, bf16[128,1024]{1,0:T(8,128)(2,1)S(1)}, u32[]{:S(2)}, u32[]{:S(2)}) %collective-permute-start.4) | collective-permute-done | bytes 262176 | tf_op jit(solution)/shard_map/ppermute | solution.py:54
  58.0 2.4 collective-permute-start.6
  62.8 9.9 %collective-permute-done.6 = bf16[128,1024]{1,0:T(8,128)(2,1)S(1)} collective-permute-done((bf16[128,1024]{1,0:T(8,128)(2,1)S(1)}, bf16[128,1024]{1,0:T(8,128)(2,1)S(1)}, u32[]{:S(2)}, u32[]{:S(2)}) %collective-permute-start.6) | collective-permute-done | bytes 262176 | tf_op jit(solution)/shard_map/ppermute | solution.py:54
  72.7 7.4 %collective-permute-start.8 = (bf16[128,1024]{1,0:T(8,128)(2,1)S(1)}, bf16[128,1024]{1,0:T(8,128)(2,1)S(1)}, u32[]{:S(2)}, u32[]{:S(2)}) collective-permute-start(bf16[128,1024]{1,0:T(8,128)(2,1)S(1)} %collective-permute-done.6), channel_id=1, source_target_pairs={{0,8},{8,16},{16,24},{24,28},{28,20},{20,12},{12,4},{4,0},{1,9},{9... | collective-permute-start | bytes 786440 | tf_op jit(solution)/shard_map/ppermute | solution.py:54
  80.2 9.4 %collective-permute-done.8 = bf16[128,1024]{1,0:T(8,128)(2,1)S(1)} collective-permute-done((bf16[128,1024]{1,0:T(8,128)(2,1)S(1)}, bf16[128,1024]{1,0:T(8,128)(2,1)S(1)}, u32[]{:S(2)}, u32[]{:S(2)}) %collective-permute-start.8) | collective-permute-done | bytes 262176 | tf_op jit(solution)/shard_map/ppermute | solution.py:54
  89.7 1.7 collective-permute-start.12
  91.9 9.0 %project.2 = (bf16[2048,256]{1,0:T(8,128)(2,1)}, bf16[2048,256]{1,0:T(8,128)(2,1)}, bf16[2048,256]{1,0:T(8,128)(2,1)}, f32[2048,256]{1,0:T(8,128)}, f32[2048,256]{1,0:T(8,128)}) custom-call(s32[1]{0:T(128)} %bitcast.m_ref, bf16[1024,1024]{1,0:T(8,128)(2,1)} %constant_dynamic-update-slice_fusion.8.x_ref, bf16[1024,1024]{1,0:T(8,128)(2,1)} %copy-done, ...), custom_call_target="tpu_custom_call" | custom-call | flops 1610612736 | bytes 8388608 | tf_op jit(solution)/shard_map/project/pallas_call | solution.py:160
  100.9 8.8 %project.3 = (bf16[2048,256]{1,0:T(8,128)(2,1)}, bf16[2048,256]{1,0:T(8,128)(2,1)}, bf16[2048,256]{1,0:T(8,128)(2,1)}, f32[2048,256]{1,0:T(8,128)}, f32[2048,256]{1,0:T(8,128)}) custom-call(s32[1]{0:T(128)} %bitcast.m_ref, ...), custom_call_target="tpu_custom_call", output_to_operand_aliasing={{0}: (8, {}), {1}: (9, {}), {2}: (10, {}), {3}: (11, {}), {... | custom-call | flops 1610612736 | bytes 8388608 | tf_op jit(solution)/shard_map/project/pallas_call | solution.py:160
  110.4 17.0 %attend.1 = (bf16[2048,256]{1,0:T(8,128)(2,1)}, f32[2048,256]{1,0:T(8,128)}) custom-call(s32[5]{0:T(128)} %pad_add_fusion.meta_ref, bf16[2048,256]{1,0:T(8,128)(2,1)} %get-tuple-element.72.q_ref, bf16[2048,256]{1,0:T(8,128)(2,1)} %get-tuple-element.73.k_ref, bf16[2048,256]{1,0:T(8,128)(2,1)} %get-tuple-element.74.v_ref, s32[8,2048]{1,0:T(8,128)} %broadcast_in_dim.185.kpos_ref), custom_call_target="tpu_custom_call" | custom-call | flops 12000000000 | bytes 4194304 | tf_op jit(solution)/shard_map/attend/pallas_call | solution.py:275
  127.3 2.1 fusion.39
  133.0 13.4 %collective-permute-done.10.a2.a3 = bf16[1024,256]{1,0:T(8,128)(2,1)S(1)} collective-permute-done((bf16[1024,256]{1,0:T(8,128)(2,1)}, bf16[1024,256]{1,0:T(8,128)(2,1)S(1)}, u32[]{:S(2)}, u32[]{:S(2)}) %collective-permute-start.10) | collective-permute-done | bytes 524320 | tf_op jit(solution)/shard_map/ppermute | solution.py:44
  147.2 5.1 attn_out.1
  154.3 16.7 %copy.73 = bf16[6144,1024]{1,0:T(8,128)(2,1)} copy(bf16[6144,1024]{0,1:T(8,128)(2,1)} %all-gather.2.cloned.1.call-done) | data formatting | bytes 25165824 | tf_op jit(solution)/shard_map/all_gather | solution.py:735
  171.0 5.9 %collective-permute-done.14.h_ref.lr_ref = bf16[512,1024]{1,0:T(8,128)(2,1)S(1)} collective-permute-done((bf16[512,1024]{1,0:T(8,128)(2,1)}, bf16[512,1024]{1,0:T(8,128)(2,1)S(1)}, u32[]{:S(2)}, u32[]{:S(2)}) %collective-permute-start.14) | collective-permute-done | bytes 1048608 | tf_op jit(solution)/shard_map/ppermute | solution.py:44
  177.9 13.1 %ffn_forward.3 = (bf16[2,512,1024]{2,1,0:T(8,128)(2,1)}, bf16[2,512,1024]{2,1,0:T(8,128)(2,1)}, bf16[2,512,1024]{2,1,0:T(8,128)(2,1)}, bf16[2,512,1024]{2,1,0:T(8,128)(2,1)}, bf16[512,1024]{1,0:T(8,128)(2,1)}) custom-call(bf16[512,1024]{1,0:T(8,128)(2,1)} %copy-done.31, bf16[8,2,3,128,1024]{4,3,2,1,0:T(8,128)(2,1)} %bitcast.122, ...), custom_call_target="tpu_custom_call" | custom-call | flops 6442450944 | bytes 18874368 | tf_op jit(solution)/shard_map/ffn_forward/pallas_call | solution.py:518
  192.3 13.5 %ffn_forward.2 = (bf16[2,512,1024]{2,1,0:T(8,128)(2,1)}, bf16[2,512,1024]{2,1,0:T(8,128)(2,1)}, bf16[2,512,1024]{2,1,0:T(8,128)(2,1)}, bf16[2,512,1024]{2,1,0:T(8,128)(2,1)}, f32[512,1024]{1,0:T(8,128)}) custom-call(bf16[512,1024]{1,0:T(8,128)(2,1)} %get-tuple-element.76.h_ref.lo_ref, bf16[8,2,3,128,1024]{4,3,2,1,0:T(8,128)(2,1)} %bitcast.123, ...), custom_call_target="tpu_custom_call" | custom-call | flops 6442450944 | bytes 18874368 | tf_op jit(solution)/shard_map/ffn_forward/pallas_call | solution.py:518
  205.8 8.8 %collective-permute-done.15.far_ref = bf16[512,1024]{1,0:T(8,128)(2,1)S(1)} collective-permute-done((bf16[512,1024]{1,0:T(8,128)(2,1)}, bf16[512,1024]{1,0:T(8,128)(2,1)S(1)}, u32[]{:S(2)}, u32[]{:S(2)}) %collective-permute-start.15) | collective-permute-done | bytes 1048608 | tf_op jit(solution)/shard_map/ppermute | solution.py:44
  215.7 6.7 %turn.1 = (bf16[512,1024]{1,0:T(8,128)(2,1)}, bf16[512,1024]{1,0:T(8,128)(2,1)}, f32[512,1024]{1,0:T(8,128)}, f32[8,1024]{1,0:T(8,128)}) custom-call(f32[512,1024]{1,0:T(8,128)} %get-tuple-element.77.own_ref, bf16[512,1024]{1,0:T(8,128)(2,1)} %copy-done.17, f32[512,1024]{1,0:T(8,128)} %get-tuple-element.79.branch_ref, bf16[512,1024]{1,0:T(8,128)(2,1)} %x_ref.5, ...), custom_call_target="tpu_custom_call" | custom-call | flops 31457280 | bytes 10485760 | tf_op jit(solution)/shard_map/turn/pallas_call | solution.py:643
  225.9 14.5 %ffn_backward.2 = (bf16[2,512,1024]{2,1,0:T(8,128)(2,1)}, bf16[2,512,1024]{2,1,0:T(8,128)(2,1)}, f32[2,8,1024]{2,1,0:T(8,128)}, f32[2,8,1024]{2,1,0:T(8,128)}, f32[512,1024]{1,0:T(8,128)}) custom-call(bf16[512,1024]{1,0:T(8,128)(2,1)} %get-tuple-element.81.gm_ref.lo_ref, bf16[8,2,3,128,1024]{4,3,2,1,0:T(8,128)(2,1)} %bitcast.124, ...), custom_call_target="tpu_custom_call" | custom-call | flops 6442450944 | bytes 25165824 | tf_op jit(solution)/shard_map/ffn_backward/pallas_call | solution.py:561
  240.4 4.8 collective-permute-done.16.gm_ref.lr_ref
  246.2 13.8 %ffn_backward.3 = (bf16[2,512,1024]{2,1,0:T(8,128)(2,1)}, bf16[2,512,1024]{2,1,0:T(8,128)(2,1)}, f32[2,8,1024]{2,1,0:T(8,128)}, f32[2,8,1024]{2,1,0:T(8,128)}, bf16[512,1024]{1,0:T(8,128)(2,1)}) custom-call(bf16[512,1024]{1,0:T(8,128)(2,1)} %copy-done.34, bf16[8,2,3,128,1024]{4,3,2,1,0:T(8,128)(2,1)} %bitcast.125, ...), custom_call_target="tpu_custom_call" | custom-call | flops 6442450944 | bytes 25165824 | tf_op jit(solution)/shard_map/ffn_backward/pallas_call | solution.py:561
  260.8 13.9 %weight_grad.2 = bf16[8,2,2,128,1024]{4,3,2,1,0:T(8,128)(2,1)} custom-call(s32[1]{0:T(128)} %bitcast.m_ref, bf16[512,1024]{1,0:T(8,128)(2,1)} %get-tuple-element.76.h_ref.lo_ref, bf16[512,1024]{1,0:T(8,128)(2,1)} %copy-done.31, bf16[2,512,1024]{2,1,0:T(8,128)(2,1)} %get-tuple-element.103.uo_ref, bf16[2,512,1024]{2,1,0:T(8,128)(2,1)} %get-tuple-element.104.ur_ref, ...), custom_call_target="tpu_custom_call" | custom-call | flops 8589934592 | bytes 16777216 | tf_op jit(solution)/shard_map/weight_grad/pallas_call | solution.py:610
  274.8 9.1 %weight_grad.3 = (bf16[1024,1024]{1,0:T(8,128)(2,1)}, bf16[1024,1024]{1,0:T(8,128)(2,1)}) custom-call(s32[1]{0:T(128)} %bitcast.m_ref, bf16[512,1024]{1,0:T(8,128)(2,1)} %get-tuple-element.81.gm_ref.lo_ref, bf16[512,1024]{1,0:T(8,128)(2,1)} %copy-done.34, bf16[2,512,1024]{2,1,0:T(8,128)(2,1)} %get-tuple-element.83.act_ref.ro_ref, ...), custom_call_target="tpu_custom_call" | custom-call | flops 4294967296 | bytes 8388608 | tf_op jit(solution)/shard_map/weight_grad/pallas_call | solution.py:610
  285.6 8.2 %attn_back_out.1 = (bf16[512,1024]{1,0:T(8,128)(2,1)}, f32[512,1024]{1,0:T(8,128)}, bf16[512,256]{1,0:T(8,128)(2,1)}, bf16[512,256]{1,0:T(8,128)(2,1)}, bf16[512...) custom-call(f32[512,1024]{1,0:T(8,128)} %get-tuple-element.86.own_ref, ...), custom_call_target="tpu_custom_call" | custom-call | flops 1073741824 | bytes 10485760 | tf_op jit(solution)/shard_map/attn_back_out/pallas_call | solution.py:643
  296.5 13.0 %collective-permute-done.18 = bf16[1024,256]{1,0:T(8,128)(2,1)S(1)} collective-permute-done((bf16[1024,256]{1,0:T(8,128)(2,1)S(1)}, bf16[1024,256]{1,0:T(8,128)(2,1)S(1)}, u32[]{:S(2)}, u32[]{:S(2)}) %collective-permute-start.18) | collective-permute-done | bytes 524320 | tf_op jit(solution)/shard_map/ppermute | solution.py:44
  313.1 2.2 pad_maximum_fusion.do_ref
  316.6 38.5 %attend_back.1 = (bf16[2048,768]{1,0:T(8,128)(2,1)}, f32[8,256]{1,0:T(8,128)}) custom-call(s32[5]{0:T(128)} %pad_add_fusion.meta_ref, bf16[2048,256]{1,0:T(8,128)(2,1)} %get-tuple-element.72.q_ref, f32[2048,256]{1,0:T(8,128)} %get-tuple-element.94.qr_ref, bf16[2048,256]{1,0:T(8,128)(2,1)} %get-tuple-element.75.o_ref, f32[2048,256]{1,0:T(8,128)} %get-tuple-element.95.inv_ref, ...), custom_call_target="tpu_custom_call" | custom-call | flops 30000001024 | bytes 12582912 | tf_op jit(solution)/shard_map/attend_back/pallas_call | solution.py:431
  355.1 4.2 fusion.6
  359.3 3.6 convolution_add_fusion
  363.9 12.5 %collective-permute-start.22 = (bf16[4,128,768]{2,1,0:T(8,128)(2,1)}, bf16[4,128,768]{2,1,0:T(8,128)(2,1)}, u32[]{:S(2)}, u32[]{:S(2)}) collective-permute-start(bf16[4,128,768]{2,1,0:T(8,128)(2,1)} %fusion.13), channel_id=1, source_target_pairs={{0,4},{4,0},{8,12},{12,8},{16,20},{20,16},{24,28},{28,24},{1,5},{5... | collective-permute-start | bytes 2359304 | tf_op jit(solution)/shard_map/ppermute | solution.py:44
  376.4 2.3 fusion.12
  380.9 1.9 copy-done.3
  384.3 3.0 copy.79
  388.1 4.7 convolution_convert_fusion
  392.9 3.9 fusion.4
  397.6 3.8 all-to-all-start.1
  401.5 1.8 constant_dynamic-slice_fusion
  403.9 1.9 collective-permute-start.33
  405.8 3.0 all-to-all-done.1
  410.2 2.1 fusion.11
  417.1 18.1 %collective-permute-done.28 = bf16[4,128,256]{1,2,0:T(8,128)(2,1)S(1)} collective-permute-done((bf16[4,128,256]{1,2,0:T(8,128)(2,1)}, bf16[4,128,256]{1,2,0:T(8,128)(2,1)S(1)}, u32[]{:S(2)}, u32[]{:S(2)}) %collective-permute-start.28) | collective-permute-done | bytes 262176 | tf_op jit(solution)/shard_map/ppermute | solution.py:44
  435.3 1.6 collective-permute-start.29
  436.9 2.3 collective-permute-start.30
  440.6 1.8 bitcast_add_fusion.1
  444.6 3.0 collective-permute-start.25
  449.2 1.9 copy-done.6
  451.1 1.6 fusion
  455.7 5.1 collective-permute-start.35
  460.8 6.1 %collective-permute-done.24 = bf16[128,768]{1,0:T(8,128)(2,1)S(1)} collective-permute-done((bf16[128,768]{1,0:T(8,128)(2,1)S(1)}, bf16[128,768]{1,0:T(8,128)(2,1)S(1)}, u32[]{:S(2)}, u32[]{:S(2)}) %collective-permute-start.24) | collective-permute-done | bytes 196640 | tf_op jit(solution)/shard_map/ppermute | solution.py:48
  466.9 7.5 %collective-permute-start.36 = (bf16[128,1024]{0,1:T(8,128)(2,1)}, bf16[128,1024]{0,1:T(8,128)(2,1)}, u32[]{:S(2)}, u32[]{:S(2)}) collective-permute-start(bf16[128,1024]{0,1:T(8,128)(2,1)} %get-tuple-element.143), channel_id=1, source_target_pairs={{0,24},{4,28},{8,0},{12,4},{16,8},{20,12},{24,16},{28,20},{1,25},{... | collective-permute-start | bytes 786440 | tf_op jit(solution)/shard_map/ppermute | solution.py:48
  479.4 2.4 collective-permute-done.36
  481.8 2.6 multiply_reduce_fusion
  484.4 2.9 multiply_reduce_fusion.1
  493.0 6.4 %all-to-all-start.2 = ((f32[32,1,128]{2,1,0:T(1,128)}), f32[32,1,128]{2,1,0:T(1,128)S(1)}, u32[]{:S(2)}, u32[]{:S(2)}) async-start(f32[32,1,128]{2,1,0:T(1,128)} %broadcast_in_dim.218), calls=%async_computation.3 | async-start | bytes 32768 | tf_op jit(solution)/shard_map/all_to_all | solution.py:104
  499.4 4.2 fusion.2
  503.5 3.0 all-to-all-done.2
  (226 shorter events, 60.9 us)
Async XLA Ops:
  7.2 7.5 %copy-start.20 = (bf16[256,128]{1,0:T(8,128)(2,1)S(1)}, bf16[256,128]{1,0:T(8,128)(2,1)}, u32[]{:S(2)}) copy-start(bf16[256,128]{1,0:T(8,128)(2,1)} %param.23) | copy-start | bytes 196612
  7.2 147.1 %all-gather.2.cloned.1.call-start = ((), (), s32[]{:S(2)}) async-start(), calls=%async_computation.4 | async-start | bytes 13369344 | tf_op jit(solution)/shard_map/all_gather | solution.py:735
  11.6 6.3 %copy-start.26 = (f32[128]{0:T(128)S(1)}, f32[128]{0:T(128)}, u32[]{:S(2)}) copy-start(f32[128]{0:T(128)} %param.28) | copy-start | bytes 1540
  11.6 6.3 %copy-start.27 = (f32[128]{0:T(128)S(1)}, f32[128]{0:T(128)}, u32[]{:S(2)}) copy-start(f32[128]{0:T(128)} %param.29) | copy-start | bytes 1540
  11.6 6.3 %copy-start.28 = (f32[32]{0:T(128)S(1)}, f32[32]{0:T(128)}, u32[]{:S(2)}) copy-start(f32[32]{0:T(128)} %param.27) | copy-start | bytes 388
  11.6 6.3 %copy-start.29 = (f32[32]{0:T(128)S(1)}, f32[32]{0:T(128)}, u32[]{:S(2)}) copy-start(f32[32]{0:T(128)} %param.30) | copy-start | bytes 388
  11.6 6.3 %copy-start.30 = (f32[32]{0:T(128)S(1)}, f32[32]{0:T(128)}, u32[]{:S(2)}) copy-start(f32[32]{0:T(128)} %param.31) | copy-start | bytes 388
  11.6 12.1 %copy-start.25 = (s32[1,4]{1,0:T(1,128)S(1)}, s32[1,4]{1,0:T(1,128)}, u32[]{:S(2)}) copy-start(s32[1,4]{1,0:T(1,128)} %param.18) | copy-start | bytes 52
  11.7 26.7 %collective-permute-start = (bf16[512,1024]{1,0:T(8,128)(2,1)S(1)}, bf16[512,1024]{1,0:T(8,128)(2,1)}, u32[]{:S(2)}, u32[]{:S(2)}) collective-permute-start(bf16[512,1024]{1,0:T(8,128)(2,1)S(1)} %copy-done.2), channel_id=1, source_target_pairs={{0,2},{1,3},{2,0},{3,1},{4,6},{5,7},{6,4},{7,5},{8,10},{9,11},{10,... | collective-permute-start | bytes 3145736 | tf_op jit(solution)/shard_map/ppermute | solution.py:44
  15.9 30.4 %collective-permute-start.2 = (bf16[128,1024]{1,0:T(8,128)(2,1)}, bf16[128,1024]{1,0:T(8,128)(2,1)}, u32[]{:S(2)}, u32[]{:S(2)}) collective-permute-start(bf16[128,1024]{1,0:T(8,128)(2,1)} %get-tuple-element.161), channel_id=1, source_target_pairs={{0,8},{8,16},{16,24},{24,28},{28,20},{20,12},{12,4},{4,0},{1,9},{9... | collective-permute-start | bytes 786440 | tf_op jit(solution)/shard_map/ppermute | solution.py:54
  17.4 31.3 %collective-permute-start.3 = (bf16[128,1024]{1,0:T(8,128)(2,1)}, bf16[128,1024]{1,0:T(8,128)(2,1)S(1)}, u32[]{:S(2)}, u32[]{:S(2)}) collective-permute-start(bf16[128,1024]{1,0:T(8,128)(2,1)} %get-tuple-element.161), channel_id=1, source_target_pairs={{0,4},{8,0},{16,8},{24,16},{28,24},{20,28},{12,20},{4,12},{1,5},{9... | collective-permute-start | bytes 786440 | tf_op jit(solution)/shard_map/ppermute | solution.py:54
  18.6 30.1 %all-to-all-start = ((f32[32,1,352]{2,1,0:T(1,128)}), f32[32,1,352]{2,1,0:T(1,128)S(1)}, u32[]{:S(2)}, u32[]{:S(2)}) async-start(f32[32,1,352]{2,1,0:T(1,128)} %broadcast_in_dim.177), calls=%async_computation | async-start | bytes 98304 | tf_op jit(solution)/shard_map/all_to_all | solution.py:104
  23.6 460.8 %reduce-scatter.2.cloned.1.call-start = ((), (), s32[]{:S(2)}) async-start(), calls=%async_computation.5 | async-start | bytes 8912896 | tf_op jit(solution)/shard_map/reduce_scatter | solution.py:836
  30.6 15.6 %copy-start.24 = (s32[1,2048]{1,0:T(1,128)S(1)}, s32[1,2048]{1,0:T(1,128)}, u32[]{:S(2)}) copy-start(s32[1,2048]{1,0:T(1,128)} %param.19) | copy-start | bytes 24580
  40.7 60.3 %collective-permute-start.1 = (bf16[1024,1024]{1,0:T(8,128)(2,1)}, bf16[1024,1024]{1,0:T(8,128)(2,1)}, u32[]{:S(2)}, u32[]{:S(2)}) collective-permute-start(bf16[1024,1024]{1,0:T(8,128)(2,1)} %constant_dynamic-update-slice_fusion.8.x_ref), channel_id=1, source_target_pairs={{0,1},{1,0},{2,3},{3,2},{4,5},{5,4},{6,7},{7,6},{8,9},{9,8},{10,11... | collective-permute-start | bytes 6291464 | tf_op jit(solution)/shard_map/ppermute | solution.py:44
  46.2 11.8 %collective-permute-start.4 = (bf16[128,1024]{1,0:T(8,128)(2,1)}, bf16[128,1024]{1,0:T(8,128)(2,1)S(1)}, u32[]{:S(2)}, u32[]{:S(2)}) collective-permute-start(bf16[128,1024]{1,0:T(8,128)(2,1)} %collective-permute-done.2), channel_id=1, source_target_pairs={{0,8},{8,16},{16,24},{24,28},{28,20},{20,12},{12,4},{4,0},{1,9},{9... | collective-permute-start | bytes 786440 | tf_op jit(solution)/shard_map/ppermute | solution.py:54
  48.7 12.7 %collective-permute-start.5 = (bf16[128,1024]{1,0:T(8,128)(2,1)S(1)}, bf16[128,1024]{1,0:T(8,128)(2,1)S(1)}, u32[]{:S(2)}, u32[]{:S(2)}) collective-permute-start(bf16[128,1024]{1,0:T(8,128)(2,1)S(1)} %collective-permute-done.3), channel_id=1, source_target_pairs={{0,4},{8,0},{16,8},{24,16},{28,24},{20,28},{12,20},{4,12},{1,5},{9... | collective-permute-start | bytes 786440 | tf_op jit(solution)/shard_map/ppermute | solution.py:54
  58.0 14.7 %collective-permute-start.6 = (bf16[128,1024]{1,0:T(8,128)(2,1)S(1)}, bf16[128,1024]{1,0:T(8,128)(2,1)S(1)}, u32[]{:S(2)}, u32[]{:S(2)}) collective-permute-start(bf16[128,1024]{1,0:T(8,128)(2,1)S(1)} %collective-permute-done.4), channel_id=1, source_target_pairs={{0,8},{8,16},{16,24},{24,28},{28,20},{20,12},{12,4},{4,0},{1,9},{9... | collective-permute-start | bytes 786440 | tf_op jit(solution)/shard_map/ppermute | solution.py:54
  61.4 18.7 %collective-permute-start.7 = (bf16[128,1024]{1,0:T(8,128)(2,1)S(1)}, bf16[128,1024]{1,0:T(8,128)(2,1)S(1)}, u32[]{:S(2)}, u32[]{:S(2)}) collective-permute-start(bf16[128,1024]{1,0:T(8,128)(2,1)S(1)} %collective-permute-done.5), channel_id=1, source_target_pairs={{0,4},{8,0},{16,8},{24,16},{28,24},{20,28},{12,20},{4,12},{1,5},{9... | collective-permute-start | bytes 786440 | tf_op jit(solution)/shard_map/ppermute | solution.py:54
  72.7 16.8 %collective-permute-start.8 = (bf16[128,1024]{1,0:T(8,128)(2,1)S(1)}, bf16[128,1024]{1,0:T(8,128)(2,1)S(1)}, u32[]{:S(2)}, u32[]{:S(2)}) collective-permute-start(bf16[128,1024]{1,0:T(8,128)(2,1)S(1)} %collective-permute-done.6), channel_id=1, source_target_pairs={{0,8},{8,16},{16,24},{24,28},{28,20},{20,12},{12,4},{4,0},{1,9},{9... | collective-permute-start | bytes 786440 | tf_op jit(solution)/shard_map/ppermute | solution.py:54
  89.7 39.7 %copy-start.5 = (bf16[1024,256]{1,0:T(8,128)(2,1)}, bf16[1024,256]{1,0:T(8,128)(2,1)S(1)}, u32[]{:S(2)}) copy-start(bf16[1024,256]{1,0:T(8,128)(2,1)S(1)} %slice.209.w0) | copy-start | bytes 1572868
  89.7 40.2 %collective-permute-start.12 = (bf16[1024,256]{1,0:T(8,128)(2,1)S(1)}, bf16[1024,256]{1,0:T(8,128)(2,1)S(1)}, u32[]{:S(2)}, u32[]{:S(2)}) collective-permute-start(bf16[1024,256]{1,0:T(8,128)(2,1)S(1)} %slice.209.w0), channel_id=1, source_target_pairs={{0,2},{1,3},{2,0},{3,1},{4,6},{5,7},{6,4},{7,5},{8,10},{9,11},{10,... | collective-permute-start | bytes 1572872 | tf_op jit(solution)/shard_map/ppermute | solution.py:44
  129.4 1.9 collective-permute-start.9
  129.4 3.6 collective-permute-start.11
  129.9 17.1 %copy-start.9 = (bf16[1024,256]{1,0:T(8,128)(2,1)}, bf16[1024,256]{1,0:T(8,128)(2,1)S(1)}, u32[]{:S(2)}) copy-start(bf16[1024,256]{1,0:T(8,128)(2,1)S(1)} %collective-permute-done.12.w2) | copy-start | bytes 1572868
  129.9 3.1 collective-permute-start.13
  131.3 15.8 %copy-start.15 = (bf16[1024,256]{1,0:T(8,128)(2,1)}, bf16[1024,256]{1,0:T(8,128)(2,1)S(1)}, u32[]{:S(2)}) copy-start(bf16[1024,256]{1,0:T(8,128)(2,1)S(1)} %collective-permute-done.9.a1) | copy-start | bytes 1572868
  132.2 14.2 %collective-permute-start.10 = (bf16[1024,256]{1,0:T(8,128)(2,1)}, bf16[1024,256]{1,0:T(8,128)(2,1)S(1)}, u32[]{:S(2)}, u32[]{:S(2)}) collective-permute-start(bf16[1024,256]{1,0:T(8,128)(2,1)} %pad_maximum_fusion.3), channel_id=1, source_target_pairs={{0,2},{1,3},{2,0},{3,1},{4,6},{5,7},{6,4},{7,5},{8,10},{9,11},{10,... | collective-permute-start | bytes 1572872 | tf_op jit(solution)/shard_map/ppermute | solution.py:44
  133.0 14.1 %copy-start.10 = (bf16[1024,256]{1,0:T(8,128)(2,1)}, bf16[1024,256]{1,0:T(8,128)(2,1)S(1)}, u32[]{:S(2)}) copy-start(bf16[1024,256]{1,0:T(8,128)(2,1)S(1)} %collective-permute-done.11.w1) | copy-start | bytes 1572868
  133.0 14.1 %copy-start.11 = (bf16[1024,256]{1,0:T(8,128)(2,1)}, bf16[1024,256]{1,0:T(8,128)(2,1)S(1)}, u32[]{:S(2)}) copy-start(bf16[1024,256]{1,0:T(8,128)(2,1)S(1)} %collective-permute-done.13.w3) | copy-start | bytes 1572868
  152.3 24.6 %collective-permute-start.14 = (bf16[512,1024]{1,0:T(8,128)(2,1)}, bf16[512,1024]{1,0:T(8,128)(2,1)S(1)}, u32[]{:S(2)}, u32[]{:S(2)}) collective-permute-start(bf16[512,1024]{1,0:T(8,128)(2,1)} %get-tuple-element.76.h_ref.lo_ref), channel_id=1, source_target_pairs={{0,2},{1,3},{2,0},{3,1},{4,6},{5,7},{6,4},{7,5},{8,10},{9,11},{10,... | collective-permute-start | bytes 3145736 | tf_op jit(solution)/shard_map/ppermute | solution.py:44
  190.9 23.7 %collective-permute-start.15 = (bf16[512,1024]{1,0:T(8,128)(2,1)}, bf16[512,1024]{1,0:T(8,128)(2,1)S(1)}, u32[]{:S(2)}, u32[]{:S(2)}) collective-permute-start(bf16[512,1024]{1,0:T(8,128)(2,1)} %get-tuple-element.78), channel_id=1, source_target_pairs={{0,2},{1,3},{2,0},{3,1},{4,6},{5,7},{6,4},{7,5},{8,10},{9,11},{10,... | collective-permute-start | bytes 3145736 | tf_op jit(solution)/shard_map/ppermute | solution.py:44
  222.4 22.8 %collective-permute-start.16 = (bf16[512,1024]{1,0:T(8,128)(2,1)}, bf16[512,1024]{1,0:T(8,128)(2,1)S(1)}, u32[]{:S(2)}, u32[]{:S(2)}) collective-permute-start(bf16[512,1024]{1,0:T(8,128)(2,1)} %get-tuple-element.81.gm_ref.lo_ref), channel_id=1, source_target_pairs={{0,2},{1,3},{2,0},{3,1},{4,6},{5,7},{6,4},{7,5},{8,10},{9,11},{10,... | collective-permute-start | bytes 3145736 | tf_op jit(solution)/shard_map/ppermute | solution.py:44
  260.0 25.6 %collective-permute-start.17 = (bf16[512,1024]{1,0:T(8,128)(2,1)}, bf16[512,1024]{1,0:T(8,128)(2,1)}, u32[]{:S(2)}, u32[]{:S(2)}) collective-permute-start(bf16[512,1024]{1,0:T(8,128)(2,1)} %get-tuple-element.91), channel_id=1, source_target_pairs={{0,2},{1,3},{2,0},{3,1},{4,6},{5,7},{6,4},{7,5},{8,10},{9,11},{10,... | collective-permute-start | bytes 3145736 | tf_op jit(solution)/shard_map/ppermute | solution.py:44
  283.8 96.2 %collective-permute-start.32 = (bf16[1024,1024]{1,0:T(8,128)(2,1)}, bf16[1024,1024]{1,0:T(8,128)(2,1)S(1)}, u32[]{:S(2)}, u32[]{:S(2)}) collective-permute-start(bf16[1024,1024]{1,0:T(8,128)(2,1)} %get-tuple-element.108), channel_id=1, source_target_pairs={{0,1},{1,0},{2,3},{3,2},{4,5},{5,4},{6,7},{7,6},{8,9},{9,8},{10,11... | collective-permute-start | bytes 6291464 | tf_op jit(solution)/shard_map/ppermute | solution.py:44
  293.8 15.8 %copy-start.19 = (bf16[512,256]{1,0:T(8,128)(2,1)S(1)}, bf16[512,256]{1,0:T(8,128)(2,1)}, u32[]{:S(2)}) copy-start(bf16[512,256]{1,0:T(8,128)(2,1)} %get-tuple-element.99) | copy-start | bytes 786436
  293.8 15.9 %copy-start.16 = (bf16[1024,256]{1,0:T(8,128)(2,1)S(1)}, bf16[1024,256]{1,0:T(8,128)(2,1)}, u32[]{:S(2)}) copy-start(bf16[1024,256]{1,0:T(8,128)(2,1)} %copy-done.15) | copy-start | bytes 1572868
  293.8 15.9 %copy-start.32 = (bf16[512,1024]{1,0:T(8,128)(2,1)S(1)}, bf16[512,1024]{1,0:T(8,128)(2,1)}, u32[]{:S(2)}) copy-start(bf16[512,1024]{1,0:T(8,128)(2,1)} %get-tuple-element.102) | copy-start | bytes 3145732
  295.1 14.5 %collective-permute-start.18 = (bf16[1024,256]{1,0:T(8,128)(2,1)S(1)}, bf16[1024,256]{1,0:T(8,128)(2,1)S(1)}, u32[]{:S(2)}, u32[]{:S(2)}) collective-permute-start(bf16[1024,256]{1,0:T(8,128)(2,1)S(1)} %pad_maximum_fusion.4), channel_id=1, source_target_pairs={{0,2},{1,3},{2,0},{3,1},{4,6},{5,7},{6,4},{7,5},{8,10},{9,11},{10,... | collective-permute-start | bytes 1572872 | tf_op jit(solution)/shard_map/ppermute | solution.py:44
  296.5 13.7 %copy-start.8 = (bf16[1024,256]{1,0:T(8,128)(2,1)S(1)}, bf16[1024,256]{1,0:T(8,128)(2,1)}, u32[]{:S(2)}) copy-start(bf16[1024,256]{1,0:T(8,128)(2,1)} %copy-done.7) | copy-start | bytes 1572868
  309.6 3.5 collective-permute-start.19
  311.7 64.6 %collective-permute-start.26 = (bf16[1024,512]{1,0:T(8,128)(2,1)}, bf16[1024,512]{1,0:T(8,128)(2,1)}, u32[]{:S(2)}, u32[]{:S(2)}) collective-permute-start(bf16[1024,512]{1,0:T(8,128)(2,1)} %pad_maximum_fusion.1), channel_id=1, source_target_pairs={{0,1},{1,0},{2,3},{3,2},{4,5},{5,4},{6,7},{7,6},{8,9},{9,8},{10,11... | collective-permute-start | bytes 3145736 | tf_op jit(solution)/shard_map/ppermute | solution.py:44
  359.2 17.1 %copy-start.33 = (bf16[512,1024]{1,0:T(8,128)(2,1)S(1)}, bf16[512,1024]{1,0:T(8,128)(2,1)}, u32[]{:S(2)}) copy-start(bf16[512,1024]{1,0:T(8,128)(2,1)} %get-tuple-element.102) | copy-start | bytes 3145732
  362.9 15.9 %copy-start.14 = (f32[1024,768]{1,0:T(8,128)}, f32[1024,768]{1,0:T(8,128)S(1)}, u32[]{:S(2)}) copy-start(f32[1024,768]{1,0:T(8,128)S(1)} %convolution_add_fusion) | copy-start | bytes 9437188
  362.9 17.1 %copy-start.13 = (bf16[1024,1024]{1,0:T(8,128)(2,1)S(1)}, bf16[1024,1024]{1,0:T(8,128)(2,1)}, u32[]{:S(2)}) copy-start(bf16[1024,1024]{1,0:T(8,128)(2,1)} %get-tuple-element.107) | copy-start | bytes 6291460
  363.9 75.4 %collective-permute-start.22 = (bf16[4,128,768]{2,1,0:T(8,128)(2,1)}, bf16[4,128,768]{2,1,0:T(8,128)(2,1)}, u32[]{:S(2)}, u32[]{:S(2)}) collective-permute-start(bf16[4,128,768]{2,1,0:T(8,128)(2,1)} %fusion.13), channel_id=1, source_target_pairs={{0,4},{4,0},{8,12},{12,8},{16,20},{20,16},{24,28},{28,24},{1,5},{5... | collective-permute-start | bytes 2359304 | tf_op jit(solution)/shard_map/ppermute | solution.py:44
  378.7 31.4 %collective-permute-start.27 = (bf16[1024,256]{1,0:T(8,128)(2,1)}, bf16[1024,256]{1,0:T(8,128)(2,1)}, u32[]{:S(2)}, u32[]{:S(2)}) collective-permute-start(bf16[1024,256]{1,0:T(8,128)(2,1)} %fusion.12), channel_id=1, source_target_pairs={{0,2},{1,3},{2,0},{3,1},{4,6},{5,7},{6,4},{7,5},{8,10},{9,11},{10,... | collective-permute-start | bytes 1572872 | tf_op jit(solution)/shard_map/ppermute | solution.py:44
  397.6 11.3 %all-to-all-start.1 = ((f32[32,1,352]{2,1,0:T(1,128)}), f32[32,1,352]{2,1,0:T(1,128)S(1)}, u32[]{:S(2)}, u32[]{:S(2)}) async-start(f32[32,1,352]{2,1,0:T(1,128)} %all_to_all.18), calls=%async_computation.2 | async-start | bytes 98304 | tf_op jit(solution)/shard_map/all_to_all | solution.py:104
  403.9 45.0 %collective-permute-start.33 = (bf16[4,128,1024]{1,2,0:T(8,128)(2,1)S(1)}, bf16[4,128,1024]{1,2,0:T(8,128)(2,1)S(1)}, u32[]{:S(2)}, u32[]{:S(2)}) collective-permute-start(bf16[4,128,1024]{1,2,0:T(8,128)(2,1)S(1)} %bitcast.129), channel_id=1, source_target_pairs={{0,4},{4,0},{8,12},{12,8},{16,20},{20,16},{24,28},{28,24},{1,5},{5... | collective-permute-start | bytes 3145736 | tf_op jit(solution)/shard_map/ppermute | solution.py:44
  405.8 43.4 %collective-permute-start.20 = (bf16[1024,1024]{1,0:T(8,128)(2,1)}, bf16[1024,1024]{1,0:T(8,128)(2,1)}, u32[]{:S(2)}, u32[]{:S(2)}) collective-permute-start(bf16[1024,1024]{1,0:T(8,128)(2,1)} %convolution_convert_fusion), channel_id=1, source_target_pairs={{0,1},{1,0},{2,3},{3,2},{4,5},{5,4},{6,7},{7,6},{8,9},{9,8},{10,11... | collective-permute-start | bytes 6291464 | tf_op jit(solution)/shard_map/ppermute | solution.py:44
  414.1 21.1 %collective-permute-start.28 = (bf16[4,128,256]{1,2,0:T(8,128)(2,1)}, bf16[4,128,256]{1,2,0:T(8,128)(2,1)S(1)}, u32[]{:S(2)}, u32[]{:S(2)}) collective-permute-start(bf16[4,128,256]{1,2,0:T(8,128)(2,1)} %bitcast.107), channel_id=1, source_target_pairs={{0,4},{4,0},{8,12},{12,8},{16,20},{20,16},{24,28},{28,24},{1,5},{5... | collective-permute-start | bytes 786440 | tf_op jit(solution)/shard_map/ppermute | solution.py:44
  435.3 7.3 %collective-permute-start.29 = (bf16[128,256]{0,1:T(8,128)(2,1)S(1)}, bf16[128,256]{0,1:T(8,128)(2,1)S(1)}, u32[]{:S(2)}, u32[]{:S(2)}) collective-permute-start(bf16[128,256]{0,1:T(8,128)(2,1)S(1)} %get-tuple-element.152), channel_id=1, source_target_pairs={{0,8},{4,12},{8,16},{12,20},{16,24},{20,28},{24,0},{28,4},{1,9},{5... | collective-permute-start | bytes 196616 | tf_op jit(solution)/shard_map/ppermute | solution.py:48
  436.9 6.9 %collective-permute-start.30 = (bf16[128,256]{0,1:T(8,128)(2,1)S(1)}, bf16[128,256]{0,1:T(8,128)(2,1)S(1)}, u32[]{:S(2)}, u32[]{:S(2)}) collective-permute-start(bf16[128,256]{0,1:T(8,128)(2,1)S(1)} %get-tuple-element.154), channel_id=1, source_target_pairs={{0,16},{4,20},{8,24},{12,28},{16,0},{20,4},{24,8},{28,12},{1,17},{... | collective-permute-start | bytes 196616 | tf_op jit(solution)/shard_map/ppermute | solution.py:48
  439.2 9.7 %copy-start.4 = (f32[4,1,128,1024]{2,3,0,1:T(8,128)S(1)}, f32[4,1,128,1024]{2,3,0,1:T(8,128)}, u32[]{:S(2)}) copy-start(f32[4,1,128,1024]{2,3,0,1:T(8,128)} %copy.79) | copy-start | bytes 6291460
  439.2 5.4 %collective-permute-start.31 = (bf16[128,256]{0,1:T(8,128)(2,1)S(1)}, bf16[128,256]{0,1:T(8,128)(2,1)S(1)}, u32[]{:S(2)}, u32[]{:S(2)}) collective-permute-start(bf16[128,256]{0,1:T(8,128)(2,1)S(1)} %get-tuple-element.153), channel_id=1, source_target_pairs={{0,24},{4,28},{8,0},{12,4},{16,8},{20,12},{24,16},{28,20},{1,25},{... | collective-permute-start | bytes 196616 | tf_op jit(solution)/shard_map/ppermute | solution.py:48
  442.6 13.1 %collective-permute-start.23 = (bf16[128,768]{1,0:T(8,128)(2,1)S(1)}, bf16[128,768]{1,0:T(8,128)(2,1)S(1)}, u32[]{:S(2)}, u32[]{:S(2)}) collective-permute-start(bf16[128,768]{1,0:T(8,128)(2,1)S(1)} %get-tuple-element.145), channel_id=1, source_target_pairs={{0,8},{4,12},{8,16},{12,20},{16,24},{20,28},{24,0},{28,4},{1,9},{5... | collective-permute-start | bytes 589832 | tf_op jit(solution)/shard_map/ppermute | solution.py:48
  443.8 23.1 %collective-permute-start.24 = (bf16[128,768]{1,0:T(8,128)(2,1)S(1)}, bf16[128,768]{1,0:T(8,128)(2,1)S(1)}, u32[]{:S(2)}, u32[]{:S(2)}) collective-permute-start(bf16[128,768]{1,0:T(8,128)(2,1)S(1)} %get-tuple-element.147), channel_id=1, source_target_pairs={{0,16},{4,20},{8,24},{12,28},{16,0},{20,4},{24,8},{28,12},{1,17},{... | collective-permute-start | bytes 589832 | tf_op jit(solution)/shard_map/ppermute | solution.py:48
  444.6 29.8 %collective-permute-start.25 = (bf16[128,768]{1,0:T(8,128)(2,1)S(1)}, bf16[128,768]{1,0:T(8,128)(2,1)S(1)}, u32[]{:S(2)}, u32[]{:S(2)}) collective-permute-start(bf16[128,768]{1,0:T(8,128)(2,1)S(1)} %get-tuple-element.146), channel_id=1, source_target_pairs={{0,24},{4,28},{8,0},{12,4},{16,8},{20,12},{24,16},{28,20},{1,25},{... | collective-permute-start | bytes 589832 | tf_op jit(solution)/shard_map/ppermute | solution.py:48
  452.7 46.6 %collective-permute-start.21 = (bf16[512,1024]{1,0:T(8,128)(2,1)S(1)}, bf16[512,1024]{1,0:T(8,128)(2,1)}, u32[]{:S(2)}, u32[]{:S(2)}) collective-permute-start(bf16[512,1024]{1,0:T(8,128)(2,1)S(1)} %fusion), channel_id=1, source_target_pairs={{0,2},{1,3},{2,0},{3,1},{4,6},{5,7},{6,4},{7,5},{8,10},{9,11},{10,... | collective-permute-start | bytes 3145736 | tf_op jit(solution)/shard_map/ppermute | solution.py:44
  455.1 23.2 %collective-permute-start.34 = (bf16[128,1024]{0,1:T(8,128)(2,1)}, bf16[128,1024]{0,1:T(8,128)(2,1)S(1)}, u32[]{:S(2)}, u32[]{:S(2)}) collective-permute-start(bf16[128,1024]{0,1:T(8,128)(2,1)} %get-tuple-element.142), channel_id=1, source_target_pairs={{0,8},{4,12},{8,16},{12,20},{16,24},{20,28},{24,0},{28,4},{1,9},{5... | collective-permute-start | bytes 786440 | tf_op jit(solution)/shard_map/ppermute | solution.py:48
  455.7 23.7 %collective-permute-start.35 = (bf16[128,1024]{0,1:T(8,128)(2,1)}, bf16[128,1024]{0,1:T(8,128)(2,1)}, u32[]{:S(2)}, u32[]{:S(2)}) collective-permute-start(bf16[128,1024]{0,1:T(8,128)(2,1)} %get-tuple-element.144), channel_id=1, source_target_pairs={{0,16},{4,20},{8,24},{12,28},{16,0},{20,4},{24,8},{28,12},{1,17},{... | collective-permute-start | bytes 786440 | tf_op jit(solution)/shard_map/ppermute | solution.py:48
  466.9 14.9 %collective-permute-start.36 = (bf16[128,1024]{0,1:T(8,128)(2,1)}, bf16[128,1024]{0,1:T(8,128)(2,1)}, u32[]{:S(2)}, u32[]{:S(2)}) collective-permute-start(bf16[128,1024]{0,1:T(8,128)(2,1)} %get-tuple-element.143), channel_id=1, source_target_pairs={{0,24},{4,28},{8,0},{12,4},{16,8},{20,12},{24,16},{28,20},{1,25},{... | collective-permute-start | bytes 786440 | tf_op jit(solution)/shard_map/ppermute | solution.py:48
  484.4 15.0 %copy-start.12 = (f32[512,1024]{1,0:T(8,128)S(1)}, f32[512,1024]{1,0:T(8,128)}, u32[]{:S(2)}) copy-start(f32[512,1024]{1,0:T(8,128)} %get-tuple-element.93) | copy-start | bytes 6291460
  493.0 13.5 %all-to-all-start.2 = ((f32[32,1,128]{2,1,0:T(1,128)}), f32[32,1,128]{2,1,0:T(1,128)S(1)}, u32[]{:S(2)}, u32[]{:S(2)}) async-start(f32[32,1,128]{2,1,0:T(1,128)} %broadcast_in_dim.218), calls=%async_computation.3 | async-start | bytes 32768 | tf_op jit(solution)/shard_map/all_to_all | solution.py:104
  (15 other events, 44.9 us)
Sparse Core Ops, SparseCore 0:
  11.8 115.3 all-gather.1
  274.9 116.4 reduce-scatter.1

commit v3 on v2

--- a/solution.py
+++ b/solution.py
@@ -4,6 +4,7 @@
 import jax.numpy as jnp
 from jax import lax
 from jax.experimental import pallas as pl
+from jax.experimental.layout import Layout, with_layout_constraint
 from jax.experimental.pallas import tpu as pltpu
 from jax.sharding import PartitionSpec as P
 
@@ -54,7 +55,13 @@
     return lax.ppermute(array, "dp", [(RING[p], RING[(p + step) % 8]) for p in range(8)])
 
 
-def gather(shard, before_last=()):
+def after(array, *others):
+    if not others:
+        return array
+    return lax.optimization_barrier((array,) + others)[0]
+
+
+def gather(shard, before):
     if lax.axis_size("dp") != 8:
         return lax.all_gather(shard, "dp", axis=0, tiled=True)
     d = lax.axis_index("dp")
@@ -68,12 +75,15 @@
 
     full = put(jnp.zeros((8 * rows, width), shard.dtype), shard, 0)
     ahead = behind = shard
-    for step in (1, 2, 3):
-        ahead, behind = around(ahead, 1), around(behind, -1)
-        full = put(put(full, ahead, -step), behind, step)
-    if before_last:
-        ahead = lax.optimization_barrier((ahead,) + tuple(before_last))[0]
-    return put(full, around(ahead, 1), 4)
+    for step in (1, 2, 3, 4):
+        if step > 1:
+            ahead, behind = lax.optimization_barrier((ahead, behind) + tuple(before[step - 1]))[:2]
+        ahead = around(ahead, 1)
+        full = put(full, ahead, -step)
+        if step < 4:
+            behind = around(behind, -1)
+            full = put(full, behind, step)
+    return full
 
 
 def chip_groups():
@@ -83,21 +93,34 @@
     ]
 
 
-def scatter(grad):
+def scatter_y(*grads):
     if lax.axis_size("dp") != 8:
-        return lax.psum_scatter(grad.astype(F32), "dp", scatter_dimension=0, tiled=True)
-    d = lax.axis_index("dp")
-    z, y = d >> 1, d & 1
-    rows, width = grad.shape[0] // 8, grad.shape[1]
-    grad = grad.reshape(4, 2, rows, width)
-    theirs = lax.dynamic_index_in_dim(grad, 1 - y, axis=1, keepdims=False)
-    mine = lax.dynamic_index_in_dim(grad, y, axis=1, keepdims=False)
-    half = mine.astype(F32) + swap(theirs.astype(BF16), "dp", 1).astype(F32)
+        whole = jnp.concatenate(grads, axis=1)
+        return whole, whole
+    y = lax.axis_index("dp") & 1
+    grads = [g.reshape(4, 2, g.shape[0] // 8, g.shape[1]) for g in grads]
+
+    def rows(index, kind):
+        parts = [lax.dynamic_index_in_dim(g, index, axis=1, keepdims=False).astype(kind) for g in grads]
+        return jnp.concatenate(parts, axis=2)
+
+    sent = rows(1 - y, BF16)
+    return rows(y, F32) + swap(sent, "dp", 1).astype(F32), sent
+
+
+def scatter_z(half):
+    if lax.axis_size("dp") != 8:
+        return lax.psum_scatter(half.astype(F32), "dp", scatter_dimension=0, tiled=True)
+    z = lax.axis_index("dp") >> 1
     total = lax.dynamic_index_in_dim(half, z, axis=0, keepdims=False)
     for step in (1, 2, 3):
         part = lax.dynamic_index_in_dim(half, (z + step) & 3, axis=0, keepdims=False)
         total = total + to_z(part.astype(BF16), step).astype(F32)
     return total
+
+
+def turned(array):
+    return with_layout_constraint(array, Layout(major_to_minor=(0, 1))).T
 
 
 def to_all(rows):
@@ -126,18 +149,19 @@
     return jnp.concatenate([table, table], axis=1)
 
 
-def project_body(m_ref, x_ref, wq_ref, wk_ref, wv_ref, cos_ref, sin_ref, sqk_ref, *refs):
+def project_body(m_ref, x_ref, w_ref, cos_ref, sin_ref, sqk_ref, *refs):
     q_ref, k_ref, v_ref, qr_ref, kr_ref = refs[-5:]
     rows = x_ref[...]
     cosine, sine = wide(cos_ref[...]), wide(sin_ref[...])
     scale = sqk_ref[0:1, :]
-    for weight_ref, out_ref, rot_ref in ((wq_ref, q_ref, qr_ref), (wk_ref, k_ref, kr_ref)):
-        raw = jnp.dot(rows, weight_ref[...], preferred_element_type=F32)
+    width = q_ref.shape[1]
+    raws = [dot(rows, w_ref[:, i * width : (i + 1) * width]) for i in range(3)]
+    v_ref[...] = raws[2].astype(BF16)
+    for raw, out_ref, rot_ref in ((raws[0], q_ref, qr_ref), (raws[1], k_ref, kr_ref)):
         turned = raw * cosine + rotate_half(raw) * sine
         rot_ref[...] = turned
         unit = turned * lax.rsqrt(head_mean(turned * turned) + EPS)
         out_ref[...] = (unit * scale).astype(BF16)
-    v_ref[...] = jnp.dot(rows, wv_ref[...], preferred_element_type=F32).astype(BF16)
 
 
 def project(place, x_rows, weight, cosine, sine, sqk, previous, first):
@@ -149,10 +173,6 @@
         return ((m[0] ^ (first + 2 * (i // per))) * per + i % per, 0)
 
     any_spec = pl.BlockSpec(memory_space=pl.ANY)
-
-    def column(index):
-        return pl.BlockSpec((x_rows.shape[1], width), lambda i, m: (0, index))
-
     table = pl.BlockSpec((BLOCK, cosine.shape[1]), row_block)
     out = pl.BlockSpec((BLOCK, width), row_block)
     shapes = [jax.ShapeDtypeStruct((total, width), t) for t in (BF16, BF16, BF16, F32, F32)]
@@ -165,9 +185,7 @@
             grid=(rows // BLOCK,),
             in_specs=[
                 pl.BlockSpec((BLOCK, x_rows.shape[1]), lambda i, m: (i, 0)),
-                column(0),
-                column(1),
-                column(2),
+                pl.BlockSpec((x_rows.shape[1], 3 * width), lambda i, m: (0, 0)),
                 table,
                 table,
                 pl.BlockSpec((8, width), lambda i, m: (0, 0)),
@@ -175,12 +193,12 @@
             + [any_spec] * len(extra),
             out_specs=[out] * 5,
         ),
-        input_output_aliases={8 + i: i for i in range(len(extra))},
+        input_output_aliases={6 + i: i for i in range(len(extra))},
         cost_estimate=pl.CostEstimate(
             flops=6 * rows * D * width, bytes_accessed=8 * rows * D, transcendentals=rows
         ),
         name="project",
-    )(place, x_rows, weight, weight, weight, cosine, sine, sqk, *extra)
+    )(place, x_rows, weight, cosine, sine, sqk, *extra)
 
 
 def head_lanes(array, head):
@@ -219,13 +237,16 @@
     lax.fori_loop(0, source_ref.shape[0] // BLOCK, one, 0)
 
 
-def attend_body(docs, meta_ref, q_ref, k_ref, v_ref, kpos_ref, o_ref, inv_ref, acc_ref, sum_ref, vs_ref):
-    step = pl.program_id(0)
+def attend_body(docs, first, meta_ref, q_ref, k_ref, v_ref, kpos_ref, *refs):
+    o_ref, inv_ref, acc_ref, sum_ref, vs_ref = refs[-5:]
+    per = k_ref.shape[0] // 4 // BLOCK
+    index = pl.program_id(0)
+    step = ((first + index // per) ^ meta_ref[0]) * per + index % per
     heads = q_ref.shape[1] // HEAD
     base = step * BLOCK
     low = doc_start(meta_ref, docs, base) // BLOCK
 
-    @pl.when(step == 0)
+    @pl.when(index == 0)
     def _():
         split_heads(v_ref, vs_ref)
 
@@ -262,38 +283,42 @@
     o_ref[...] = (acc_ref[...] * inverse).astype(BF16)
 
 
-def attend(meta, queries, keys, vals, kpos, docs):
+def attend(meta, queries, keys, vals, kpos, docs, first, previous):
     total, width = queries.shape
     per = total // 4 // BLOCK
     heads = width // HEAD
     whole = pl.BlockSpec((total, width), lambda i, m: (0, 0))
-    block = pl.BlockSpec((BLOCK, width), lambda i, m: (i, 0))
-
-    def rel(i, m):
-        return (slot_place(m[0] ^ (i // per)) * per + i % per, 0)
-
+
+    def natural(i, m):
+        return (((first + i // per) ^ m[0]) * per + i % per, 0)
+
+    block = pl.BlockSpec((BLOCK, width), natural)
+    out = pl.BlockSpec((BLOCK, width), lambda i, m: ((first ^ 2) * per + i, 0))
+    extra = list(previous)
     return pl.pallas_call(
-        functools.partial(attend_body, docs),
+        functools.partial(attend_body, docs, first),
         out_shape=[
             jax.ShapeDtypeStruct((total, width), BF16),
             jax.ShapeDtypeStruct((total, width), F32),
         ],
         grid_spec=pltpu.PrefetchScalarGridSpec(
             num_scalar_prefetch=1,
-            grid=(total // BLOCK,),
-            in_specs=[block, whole, whole, pl.BlockSpec((8, total), lambda i, m: (0, 0))],
-            out_specs=[pl.BlockSpec((BLOCK, width), rel), block],
+            grid=(2 * per,),
+            in_specs=[block, whole, whole, pl.BlockSpec((8, total), lambda i, m: (0, 0))]
+            + [pl.BlockSpec(memory_space=pl.ANY)] * len(extra),
+            out_specs=[out, block],
             scratch_shapes=[
                 pltpu.VMEM((BLOCK, width), F32),
                 pltpu.VMEM((heads * BLOCK, 128), F32),
                 pltpu.VMEM((total // BLOCK, heads * BLOCK, width), BF16),
             ],
         ),
+        input_output_aliases={5 + i: i for i in range(len(extra))},
         cost_estimate=pl.CostEstimate(
-            flops=12_000_000_000, bytes_accessed=8 * total * width, transcendentals=6_000_000
+            flops=8_000_000_000, bytes_accessed=8 * total * width, transcendentals=3_000_000
         ),
         name="attend",
-    )(meta, queries, keys, vals, kpos)
+    )(meta, queries, keys, vals, kpos, *extra)
 
 
 def finish(grad, turned, cosine, sine, scale):
@@ -421,13 +446,12 @@
     per = total // 4 // BLOCK
 
     def rel(i, m):
-        return (slot_place(m[0] ^ (i // per)) * per + i % per, 0)
+        return ((m[0] ^ (i // per) ^ 2) * per + i % per, 0)
 
     whole = pl.BlockSpec((total, width), lambda i, m: (0, 0))
     half = pl.BlockSpec((total, 128), lambda i, m: (0, 0))
     block = pl.BlockSpec((BLOCK, width), lambda i, m: (i, 0))
     moved = pl.BlockSpec((BLOCK, width), rel)
-    small = pl.BlockSpec((8, width), lambda i, m: (0, 0))
     return pl.pallas_call(
         functools.partial(back_body, docs),
         out_shape=[
@@ -437,8 +461,12 @@
         grid_spec=pltpu.PrefetchScalarGridSpec(
             num_scalar_prefetch=1,
             grid=(total // BLOCK,),
-            in_specs=[block, block, moved, block, moved, whole, whole, whole, half, half, half, small],
-            out_specs=[pl.BlockSpec((total, 3 * width), lambda i, m: (0, 0)), small],
+            in_specs=[block, block, moved, block, moved, whole, whole, whole, half, half, half]
+            + [pl.BlockSpec((8, width), lambda i, m: (0, 0))],
+            out_specs=[
+                pl.BlockSpec((total, 3 * width), lambda i, m: (0, 0)),
+                pl.BlockSpec((8, width), lambda i, m: (0, 0)),
+            ],
             scratch_shapes=[
                 pltpu.VMEM((BLOCK, width), F32),
                 pltpu.VMEM((total, width), F32),
@@ -447,7 +475,7 @@
             ],
         ),
         cost_estimate=pl.CostEstimate(
-            flops=30_000_000_000, bytes_accessed=24 * total * width, transcendentals=6_000_000
+            flops=40_000_000_000, bytes_accessed=12 * total * width, transcendentals=6_000_000
         ),
         name="attend_back",
     )(meta, queries, qrot, out, inverse, grad, keys, vals, krot, kpos, cosine, sine, sqk)
@@ -532,11 +560,11 @@
     )(rows, weights, sup, sgate)
 
 
-def backward_body(
-    gm_ref, w_ref, gate_ref, act_ref, by_up_ref, by_gate_ref, sup_ref, sgate_ref, gu_ref, gg_ref, bu_ref, bg_ref, out_ref, acc_ref
-):
+def backward_body(pieces, *refs):
+    rows = jnp.concatenate([ref[...] for ref in refs[:pieces]], axis=0)
+    w_ref, gate_ref, act_ref, by_up_ref, by_gate_ref, sup_ref, sgate_ref = refs[pieces : pieces + 7]
+    gu_ref, gg_ref, bu_ref, bg_ref, out_ref, acc_ref = refs[pieces + 7 :]
     t = pl.program_id(0)
-    rows = gm_ref[...]
     lefts, rights = [], []
     for part in range(2):
         g_act = dot(rows, weight_tile(w_ref, part, 2))
@@ -556,15 +584,18 @@
 
 
 def ffn_backward(grads, weights, saved, sup, sgate, kind):
-    count, hidden = grads.shape[0], sup.shape[2]
+    count, hidden = sum(g.shape[0] for g in grads), sup.shape[2]
     whole, tile, scale = ffn_specs(count)
     return pl.pallas_call(
-        backward_body,
+        functools.partial(backward_body, len(grads)),
         out_shape=[jax.ShapeDtypeStruct((2, count, hidden), BF16)] * 2
         + [jax.ShapeDtypeStruct((2, 8, hidden), F32)] * 2
         + [jax.ShapeDtypeStruct((count, D), kind)],
         grid=(hidden // TILE,),
-        in_specs=[whole, weight_spec(weights)] + [tile] * 4 + [scale, scale],
+        in_specs=[pl.BlockSpec(g.shape, lambda t: (0, 0)) for g in grads]
+        + [weight_spec(weights)]
+        + [tile] * 4
+        + [scale, scale],
         out_specs=[tile, tile, scale, scale, whole],
         scratch_shapes=[pltpu.VMEM((count, D), F32)],
         cost_estimate=pl.CostEstimate(
@@ -573,57 +604,57 @@
             transcendentals=0,
         ),
         name="ffn_backward",
-    )(grads, weights, *saved, sup, sgate)
-
-
-def turn_rows(own_ref, far_ref, turned_ref):
-    count = own_ref.shape[0]
+    )(*grads, weights, *saved, sup, sgate)
+
+
+def weight_body(counts, *refs):
+    h_count, g_count, m_count = counts
+    take = iter(refs)
+    hs = [next(take) for _ in range(h_count)]
+    ms = [next(take) for _ in range(m_count)]
+    ups, gates, acts = [[next(take) for _ in range(g_count)] for _ in range(3)]
+    out_ref, ht_ref, mt_ref = refs[-3:]
 
     @pl.when(pl.program_id(0) == 0)
     def _():
-        turned_ref[:, :count] = own_ref[...].T
-        turned_ref[:, count:] = far_ref[...].T
-
-
-def down_grad_body(m_ref, lo_ref, lr_ref, ro_ref, rr_ref, mine_ref, other_ref, turned_ref):
-    turn_rows(lo_ref, lr_ref, turned_ref)
-    core = m_ref[0] & 1
-    for part, out_ref in ((core, mine_ref), (1 - core, other_ref)):
-        right = jnp.concatenate([ro_ref[part], rr_ref[part]], axis=0)
-        out_ref[...] = dot(turned_ref[...], right).astype(BF16)
-
-
-def up_grad_body(m_ref, lo_ref, lr_ref, uo_ref, ur_ref, go_ref, gr_ref, out_ref, turned_ref):
-    turn_rows(lo_ref, lr_ref, turned_ref)
-    for index, (own_ref, far_ref) in enumerate(((uo_ref, ur_ref), (go_ref, gr_ref))):
+        for pieces, to_ref in ((hs, ht_ref), (ms, mt_ref)):
+            start = 0
+            for ref in pieces:
+                to_ref[:, start : start + ref.shape[0]] = ref[...].T
+                start += ref.shape[0]
+
+    for index, (left_ref, rights) in enumerate(((ht_ref, ups), (ht_ref, gates), (mt_ref, acts))):
         for part in range(2):
-            right = jnp.concatenate([own_ref[part], far_ref[part]], axis=0)
-            total = dot(turned_ref[...], right).astype(BF16)
+            right = jnp.concatenate([ref[part] for ref in rights], axis=0)
+            total = dot(left_ref[...], right).astype(BF16)
             out_ref[:, part, index] = total.reshape(out_ref.shape[0], out_ref.shape[3], TILE)
 
 
-def weight_grad(body, place, lefts, rights, out_shape, out_specs):
-    _, count, hidden = rights[0].shape
-    whole = pl.BlockSpec((count, D), lambda t, m: (0, 0))
-    tile = pl.BlockSpec((2, count, TILE), lambda t, m: (0, 0, t))
-    pairs = len(rights) // 2
+def weight_grads(hs, ms, ups, gates, acts, shape):
+    hidden = ups[0].shape[2]
+    count = sum(h.shape[0] for h in hs)
+
+    def whole(array):
+        return pl.BlockSpec(array.shape, lambda t: (0, 0))
+
+    def tile(array):
+        return pl.BlockSpec((2, array.shape[1], TILE), lambda t: (0, 0, t))
+
+    lefts, rights = list(hs) + list(ms), list(ups) + list(gates) + list(acts)
     return pl.pallas_call(
-        body,
-        out_shape=out_shape,
-        grid_spec=pltpu.PrefetchScalarGridSpec(
-            num_scalar_prefetch=1,
-            grid=(hidden // TILE,),
-            in_specs=[whole, whole] + [tile] * len(rights),
-            out_specs=out_specs,
-            scratch_shapes=[pltpu.VMEM((D, 2 * count), BF16)],
-        ),
+        functools.partial(weight_body, (len(hs), len(ups), len(ms))),
+        out_shape=jax.ShapeDtypeStruct(shape, BF16),
+        grid=(hidden // TILE,),
+        in_specs=[whole(a) for a in lefts] + [tile(a) for a in rights],
+        out_specs=pl.BlockSpec(shape[:4] + (TILE,), lambda t: (0, 0, 0, 0, t)),
+        scratch_shapes=[pltpu.VMEM((D, count), BF16)] * 2,
         cost_estimate=pl.CostEstimate(
-            flops=8 * pairs * count * D * hidden,
-            bytes_accessed=pairs * (4 * D * hidden + 8 * count * hidden),
+            flops=12 * count * D * hidden,
+            bytes_accessed=12 * D * hidden + 12 * count * hidden,
             transcendentals=0,
         ),
-        name="weight_grad",
-    )(place, *lefts, *rights)
+        name="weight_grads",
+    )(*lefts, *rights)
 
 
 def own_call(body, name, rows_in, vectors, wholes, outs, sums, flops):
@@ -667,7 +698,8 @@
     low_ref[...] = hidden.astype(BF16)
 
 
-def turn_body(own_ref, far_ref, branch_ref, x_ref, cot_ref, one_ref, two_ref, out_ref, gm_ref, keep_ref, sum_ref):
+def turn_body(own_ref, far_ref, branch_ref, x_ref, cot_ref, one_ref, two_ref, *refs):
+    out_ref, keep_ref, gm_ref, sum_ref = refs[-4:]
     hidden = first_update(branch_ref[...], x_ref[...].astype(F32), one_ref[0:1, :])[2]
     alpha = two_ref[0:1, :]
     h_mlp, mlp_factor = normed(own_ref[...] + far_ref[...].astype(F32))
@@ -678,11 +710,33 @@
     keep_ref[...] = grad_two * (1.0 - alpha)
     gm_ref[...] = normed_back(grad_two * alpha, h_mlp, mlp_factor).astype(BF16)
 
-    @pl.when(pl.program_id(0) == 0)
-    def _():
-        sum_ref[...] = jnp.zeros_like(sum_ref)
-
-    sum_ref[0:1, :] += jnp.sum(grad_two * step, axis=0, keepdims=True)
+    sum_ref[0:1, :] = jnp.sum(grad_two * step, axis=0, keepdims=True)
+
+
+def turn(chunk, own, far, branch, x_rows, cotangent, one, two, previous):
+    count = branch.shape[0]
+    rows = pl.BlockSpec((BLOCK, D), lambda i: (chunk, 0))
+    first = pl.BlockSpec((BLOCK, D), lambda i: (0, 0))
+    vector = pl.BlockSpec((8, D), lambda i: (0, 0))
+    extra = list(previous)
+    return pl.pallas_call(
+        turn_body,
+        out_shape=[
+            jax.ShapeDtypeStruct((count, D), BF16),
+            jax.ShapeDtypeStruct((count, D), F32),
+            jax.ShapeDtypeStruct((BLOCK, D), BF16),
+            jax.ShapeDtypeStruct((8, D), F32),
+        ],
+        grid=(1,),
+        in_specs=[rows, first, rows, rows, rows, vector, vector]
+        + [pl.BlockSpec(memory_space=pl.ANY)] * len(extra),
+        out_specs=[rows, rows, first, vector],
+        input_output_aliases={7 + i: i for i in range(len(extra))},
+        cost_estimate=pl.CostEstimate(
+            flops=60 * BLOCK * D, bytes_accessed=20 * BLOCK * D, transcendentals=BLOCK
+        ),
+        name="turn",
+    )(own, far, branch, x_rows, cotangent, one, two, *extra)
 
 
 def attn_back_body(
@@ -731,40 +785,6 @@
     part = w_up.shape[1]
     width = w_query.shape[1]
 
-    shard = jnp.concatenate([w_up, w_gate, w_down.T], axis=0)
-    weights = lax.all_gather(
-        shard, ("dp", "mp"), axis=0, tiled=True, axis_index_groups=chip_groups()
-    ).reshape(-1, 2, 3, shard.shape[0] // 3, part)
-    x_over = swap(tokens, "mp", 2)
-    vector = jnp.concatenate([s_up, s_gate, s_qk, alpha_attn, alpha_mlp])[None]
-    every = to_all(jnp.broadcast_to(vector, (devices, vector.shape[1])))
-    attn = gather(jnp.concatenate([w_query, w_key, w_value, w_out.T], axis=1), (x_over, every))
-    cuts, start = [], 0
-    for piece in (s_up, s_gate, s_qk, alpha_attn, alpha_mlp):
-        cuts.append(every[:, start : start + piece.shape[0]].reshape(-1))
-        start += piece.shape[0]
-    sup_all, sgate_all, sqk_all, alpha_one, alpha_two = cuts
-
-    def quarter(array, index):
-        size = array.shape[0] // 4
-        return lax.dynamic_slice_in_dim(array, index * size, size)
-
-    def eight(array):
-        return jnp.broadcast_to(array[None], (8, array.shape[0]))
-
-    sqk = eight(quarter(sqk_all, m))
-    low = m & 2
-    sup = jnp.stack([eight(quarter(sup_all, low)), eight(quarter(sup_all, low + 1))])
-    sgate = jnp.stack([eight(quarter(sgate_all, low)), eight(quarter(sgate_all, low + 1))])
-    one, two = eight(alpha_one), eight(alpha_two)
-    x_first = jnp.concatenate([tokens, x_over], axis=0)
-    x_second = swap(x_first, "mp", 1)
-    out_mine = attn[:, 3 * width :]
-    out_core = swap(out_mine, "mp", 1)
-    out_over = swap(out_mine, "mp", 2)
-    out_cross = swap(out_over, "mp", 1)
-    out_parts = [(w, width, 0) for w in (out_mine, out_core, out_over, out_cross)]
-
     place = m.reshape(1)
     meta = jnp.concatenate([place, lengths[0]])
     slot_ids = jnp.arange(row_len, dtype=jnp.int32)
@@ -776,17 +796,58 @@
     frequencies = jnp.power(jnp.float32(10000.0), -steps_even / HEAD)
     angles = positions.astype(F32)[:, None] * jnp.tile(frequencies, 4)[None, :]
     cosine, sine = jnp.cos(angles), jnp.sin(angles)
+    shard = jnp.concatenate([w_up, w_gate, w_down.T], axis=0)
+    shard = with_layout_constraint(shard, Layout(major_to_minor=(0, 1)))
+    weights = lax.all_gather(
+        shard, ("dp", "mp"), axis=0, tiled=True, axis_index_groups=chip_groups()
+    ).reshape(-1, 2, 3, shard.shape[0] // 3, part)
+    x_halves = [swap(tokens[i * local // 2 : (i + 1) * local // 2], "mp", 2) for i in range(2)]
+    x_first = jnp.concatenate([tokens] + x_halves, axis=0)
+    x_second = swap(x_first, "mp", 1)
+    vector = jnp.concatenate([s_up, s_gate, s_qk, alpha_attn, alpha_mlp])[None]
+    every = to_all(jnp.broadcast_to(vector, (devices, vector.shape[1])))
+    attn = gather(
+        jnp.concatenate([w_query, w_key, w_value, w_out.T], axis=1),
+        [(), (x_halves[0], cosine, sine), (), (x_halves[1], every)],
+    )
+    cuts, start = [], 0
+    for piece in (s_up, s_gate, s_qk, alpha_attn, alpha_mlp):
+        cuts.append(every[:, start : start + piece.shape[0]].reshape(-1))
+        start += piece.shape[0]
+    sup_all, sgate_all, sqk_all, alpha_one, alpha_two = cuts
+
+    def quarter(array, index):
+        size = array.shape[0] // 4
+        return lax.dynamic_slice_in_dim(array, index * size, size)
+
+    def eight(array):
+        return jnp.broadcast_to(array[None], (8, array.shape[0]))
+
+    sqk = eight(quarter(sqk_all, m))
+    low = m & 2
+    sup = jnp.stack([eight(quarter(sup_all, low)), eight(quarter(sup_all, low + 1))])
+    sgate = jnp.stack([eight(quarter(sgate_all, low)), eight(quarter(sgate_all, low + 1))])
+    one, two = eight(alpha_one), eight(alpha_two)
+    out_mine = attn[:, 3 * width :]
+    out_core = swap(out_mine, "mp", 1)
+    out_over = swap(out_mine, "mp", 2)
+    out_cross = swap(out_over, "mp", 1)
+    out_parts = [(w, width, 0) for w in (out_mine, out_core, out_over, out_cross)]
+
     kpos = jnp.where(key_mask[0] == 1, slot_ids, -1)
     kpos_rows = jnp.broadcast_to(kpos[None, :], (8, row_len))
     kpos_cols = jnp.broadcast_to(kpos[:, None], (row_len, 128))
 
     half = project(place, x_first, attn, cosine, sine, sqk, None, 0)
     queries, keys, vals, qrot, krot = project(place, x_second, attn, cosine, sine, sqk, half, 1)
-    attended, inverse_mass = attend(meta, queries, keys, vals, kpos_rows, docs)
-    near = attended[: 2 * local]
-    by_core = swap(attended[2 * local :], "mp", 1)
-    by_x = swap(jnp.concatenate([near[local:], by_core[local:]]), "mp", 2)
-    heads_in = [(near, width, 0, 0), (by_core, width, 0, 0), (by_x, width, 0, 0), (by_x, width, local, 0)]
+    half = attend(meta, queries, keys, vals, kpos_rows, docs, 2, ())
+    far_core = swap(half[0][local : 2 * local], "mp", 1)
+    for_x = jnp.concatenate([half[0][:local], far_core])
+    by_x = swap(for_x, "mp", 2)
+    half = [after(half[0], for_x), half[1]]
+    attended, inverse_mass = attend(meta, queries, keys, vals, kpos_rows, docs, 0, half)
+    by_core = swap(attended[3 * local :], "mp", 1)
+    heads_in = [(attended, width, 2 * local, 0), (by_core, width, 0, 0), (by_x, width, 0, 0), (by_x, width, local, 0)]
     branch, h_own = own_call(
         attn_body,
         "attn_out",
@@ -798,46 +859,43 @@
         2 * local * D * D,
     )
 
-    h_far = swap(h_own, "mp", 2)
+    chunks = range(local // BLOCK)
+    h_far = [swap(h_own[c * BLOCK : (c + 1) * BLOCK], "mp", 2) for c in chunks]
     *saved_own, sum_own = ffn_forward(h_own, weights, sup, sgate, F32)
-    *saved_far, sum_far = ffn_forward(h_far, weights, sup, sgate, BF16)
-    result, gm_own, keep_two, by_two = own_call(
-        turn_body,
-        "turn",
-        [(sum_own, D, 0, 0), (swap(sum_far, "mp", 2), D, 0, 0), (branch, D, 0, 0), (tokens, D, 0, 0), (cotangent, D, 0, 0)],
-        [one, two],
-        [],
-        [(local, D, BF16), (local, D, BF16), (local, D, F32)],
-        1,
-        60 * local * D,
-    )
-    gm_far = swap(gm_own, "mp", 2)
-    gu_own, gg_own, bu_own, bg_own, gh_own = ffn_backward(gm_own, weights, saved_own, sup, sgate, F32)
-    gu_far, gg_far, bu_far, bg_far, gh_far = ffn_backward(gm_far, weights, saved_far, sup, sgate, BF16)
-    gh_over = swap(gh_far, "mp", 2)
-
-    down_mine, down_other = weight_grad(
-        down_grad_body,
-        place,
-        (gm_own, gm_far),
-        (saved_own[1], saved_far[1]),
-        [jax.ShapeDtypeStruct((D, part), BF16)] * 2,
-        [pl.BlockSpec((D, TILE), lambda t, m: (0, t))] * 2,
-    )
-    ups = weights.shape[:2] + (2,) + weights.shape[3:]
-    ups = weight_grad(
-        up_grad_body,
-        place,
-        (h_own, h_far),
-        (gu_own, gu_far, gg_own, gg_far),
-        jax.ShapeDtypeStruct(ups, BF16),
-        pl.BlockSpec(ups[:4] + (TILE,), lambda t, m: (0, 0, 0, 0, t)),
-    )
-    grad_ups = lax.psum_scatter(
-        ups.reshape(-1, part), ("dp", "mp"), scatter_dimension=0, tiled=True, axis_index_groups=chip_groups()
+    saved_far, sum_far, last = [], [], sum_own
+    for c in chunks:
+        *saved, last = ffn_forward(after(h_far[c], last), weights, sup, sgate, BF16)
+        saved_far.append(saved)
+        sum_far.append(swap(last, "mp", 2))
+    done, gm_own, gm_far, by_two = (), [], [], 0.0
+    for c in chunks:
+        *done, gm, by = turn(c, after(sum_own, last), sum_far[c], branch, tokens, cotangent, one, two, done)
+        gm_own.append(gm)
+        gm_far.append(swap(gm, "mp", 2))
+        by_two = by_two + by
+    result, keep_two = done
+    gu, gg, bu, bg, gh_own = ffn_backward(gm_own, weights, saved_own, sup, sgate, F32)
+    gus, ggs, last, gh_over = [gu], [gg], gh_own, []
+    for c in chunks:
+        gu, gg, bu_c, bg_c, last = ffn_backward([after(gm_far[c], last)], weights, saved_far[c], sup, sgate, BF16)
+        gh_over.append(swap(last, "mp", 2))
+        gus.append(gu)
+        ggs.append(gg)
+        bu, bg = bu + bu_c, bg + bg_c
+    grad_mlp = weight_grads(
+        [h_own] + h_far,
+        gm_own + gm_far,
+        gus,
+        ggs,
+        [saved_own[1]] + [saved[1] for saved in saved_far],
+        weights.shape,
+    )
+    grad_mlp, *gh_over = lax.optimization_barrier((grad_mlp, *gh_over))
+    gh_over = jnp.concatenate(gh_over)
+    grad_mlp = lax.psum_scatter(
+        grad_mlp.reshape(-1, part), ("dp", "mp"), scatter_dimension=0, tiled=True, axis_index_groups=chip_groups()
     ).astype(F32)
-    grad_up, grad_gate = jnp.split(grad_ups, 2, axis=0)
-    grad_down = scatter(down_mine.astype(F32) + swap(down_other, "mp", 1).astype(F32)).T
+    grad_up, grad_gate, grad_down = jnp.split(grad_mlp, 3, axis=0)
 
     grad_attn, grad_x, att0, att1, att2, att3, by_one = own_call(
         attn_back_body,
@@ -851,51 +909,53 @@
     )
     back_x = swap(jnp.concatenate([att2, att3]), "mp", 2)
     back_core = swap(jnp.concatenate([att1, back_x[local:]]), "mp", 1)
-    g_att = jnp.concatenate([att0, back_x[:local], back_core])
+    g_att = jnp.concatenate([back_x[:local], back_core[local:], att0, back_core[:local]])
     outs = [dot(grad_attn, a[s : s + local], 0, 0) for a, _, s, _ in heads_in]
     core_out = swap(jnp.concatenate([outs[1], outs[3]], axis=1).astype(BF16), "mp", 1)
+    core_out, g_att = lax.optimization_barrier((core_out, g_att))
     over_out = swap((outs[2] + core_out[:, width:].astype(F32)).astype(BF16), "mp", 2)
-    grad_out = scatter(outs[0] + core_out[:, :width].astype(F32) + over_out.astype(F32)).T
-
+    grad_out = outs[0] + core_out[:, :width].astype(F32) + over_out.astype(F32)
     grads, g_sqk = attend_back(
         meta, queries, qrot, attended, inverse_mass, g_att, keys, vals, krot, kpos_cols, cosine, sine, sqk, docs
     )
-    g_first, g_second = grads[: 2 * local], grads[2 * local :]
-    qkv = attn[:, : 3 * width]
-    to_core = swap(dot(g_second, qkv, 1, 1).astype(BF16), "mp", 1)
-    partial = dot(g_first, qkv, 1, 1)
-    to_x = swap((partial[local:] + to_core[local:].astype(F32)).astype(BF16), "mp", 2)
-    grad_tokens = grad_x + partial[:local] + to_core[:local].astype(F32) + to_x.astype(F32)
-    grad_qkv = scatter(dot(x_first, g_first, 0, 0) + dot(x_second, g_second, 0, 0))
-    g_qkv = [grad_qkv[:, i * width : (i + 1) * width] for i in range(3)]
+    first, second = grads[: 2 * local], grads[2 * local :]
+    qkv_sum = dot(x_first, first, 0, 0) + dot(x_second, second, 0, 0)
+    half_sum, sent = scatter_y(qkv_sum, grad_out)
+    qkv = after(attn, sent)[:, : 3 * width]
+    second_tokens = dot(second, qkv, 1, 1).astype(BF16)
+    to_core = swap(second_tokens, "mp", 1)
+    partial = dot(first, after(qkv, second_tokens), 1, 1)
+    for_x = (partial[local:] + to_core[local:].astype(F32)).astype(BF16)
+    to_x = swap(for_x, "mp", 2)
 
     def placed(array, index):
         slots = lax.broadcasted_iota(jnp.int32, (4, 1), 0)
         return jnp.where(slots == index, array[None], 0.0)
 
-    def quarters(own, far):
-        by = own[:, 0] + far[:, 0]
-        return (placed(by[0], m & 2) + placed(by[1], (m & 2) + 1)).reshape(devices, -1)
-
-    rows = [
-        quarters(bu_own, bu_far),
-        quarters(bg_own, bg_far),
-        placed(g_sqk[0], m).reshape(devices, -1),
-        by_one[0].reshape(devices, -1),
-        by_two[0].reshape(devices, -1),
-    ]
-    small = jnp.sum(to_all(jnp.concatenate(rows, axis=1)), axis=0)
+    def quarters(by):
+        return placed(by[0, 0], m & 2) + placed(by[1, 0], (m & 2) + 1)
+
+    rows = [quarters(bu), quarters(bg), placed(g_sqk[0], m), by_one[0], by_two[0]]
+    rows = [row.reshape(devices, -1) for row in rows]
+    small = jnp.sum(to_all(after(jnp.concatenate(rows, axis=1), for_x)), axis=0)
     cuts, start = [], 0
-    for piece in rows:
-        cuts.append(small[start : start + piece.shape[1]])
-        start += piece.shape[1]
+    for row in rows:
+        cuts.append(small[start : start + row.shape[1]])
+        start += row.shape[1]
     g_sup, g_sgate, g_sqk, g_alpha_one, g_alpha_two = cuts
 
+    def squared(*arrays):
+        return sum(jnp.sum(array * array) for array in arrays)
+
+    squares = squared(grad_mlp)
+    grad_attn = scatter_z(after(half_sum, for_x, squares))
+    squares = squares + squared(grad_attn, small)
+    g_qkv = [grad_attn[:, i * width : (i + 1) * width] for i in range(3)]
+    grad_down, grad_out = turned(grad_down), turned(grad_attn[:, 3 * width :])
+    to_x = after(to_x, squares)
+    grad_tokens = grad_x + partial[:local] + to_core[:local].astype(F32) + to_x.astype(F32)
     pieces = tuple(g_qkv) + (grad_out, grad_up, grad_gate, grad_down)
     pieces = pieces + (g_sqk, g_sup, g_sgate, g_alpha_one, g_alpha_two)
-    squares = jnp.float32(0.0)
-    for piece in pieces:
-        squares = squares + jnp.sum(piece * piece)
     squares = jnp.sum(to_all(jnp.broadcast_to(squares, (devices, 128))), axis=0)
     grad_norm = jnp.sqrt(squares[0])
     mean_alphas = jnp.stack([jnp.mean(alpha_one), jnp.mean(alpha_two)])

time: 520 us -> 468 us (0.900)
  starting transfers between devices: 82 us -> 55 us
  local copies, waits for them, and re-layouts: 55.4 us -> 42 us
  Pallas kernels: 171 us -> 184 us
  waiting for transfers between devices: 116 us -> 104 us
  between operations: 27.7 us -> 22.2 us
    ppermute x21 -> x24, waiting for transfers between devices: 72.2 us -> 38.6 us  [swap(): return lax.ppermute(array, axis, [(i, i ^ bit) for i in range(size)])]
    ppermute x9 -> x3, starting transfers between devices: 23 us -> 3.83 us  [to_z(): lax.ppermute(array, 'dp', [(z * 2 + y, (z + step) % 4 * 2 + y) for z in r...]
    pallas_call x5 -> x8, Pallas kernels: 68.3 us -> 85 us  [the longest x3 34.7 us: ffn_backward(): pl.pallas_call(functools.partial(backward_body, len(grads)), out_shape=[j...]
    all_gather x1 -> x0, local copies, waits for them, and re-layouts: 16.7 us -> none  [shards(): lax.all_gather(shard, ('dp', 'mp'), axis=0, tiled=True, axis_index_groups...]
    reduce_scatter x1, waiting for transfers between devices: 0.01 us -> 10.9 us  [shards(): lax.psum_scatter(grad_mlp.reshape(-1, part), ('dp', 'mp'), scatter_dimens...]
    ppermute x7, waiting for transfers between devices: 27.6 us -> 37.8 us  [around(): lax.ppermute(array, 'dp', [(RING[p], RING[(p + step) % 8]) for p in range...]
    ppermute x21 -> x24, starting transfers between devices: 28.6 us -> 18.8 us  [swap(): return lax.ppermute(array, axis, [(i, i ^ bit) for i in range(size)])]
    all_to_all x3, starting transfers between devices: 15.1 us -> 23.9 us  [to_all(): return lax.all_to_all(rows, ('dp', 'mp'), 0, 0, tiled=True)]
  transfers between devices with their start and end apart: 42 -> 39, of which waited for: 17 -> 16; matrix products, arithmetic and copies ran while one was open for 20% -> 19% of each run, Pallas kernels for 27% -> 40%
where the time goes in v3:
time: 468 us; the launch traced here: 465 us
  Pallas kernels  184 us (39%)
  waiting for transfers between devices  104 us (22%)
  starting transfers between devices  55 us (12%)
  local copies, waits for them, and re-layouts  42 us (9%)
  other arithmetic  37.7 us (8%)
  between operations  22.2 us (5%)
  matrix products  19.6 us (4%)
    pallas_call x1, Pallas kernels, attend_back(): pl.pallas_call(functools.partial(back_body, docs), out_shape=[jax.ShapeDt...  39.1 us
    ppermute x24, waiting for transfers between devices, swap(): return lax.ppermute(array, axis, [(i, i ^ bit) for i in range(size)])  38.6 us
    ppermute x7, waiting for transfers between devices, around(): lax.ppermute(array, 'dp', [(RING[p], RING[(p + step) % 8]) for p in range...  37.8 us
    pallas_call x3, Pallas kernels, ffn_backward(): pl.pallas_call(functools.partial(backward_body, len(grads)), out_shape=[j...  34.7 us
    pallas_call x3, Pallas kernels, ffn_forward(): pl.pallas_call(forward_body, out_shape=[jax.ShapeDtypeStruct((2, count, h...  32.5 us
    all_to_all x3, starting transfers between devices, to_all(): return lax.all_to_all(rows, ('dp', 'mp'), 0, 0, tiled=True)  23.9 us
    pallas_call x2, Pallas kernels, attend(): pl.pallas_call(functools.partial(attend_body, docs, first), out_shape=[ja...  20.8 us
    pallas_call x1, Pallas kernels, weight_grads(): pl.pallas_call(functools.partial(weight_body, (len(hs), len(ups), len(ms)...  20.5 us
  transfers between devices with their start and end apart: 39, of which 16 were waited for; matrix products, arithmetic and copies ran while one was open for 19% of the time, Pallas kernels for 40%

profile of v3, /device:TPU:0, one launch (start us, length us, event | category | flops | bytes accessed | tf_op | source)
XLA Modules:
  0.0 464.6 jit_solution(8546730457483858300)
XLA Ops:
  8.4 2.0 pad_maximum_fusion.4
  11.6 2.9 collective-permute-start
  15.7 1.6 collective-permute-start.3
  18.6 6.3 %all-to-all-start = ((f32[32,1,352]{2,1,0:T(1,128)}), f32[32,1,352]{2,1,0:T(1,128)S(1)}, u32[]{:S(2)}, u32[]{:S(2)}) async-start(f32[32,1,352]{2,1,0:T(1,128)} %broadcast_in_dim.181), calls=%async_computation | async-start | bytes 98304 | tf_op jit(solution)/shard_map/all_to_all | solution.py:127
  28.2 2.6 subtract_convert_fusion
  31.9 1.9 constant_dynamic-update-slice_fusion.1
  33.7 4.7 %collective-permute-done.1 = bf16[256,1024]{1,0:T(8,128)(2,1)} collective-permute-done((bf16[256,1024]{1,0:T(8,128)(2,1)}, bf16[256,1024]{1,0:T(8,128)(2,1)}, u32[]{:S(2)}, u32[]{:S(2)}) %collective-permute-start.1) | collective-permute-done | bytes 524320 | tf_op jit(solution)/shard_map/ppermute | solution.py:45
  38.5 1.9 constant_dynamic-update-slice_fusion.x_ref
  40.3 5.6 %multiply_sine_fusion = (f32[2048,128]{1,0:T(8,128)}, f32[2048,128]{1,0:T(8,128)}) fusion(f32[128]{0:T(128)S(1)} %mul.129, f32[2048]{0:T(1024)S(1)} %subtract_convert_fusion), kind=kLoop, calls=%fused_computation.11 | loop fusion | flops 262144 | bytes 2105856 | tf_op jit(solution)/shard_map/sin | solution.py:798
  45.9 1.9 collective-permute-start.5
  49.4 5.3 %collective-permute-done.5 = bf16[128,1024]{1,0:T(8,128)(2,1)S(1)} collective-permute-done((bf16[128,1024]{1,0:T(8,128)(2,1)S(1)}, bf16[128,1024]{1,0:T(8,128)(2,1)S(1)}, u32[]{:S(2)}, u32[]{:S(2)}) %collective-permute-start.5) | collective-permute-done | bytes 262176 | tf_op jit(solution)/shard_map/ppermute | solution.py:55
  54.7 2.5 collective-permute-done.6
  57.2 1.6 collective-permute-start.7
  60.3 10.8 %collective-permute-done.7 = bf16[128,1024]{1,0:T(8,128)(2,1)S(1)} collective-permute-done((bf16[128,1024]{1,0:T(8,128)(2,1)S(1)}, bf16[128,1024]{1,0:T(8,128)(2,1)S(1)}, u32[]{:S(2)}, u32[]{:S(2)}) %collective-permute-start.7) | collective-permute-done | bytes 262176 | tf_op jit(solution)/shard_map/ppermute | solution.py:55
  71.1 7.1 %collective-permute-done.8 = bf16[128,1024]{1,0:T(8,128)(2,1)S(1)} collective-permute-done((bf16[128,1024]{1,0:T(8,128)(2,1)S(1)}, bf16[128,1024]{1,0:T(8,128)(2,1)S(1)}, u32[]{:S(2)}, u32[]{:S(2)}) %collective-permute-start.8) | collective-permute-done | bytes 262176 | tf_op jit(solution)/shard_map/ppermute | solution.py:55
  78.2 2.2 collective-permute-start.9
  80.5 12.1 %collective-permute-done.9 = bf16[128,1024]{1,0:T(8,128)(2,1)S(1)} collective-permute-done((bf16[128,1024]{1,0:T(8,128)(2,1)S(1)}, bf16[128,1024]{1,0:T(8,128)(2,1)S(1)}, u32[]{:S(2)}, u32[]{:S(2)}) %collective-permute-start.9) | collective-permute-done | bytes 262176 | tf_op jit(solution)/shard_map/ppermute | solution.py:55
  94.5 6.8 %project.2 = (bf16[2048,256]{1,0:T(8,128)(2,1)}, bf16[2048,256]{1,0:T(8,128)(2,1)}, bf16[2048,256]{1,0:T(8,128)(2,1)}, f32[2048,256]{1,0:T(8,128)}, f32[2048,256]{1,0:T(8,128)}) custom-call(s32[1]{0:T(128)} %bitcast.m_ref, bf16[1024,1024]{1,0:T(8,128)(2,1)} %constant_dynamic-update-slice_fusion.x_ref, bf16[1024,1024]{1,0:T(8,128)(2,1)} %copy-done.1, ...), custom_call_target="tpu_custom_call" | custom-call | flops 1610612736 | bytes 8388608 | tf_op jit(solution)/shard_map/project/pallas_call | solution.py:180
  101.3 7.0 %project.3 = (bf16[2048,256]{1,0:T(8,128)(2,1)}, bf16[2048,256]{1,0:T(8,128)(2,1)}, bf16[2048,256]{1,0:T(8,128)(2,1)}, f32[2048,256]{1,0:T(8,128)}, f32[2048,256]{1,0:T(8,128)}) custom-call(s32[1]{0:T(128)} %bitcast.m_ref, ...), custom_call_target="tpu_custom_call", output_to_operand_aliasing={{0}: (6, {}), {1}: (7, {}), {2}: (8, {}), {3}: (9, {}), {4}... | custom-call | flops 1610612736 | bytes 8388608 | tf_op jit(solution)/shard_map/project/pallas_call | solution.py:180
  109.0 11.9 %attend.2 = (bf16[2048,256]{1,0:T(8,128)(2,1)}, f32[2048,256]{1,0:T(8,128)}) custom-call(s32[5]{0:T(128)} %pad_add_fusion.meta_ref, bf16[2048,256]{1,0:T(8,128)(2,1)} %get-tuple-element.110.q_ref, bf16[2048,256]{1,0:T(8,128)(2,1)} %get-tuple-element.111.k_ref, bf16[2048,256]{1,0:T(8,128)(2,1)} %get-tuple-element.112.v_ref, s32[8,2048]{1,0:T(8,128)} %broadcast_in_dim.185.kpos_ref), custom_call_target="tpu_custom_call" | custom-call | flops 8000000000 | bytes 4194304 | tf_op jit(solution)/shard_map/attend/pallas_call | solution.py:298
  124.4 8.9 %attend.3 = (bf16[2048,256]{1,0:T(8,128)(2,1)}, f32[2048,256]{1,0:T(8,128)}) custom-call(s32[5]{0:T(128)} %pad_add_fusion.meta_ref, bf16[2048,256]{1,0:T(8,128)(2,1)} %get-tuple-element.110.q_ref, bf16[2048,256]{1,0:T(8,128)(2,1)} %get-tuple-element.111.k_ref, ...), custom_call_target="tpu_custom_call", output_to_operand_aliasing={{0}: (5, {}), {1}: (6, {})} | custom-call | flops 8000000000 | bytes 4194304 | tf_op jit(solution)/shard_map/attend/pallas_call | solution.py:298
  136.0 2.6 collective-permute-done.12.a2.a3
  139.4 5.1 %attn_out.1 = (f32[512,1024]{1,0:T(8,128)}, bf16[512,1024]{1,0:T(8,128)(2,1)}) custom-call(bf16[2048,256]{1,0:T(8,128)(2,1)} %get-tuple-element.116.a0.o_ref, bf16[512,256]{1,0:T(8,128)(2,1)} %copy-done.16, bf16[1024,256]{1,0:T(8,128)(2,1)} %copy-done.13, bf16[1024,256]{1,0:T(8,128)(2,1)} %copy-done.13, bf16[512,1024]{1,0:T(8,128)(2,1)} %x_ref.7, ...), custom_call_target="tpu_custom_call" | custom-call | flops 1073741824 | bytes 10485760 | tf_op jit(solution)/shard_map/attn_out/pallas_call | solution.py:674
  145.8 2.6 collective-permute-start.17
  148.4 13.5 %ffn_forward.3 = (bf16[2,512,1024]{2,1,0:T(8,128)(2,1)}, bf16[2,512,1024]{2,1,0:T(8,128)(2,1)}, bf16[2,512,1024]{2,1,0:T(8,128)(2,1)}, bf16[2,512,1024]{2,1,0:T(8,128)(2,1)}, f32[512,1024]{1,0:T(8,128)}) custom-call(bf16[512,1024]{1,0:T(8,128)(2,1)} %get-tuple-element.117.h_ref.refs_0_, bf16[8,2,3,128,1024]{4,3,2,1,0:T(8,128)(2,1)} %bitcast.88, ...), custom_call_target="tpu_custom_call" | custom-call | flops 6442450944 | bytes 18874368 | tf_op jit(solution)/shard_map/ffn_forward/pallas_call | solution.py:546
  162.8 9.3 %ffn_forward.4 = (bf16[2,256,1024]{2,1,0:T(8,128)(2,1)}, bf16[2,256,1024]{2,1,0:T(8,128)(2,1)}, bf16[2,256,1024]{2,1,0:T(8,128)(2,1)}, bf16[2,256,1024]{2,1,0:T(8,128)(2,1)}, bf16[256,1024]{1,0:T(8,128)(2,1)}) custom-call(bf16[256,1024]{1,0:T(8,128)(2,1)} %copy-done.18, bf16[8,2,3,128,1024]{4,3,2,1,0:T(8,128)(2,1)} %bitcast.89, ...), custom_call_target="tpu_custom_call" | custom-call | flops 3221225472 | bytes 15728640 | tf_op jit(solution)/shard_map/ffn_forward/pallas_call | solution.py:546
  172.1 2.0 collective-permute-start.19
  175.0 9.6 %ffn_forward.5 = (bf16[2,256,1024]{2,1,0:T(8,128)(2,1)}, bf16[2,256,1024]{2,1,0:T(8,128)(2,1)}, bf16[2,256,1024]{2,1,0:T(8,128)(2,1)}, bf16[2,256,1024]{2,1,0:T(8,128)(2,1)}, bf16[256,1024]{1,0:T(8,128)(2,1)}) custom-call(bf16[256,1024]{1,0:T(8,128)(2,1)} %copy-done.19, bf16[8,2,3,128,1024]{4,3,2,1,0:T(8,128)(2,1)} %bitcast.90, ...), custom_call_target="tpu_custom_call" | custom-call | flops 3221225472 | bytes 15728640 | tf_op jit(solution)/shard_map/ffn_forward/pallas_call | solution.py:546
  184.8 1.7 collective-permute-done.19.far_ref
  187.3 4.5 turn.2
  191.7 2.3 collective-permute-start.20
  194.1 5.6 %collective-permute-done.18.far_ref = bf16[256,1024]{1,0:T(8,128)(2,1)S(1)} collective-permute-done((bf16[256,1024]{1,0:T(8,128)(2,1)}, bf16[256,1024]{1,0:T(8,128)(2,1)S(1)}, u32[]{:S(2)}, u32[]{:S(2)}) %collective-permute-start.18) | collective-permute-done | bytes 524320 | tf_op jit(solution)/shard_map/ppermute | solution.py:45
  200.5 4.5 turn.3
  205.3 14.3 %ffn_backward.3 = (bf16[2,512,1024]{2,1,0:T(8,128)(2,1)}, bf16[2,512,1024]{2,1,0:T(8,128)(2,1)}, f32[2,8,1024]{2,1,0:T(8,128)}, f32[2,8,1024]{2,1,0:T(8,128)}, f32[512,1024]{1,0:T(8,128)}) custom-call(bf16[256,1024]{1,0:T(8,128)(2,1)} %get-tuple-element.128.refs_0_.refs_3_, bf16[256,1024]{1,0:T(8,128)(2,1)} %get-tuple-element.129.refs_1_.refs_4_, ...), custom_call_target="tpu_custom_call" | custom-call | flops 6442450944 | bytes 25165824 | tf_op jit(solution)/shard_map/ffn_backward/pallas_call | solution.py:589
  220.4 10.2 %ffn_backward.4 = (bf16[2,256,1024]{2,1,0:T(8,128)(2,1)}, bf16[2,256,1024]{2,1,0:T(8,128)(2,1)}, f32[2,8,1024]{2,1,0:T(8,128)}, f32[2,8,1024]{2,1,0:T(8,128)}, bf16[256,1024]{1,0:T(8,128)(2,1)}) custom-call(bf16[256,1024]{1,0:T(8,128)(2,1)} %copy-done.20, bf16[8,2,3,128,1024]{4,3,2,1,0:T(8,128)(2,1)} %bitcast.92, ...), custom_call_target="tpu_custom_call" | custom-call | flops 3221225472 | bytes 18874368 | tf_op jit(solution)/shard_map/ffn_backward/pallas_call | solution.py:589
  230.6 1.8 collective-permute-start.22
  233.2 10.2 %ffn_backward.5 = (bf16[2,256,1024]{2,1,0:T(8,128)(2,1)}, bf16[2,256,1024]{2,1,0:T(8,128)(2,1)}, f32[2,8,1024]{2,1,0:T(8,128)}, f32[2,8,1024]{2,1,0:T(8,128)}, bf16[256,1024]{1,0:T(8,128)(2,1)}) custom-call(bf16[256,1024]{1,0:T(8,128)(2,1)} %copy-done.21, bf16[8,2,3,128,1024]{4,3,2,1,0:T(8,128)(2,1)} %bitcast.93, ...), custom_call_target="tpu_custom_call" | custom-call | flops 3221225472 | bytes 18874368 | tf_op jit(solution)/shard_map/ffn_backward/pallas_call | solution.py:589
  243.8 20.5 %weight_grads.1 = bf16[8,2,3,128,1024]{4,3,2,1,0:T(8,128)(2,1)} custom-call(bf16[512,1024]{1,0:T(8,128)(2,1)} %get-tuple-element.117.h_ref.refs_0_, bf16[256,1024]{1,0:T(8,128)(2,1)} %copy-done.18, bf16[256,1024]{1,0:T(8,128)(2,1)} %copy-done.19, bf16[256,1024]{1,0:T(8,128)(2,1)} %get-tuple-element.128.refs_0_.refs_3_, ...), custom_call_target="tpu_custom_call" | custom-call | flops 12884901888 | bytes 25165824 | tf_op jit(solution)/shard_map/weight_grads/pallas_call | solution.py:644
  265.9 8.6 %attn_back_out.1 = (bf16[512,1024]{1,0:T(8,128)(2,1)}, f32[512,1024]{1,0:T(8,128)}, bf16[512,256]{1,0:T(8,128)(2,1)}, bf16[512,256]{1,0:T(8,128)(2,1)}, bf16[512...) custom-call(f32[512,1024]{1,0:T(8,128)} %get-tuple-element.134.own_ref, ...), custom_call_target="tpu_custom_call" | custom-call | flops 1073741824 | bytes 10485760 | tf_op jit(solution)/shard_map/attn_back_out/pallas_call | solution.py:674
  275.7 1.8 collective-permute-start.25
  277.4 1.9 convolution_convert_fusion.2
  280.0 7.6 %collective-permute-done.25 = bf16[1024,256]{1,0:T(8,128)(2,1)S(1)} collective-permute-done((bf16[1024,256]{1,0:T(8,128)(2,1)S(1)}, bf16[1024,256]{1,0:T(8,128)(2,1)S(1)}, u32[]{:S(2)}, u32[]{:S(2)}) %collective-permute-start.25) | collective-permute-done | bytes 524320 | tf_op jit(solution)/shard_map/ppermute | solution.py:45
  291.3 2.0 pad_maximum_fusion.2.do_ref
  296.7 39.1 %attend_back.1 = (bf16[2048,768]{1,0:T(8,128)(2,1)}, f32[8,256]{1,0:T(8,128)}) custom-call(s32[5]{0:T(128)} %pad_add_fusion.meta_ref, bf16[2048,256]{1,0:T(8,128)(2,1)} %get-tuple-element.110.q_ref, f32[2048,256]{1,0:T(8,128)} %get-tuple-element.157.qr_ref, bf16[2048,256]{1,0:T(8,128)(2,1)} %get-tuple-element.116.a0.o_ref, ...), custom_call_target="tpu_custom_call" | custom-call | flops 40000000000 | bytes 6291456 | tf_op jit(solution)/shard_map/attend_back/pallas_call | solution.py:455
  335.8 4.1 fusion.4
  339.9 3.5 convolution_add_fusion
  345.4 1.6 fusion.9
  349.4 2.2 pad_maximum_fusion.3
  351.7 4.6 convolution_convert_fusion
  358.6 2.9 dynamic-slice_bitcast_fusion
  363.6 1.8 fusion.6
  365.5 3.5 fusion
  369.7 11.2 %all-to-all-start.1 = ((f32[32,1,352]{2,1,0:T(1,128)}), f32[32,1,352]{2,1,0:T(1,128)S(1)}, u32[]{:S(2)}, u32[]{:S(2)}) async-start(f32[32,1,352]{2,1,0:T(1,128)} %all_to_all.18), calls=%async_computation.2 | async-start | bytes 98304 | tf_op jit(solution)/shard_map/all_to_all | solution.py:127
  380.8 15.5 %collective-permute-done.30 = bf16[4,128,1024]{2,1,0:T(8,128)(2,1)S(1)} collective-permute-done((bf16[4,128,1024]{2,1,0:T(8,128)(2,1)}, bf16[4,128,1024]{2,1,0:T(8,128)(2,1)S(1)}, u32[]{:S(2)}, u32[]{:S(2)}) %collective-permute-start.30) | collective-permute-done | bytes 1048608 | tf_op jit(solution)/shard_map/ppermute | solution.py:45
  396.4 1.6 maximum_add_fusion
  401.2 10.9 %reduce-scatter.2.cloned.1.call-done = bf16[384,1024]{1,0:T(8,128)(2,1)} async-done(((bf16[6144,1024]{1,0:T(8,128)(2,1)}), bf16[384,1024]{1,0:T(8,128)(2,1)}) %reduce-scatter.2.cloned.1.call-update) | async-done | bytes 786448 | tf_op jit(solution)/shard_map/reduce_scatter | solution.py:895
  412.1 2.2 multiply_reduce_fusion
  414.3 2.3 fusion.14
  417.7 2.8 collective-permute-start.33
  422.7 5.2 %collective-permute-done.31 = bf16[128,1024]{1,0:T(8,128)(2,1)S(1)} collective-permute-done((bf16[128,1024]{1,0:T(8,128)(2,1)}, bf16[128,1024]{1,0:T(8,128)(2,1)S(1)}, u32[]{:S(2)}, u32[]{:S(2)}) %collective-permute-start.31) | collective-permute-done | bytes 262176 | tf_op jit(solution)/shard_map/ppermute | solution.py:49
  427.9 10.3 %collective-permute-done.32 = bf16[128,1024]{1,0:T(8,128)(2,1)} collective-permute-done((bf16[128,1024]{1,0:T(8,128)(2,1)}, bf16[128,1024]{1,0:T(8,128)(2,1)}, u32[]{:S(2)}, u32[]{:S(2)}) %collective-permute-start.32) | collective-permute-done | bytes 262176 | tf_op jit(solution)/shard_map/ppermute | solution.py:49
  438.2 2.0 multiply_reduce_fusion.1
  442.7 6.4 %all-to-all-start.2 = ((f32[32,1,128]{2,1,0:T(1,128)}), f32[32,1,128]{2,1,0:T(1,128)S(1)}, u32[]{:S(2)}, u32[]{:S(2)}) async-start(f32[32,1,128]{2,1,0:T(1,128)} %broadcast_in_dim.218), calls=%async_computation.3 | async-start | bytes 32768 | tf_op jit(solution)/shard_map/all_to_all | solution.py:127
  449.2 4.2 fusion.2
  (236 shorter events, 55.0 us)
Async XLA Ops:
  7.2 141.3 %all-gather.2.cloned.1.call-start = ((), (), s32[]{:S(2)}) async-start(), calls=%async_computation.4 | async-start | bytes 13369344 | tf_op jit(solution)/shard_map/all_gather | solution.py:801
  8.4 6.1 %copy-start.25 = (bf16[256,128]{1,0:T(8,128)(2,1)S(1)}, bf16[256,128]{1,0:T(8,128)(2,1)}, u32[]{:S(2)}) copy-start(bf16[256,128]{1,0:T(8,128)(2,1)} %param.23) | copy-start | bytes 196612
  10.4 4.5 copy-start.32
  10.5 7.3 %copy-start.37 = (f32[128]{0:T(128)S(1)}, f32[128]{0:T(128)}, u32[]{:S(2)}) copy-start(f32[128]{0:T(128)} %param.28) | copy-start | bytes 1540
  10.5 7.3 %copy-start.38 = (f32[128]{0:T(128)S(1)}, f32[128]{0:T(128)}, u32[]{:S(2)}) copy-start(f32[128]{0:T(128)} %param.29) | copy-start | bytes 1540
  10.5 7.3 %copy-start.39 = (f32[32]{0:T(128)S(1)}, f32[32]{0:T(128)}, u32[]{:S(2)}) copy-start(f32[32]{0:T(128)} %param.27) | copy-start | bytes 388
  10.5 7.3 %copy-start.40 = (f32[32]{0:T(128)S(1)}, f32[32]{0:T(128)}, u32[]{:S(2)}) copy-start(f32[32]{0:T(128)} %param.30) | copy-start | bytes 388
  10.5 7.3 %copy-start.41 = (f32[32]{0:T(128)S(1)}, f32[32]{0:T(128)}, u32[]{:S(2)}) copy-start(f32[32]{0:T(128)} %param.31) | copy-start | bytes 388
  11.6 13.5 %copy-start.36 = (s32[1,4]{1,0:T(1,128)S(1)}, s32[1,4]{1,0:T(1,128)}, u32[]{:S(2)}) copy-start(s32[1,4]{1,0:T(1,128)} %param.18) | copy-start | bytes 52
  11.6 20.3 %collective-permute-start = (bf16[256,1024]{1,0:T(8,128)(2,1)}, bf16[256,1024]{1,0:T(8,128)(2,1)}, u32[]{:S(2)}, u32[]{:S(2)}) collective-permute-start(bf16[256,1024]{1,0:T(8,128)(2,1)} %get-tuple-element.276), channel_id=1, source_target_pairs={{0,2},{1,3},{2,0},{3,1},{4,6},{5,7},{6,4},{7,5},{8,10},{9,11},{10,... | collective-permute-start | bytes 1572872 | tf_op jit(solution)/shard_map/ppermute | solution.py:45
  15.7 30.2 %collective-permute-start.3 = (bf16[128,1024]{1,0:T(8,128)(2,1)}, bf16[128,1024]{1,0:T(8,128)(2,1)S(1)}, u32[]{:S(2)}, u32[]{:S(2)}) collective-permute-start(bf16[128,1024]{1,0:T(8,128)(2,1)} %get-tuple-element.287), channel_id=1, source_target_pairs={{0,8},{8,16},{16,24},{24,28},{28,20},{20,12},{12,4},{4,0},{1,9},{9... | collective-permute-start | bytes 786440 | tf_op jit(solution)/shard_map/ppermute | solution.py:55
  17.3 28.6 %collective-permute-start.4 = (bf16[128,1024]{1,0:T(8,128)(2,1)}, bf16[128,1024]{1,0:T(8,128)(2,1)}, u32[]{:S(2)}, u32[]{:S(2)}) collective-permute-start(bf16[128,1024]{1,0:T(8,128)(2,1)} %get-tuple-element.287), channel_id=1, source_target_pairs={{0,4},{8,0},{16,8},{24,16},{28,24},{20,28},{12,20},{4,12},{1,5},{9... | collective-permute-start | bytes 786440 | tf_op jit(solution)/shard_map/ppermute | solution.py:55
  17.7 20.7 %collective-permute-start.1 = (bf16[256,1024]{1,0:T(8,128)(2,1)}, bf16[256,1024]{1,0:T(8,128)(2,1)}, u32[]{:S(2)}, u32[]{:S(2)}) collective-permute-start(bf16[256,1024]{1,0:T(8,128)(2,1)} %get-tuple-element.275), channel_id=1, source_target_pairs={{0,2},{1,3},{2,0},{3,1},{4,6},{5,7},{6,4},{7,5},{8,10},{9,11},{10,... | collective-permute-start | bytes 1572872 | tf_op jit(solution)/shard_map/ppermute | solution.py:45
  18.6 30.0 %all-to-all-start = ((f32[32,1,352]{2,1,0:T(1,128)}), f32[32,1,352]{2,1,0:T(1,128)S(1)}, u32[]{:S(2)}, u32[]{:S(2)}) async-start(f32[32,1,352]{2,1,0:T(1,128)} %broadcast_in_dim.181), calls=%async_computation | async-start | bytes 98304 | tf_op jit(solution)/shard_map/all_to_all | solution.py:127
  24.9 387.2 %reduce-scatter.2.cloned.1.call-start = ((), (), s32[]{:S(2)}) async-start(), calls=%async_computation.5 | async-start | bytes 13369344 | tf_op jit(solution)/shard_map/reduce_scatter | solution.py:895
  31.9 14.0 %copy-start.35 = (s32[1,2048]{1,0:T(1,128)S(1)}, s32[1,2048]{1,0:T(1,128)}, u32[]{:S(2)}) copy-start(s32[1,2048]{1,0:T(1,128)} %param.19) | copy-start | bytes 24580
  40.3 61.0 %collective-permute-start.2 = (bf16[1024,1024]{1,0:T(8,128)(2,1)}, bf16[1024,1024]{1,0:T(8,128)(2,1)}, u32[]{:S(2)}, u32[]{:S(2)}) collective-permute-start(bf16[1024,1024]{1,0:T(8,128)(2,1)} %constant_dynamic-update-slice_fusion.x_ref), channel_id=1, source_target_pairs={{0,1},{1,0},{2,3},{3,2},{4,5},{5,4},{6,7},{7,6},{8,9},{9,8},{10,11... | collective-permute-start | bytes 6291464 | tf_op jit(solution)/shard_map/ppermute | solution.py:45
  45.9 8.8 %collective-permute-start.5 = (bf16[128,1024]{1,0:T(8,128)(2,1)S(1)}, bf16[128,1024]{1,0:T(8,128)(2,1)S(1)}, u32[]{:S(2)}, u32[]{:S(2)}) collective-permute-start(bf16[128,1024]{1,0:T(8,128)(2,1)S(1)} %collective-permute-done.3), channel_id=1, source_target_pairs={{0,8},{8,16},{16,24},{24,28},{28,20},{20,12},{12,4},{4,0},{1,9},{9... | collective-permute-start | bytes 786440 | tf_op jit(solution)/shard_map/ppermute | solution.py:55
  47.8 9.4 %collective-permute-start.6 = (bf16[128,1024]{1,0:T(8,128)(2,1)}, bf16[128,1024]{1,0:T(8,128)(2,1)S(1)}, u32[]{:S(2)}, u32[]{:S(2)}) collective-permute-start(bf16[128,1024]{1,0:T(8,128)(2,1)} %collective-permute-done.4), channel_id=1, source_target_pairs={{0,4},{8,0},{16,8},{24,16},{28,24},{20,28},{12,20},{4,12},{1,5},{9... | collective-permute-start | bytes 786440 | tf_op jit(solution)/shard_map/ppermute | solution.py:55
  57.2 13.9 %collective-permute-start.7 = (bf16[128,1024]{1,0:T(8,128)(2,1)S(1)}, bf16[128,1024]{1,0:T(8,128)(2,1)S(1)}, u32[]{:S(2)}, u32[]{:S(2)}) collective-permute-start(bf16[128,1024]{1,0:T(8,128)(2,1)S(1)} %collective-permute-done.5), channel_id=1, source_target_pairs={{0,8},{8,16},{16,24},{24,28},{28,20},{20,12},{12,4},{4,0},{1,9},{9... | collective-permute-start | bytes 786440 | tf_op jit(solution)/shard_map/ppermute | solution.py:55
  58.9 19.3 %collective-permute-start.8 = (bf16[128,1024]{1,0:T(8,128)(2,1)S(1)}, bf16[128,1024]{1,0:T(8,128)(2,1)S(1)}, u32[]{:S(2)}, u32[]{:S(2)}) collective-permute-start(bf16[128,1024]{1,0:T(8,128)(2,1)S(1)} %collective-permute-done.6), channel_id=1, source_target_pairs={{0,4},{8,0},{16,8},{24,16},{28,24},{20,28},{12,20},{4,12},{1,5},{9... | collective-permute-start | bytes 786440 | tf_op jit(solution)/shard_map/ppermute | solution.py:55
  78.2 14.4 %collective-permute-start.9 = (bf16[128,1024]{1,0:T(8,128)(2,1)S(1)}, bf16[128,1024]{1,0:T(8,128)(2,1)S(1)}, u32[]{:S(2)}, u32[]{:S(2)}) collective-permute-start(bf16[128,1024]{1,0:T(8,128)(2,1)S(1)} %collective-permute-done.7), channel_id=1, source_target_pairs={{0,8},{8,16},{16,24},{24,28},{28,20},{20,12},{12,4},{4,0},{1,9},{9... | collective-permute-start | bytes 786440 | tf_op jit(solution)/shard_map/ppermute | solution.py:55
  92.7 29.4 %copy-start.5 = (bf16[1024,256]{1,0:T(8,128)(2,1)}, bf16[1024,256]{1,0:T(8,128)(2,1)S(1)}, u32[]{:S(2)}) copy-start(bf16[1024,256]{1,0:T(8,128)(2,1)S(1)} %slice.206.w0) | copy-start | bytes 1572868
  92.7 29.9 %collective-permute-start.14 = (bf16[1024,256]{1,0:T(8,128)(2,1)S(1)}, bf16[1024,256]{1,0:T(8,128)(2,1)S(1)}, u32[]{:S(2)}, u32[]{:S(2)}) collective-permute-start(bf16[1024,256]{1,0:T(8,128)(2,1)S(1)} %slice.206.w0), channel_id=1, source_target_pairs={{0,2},{1,3},{2,0},{3,1},{4,6},{5,7},{6,4},{7,5},{8,10},{9,11},{10,... | collective-permute-start | bytes 1572872 | tf_op jit(solution)/shard_map/ppermute | solution.py:45
  122.0 1.6 collective-permute-start.10
  122.1 13.9 %collective-permute-start.13 = (bf16[1024,256]{1,0:T(8,128)(2,1)S(1)}, bf16[1024,256]{1,0:T(8,128)(2,1)S(1)}, u32[]{:S(2)}, u32[]{:S(2)}) collective-permute-start(bf16[1024,256]{1,0:T(8,128)(2,1)S(1)} %slice.206.w0), channel_id=1, source_target_pairs={{0,1},{1,0},{2,3},{3,2},{4,5},{5,4},{6,7},{7,6},{8,9},{9,8},{10,11... | collective-permute-start | bytes 1572872 | tf_op jit(solution)/shard_map/ppermute | solution.py:45
  122.6 10.8 %copy-start.10 = (bf16[1024,256]{1,0:T(8,128)(2,1)}, bf16[1024,256]{1,0:T(8,128)(2,1)S(1)}, u32[]{:S(2)}) copy-start(bf16[1024,256]{1,0:T(8,128)(2,1)S(1)} %collective-permute-done.14.w2) | copy-start | bytes 1572868
  122.6 13.4 %collective-permute-start.15 = (bf16[1024,256]{1,0:T(8,128)(2,1)S(1)}, bf16[1024,256]{1,0:T(8,128)(2,1)S(1)}, u32[]{:S(2)}, u32[]{:S(2)}) collective-permute-start(bf16[1024,256]{1,0:T(8,128)(2,1)S(1)} %collective-permute-done.14.w2), channel_id=1, source_target_pairs={{0,1},{1,0},{2,3},{3,2},{4,5},{5,4},{6,7},{7,6},{8,9},{9,8},{10,11... | collective-permute-start | bytes 1572872 | tf_op jit(solution)/shard_map/ppermute | solution.py:45
  124.4 14.2 %collective-permute-start.12 = (bf16[1024,256]{1,0:T(8,128)(2,1)}, bf16[1024,256]{1,0:T(8,128)(2,1)S(1)}, u32[]{:S(2)}, u32[]{:S(2)}) collective-permute-start(bf16[1024,256]{1,0:T(8,128)(2,1)} %pad_maximum_fusion.5), channel_id=1, source_target_pairs={{0,2},{1,3},{2,0},{3,1},{4,6},{5,7},{6,4},{7,5},{8,10},{9,11},{10,... | collective-permute-start | bytes 1572872 | tf_op jit(solution)/shard_map/ppermute | solution.py:45
  134.3 1.7 collective-permute-start.11
  145.8 16.2 %collective-permute-start.17 = (bf16[256,1024]{1,0:T(8,128)(2,1)S(1)}, bf16[256,1024]{1,0:T(8,128)(2,1)S(1)}, u32[]{:S(2)}, u32[]{:S(2)}) collective-permute-start(bf16[256,1024]{1,0:T(8,128)(2,1)S(1)} %get-tuple-element.271), channel_id=1, source_target_pairs={{0,2},{1,3},{2,0},{3,1},{4,6},{5,7},{6,4},{7,5},{8,10},{9,11},{10,... | collective-permute-start | bytes 1572872 | tf_op jit(solution)/shard_map/ppermute | solution.py:45
  148.4 25.8 %collective-permute-start.16 = (bf16[256,1024]{1,0:T(8,128)(2,1)S(1)}, bf16[256,1024]{1,0:T(8,128)(2,1)S(1)}, u32[]{:S(2)}, u32[]{:S(2)}) collective-permute-start(bf16[256,1024]{1,0:T(8,128)(2,1)S(1)} %get-tuple-element.272), channel_id=1, source_target_pairs={{0,2},{1,3},{2,0},{3,1},{4,6},{5,7},{6,4},{7,5},{8,10},{9,11},{10,... | collective-permute-start | bytes 1572872 | tf_op jit(solution)/shard_map/ppermute | solution.py:45
  172.1 14.3 %collective-permute-start.19 = (bf16[256,1024]{1,0:T(8,128)(2,1)}, bf16[256,1024]{1,0:T(8,128)(2,1)S(1)}, u32[]{:S(2)}, u32[]{:S(2)}) collective-permute-start(bf16[256,1024]{1,0:T(8,128)(2,1)} %get-tuple-element.120), channel_id=1, source_target_pairs={{0,2},{1,3},{2,0},{3,1},{4,6},{5,7},{6,4},{7,5},{8,10},{9,11},{10,... | collective-permute-start | bytes 1572872 | tf_op jit(solution)/shard_map/ppermute | solution.py:45
  184.6 15.1 %collective-permute-start.18 = (bf16[256,1024]{1,0:T(8,128)(2,1)}, bf16[256,1024]{1,0:T(8,128)(2,1)S(1)}, u32[]{:S(2)}, u32[]{:S(2)}) collective-permute-start(bf16[256,1024]{1,0:T(8,128)(2,1)} %get-tuple-element.122), channel_id=1, source_target_pairs={{0,2},{1,3},{2,0},{3,1},{4,6},{5,7},{6,4},{7,5},{8,10},{9,11},{10,... | collective-permute-start | bytes 1572872 | tf_op jit(solution)/shard_map/ppermute | solution.py:45
  191.7 27.9 %collective-permute-start.20 = (bf16[256,1024]{1,0:T(8,128)(2,1)}, bf16[256,1024]{1,0:T(8,128)(2,1)S(1)}, u32[]{:S(2)}, u32[]{:S(2)}) collective-permute-start(bf16[256,1024]{1,0:T(8,128)(2,1)} %get-tuple-element.128.refs_0_.refs_3_), channel_id=1, source_target_pairs={{0,2},{1,3},{2,0},{3,1},{4,6},{5,7},{6,4},{7,5},{8,10},{9,11},{10,... | collective-permute-start | bytes 1572872 | tf_op jit(solution)/shard_map/ppermute | solution.py:45
  205.0 27.4 %collective-permute-start.21 = (bf16[256,1024]{1,0:T(8,128)(2,1)}, bf16[256,1024]{1,0:T(8,128)(2,1)S(1)}, u32[]{:S(2)}, u32[]{:S(2)}) collective-permute-start(bf16[256,1024]{1,0:T(8,128)(2,1)} %get-tuple-element.129.refs_1_.refs_4_), channel_id=1, source_target_pairs={{0,2},{1,3},{2,0},{3,1},{4,6},{5,7},{6,4},{7,5},{8,10},{9,11},{10,... | collective-permute-start | bytes 1572872 | tf_op jit(solution)/shard_map/ppermute | solution.py:45
  230.6 33.6 %collective-permute-start.22 = (bf16[256,1024]{1,0:T(8,128)(2,1)}, bf16[256,1024]{1,0:T(8,128)(2,1)S(1)}, u32[]{:S(2)}, u32[]{:S(2)}) collective-permute-start(bf16[256,1024]{1,0:T(8,128)(2,1)} %get-tuple-element.142), channel_id=1, source_target_pairs={{0,2},{1,3},{2,0},{3,1},{4,6},{5,7},{6,4},{7,5},{8,10},{9,11},{10,... | collective-permute-start | bytes 1572872 | tf_op jit(solution)/shard_map/ppermute | solution.py:45
  243.4 20.9 %collective-permute-start.23 = (bf16[256,1024]{1,0:T(8,128)(2,1)}, bf16[256,1024]{1,0:T(8,128)(2,1)S(1)}, u32[]{:S(2)}, u32[]{:S(2)}) collective-permute-start(bf16[256,1024]{1,0:T(8,128)(2,1)} %get-tuple-element.152), channel_id=1, source_target_pairs={{0,2},{1,3},{2,0},{3,1},{4,6},{5,7},{6,4},{7,5},{8,10},{9,11},{10,... | collective-permute-start | bytes 1572872 | tf_op jit(solution)/shard_map/ppermute | solution.py:45
  265.9 11.5 %copy-start.17 = (bf16[512,256]{1,0:T(8,128)(2,1)S(1)}, bf16[512,256]{1,0:T(8,128)(2,1)}, u32[]{:S(2)}) copy-start(bf16[512,256]{1,0:T(8,128)(2,1)} %copy-done.16) | copy-start | bytes 786436
  274.5 4.8 %copy-start.6 = (bf16[512,1024]{1,0:T(8,128)(2,1)S(1)}, bf16[512,1024]{1,0:T(8,128)(2,1)}, u32[]{:S(2)}) copy-start(bf16[512,1024]{1,0:T(8,128)(2,1)} %get-tuple-element.159) | copy-start | bytes 3145732
  274.5 4.8 %copy-start.14 = (bf16[1024,256]{1,0:T(8,128)(2,1)S(1)}, bf16[1024,256]{1,0:T(8,128)(2,1)}, u32[]{:S(2)}) copy-start(bf16[1024,256]{1,0:T(8,128)(2,1)} %copy-done.13) | copy-start | bytes 1572868
  275.7 11.9 %collective-permute-start.25 = (bf16[1024,256]{1,0:T(8,128)(2,1)S(1)}, bf16[1024,256]{1,0:T(8,128)(2,1)S(1)}, u32[]{:S(2)}, u32[]{:S(2)}) collective-permute-start(bf16[1024,256]{1,0:T(8,128)(2,1)S(1)} %pad_maximum_fusion.6), channel_id=1, source_target_pairs={{0,2},{1,3},{2,0},{3,1},{4,6},{5,7},{6,4},{7,5},{8,10},{9,11},{10,... | collective-permute-start | bytes 1572872 | tf_op jit(solution)/shard_map/ppermute | solution.py:45
  279.3 8.3 %copy-start.24 = (bf16[512,256]{1,0:T(8,128)(2,1)S(1)}, bf16[512,256]{1,0:T(8,128)(2,1)}, u32[]{:S(2)}) copy-start(bf16[512,256]{1,0:T(8,128)(2,1)} %get-tuple-element.162) | copy-start | bytes 786436
  279.9 13.5 %collective-permute-start.24 = (bf16[1024,512]{0,1:T(8,128)(2,1)S(1)}, bf16[1024,512]{0,1:T(8,128)(2,1)}, u32[]{:S(2)}, u32[]{:S(2)}) collective-permute-start(bf16[1024,512]{0,1:T(8,128)(2,1)S(1)} %pad_maximum_fusion.1), channel_id=1, source_target_pairs={{0,1},{1,0},{2,3},{3,2},{4,5},{5,4},{6,7},{7,6},{8,9},{9,8},{10,11... | collective-permute-start | bytes 3145736 | tf_op jit(solution)/shard_map/ppermute | solution.py:45
  288.4 2.9 collective-permute-start.26
  294.9 49.6 %collective-permute-start.27 = (bf16[1024,256]{0,1:T(8,128)(2,1)S(1)}, bf16[1024,256]{0,1:T(8,128)(2,1)S(1)}, u32[]{:S(2)}, u32[]{:S(2)}) collective-permute-start(bf16[1024,256]{0,1:T(8,128)(2,1)S(1)} %fusion.10), channel_id=1, source_target_pairs={{0,2},{1,3},{2,0},{3,1},{4,6},{5,7},{6,4},{7,5},{8,10},{9,11},{10,... | collective-permute-start | bytes 1572872 | tf_op jit(solution)/shard_map/ppermute | solution.py:45
  347.0 4.6 copy-start.2
  351.6 4.9 %copy-start.27 = (f32[2,8,1024]{2,1,0:T(8,128)S(1)}, f32[2,8,1024]{2,1,0:T(8,128)}, u32[]{:S(2)}) copy-start(f32[2,8,1024]{2,1,0:T(8,128)} %get-tuple-element.172) | copy-start | bytes 196612
  351.6 4.9 %copy-start.29 = (f32[2,8,1024]{2,1,0:T(8,128)S(1)}, f32[2,8,1024]{2,1,0:T(8,128)}, u32[]{:S(2)}) copy-start(f32[2,8,1024]{2,1,0:T(8,128)} %get-tuple-element.173) | copy-start | bytes 196612
  351.6 4.9 %copy-start.31 = (f32[2,8,1024]{2,1,0:T(8,128)S(1)}, f32[2,8,1024]{2,1,0:T(8,128)}, u32[]{:S(2)}) copy-start(f32[2,8,1024]{2,1,0:T(8,128)} %get-tuple-element.174) | copy-start | bytes 196612
  351.6 5.0 %copy-start.26 = (f32[2,8,1024]{2,1,0:T(8,128)S(1)}, f32[2,8,1024]{2,1,0:T(8,128)}, u32[]{:S(2)}) copy-start(f32[2,8,1024]{2,1,0:T(8,128)} %get-tuple-element.175) | copy-start | bytes 196612
  351.6 5.0 %copy-start.28 = (f32[2,8,1024]{2,1,0:T(8,128)S(1)}, f32[2,8,1024]{2,1,0:T(8,128)}, u32[]{:S(2)}) copy-start(f32[2,8,1024]{2,1,0:T(8,128)} %get-tuple-element.176) | copy-start | bytes 196612
  351.6 5.0 %copy-start.30 = (f32[2,8,1024]{2,1,0:T(8,128)S(1)}, f32[2,8,1024]{2,1,0:T(8,128)}, u32[]{:S(2)}) copy-start(f32[2,8,1024]{2,1,0:T(8,128)} %get-tuple-element.177) | copy-start | bytes 196612
  356.3 9.2 %collective-permute-start.28 = (bf16[1024,1024]{1,0:T(8,128)(2,1)}, bf16[1024,1024]{1,0:T(8,128)(2,1)}, u32[]{:S(2)}, u32[]{:S(2)}) collective-permute-start(bf16[1024,1024]{1,0:T(8,128)(2,1)} %convolution_convert_fusion), channel_id=1, source_target_pairs={{0,1},{1,0},{2,3},{3,2},{4,5},{5,4},{6,7},{7,6},{8,9},{9,8},{10,11... | collective-permute-start | bytes 6291464 | tf_op jit(solution)/shard_map/ppermute | solution.py:45
  358.5 37.8 %collective-permute-start.30 = (bf16[4,128,1024]{2,1,0:T(8,128)(2,1)}, bf16[4,128,1024]{2,1,0:T(8,128)(2,1)S(1)}, u32[]{:S(2)}, u32[]{:S(2)}) collective-permute-start(bf16[4,128,1024]{2,1,0:T(8,128)(2,1)} %pad_maximum_fusion.3), channel_id=1, source_target_pairs={{0,4},{4,0},{8,12},{12,8},{16,20},{20,16},{24,28},{28,24},{1,5},{5... | collective-permute-start | bytes 3145736 | tf_op jit(solution)/shard_map/ppermute | solution.py:45
  365.5 30.9 %copy-start.4 = (f32[4,128,768]{2,1,0:T(8,128)S(1)}, f32[4,128,768]{2,1,0:T(8,128)}, u32[]{:S(2)}) copy-start(f32[4,128,768]{2,1,0:T(8,128)} %dynamic-slice_bitcast_fusion) | copy-start | bytes 4718596
  369.7 29.7 %all-to-all-start.1 = ((f32[32,1,352]{2,1,0:T(1,128)}), f32[32,1,352]{2,1,0:T(1,128)S(1)}, u32[]{:S(2)}, u32[]{:S(2)}) async-start(f32[32,1,352]{2,1,0:T(1,128)} %all_to_all.18), calls=%async_computation.2 | async-start | bytes 98304 | tf_op jit(solution)/shard_map/all_to_all | solution.py:127
  398.0 44.1 %collective-permute-start.29 = (bf16[512,1024]{1,0:T(8,128)(2,1)}, bf16[512,1024]{1,0:T(8,128)(2,1)}, u32[]{:S(2)}, u32[]{:S(2)}) collective-permute-start(bf16[512,1024]{1,0:T(8,128)(2,1)} %fusion), channel_id=1, source_target_pairs={{0,2},{1,3},{2,0},{3,1},{4,6},{5,7},{6,4},{7,5},{8,10},{9,11},{10,... | collective-permute-start | bytes 3145736 | tf_op jit(solution)/shard_map/ppermute | solution.py:45
  412.1 8.3 %copy-start.3 = (bf16[384,1024]{1,0:T(8,128)(2,1)S(1)}, bf16[384,1024]{1,0:T(8,128)(2,1)}, u32[]{:S(2)}) copy-start(bf16[384,1024]{1,0:T(8,128)(2,1)} %reduce-scatter.2.cloned.1.call-done) | copy-start | bytes 2359300
  416.6 11.3 %collective-permute-start.31 = (bf16[128,1024]{1,0:T(8,128)(2,1)}, bf16[128,1024]{1,0:T(8,128)(2,1)S(1)}, u32[]{:S(2)}, u32[]{:S(2)}) collective-permute-start(bf16[128,1024]{1,0:T(8,128)(2,1)} %get-tuple-element.268), channel_id=1, source_target_pairs={{0,8},{4,12},{8,16},{12,20},{16,24},{20,28},{24,0},{28,4},{1,9},{5... | collective-permute-start | bytes 786440 | tf_op jit(solution)/shard_map/ppermute | solution.py:49
  416.6 21.6 %collective-permute-start.32 = (bf16[128,1024]{1,0:T(8,128)(2,1)}, bf16[128,1024]{1,0:T(8,128)(2,1)}, u32[]{:S(2)}, u32[]{:S(2)}) collective-permute-start(bf16[128,1024]{1,0:T(8,128)(2,1)} %get-tuple-element.270), channel_id=1, source_target_pairs={{0,16},{4,20},{8,24},{12,28},{16,0},{20,4},{24,8},{28,12},{1,17},{... | collective-permute-start | bytes 786440 | tf_op jit(solution)/shard_map/ppermute | solution.py:49
  417.7 20.6 %collective-permute-start.33 = (bf16[128,1024]{1,0:T(8,128)(2,1)S(1)}, bf16[128,1024]{1,0:T(8,128)(2,1)}, u32[]{:S(2)}, u32[]{:S(2)}) collective-permute-start(bf16[128,1024]{1,0:T(8,128)(2,1)S(1)} %get-tuple-element.269), channel_id=1, source_target_pairs={{0,24},{4,28},{8,0},{12,4},{16,8},{20,12},{24,16},{28,20},{1,25},{... | collective-permute-start | bytes 786440 | tf_op jit(solution)/shard_map/ppermute | solution.py:49
  421.6 27.5 %copy-start.9 = (f32[512,1024]{1,0:T(8,128)S(1)}, f32[512,1024]{1,0:T(8,128)}, u32[]{:S(2)}) copy-start(f32[512,1024]{1,0:T(8,128)} %get-tuple-element.156) | copy-start | bytes 6291460
  442.7 13.6 %all-to-all-start.2 = ((f32[32,1,128]{2,1,0:T(1,128)}), f32[32,1,128]{2,1,0:T(1,128)S(1)}, u32[]{:S(2)}, u32[]{:S(2)}) async-start(f32[32,1,128]{2,1,0:T(1,128)} %broadcast_in_dim.218), calls=%async_computation.3 | async-start | bytes 32768 | tf_op jit(solution)/shard_map/all_to_all | solution.py:127
  (19 other events, 42.5 us)
Sparse Core Ops, SparseCore 0:
  10.9 111.8 all-gather.1
  264.4 147.6 reduce-scatter.1

commit v4 on v3

--- a/solution.py
+++ b/solution.py
@@ -63,7 +63,8 @@
 
 def gather(shard, before):
     if lax.axis_size("dp") != 8:
-        return lax.all_gather(shard, "dp", axis=0, tiled=True)
+        full = lax.all_gather(shard, "dp", axis=0, tiled=True)
+        return full, full
     d = lax.axis_index("dp")
     rows, width = shard.shape
     place = jnp.where((d & 1) == 0, d >> 1, 7 - (d >> 1))
@@ -83,7 +84,9 @@
         if step < 4:
             behind = around(behind, -1)
             full = put(full, behind, step)
-    return full
+        if step == 3:
+            third = behind
+    return full, third
 
 
 def chip_groups():
@@ -108,14 +111,14 @@
     return rows(y, F32) + swap(sent, "dp", 1).astype(F32), sent
 
 
-def scatter_z(half):
+def scatter_z(half, *before_sum):
     if lax.axis_size("dp") != 8:
         return lax.psum_scatter(half.astype(F32), "dp", scatter_dimension=0, tiled=True)
     z = lax.axis_index("dp") >> 1
     total = lax.dynamic_index_in_dim(half, z, axis=0, keepdims=False)
     for step in (1, 2, 3):
         part = lax.dynamic_index_in_dim(half, (z + step) & 3, axis=0, keepdims=False)
-        total = total + to_z(part.astype(BF16), step).astype(F32)
+        total = total + after(to_z(part.astype(BF16), step), *before_sum).astype(F32)
     return total
 
 
@@ -188,7 +191,7 @@
                 pl.BlockSpec((x_rows.shape[1], 3 * width), lambda i, m: (0, 0)),
                 table,
                 table,
-                pl.BlockSpec((8, width), lambda i, m: (0, 0)),
+                pl.BlockSpec((1, width), lambda i, m: (0, 0)),
             ]
             + [any_spec] * len(extra),
             out_specs=[out] * 5,
@@ -229,6 +232,18 @@
     return pl.ds(pl.multiple_of(block * BLOCK, BLOCK), BLOCK)
 
 
+def by_pairs(low, high, visit):
+    def pair(i, carry):
+        visit(low + 2 * i, low + 2 * i + 1)
+        return carry
+
+    lax.fori_loop(0, (high - low) >> 1, pair, 0)
+
+    @pl.when(((high - low) & 1) == 1)
+    def _():
+        visit(high - 1)
+
+
 def split_heads(source_ref, split_ref):
     def one(block, carry):
         split_ref[block] = stack_heads(source_ref[block_at(block), :])
@@ -257,23 +272,27 @@
     acc_ref[...] = jnp.zeros_like(acc_ref)
     sum_ref[...] = jnp.zeros_like(sum_ref)
 
-    def visit(block, allowed):
-        keys = k_ref[block_at(block), :]
-        bias = jnp.where(allowed, 0.0, NEG)
+    def visit(blocks, allowed):
         expos = []
+        sums = [0.0] * heads
+        for block, mask in zip(blocks, allowed):
+            keys = k_ref[block_at(block), :]
+            bias = jnp.where(mask, 0.0, NEG)
+            for h in range(heads):
+                expo = jnp.exp(dot(queries[h], keys, 1, 1) + bias)
+                sums[h] = sums[h] + expo[:, :128] + expo[:, 128:]
+                expos.append(expo.astype(BF16))
         for h in range(heads):
-            expo = jnp.exp(dot(queries[h], keys, 1, 1) + bias)
-            sum_ref[h * BLOCK : (h + 1) * BLOCK, :] += expo[:, :128] + expo[:, 128:]
-            expos.append(expo.astype(BF16))
-        acc_ref[...] += dot(jnp.concatenate(expos, axis=1), vs_ref[block])
-
-    def off_diagonal(block, carry):
-        visit(block, kpos_ref[0:1, block_at(block)] >= starts)
-        return carry
-
-    lax.fori_loop(low, step, off_diagonal, 0)
+            sum_ref[h * BLOCK : (h + 1) * BLOCK, :] += sums[h]
+        vals = jnp.concatenate([vs_ref[block] for block in blocks], axis=0)
+        acc_ref[...] += dot(jnp.concatenate(expos, axis=1), vals)
+
+    def off_diagonal(*blocks):
+        visit(blocks, [kpos_ref[0:1, block_at(block)] >= starts for block in blocks])
+
+    by_pairs(low, step, off_diagonal)
     cols = lax.broadcasted_iota(jnp.int32, (BLOCK, BLOCK), 1) + base
-    visit(step, ((kpos_ref[0:1, block_at(step)] >= starts) & (cols <= rows)) | (cols == rows))
+    visit([step], [((kpos_ref[0:1, block_at(step)] >= starts) & (cols <= rows)) | (cols == rows)])
     lane = lax.broadcasted_iota(jnp.int32, (BLOCK, q_ref.shape[1]), 1) // HEAD
     inverse = jnp.zeros((BLOCK, q_ref.shape[1]), F32)
     for h in range(heads):
@@ -304,7 +323,7 @@
         grid_spec=pltpu.PrefetchScalarGridSpec(
             num_scalar_prefetch=1,
             grid=(2 * per,),
-            in_specs=[block, whole, whole, pl.BlockSpec((8, total), lambda i, m: (0, 0))]
+            in_specs=[block, whole, whole, pl.BlockSpec((1, total), lambda i, m: (0, 0))]
             + [pl.BlockSpec(memory_space=pl.ANY)] * len(extra),
             out_specs=[out, block],
             scratch_shapes=[
@@ -386,9 +405,9 @@
     cols = lax.broadcasted_iota(jnp.int32, (BLOCK, BLOCK), 1) + base
     starts = doc_start(meta_ref, docs, cols)
 
-    def visit(block, allowed):
-        at = block_at(block)
-        keys, vals = k_ref[at, :], v_ref[at, :]
+    def visit(block, count, allowed):
+        rows_at = pl.ds(pl.multiple_of(block * BLOCK, BLOCK), count * BLOCK)
+        keys, vals = k_ref[rows_at, :], v_ref[rows_at, :]
         bias = jnp.where(allowed, 0.0, NEG)
         expos, slopes = [], []
         for h in range(heads):
@@ -396,20 +415,21 @@
             expos.append(expo.astype(BF16))
             slope = expo * (dot(vals, ups[h], 1, 1) - delta[h : h + 1, :])
             slopes.append(slope.astype(BF16))
-        dv_ref[at, :] += dot(jnp.concatenate(expos, axis=1), all_ups)
-        dk_ref[at, :] += dot(jnp.concatenate(slopes, axis=1), all_queries)
-        dq_ref[...] += dot(jnp.concatenate(slopes, axis=0), ks_ref[block], 0, 0)
-
-    def key_slots(block):
-        return wide(kpos_ref[block_at(block), :])
-
-    def off_diagonal(block, carry):
-        visit(block, key_slots(block) >= starts)
-        return carry
-
-    lax.fori_loop(low, step, off_diagonal, 0)
+        dv_ref[rows_at, :] += dot(jnp.concatenate(expos, axis=1), all_ups)
+        dk_ref[rows_at, :] += dot(jnp.concatenate(slopes, axis=1), all_queries)
+        pieces = [slope[i * BLOCK : (i + 1) * BLOCK] for i in range(count) for slope in slopes]
+        split = jnp.concatenate([ks_ref[block + i] for i in range(count)], axis=0)
+        dq_ref[...] += dot(jnp.concatenate(pieces, axis=0), split, 0, 0)
+
+    def off_diagonal(*blocks):
+        keys_at = pl.ds(pl.multiple_of(blocks[0] * BLOCK, BLOCK), len(blocks) * BLOCK)
+        again = jnp.concatenate([starts] * len(blocks), axis=0)
+        visit(blocks[0], len(blocks), wide(kpos_ref[keys_at, :]) >= again)
+
+    by_pairs(low, step, off_diagonal)
     rows = lax.broadcasted_iota(jnp.int32, (BLOCK, BLOCK), 0) + base
-    visit(step, ((key_slots(step) >= starts) & (rows <= cols)) | (rows == cols))
+    key_slots = wide(kpos_ref[block_at(step), :])
+    visit(step, 1, ((key_slots >= starts) & (rows <= cols)) | (rows == cols))
 
     scale = sqk_ref[0:1, :]
     here = pl.ds(pl.multiple_of(base, BLOCK), BLOCK)
@@ -462,7 +482,7 @@
             num_scalar_prefetch=1,
             grid=(total // BLOCK,),
             in_specs=[block, block, moved, block, moved, whole, whole, whole, half, half, half]
-            + [pl.BlockSpec((8, width), lambda i, m: (0, 0))],
+            + [pl.BlockSpec((1, width), lambda i, m: (0, 0))],
             out_specs=[
                 pl.BlockSpec((total, 3 * width), lambda i, m: (0, 0)),
                 pl.BlockSpec((8, width), lambda i, m: (0, 0)),
@@ -536,7 +556,7 @@
 def ffn_specs(count):
     whole = pl.BlockSpec((count, D), lambda t: (0, 0))
     tile = pl.BlockSpec((2, count, TILE), lambda t: (0, 0, t))
-    scale = pl.BlockSpec((2, 8, TILE), lambda t: (0, 0, t))
+    scale = pl.BlockSpec((2, 1, TILE), lambda t: (0, 0, t))
     return whole, tile, scale
 
 
@@ -586,6 +606,7 @@
 def ffn_backward(grads, weights, saved, sup, sgate, kind):
     count, hidden = sum(g.shape[0] for g in grads), sup.shape[2]
     whole, tile, scale = ffn_specs(count)
+    sums = pl.BlockSpec((2, 8, TILE), lambda t: (0, 0, t))
     return pl.pallas_call(
         functools.partial(backward_body, len(grads)),
         out_shape=[jax.ShapeDtypeStruct((2, count, hidden), BF16)] * 2
@@ -596,7 +617,7 @@
         + [weight_spec(weights)]
         + [tile] * 4
         + [scale, scale],
-        out_specs=[tile, tile, scale, scale, whole],
+        out_specs=[tile, tile, sums, sums, whole],
         scratch_shapes=[pltpu.VMEM((count, D), F32)],
         cost_estimate=pl.CostEstimate(
             flops=12 * count * D * hidden,
@@ -665,7 +686,7 @@
         return pl.BlockSpec((BLOCK, width), lambda i: (skip // BLOCK + i, column))
 
     in_specs = [rows_spec(w, s, c) for _, w, s, c in rows_in]
-    in_specs += [pl.BlockSpec((8, v.shape[1]), lambda i: (0, 0)) for v in vectors]
+    in_specs += [pl.BlockSpec((1, v.shape[1]), lambda i: (0, 0)) for v in vectors]
     in_specs += [pl.BlockSpec((D, w), lambda i, c=c: (0, c)) for _, w, c in wholes]
     shapes = [jax.ShapeDtypeStruct((count, w), t) for count, w, t in outs]
     shapes += [jax.ShapeDtypeStruct((8, D), F32)] * sums
@@ -717,7 +738,8 @@
     count = branch.shape[0]
     rows = pl.BlockSpec((BLOCK, D), lambda i: (chunk, 0))
     first = pl.BlockSpec((BLOCK, D), lambda i: (0, 0))
-    vector = pl.BlockSpec((8, D), lambda i: (0, 0))
+    vector = pl.BlockSpec((1, D), lambda i: (0, 0))
+    total = pl.BlockSpec((8, D), lambda i: (0, 0))
     extra = list(previous)
     return pl.pallas_call(
         turn_body,
@@ -730,7 +752,7 @@
         grid=(1,),
         in_specs=[rows, first, rows, rows, rows, vector, vector]
         + [pl.BlockSpec(memory_space=pl.ANY)] * len(extra),
-        out_specs=[rows, rows, first, vector],
+        out_specs=[rows, rows, first, total],
         input_output_aliases={7 + i: i for i in range(len(extra))},
         cost_estimate=pl.CostEstimate(
             flops=60 * BLOCK * D, bytes_accessed=20 * BLOCK * D, transcendentals=BLOCK
@@ -788,28 +810,41 @@
     place = m.reshape(1)
     meta = jnp.concatenate([place, lengths[0]])
     slot_ids = jnp.arange(row_len, dtype=jnp.int32)
-    positions, end = slot_ids, 0
-    for i in range(docs):
-        end = end + lengths[0, i]
-        positions = positions - jnp.where(slot_ids >= end, lengths[0, i], 0)
     steps_even = jnp.arange(0, HEAD, 2).astype(F32)
     frequencies = jnp.power(jnp.float32(10000.0), -steps_even / HEAD)
-    angles = positions.astype(F32)[:, None] * jnp.tile(frequencies, 4)[None, :]
-    cosine, sine = jnp.cos(angles), jnp.sin(angles)
+    frequencies = jnp.tile(frequencies, 4)[None, :]
+
+    def turn_by(steps):
+        angles = steps.astype(F32)[:, None] * frequencies
+        return jnp.cos(angles), jnp.sin(angles)
+
+    coarse_cos, coarse_sin = (t[:, None] for t in turn_by(jnp.arange(0, row_len, 64)))
+    fine_cos, fine_sin = (t[None] for t in turn_by(jnp.arange(64)))
+    slot_cos = (coarse_cos * fine_cos - coarse_sin * fine_sin).reshape(row_len, -1)
+    slot_sin = (coarse_sin * fine_cos + coarse_cos * fine_sin).reshape(row_len, -1)
+    first_slots = jnp.cumsum(lengths[0]) - lengths[0]
+    doc_cos, doc_sin = turn_by(first_slots)
+    start_cos, start_sin = doc_cos[0:1], doc_sin[0:1]
+    for i in range(1, docs):
+        later = (slot_ids >= first_slots[i])[:, None]
+        start_cos = jnp.where(later, doc_cos[i : i + 1], start_cos)
+        start_sin = jnp.where(later, doc_sin[i : i + 1], start_sin)
+    cosine = slot_cos * start_cos + slot_sin * start_sin
+    sine = slot_sin * start_cos - slot_cos * start_sin
+    x_halves = [swap(tokens[i * local // 2 : (i + 1) * local // 2], "mp", 2) for i in range(2)]
+    x_first = jnp.concatenate([tokens] + x_halves, axis=0)
+    vector = jnp.concatenate([s_up, s_gate, s_qk, alpha_attn, alpha_mlp])[None]
+    every = to_all(jnp.broadcast_to(vector, (devices, vector.shape[1])))
+    attn, third = gather(
+        jnp.concatenate([w_query, w_key, w_value, w_out.T], axis=1),
+        [(), (), (x_halves[0],), (x_halves[1], every)],
+    )
+    x_second = swap(x_first, "mp", 1)
     shard = jnp.concatenate([w_up, w_gate, w_down.T], axis=0)
-    shard = with_layout_constraint(shard, Layout(major_to_minor=(0, 1)))
+    shard = with_layout_constraint(after(shard, third), Layout(major_to_minor=(0, 1)))
     weights = lax.all_gather(
         shard, ("dp", "mp"), axis=0, tiled=True, axis_index_groups=chip_groups()
     ).reshape(-1, 2, 3, shard.shape[0] // 3, part)
-    x_halves = [swap(tokens[i * local // 2 : (i + 1) * local // 2], "mp", 2) for i in range(2)]
-    x_first = jnp.concatenate([tokens] + x_halves, axis=0)
-    x_second = swap(x_first, "mp", 1)
-    vector = jnp.concatenate([s_up, s_gate, s_qk, alpha_attn, alpha_mlp])[None]
-    every = to_all(jnp.broadcast_to(vector, (devices, vector.shape[1])))
-    attn = gather(
-        jnp.concatenate([w_query, w_key, w_value, w_out.T], axis=1),
-        [(), (x_halves[0], cosine, sine), (), (x_halves[1], every)],
-    )
     cuts, start = [], 0
     for piece in (s_up, s_gate, s_qk, alpha_attn, alpha_mlp):
         cuts.append(every[:, start : start + piece.shape[0]].reshape(-1))
@@ -820,14 +855,14 @@
         size = array.shape[0] // 4
         return lax.dynamic_slice_in_dim(array, index * size, size)
 
-    def eight(array):
-        return jnp.broadcast_to(array[None], (8, array.shape[0]))
-
-    sqk = eight(quarter(sqk_all, m))
+    def row(array):
+        return array[None]
+
+    sqk = row(quarter(sqk_all, m))
     low = m & 2
-    sup = jnp.stack([eight(quarter(sup_all, low)), eight(quarter(sup_all, low + 1))])
-    sgate = jnp.stack([eight(quarter(sgate_all, low)), eight(quarter(sgate_all, low + 1))])
-    one, two = eight(alpha_one), eight(alpha_two)
+    sup = jnp.stack([row(quarter(sup_all, low)), row(quarter(sup_all, low + 1))])
+    sgate = jnp.stack([row(quarter(sgate_all, low)), row(quarter(sgate_all, low + 1))])
+    one, two = row(alpha_one), row(alpha_two)
     out_mine = attn[:, 3 * width :]
     out_core = swap(out_mine, "mp", 1)
     out_over = swap(out_mine, "mp", 2)
@@ -835,7 +870,7 @@
     out_parts = [(w, width, 0) for w in (out_mine, out_core, out_over, out_cross)]
 
     kpos = jnp.where(key_mask[0] == 1, slot_ids, -1)
-    kpos_rows = jnp.broadcast_to(kpos[None, :], (8, row_len))
+    kpos_rows = kpos[None, :]
     kpos_cols = jnp.broadcast_to(kpos[:, None], (row_len, 128))
 
     half = project(place, x_first, attn, cosine, sine, sqk, None, 0)
@@ -921,6 +956,7 @@
     first, second = grads[: 2 * local], grads[2 * local :]
     qkv_sum = dot(x_first, first, 0, 0) + dot(x_second, second, 0, 0)
     half_sum, sent = scatter_y(qkv_sum, grad_out)
+    mlp_squares = jnp.sum(grad_mlp * grad_mlp)
     qkv = after(attn, sent)[:, : 3 * width]
     second_tokens = dot(second, qkv, 1, 1).astype(BF16)
     to_core = swap(second_tokens, "mp", 1)
@@ -935,6 +971,7 @@
     def quarters(by):
         return placed(by[0, 0], m & 2) + placed(by[1, 0], (m & 2) + 1)
 
+    bu, bg, g_sqk, by_one, by_two, _ = lax.optimization_barrier((bu, bg, g_sqk, by_one, by_two, second_tokens))
     rows = [quarters(bu), quarters(bg), placed(g_sqk[0], m), by_one[0], by_two[0]]
     rows = [row.reshape(devices, -1) for row in rows]
     small = jnp.sum(to_all(after(jnp.concatenate(rows, axis=1), for_x)), axis=0)
@@ -947,9 +984,8 @@
     def squared(*arrays):
         return sum(jnp.sum(array * array) for array in arrays)
 
-    squares = squared(grad_mlp)
-    grad_attn = scatter_z(after(half_sum, for_x, squares))
-    squares = squares + squared(grad_attn, small)
+    grad_attn = scatter_z(after(half_sum, for_x), mlp_squares)
+    squares = mlp_squares + squared(grad_attn, small)
     g_qkv = [grad_attn[:, i * width : (i + 1) * width] for i in range(3)]
     grad_down, grad_out = turned(grad_down), turned(grad_attn[:, 3 * width :])
     to_x = after(to_x, squares)

time: 468 us -> 457 us (0.976)
  other arithmetic: 37.7 us -> 31.7 us
    ppermute x3, waiting for transfers between devices: 15.5 us -> 0.01 us  [to_z(): lax.ppermute(array, 'dp', [(z * 2 + y, (z + step) % 4 * 2 + y) for z in r...]
    all_to_all x3, starting transfers between devices: 23.9 us -> 10.4 us  [to_all(): return lax.all_to_all(rows, ('dp', 'mp'), 0, 0, tiled=True)]
    all_to_all x3, waiting for transfers between devices: 1.48 us -> 14.3 us  [to_all(): return lax.all_to_all(rows, ('dp', 'mp'), 0, 0, tiled=True)]
    ppermute x7, starting transfers between devices: 8.33 us -> 14.2 us  [around(): lax.ppermute(array, 'dp', [(RING[p], RING[(p + step) % 8]) for p in range...]
    all_gather x1, waiting for transfers between devices: 0.01 us -> 5.58 us  [shards(): lax.all_gather(shard, ('dp', 'mp'), axis=0, tiled=True, axis_index_groups...]
    sin x1 -> x0, other arithmetic: 5.55 us -> none  [shards(): cosine, sine = (jnp.cos(angles), jnp.sin(angles))]
    ppermute x7, waiting for transfers between devices: 37.8 us -> 32.4 us  [around(): lax.ppermute(array, 'dp', [(RING[p], RING[(p + step) % 8]) for p in range...]
    reduce_scatter x1, waiting for transfers between devices: 10.9 us -> 16.1 us  [shards(): lax.psum_scatter(grad_mlp.reshape(-1, part), ('dp', 'mp'), scatter_dimens...]
  transfers between devices with their start and end apart: 39 -> 39, of which waited for: 16 -> 17; matrix products, arithmetic and copies ran while one was open for 19% -> 18% of each run, Pallas kernels for 40% -> 41%
where the time goes in v4:
time: 457 us; the launch traced here: 455 us
  Pallas kernels  187 us (41%)
  waiting for transfers between devices  104 us (23%)
  starting transfers between devices  50.7 us (11%)
  local copies, waits for them, and re-layouts  41.7 us (9%)
  other arithmetic  31.7 us (7%)
  matrix products  20.4 us (4%)
  between operations  19.9 us (4%)
    pallas_call x1, Pallas kernels, attend_back(): pl.pallas_call(functools.partial(back_body, docs), out_shape=[jax.ShapeDt...  41 us
    ppermute x24, waiting for transfers between devices, swap(): return lax.ppermute(array, axis, [(i, i ^ bit) for i in range(size)])  35.1 us
    pallas_call x3, Pallas kernels, ffn_backward(): pl.pallas_call(functools.partial(backward_body, len(grads)), out_shape=[j...  34.5 us
    pallas_call x3, Pallas kernels, ffn_forward(): pl.pallas_call(forward_body, out_shape=[jax.ShapeDtypeStruct((2, count, h...  32.6 us
    ppermute x7, waiting for transfers between devices, around(): lax.ppermute(array, 'dp', [(RING[p], RING[(p + step) % 8]) for p in range...  32.4 us
    pallas_call x2, Pallas kernels, attend(): pl.pallas_call(functools.partial(attend_body, docs, first), out_shape=[ja...  20.7 us
    pallas_call x1, Pallas kernels, weight_grads(): pl.pallas_call(functools.partial(weight_body, (len(hs), len(ups), len(ms)...  20.6 us
    dot_general x8, matrix products, dot(): lax.dot_general(left, right, (((left_dim,), (right_dim,)), ((), ())), pre...  20.4 us
  transfers between devices with their start and end apart: 39, of which 17 were waited for; matrix products, arithmetic and copies ran while one was open for 18% of the time, Pallas kernels for 41%

profile of v4, /device:TPU:0, one launch (start us, length us, event | category | flops | bytes accessed | tf_op | source)
XLA Modules:
  0.0 455.0 jit_solution(11119612962925423244)
XLA Ops:
  8.7 3.1 collective-permute-start.3
  12.7 1.9 collective-permute-start
  14.6 3.4 collective-permute-done.3
  18.1 1.5 collective-permute-done.4
  19.6 1.6 collective-permute-start.5
  21.6 4.8 %collective-permute-done.5 = bf16[128,1024]{1,0:T(8,128)(2,1)S(1)} collective-permute-done((bf16[128,1024]{1,0:T(8,128)(2,1)S(1)}, bf16[128,1024]{1,0:T(8,128)(2,1)S(1)}, u32[]{:S(2)}, u32[]{:S(2)}) %collective-permute-start.5) | collective-permute-done | bytes 262176 | tf_op jit(solution)/shard_map/ppermute | solution.py:55
  26.4 1.4 collective-permute-done.6
  30.2 2.0 pad_maximum_fusion.4
  32.2 3.2 collective-permute-done.8
  35.4 1.6 collective-permute-start.1
  37.7 3.6 all-to-all-start
  47.6 1.9 constant_dynamic-update-slice_fusion.x_ref
  49.7 3.1 fusion.12
  54.8 1.7 collective-permute-start.7
  56.5 12.0 %collective-permute-done.7 = bf16[128,1024]{1,0:T(8,128)(2,1)S(1)} collective-permute-done((bf16[128,1024]{1,0:T(8,128)(2,1)S(1)}, bf16[128,1024]{1,0:T(8,128)(2,1)S(1)}, u32[]{:S(2)}, u32[]{:S(2)}) %collective-permute-start.7) | collective-permute-done | bytes 262176 | tf_op jit(solution)/shard_map/ppermute | solution.py:55
  68.5 7.0 %collective-permute-start.9 = (bf16[128,1024]{1,0:T(8,128)(2,1)S(1)}, bf16[128,1024]{1,0:T(8,128)(2,1)S(1)}, u32[]{:S(2)}, u32[]{:S(2)}) collective-permute-start(bf16[128,1024]{1,0:T(8,128)(2,1)S(1)} %collective-permute-done.7), channel_id=1, source_target_pairs={{0,8},{8,16},{16,24},{24,28},{28,20},{20,12},{12,4},{4,0},{1,9},{9... | collective-permute-start | bytes 786440 | tf_op jit(solution)/shard_map/ppermute | solution.py:55
  77.5 6.1 %collective-permute-done.9 = bf16[128,1024]{1,0:T(8,128)(2,1)S(1)} collective-permute-done((bf16[128,1024]{1,0:T(8,128)(2,1)S(1)}, bf16[128,1024]{1,0:T(8,128)(2,1)S(1)}, u32[]{:S(2)}, u32[]{:S(2)}) %collective-permute-start.9) | collective-permute-done | bytes 262176 | tf_op jit(solution)/shard_map/ppermute | solution.py:55
  83.7 1.6 collective-permute-start.14
  85.2 7.5 %project.2 = (bf16[2048,256]{1,0:T(8,128)(2,1)}, bf16[2048,256]{1,0:T(8,128)(2,1)}, bf16[2048,256]{1,0:T(8,128)(2,1)}, f32[2048,256]{1,0:T(8,128)}, f32[2048,256]{1,0:T(8,128)}) custom-call(s32[1]{0:T(128)} %bitcast.m_ref, bf16[1024,1024]{1,0:T(8,128)(2,1)} %constant_dynamic-update-slice_fusion.x_ref, bf16[1024,1024]{1,0:T(8,128)(2,1)} %copy-done.1, ...), custom_call_target="tpu_custom_call" | custom-call | flops 1610612736 | bytes 8388608 | tf_op jit(solution)/shard_map/project/pallas_call | solution.py:183
  92.8 6.8 %project.3 = (bf16[2048,256]{1,0:T(8,128)(2,1)}, bf16[2048,256]{1,0:T(8,128)(2,1)}, bf16[2048,256]{1,0:T(8,128)(2,1)}, f32[2048,256]{1,0:T(8,128)}, f32[2048,256]{1,0:T(8,128)}) custom-call(s32[1]{0:T(128)} %bitcast.m_ref, ...), custom_call_target="tpu_custom_call", output_to_operand_aliasing={{0}: (6, {}), {1}: (7, {}), {2}: (8, {}), {3}: (9, {}), {4}... | custom-call | flops 1610612736 | bytes 8388608 | tf_op jit(solution)/shard_map/project/pallas_call | solution.py:183
  99.6 11.2 %attend.2 = (bf16[2048,256]{1,0:T(8,128)(2,1)}, f32[2048,256]{1,0:T(8,128)}) custom-call(s32[5]{0:T(128)} %pad_add_fusion.meta_ref, bf16[2048,256]{1,0:T(8,128)(2,1)} %get-tuple-element.119.q_ref, bf16[2048,256]{1,0:T(8,128)(2,1)} %get-tuple-element.120.k_ref, bf16[2048,256]{1,0:T(8,128)(2,1)} %get-tuple-element.121.v_ref, s32[1,2048]{1,0:T(1,128)} %compare_select_fusion.kpos_ref), custom_call_target="tpu_custom_call" | custom-call | flops 8000000000 | bytes 4194304 | tf_op jit(solution)/shard_map/attend/pallas_call | solution.py:317
  114.2 9.5 %attend.3 = (bf16[2048,256]{1,0:T(8,128)(2,1)}, f32[2048,256]{1,0:T(8,128)}) custom-call(s32[5]{0:T(128)} %pad_add_fusion.meta_ref, bf16[2048,256]{1,0:T(8,128)(2,1)} %get-tuple-element.119.q_ref, bf16[2048,256]{1,0:T(8,128)(2,1)} %get-tuple-element.120.k_ref, ...), custom_call_target="tpu_custom_call", output_to_operand_aliasing={{0}: (5, {}), {1}: (6, {})} | custom-call | flops 8000000000 | bytes 4194304 | tf_op jit(solution)/shard_map/attend/pallas_call | solution.py:317
  126.9 1.5 collective-permute-done.12.a2.a3
  129.2 5.1 %attn_out.1 = (f32[512,1024]{1,0:T(8,128)}, bf16[512,1024]{1,0:T(8,128)(2,1)}) custom-call(bf16[2048,256]{1,0:T(8,128)(2,1)} %get-tuple-element.125.a0.o_ref, bf16[512,256]{1,0:T(8,128)(2,1)} %copy-done.15, bf16[1024,256]{1,0:T(8,128)(2,1)} %copy-done.10, bf16[1024,256]{1,0:T(8,128)(2,1)} %copy-done.10, bf16[512,1024]{1,0:T(8,128)(2,1)} %x_ref.7, ...), custom_call_target="tpu_custom_call" | custom-call | flops 1073741824 | bytes 10485760 | tf_op jit(solution)/shard_map/attn_out/pallas_call | solution.py:695
  135.6 3.2 collective-permute-start.17
  138.9 5.6 %all-gather.2.cloned.1.call-done = bf16[6144,1024]{1,0:T(8,128)(2,1)} async-done(((bf16[384,1024]{1,0:T(8,128)(2,1)}), bf16[6144,1024]{1,0:T(8,128)(2,1)}) %all-gather.2.cloned.1.call-update) | async-done | bytes 12582928 | tf_op jit(solution)/shard_map/all_gather | solution.py:845
  144.5 13.5 %ffn_forward.3 = (bf16[2,512,1024]{2,1,0:T(8,128)(2,1)}, bf16[2,512,1024]{2,1,0:T(8,128)(2,1)}, bf16[2,512,1024]{2,1,0:T(8,128)(2,1)}, bf16[2,512,1024]{2,1,0:T(8,128)(2,1)}, f32[512,1024]{1,0:T(8,128)}) custom-call(bf16[512,1024]{1,0:T(8,128)(2,1)} %get-tuple-element.126.h_ref.refs_0_, bf16[8,2,3,128,1024]{4,3,2,1,0:T(8,128)(2,1)} %bitcast.127, ...), custom_call_target="tpu_custom_call" | custom-call | flops 6442450944 | bytes 18874368 | tf_op jit(solution)/shard_map/ffn_forward/pallas_call | solution.py:566
  158.8 9.3 %ffn_forward.4 = (bf16[2,256,1024]{2,1,0:T(8,128)(2,1)}, bf16[2,256,1024]{2,1,0:T(8,128)(2,1)}, bf16[2,256,1024]{2,1,0:T(8,128)(2,1)}, bf16[2,256,1024]{2,1,0:T(8,128)(2,1)}, bf16[256,1024]{1,0:T(8,128)(2,1)}) custom-call(bf16[256,1024]{1,0:T(8,128)(2,1)} %copy-done.17, bf16[8,2,3,128,1024]{4,3,2,1,0:T(8,128)(2,1)} %bitcast.128, ...), custom_call_target="tpu_custom_call" | custom-call | flops 3221225472 | bytes 15728640 | tf_op jit(solution)/shard_map/ffn_forward/pallas_call | solution.py:566
  168.1 1.5 collective-permute-start.19
  170.5 9.9 %ffn_forward.5 = (bf16[2,256,1024]{2,1,0:T(8,128)(2,1)}, bf16[2,256,1024]{2,1,0:T(8,128)(2,1)}, bf16[2,256,1024]{2,1,0:T(8,128)(2,1)}, bf16[2,256,1024]{2,1,0:T(8,128)(2,1)}, bf16[256,1024]{1,0:T(8,128)(2,1)}) custom-call(bf16[256,1024]{1,0:T(8,128)(2,1)} %copy-done.18, bf16[8,2,3,128,1024]{4,3,2,1,0:T(8,128)(2,1)} %bitcast.129, ...), custom_call_target="tpu_custom_call" | custom-call | flops 3221225472 | bytes 15728640 | tf_op jit(solution)/shard_map/ffn_forward/pallas_call | solution.py:566
  183.2 4.5 turn.2
  187.7 1.7 collective-permute-start.20
  189.4 6.0 %collective-permute-done.18.far_ref = bf16[256,1024]{1,0:T(8,128)(2,1)S(1)} collective-permute-done((bf16[256,1024]{1,0:T(8,128)(2,1)}, bf16[256,1024]{1,0:T(8,128)(2,1)S(1)}, u32[]{:S(2)}, u32[]{:S(2)}) %collective-permute-start.18) | collective-permute-done | bytes 524320 | tf_op jit(solution)/shard_map/ppermute | solution.py:45
  196.3 4.5 turn.3
  201.3 14.2 %ffn_backward.3 = (bf16[2,512,1024]{2,1,0:T(8,128)(2,1)}, bf16[2,512,1024]{2,1,0:T(8,128)(2,1)}, f32[2,8,1024]{2,1,0:T(8,128)}, f32[2,8,1024]{2,1,0:T(8,128)}, f32[512,1024]{1,0:T(8,128)}) custom-call(bf16[256,1024]{1,0:T(8,128)(2,1)} %get-tuple-element.138.refs_0_.refs_3_, bf16[256,1024]{1,0:T(8,128)(2,1)} %get-tuple-element.139.refs_1_.refs_4_, ...), custom_call_target="tpu_custom_call" | custom-call | flops 6442450944 | bytes 25165824 | tf_op jit(solution)/shard_map/ffn_backward/pallas_call | solution.py:610
  216.4 10.2 %ffn_backward.4 = (bf16[2,256,1024]{2,1,0:T(8,128)(2,1)}, bf16[2,256,1024]{2,1,0:T(8,128)(2,1)}, f32[2,8,1024]{2,1,0:T(8,128)}, f32[2,8,1024]{2,1,0:T(8,128)}, bf16[256,1024]{1,0:T(8,128)(2,1)}) custom-call(bf16[256,1024]{1,0:T(8,128)(2,1)} %copy-done.19, bf16[8,2,3,128,1024]{4,3,2,1,0:T(8,128)(2,1)} %bitcast.131, ...), custom_call_target="tpu_custom_call" | custom-call | flops 3221225472 | bytes 18874368 | tf_op jit(solution)/shard_map/ffn_backward/pallas_call | solution.py:610
  226.5 1.5 collective-permute-start.22
  228.9 10.1 %ffn_backward.5 = (bf16[2,256,1024]{2,1,0:T(8,128)(2,1)}, bf16[2,256,1024]{2,1,0:T(8,128)(2,1)}, f32[2,8,1024]{2,1,0:T(8,128)}, f32[2,8,1024]{2,1,0:T(8,128)}, bf16[256,1024]{1,0:T(8,128)(2,1)}) custom-call(bf16[256,1024]{1,0:T(8,128)(2,1)} %copy-done.20, bf16[8,2,3,128,1024]{4,3,2,1,0:T(8,128)(2,1)} %bitcast.132, ...), custom_call_target="tpu_custom_call" | custom-call | flops 3221225472 | bytes 18874368 | tf_op jit(solution)/shard_map/ffn_backward/pallas_call | solution.py:610
  239.6 20.6 %weight_grads.1 = bf16[8,2,3,128,1024]{4,3,2,1,0:T(8,128)(2,1)} custom-call(bf16[512,1024]{1,0:T(8,128)(2,1)} %get-tuple-element.126.h_ref.refs_0_, bf16[256,1024]{1,0:T(8,128)(2,1)} %copy-done.17, bf16[256,1024]{1,0:T(8,128)(2,1)} %copy-done.18, bf16[256,1024]{1,0:T(8,128)(2,1)} %get-tuple-element.138.refs_0_.refs_3_, ...), custom_call_target="tpu_custom_call" | custom-call | flops 12884901888 | bytes 25165824 | tf_op jit(solution)/shard_map/weight_grads/pallas_call | solution.py:665
  263.2 9.1 %attn_back_out.1 = (bf16[512,1024]{1,0:T(8,128)(2,1)}, f32[512,1024]{1,0:T(8,128)}, bf16[512,256]{1,0:T(8,128)(2,1)}, bf16[512,256]{1,0:T(8,128)(2,1)}, bf16[512...) custom-call(f32[512,1024]{1,0:T(8,128)} %get-tuple-element.144.own_ref, ...), custom_call_target="tpu_custom_call" | custom-call | flops 1073741824 | bytes 10485760 | tf_op jit(solution)/shard_map/attn_back_out/pallas_call | solution.py:695
  273.6 1.6 collective-permute-start.25
  275.3 1.9 convolution_convert_fusion.2
  277.9 6.5 %collective-permute-done.25 = bf16[1024,256]{1,0:T(8,128)(2,1)S(1)} collective-permute-done((bf16[1024,256]{1,0:T(8,128)(2,1)S(1)}, bf16[1024,256]{1,0:T(8,128)(2,1)S(1)}, u32[]{:S(2)}, u32[]{:S(2)}) %collective-permute-start.25) | collective-permute-done | bytes 524320 | tf_op jit(solution)/shard_map/ppermute | solution.py:45
  291.0 41.0 %attend_back.1 = (bf16[2048,768]{1,0:T(8,128)(2,1)}, f32[8,256]{1,0:T(8,128)}) custom-call(s32[5]{0:T(128)} %pad_add_fusion.meta_ref, bf16[2048,256]{1,0:T(8,128)(2,1)} %get-tuple-element.119.q_ref, f32[2048,256]{1,0:T(8,128)} %get-tuple-element.167.qr_ref, bf16[2048,256]{1,0:T(8,128)(2,1)} %get-tuple-element.125.a0.o_ref, ...), custom_call_target="tpu_custom_call" | custom-call | flops 40000000000 | bytes 6291456 | tf_op jit(solution)/shard_map/attend_back/pallas_call | solution.py:475
  332.1 4.2 fusion.4
  336.3 3.6 convolution_add_fusion
  342.1 1.4 fusion.9
  346.0 2.3 pad_maximum_fusion.3
  348.3 4.6 %convolution_convert_fusion = bf16[1024,1024]{1,0:T(8,128)(2,1)} fusion(bf16[2048,768]{1,0:T(8,128)(2,1)} %get-tuple-element.176, bf16[1024,1024]{1,0:T(8,128)(2,1)S(1)} %copy-done.2), kind=kOutput, calls=%fused_computation.6 | convolution fusion | flops 1611661312 | bytes 5242880 | tf_op jit(solution)/shard_map/dot_general | solution.py:35
  356.3 3.8 fusion.6
  360.1 18.2 %collective-permute-done.30 = bf16[4,128,1024]{2,1,0:T(8,128)(2,1)} collective-permute-done((bf16[4,128,1024]{2,1,0:T(8,128)(2,1)}, bf16[4,128,1024]{2,1,0:T(8,128)(2,1)}, u32[]{:S(2)}, u32[]{:S(2)}) %collective-permute-start.30) | collective-permute-done | bytes 1048608 | tf_op jit(solution)/shard_map/ppermute | solution.py:45
  378.3 1.5 maximum_add_fusion
  379.9 2.6 fusion
  382.5 1.4 collective-permute-start.29
  384.5 2.7 all-to-all-start.1
  388.1 1.8 collective-permute-start.31
  389.9 2.4 collective-permute-start.32
  392.3 1.4 collective-permute-start.33
  393.7 14.3 %all-to-all-done.1 = f32[32,1,352]{2,1,0:T(1,128)S(1)} async-done(((f32[32,1,352]{2,1,0:T(1,128)}), f32[32,1,352]{2,1,0:T(1,128)S(1)}, u32[]{:S(2)}, u32[]{:S(2)}) %all-to-all-start.1) | async-done | bytes 45088 | tf_op jit(solution)/shard_map/all_to_all | solution.py:130
  409.8 16.1 %reduce-scatter.2.cloned.1.call-done = bf16[384,1024]{1,0:T(8,128)(2,1)} async-done(((bf16[6144,1024]{1,0:T(8,128)(2,1)}), bf16[384,1024]{1,0:T(8,128)(2,1)}) %reduce-scatter.2.cloned.1.call-update) | async-done | bytes 786448 | tf_op jit(solution)/shard_map/reduce_scatter | solution.py:930
  426.0 2.2 multiply_reduce_fusion
  428.9 1.9 multiply_reduce_fusion.1
  433.3 4.1 all-to-all-start.2
  440.0 4.2 fusion.2
  (261 shorter events, 61.2 us)
Async XLA Ops:
  7.2 137.3 %all-gather.2.cloned.1.call-start = ((), (), s32[]{:S(2)}) async-start(), calls=%async_computation.4 | async-start | bytes 13369344 | tf_op jit(solution)/shard_map/all_gather | solution.py:845
  8.7 28.3 %copy-start.48 = (f32[128]{0:T(128)S(1)}, f32[128]{0:T(128)}, u32[]{:S(2)}) copy-start(f32[128]{0:T(128)} %param.28) | copy-start | bytes 1540
  8.7 28.2 %copy-start.49 = (f32[128]{0:T(128)S(1)}, f32[128]{0:T(128)}, u32[]{:S(2)}) copy-start(f32[128]{0:T(128)} %param.29) | copy-start | bytes 1540
  8.7 28.2 %copy-start.50 = (f32[32]{0:T(128)S(1)}, f32[32]{0:T(128)}, u32[]{:S(2)}) copy-start(f32[32]{0:T(128)} %param.27) | copy-start | bytes 388
  8.7 28.2 %copy-start.51 = (f32[32]{0:T(128)S(1)}, f32[32]{0:T(128)}, u32[]{:S(2)}) copy-start(f32[32]{0:T(128)} %param.30) | copy-start | bytes 388
  8.7 28.2 %copy-start.52 = (f32[32]{0:T(128)S(1)}, f32[32]{0:T(128)}, u32[]{:S(2)}) copy-start(f32[32]{0:T(128)} %param.31) | copy-start | bytes 388
  8.7 9.3 %collective-permute-start.3 = (bf16[128,1024]{1,0:T(8,128)(2,1)S(1)}, bf16[128,1024]{1,0:T(8,128)(2,1)S(1)}, u32[]{:S(2)}, u32[]{:S(2)}) collective-permute-start(bf16[128,1024]{1,0:T(8,128)(2,1)S(1)} %get-tuple-element.309), channel_id=1, source_target_pairs={{0,8},{8,16},{16,24},{24,28},{28,20},{20,12},{12,4},{4,0},{1,9},{9... | collective-permute-start | bytes 786440 | tf_op jit(solution)/shard_map/ppermute | solution.py:55
  11.8 7.8 %collective-permute-start.4 = (bf16[128,1024]{1,0:T(8,128)(2,1)S(1)}, bf16[128,1024]{1,0:T(8,128)(2,1)S(1)}, u32[]{:S(2)}, u32[]{:S(2)}) collective-permute-start(bf16[128,1024]{1,0:T(8,128)(2,1)S(1)} %get-tuple-element.309), channel_id=1, source_target_pairs={{0,4},{8,0},{16,8},{24,16},{28,24},{20,28},{12,20},{4,12},{1,5},{9... | collective-permute-start | bytes 786440 | tf_op jit(solution)/shard_map/ppermute | solution.py:55
  12.7 28.8 %copy-start.53 = (s32[1,4]{1,0:T(1,128)S(1)}, s32[1,4]{1,0:T(1,128)}, u32[]{:S(2)}) copy-start(s32[1,4]{1,0:T(1,128)} %param.18) | copy-start | bytes 52
  12.7 15.2 %collective-permute-start = (bf16[256,1024]{1,0:T(8,128)(2,1)S(1)}, bf16[256,1024]{1,0:T(8,128)(2,1)S(1)}, u32[]{:S(2)}, u32[]{:S(2)}) collective-permute-start(bf16[256,1024]{1,0:T(8,128)(2,1)S(1)} %get-tuple-element.298), channel_id=1, source_target_pairs={{0,2},{1,3},{2,0},{3,1},{4,6},{5,7},{6,4},{7,5},{8,10},{9,11},{10,... | collective-permute-start | bytes 1572872 | tf_op jit(solution)/shard_map/ppermute | solution.py:45
  18.1 9.8 %copy-start.26 = (bf16[128,1024]{1,0:T(8,128)(2,1)}, bf16[128,1024]{1,0:T(8,128)(2,1)S(1)}, u32[]{:S(2)}) copy-start(bf16[128,1024]{1,0:T(8,128)(2,1)S(1)} %collective-permute-done.3) | copy-start | bytes 786436
  19.6 8.3 %copy-start.28 = (bf16[128,1024]{1,0:T(8,128)(2,1)}, bf16[128,1024]{1,0:T(8,128)(2,1)S(1)}, u32[]{:S(2)}) copy-start(bf16[128,1024]{1,0:T(8,128)(2,1)S(1)} %collective-permute-done.4) | copy-start | bytes 786436
  19.6 6.9 %collective-permute-start.5 = (bf16[128,1024]{1,0:T(8,128)(2,1)S(1)}, bf16[128,1024]{1,0:T(8,128)(2,1)S(1)}, u32[]{:S(2)}, u32[]{:S(2)}) collective-permute-start(bf16[128,1024]{1,0:T(8,128)(2,1)S(1)} %collective-permute-done.3), channel_id=1, source_target_pairs={{0,8},{8,16},{16,24},{24,28},{28,20},{20,12},{12,4},{4,0},{1,9},{9... | collective-permute-start | bytes 786440 | tf_op jit(solution)/shard_map/ppermute | solution.py:55
  21.2 6.7 %collective-permute-start.6 = (bf16[128,1024]{1,0:T(8,128)(2,1)S(1)}, bf16[128,1024]{1,0:T(8,128)(2,1)}, u32[]{:S(2)}, u32[]{:S(2)}) collective-permute-start(bf16[128,1024]{1,0:T(8,128)(2,1)S(1)} %collective-permute-done.4), channel_id=1, source_target_pairs={{0,4},{8,0},{16,8},{24,16},{28,24},{20,28},{12,20},{4,12},{1,5},{9... | collective-permute-start | bytes 786440 | tf_op jit(solution)/shard_map/ppermute | solution.py:55
  28.7 6.7 %collective-permute-start.8 = (bf16[128,1024]{1,0:T(8,128)(2,1)}, bf16[128,1024]{1,0:T(8,128)(2,1)}, u32[]{:S(2)}, u32[]{:S(2)}) collective-permute-start(bf16[128,1024]{1,0:T(8,128)(2,1)} %collective-permute-done.6), channel_id=1, source_target_pairs={{0,4},{8,0},{16,8},{24,16},{28,24},{20,28},{12,20},{4,12},{1,5},{9... | collective-permute-start | bytes 786440 | tf_op jit(solution)/shard_map/ppermute | solution.py:55
  35.4 12.2 %collective-permute-start.1 = (bf16[256,1024]{1,0:T(8,128)(2,1)}, bf16[256,1024]{1,0:T(8,128)(2,1)}, u32[]{:S(2)}, u32[]{:S(2)}) collective-permute-start(bf16[256,1024]{1,0:T(8,128)(2,1)} %get-tuple-element.297), channel_id=1, source_target_pairs={{0,2},{1,3},{2,0},{3,1},{4,6},{5,7},{6,4},{7,5},{8,10},{9,11},{10,... | collective-permute-start | bytes 1572872 | tf_op jit(solution)/shard_map/ppermute | solution.py:45
  37.7 15.7 %all-to-all-start = ((f32[32,1,352]{2,1,0:T(1,128)}), f32[32,1,352]{2,1,0:T(1,128)S(1)}, u32[]{:S(2)}, u32[]{:S(2)}) async-start(f32[32,1,352]{2,1,0:T(1,128)} %broadcast_in_dim.235), calls=%async_computation | async-start | bytes 98304 | tf_op jit(solution)/shard_map/all_to_all | solution.py:130
  41.3 384.7 %reduce-scatter.2.cloned.1.call-start = ((), (), s32[]{:S(2)}) async-start(), calls=%async_computation.5 | async-start | bytes 13369344 | tf_op jit(solution)/shard_map/reduce_scatter | solution.py:930
  49.4 43.3 %collective-permute-start.2 = (bf16[1024,1024]{1,0:T(8,128)(2,1)}, bf16[1024,1024]{1,0:T(8,128)(2,1)}, u32[]{:S(2)}, u32[]{:S(2)}) collective-permute-start(bf16[1024,1024]{1,0:T(8,128)(2,1)} %constant_dynamic-update-slice_fusion.x_ref), channel_id=1, source_target_pairs={{0,1},{1,0},{2,3},{3,2},{4,5},{5,4},{6,7},{7,6},{8,9},{9,8},{10,11... | collective-permute-start | bytes 6291464 | tf_op jit(solution)/shard_map/ppermute | solution.py:45
  49.7 6.8 %copy-start.29 = (bf16[128,1024]{1,0:T(8,128)(2,1)S(1)}, bf16[128,1024]{1,0:T(8,128)(2,1)}, u32[]{:S(2)}) copy-start(bf16[128,1024]{1,0:T(8,128)(2,1)} %copy-done.28) | copy-start | bytes 786436
  54.8 13.8 %collective-permute-start.7 = (bf16[128,1024]{1,0:T(8,128)(2,1)S(1)}, bf16[128,1024]{1,0:T(8,128)(2,1)S(1)}, u32[]{:S(2)}, u32[]{:S(2)}) collective-permute-start(bf16[128,1024]{1,0:T(8,128)(2,1)S(1)} %copy-done.31), channel_id=1, source_target_pairs={{0,8},{8,16},{16,24},{24,28},{28,20},{20,12},{12,4},{4,0},{1,9},{9... | collective-permute-start | bytes 786440 | tf_op jit(solution)/shard_map/ppermute | solution.py:55
  68.5 15.0 %collective-permute-start.9 = (bf16[128,1024]{1,0:T(8,128)(2,1)S(1)}, bf16[128,1024]{1,0:T(8,128)(2,1)S(1)}, u32[]{:S(2)}, u32[]{:S(2)}) collective-permute-start(bf16[128,1024]{1,0:T(8,128)(2,1)S(1)} %collective-permute-done.7), channel_id=1, source_target_pairs={{0,8},{8,16},{16,24},{24,28},{28,20},{20,12},{12,4},{4,0},{1,9},{9... | collective-permute-start | bytes 786440 | tf_op jit(solution)/shard_map/ppermute | solution.py:55
  83.7 28.2 %copy-start.5 = (bf16[1024,256]{1,0:T(8,128)(2,1)}, bf16[1024,256]{1,0:T(8,128)(2,1)S(1)}, u32[]{:S(2)}) copy-start(bf16[1024,256]{1,0:T(8,128)(2,1)S(1)} %slice.230.w0) | copy-start | bytes 1572868
  83.7 28.7 %collective-permute-start.14 = (bf16[1024,256]{1,0:T(8,128)(2,1)S(1)}, bf16[1024,256]{1,0:T(8,128)(2,1)S(1)}, u32[]{:S(2)}, u32[]{:S(2)}) collective-permute-start(bf16[1024,256]{1,0:T(8,128)(2,1)S(1)} %slice.230.w0), channel_id=1, source_target_pairs={{0,2},{1,3},{2,0},{3,1},{4,6},{5,7},{6,4},{7,5},{8,10},{9,11},{10,... | collective-permute-start | bytes 1572872 | tf_op jit(solution)/shard_map/ppermute | solution.py:45
  111.8 1.6 collective-permute-start.10
  111.9 15.0 %collective-permute-start.13 = (bf16[1024,256]{1,0:T(8,128)(2,1)S(1)}, bf16[1024,256]{1,0:T(8,128)(2,1)S(1)}, u32[]{:S(2)}, u32[]{:S(2)}) collective-permute-start(bf16[1024,256]{1,0:T(8,128)(2,1)S(1)} %slice.230.w0), channel_id=1, source_target_pairs={{0,1},{1,0},{2,3},{3,2},{4,5},{5,4},{6,7},{7,6},{8,9},{9,8},{10,11... | collective-permute-start | bytes 1572872 | tf_op jit(solution)/shard_map/ppermute | solution.py:45
  112.4 11.3 %copy-start.12 = (bf16[1024,256]{1,0:T(8,128)(2,1)}, bf16[1024,256]{1,0:T(8,128)(2,1)S(1)}, u32[]{:S(2)}) copy-start(bf16[1024,256]{1,0:T(8,128)(2,1)S(1)} %collective-permute-done.14.w2) | copy-start | bytes 1572868
  112.4 14.5 %collective-permute-start.15 = (bf16[1024,256]{1,0:T(8,128)(2,1)S(1)}, bf16[1024,256]{1,0:T(8,128)(2,1)S(1)}, u32[]{:S(2)}, u32[]{:S(2)}) collective-permute-start(bf16[1024,256]{1,0:T(8,128)(2,1)S(1)} %collective-permute-done.14.w2), channel_id=1, source_target_pairs={{0,1},{1,0},{2,3},{3,2},{4,5},{5,4},{6,7},{7,6},{8,9},{9,8},{10,11... | collective-permute-start | bytes 1572872 | tf_op jit(solution)/shard_map/ppermute | solution.py:45
  114.2 14.2 %collective-permute-start.12 = (bf16[1024,256]{1,0:T(8,128)(2,1)}, bf16[1024,256]{1,0:T(8,128)(2,1)S(1)}, u32[]{:S(2)}, u32[]{:S(2)}) collective-permute-start(bf16[1024,256]{1,0:T(8,128)(2,1)} %pad_maximum_fusion.5), channel_id=1, source_target_pairs={{0,2},{1,3},{2,0},{3,1},{4,6},{5,7},{6,4},{7,5},{8,10},{9,11},{10,... | collective-permute-start | bytes 1572872 | tf_op jit(solution)/shard_map/ppermute | solution.py:45
  124.7 2.2 collective-permute-start.11
  135.6 22.4 %collective-permute-start.17 = (bf16[256,1024]{1,0:T(8,128)(2,1)S(1)}, bf16[256,1024]{1,0:T(8,128)(2,1)S(1)}, u32[]{:S(2)}, u32[]{:S(2)}) collective-permute-start(bf16[256,1024]{1,0:T(8,128)(2,1)S(1)} %get-tuple-element.293), channel_id=1, source_target_pairs={{0,2},{1,3},{2,0},{3,1},{4,6},{5,7},{6,4},{7,5},{8,10},{9,11},{10,... | collective-permute-start | bytes 1572872 | tf_op jit(solution)/shard_map/ppermute | solution.py:45
  138.9 30.8 %collective-permute-start.16 = (bf16[256,1024]{1,0:T(8,128)(2,1)S(1)}, bf16[256,1024]{1,0:T(8,128)(2,1)S(1)}, u32[]{:S(2)}, u32[]{:S(2)}) collective-permute-start(bf16[256,1024]{1,0:T(8,128)(2,1)S(1)} %get-tuple-element.294), channel_id=1, source_target_pairs={{0,2},{1,3},{2,0},{3,1},{4,6},{5,7},{6,4},{7,5},{8,10},{9,11},{10,... | collective-permute-start | bytes 1572872 | tf_op jit(solution)/shard_map/ppermute | solution.py:45
  168.1 14.3 %collective-permute-start.19 = (bf16[256,1024]{1,0:T(8,128)(2,1)}, bf16[256,1024]{1,0:T(8,128)(2,1)S(1)}, u32[]{:S(2)}, u32[]{:S(2)}) collective-permute-start(bf16[256,1024]{1,0:T(8,128)(2,1)} %get-tuple-element.130), channel_id=1, source_target_pairs={{0,2},{1,3},{2,0},{3,1},{4,6},{5,7},{6,4},{7,5},{8,10},{9,11},{10,... | collective-permute-start | bytes 1572872 | tf_op jit(solution)/shard_map/ppermute | solution.py:45
  180.3 15.1 %collective-permute-start.18 = (bf16[256,1024]{1,0:T(8,128)(2,1)}, bf16[256,1024]{1,0:T(8,128)(2,1)S(1)}, u32[]{:S(2)}, u32[]{:S(2)}) collective-permute-start(bf16[256,1024]{1,0:T(8,128)(2,1)} %get-tuple-element.132), channel_id=1, source_target_pairs={{0,2},{1,3},{2,0},{3,1},{4,6},{5,7},{6,4},{7,5},{8,10},{9,11},{10,... | collective-permute-start | bytes 1572872 | tf_op jit(solution)/shard_map/ppermute | solution.py:45
  187.7 27.8 %collective-permute-start.20 = (bf16[256,1024]{1,0:T(8,128)(2,1)}, bf16[256,1024]{1,0:T(8,128)(2,1)S(1)}, u32[]{:S(2)}, u32[]{:S(2)}) collective-permute-start(bf16[256,1024]{1,0:T(8,128)(2,1)} %get-tuple-element.138.refs_0_.refs_3_), channel_id=1, source_target_pairs={{0,2},{1,3},{2,0},{3,1},{4,6},{5,7},{6,4},{7,5},{8,10},{9,11},{10,... | collective-permute-start | bytes 1572872 | tf_op jit(solution)/shard_map/ppermute | solution.py:45
  200.8 27.3 %collective-permute-start.21 = (bf16[256,1024]{1,0:T(8,128)(2,1)}, bf16[256,1024]{1,0:T(8,128)(2,1)S(1)}, u32[]{:S(2)}, u32[]{:S(2)}) collective-permute-start(bf16[256,1024]{1,0:T(8,128)(2,1)} %get-tuple-element.139.refs_1_.refs_4_), channel_id=1, source_target_pairs={{0,2},{1,3},{2,0},{3,1},{4,6},{5,7},{6,4},{7,5},{8,10},{9,11},{10,... | collective-permute-start | bytes 1572872 | tf_op jit(solution)/shard_map/ppermute | solution.py:45
  226.5 33.7 %collective-permute-start.22 = (bf16[256,1024]{1,0:T(8,128)(2,1)}, bf16[256,1024]{1,0:T(8,128)(2,1)S(1)}, u32[]{:S(2)}, u32[]{:S(2)}) collective-permute-start(bf16[256,1024]{1,0:T(8,128)(2,1)} %get-tuple-element.152), channel_id=1, source_target_pairs={{0,2},{1,3},{2,0},{3,1},{4,6},{5,7},{6,4},{7,5},{8,10},{9,11},{10,... | collective-permute-start | bytes 1572872 | tf_op jit(solution)/shard_map/ppermute | solution.py:45
  239.0 21.3 %collective-permute-start.23 = (bf16[256,1024]{1,0:T(8,128)(2,1)}, bf16[256,1024]{1,0:T(8,128)(2,1)S(1)}, u32[]{:S(2)}, u32[]{:S(2)}) collective-permute-start(bf16[256,1024]{1,0:T(8,128)(2,1)} %get-tuple-element.162), channel_id=1, source_target_pairs={{0,2},{1,3},{2,0},{3,1},{4,6},{5,7},{6,4},{7,5},{8,10},{9,11},{10,... | collective-permute-start | bytes 1572872 | tf_op jit(solution)/shard_map/ppermute | solution.py:45
  263.2 12.0 %copy-start.16 = (bf16[512,256]{1,0:T(8,128)(2,1)S(1)}, bf16[512,256]{1,0:T(8,128)(2,1)}, u32[]{:S(2)}) copy-start(bf16[512,256]{1,0:T(8,128)(2,1)} %copy-done.15) | copy-start | bytes 786436
  273.6 10.8 %collective-permute-start.25 = (bf16[1024,256]{1,0:T(8,128)(2,1)S(1)}, bf16[1024,256]{1,0:T(8,128)(2,1)S(1)}, u32[]{:S(2)}, u32[]{:S(2)}) collective-permute-start(bf16[1024,256]{1,0:T(8,128)(2,1)S(1)} %pad_maximum_fusion.6), channel_id=1, source_target_pairs={{0,2},{1,3},{2,0},{3,1},{4,6},{5,7},{6,4},{7,5},{8,10},{9,11},{10,... | collective-permute-start | bytes 1572872 | tf_op jit(solution)/shard_map/ppermute | solution.py:45
  277.2 7.3 %copy-start.34 = (bf16[512,256]{1,0:T(8,128)(2,1)S(1)}, bf16[512,256]{1,0:T(8,128)(2,1)}, u32[]{:S(2)}) copy-start(bf16[512,256]{1,0:T(8,128)(2,1)} %get-tuple-element.172) | copy-start | bytes 786436
  277.7 7.5 %copy-start.45 = (f32[8,1024]{1,0:T(8,128)S(1)}, f32[8,1024]{1,0:T(8,128)}, u32[]{:S(2)}) copy-start(f32[8,1024]{1,0:T(8,128)} %get-tuple-element.193) | copy-start | bytes 98308
  277.7 7.5 %copy-start.46 = (f32[8,1024]{1,0:T(8,128)S(1)}, f32[8,1024]{1,0:T(8,128)}, u32[]{:S(2)}) copy-start(f32[8,1024]{1,0:T(8,128)} %get-tuple-element.194) | copy-start | bytes 98308
  277.7 7.5 %copy-start.37 = (f32[2,8,1024]{2,1,0:T(8,128)S(1)}, f32[2,8,1024]{2,1,0:T(8,128)}, u32[]{:S(2)}) copy-start(f32[2,8,1024]{2,1,0:T(8,128)} %get-tuple-element.188) | copy-start | bytes 196612
  277.7 7.5 %copy-start.39 = (f32[2,8,1024]{2,1,0:T(8,128)S(1)}, f32[2,8,1024]{2,1,0:T(8,128)}, u32[]{:S(2)}) copy-start(f32[2,8,1024]{2,1,0:T(8,128)} %get-tuple-element.189) | copy-start | bytes 196612
  277.7 7.5 %copy-start.41 = (f32[2,8,1024]{2,1,0:T(8,128)S(1)}, f32[2,8,1024]{2,1,0:T(8,128)}, u32[]{:S(2)}) copy-start(f32[2,8,1024]{2,1,0:T(8,128)} %get-tuple-element.190) | copy-start | bytes 196612
  277.7 7.5 %copy-start.36 = (f32[2,8,1024]{2,1,0:T(8,128)S(1)}, f32[2,8,1024]{2,1,0:T(8,128)}, u32[]{:S(2)}) copy-start(f32[2,8,1024]{2,1,0:T(8,128)} %get-tuple-element.185) | copy-start | bytes 196612
  277.7 7.5 %copy-start.38 = (f32[2,8,1024]{2,1,0:T(8,128)S(1)}, f32[2,8,1024]{2,1,0:T(8,128)}, u32[]{:S(2)}) copy-start(f32[2,8,1024]{2,1,0:T(8,128)} %get-tuple-element.186) | copy-start | bytes 196612
  277.8 7.5 %copy-start.40 = (f32[2,8,1024]{2,1,0:T(8,128)S(1)}, f32[2,8,1024]{2,1,0:T(8,128)}, u32[]{:S(2)}) copy-start(f32[2,8,1024]{2,1,0:T(8,128)} %get-tuple-element.187) | copy-start | bytes 196612
  277.8 8.7 %copy-start.35 = (bf16[512,256]{1,0:T(8,128)(2,1)S(1)}, bf16[512,256]{1,0:T(8,128)(2,1)}, u32[]{:S(2)}) copy-start(bf16[512,256]{1,0:T(8,128)(2,1)} %get-tuple-element.173) | copy-start | bytes 786436
  277.9 9.8 %collective-permute-start.24 = (bf16[1024,512]{0,1:T(8,128)(2,1)S(1)}, bf16[1024,512]{0,1:T(8,128)(2,1)S(1)}, u32[]{:S(2)}, u32[]{:S(2)}) collective-permute-start(bf16[1024,512]{0,1:T(8,128)(2,1)S(1)} %pad_maximum_fusion.1), channel_id=1, source_target_pairs={{0,1},{1,0},{2,3},{3,2},{4,5},{5,4},{6,7},{7,6},{8,9},{9,8},{10,11... | collective-permute-start | bytes 3145736 | tf_op jit(solution)/shard_map/ppermute | solution.py:45
  284.5 2.0 collective-permute-start.26
  288.6 53.5 %collective-permute-start.27 = (bf16[1024,256]{0,1:T(8,128)(2,1)S(1)}, bf16[1024,256]{0,1:T(8,128)(2,1)S(1)}, u32[]{:S(2)}, u32[]{:S(2)}) collective-permute-start(bf16[1024,256]{0,1:T(8,128)(2,1)S(1)} %fusion.10), channel_id=1, source_target_pairs={{0,2},{1,3},{2,0},{3,1},{4,6},{5,7},{6,4},{7,5},{8,10},{9,11},{10,... | collective-permute-start | bytes 1572872 | tf_op jit(solution)/shard_map/ppermute | solution.py:45
  348.3 30.1 %collective-permute-start.30 = (bf16[4,128,1024]{2,1,0:T(8,128)(2,1)}, bf16[4,128,1024]{2,1,0:T(8,128)(2,1)}, u32[]{:S(2)}, u32[]{:S(2)}) collective-permute-start(bf16[4,128,1024]{2,1,0:T(8,128)(2,1)} %pad_maximum_fusion.3), channel_id=1, source_target_pairs={{0,4},{4,0},{8,12},{12,8},{16,20},{20,16},{24,28},{28,24},{1,5},{5... | collective-permute-start | bytes 3145736 | tf_op jit(solution)/shard_map/ppermute | solution.py:45
  352.8 27.1 %collective-permute-start.28 = (bf16[1024,1024]{1,0:T(8,128)(2,1)}, bf16[1024,1024]{1,0:T(8,128)(2,1)}, u32[]{:S(2)}, u32[]{:S(2)}) collective-permute-start(bf16[1024,1024]{1,0:T(8,128)(2,1)} %convolution_convert_fusion), channel_id=1, source_target_pairs={{0,1},{1,0},{2,3},{3,2},{4,5},{5,4},{6,7},{7,6},{8,9},{9,8},{10,11... | collective-permute-start | bytes 6291464 | tf_op jit(solution)/shard_map/ppermute | solution.py:45
  356.3 22.0 %copy-start.4 = (f32[4,128,768]{2,1,0:T(8,128)S(1)}, f32[4,128,768]{2,1,0:T(8,128)}, u32[]{:S(2)}) copy-start(f32[4,128,768]{2,1,0:T(8,128)} %dynamic-slice_bitcast_fusion) | copy-start | bytes 4718596
  360.1 19.8 %copy-start.7 = (f32[1024,1024]{1,0:T(8,128)}, f32[1024,1024]{1,0:T(8,128)S(1)}, u32[]{:S(2)}) copy-start(f32[1024,1024]{1,0:T(8,128)S(1)} %fusion.6) | copy-start | bytes 12582916
  382.5 50.2 %collective-permute-start.29 = (bf16[512,1024]{1,0:T(8,128)(2,1)}, bf16[512,1024]{1,0:T(8,128)(2,1)}, u32[]{:S(2)}, u32[]{:S(2)}) collective-permute-start(bf16[512,1024]{1,0:T(8,128)(2,1)} %fusion), channel_id=1, source_target_pairs={{0,2},{1,3},{2,0},{3,1},{4,6},{5,7},{6,4},{7,5},{8,10},{9,11},{10,... | collective-permute-start | bytes 3145736 | tf_op jit(solution)/shard_map/ppermute | solution.py:45
  384.5 23.5 %all-to-all-start.1 = ((f32[32,1,352]{2,1,0:T(1,128)}), f32[32,1,352]{2,1,0:T(1,128)S(1)}, u32[]{:S(2)}, u32[]{:S(2)}) async-start(f32[32,1,352]{2,1,0:T(1,128)} %all_to_all.18), calls=%async_computation.2 | async-start | bytes 98304 | tf_op jit(solution)/shard_map/all_to_all | solution.py:130
  388.1 40.0 %collective-permute-start.31 = (bf16[128,1024]{1,0:T(8,128)(2,1)}, bf16[128,1024]{1,0:T(8,128)(2,1)S(1)}, u32[]{:S(2)}, u32[]{:S(2)}) collective-permute-start(bf16[128,1024]{1,0:T(8,128)(2,1)} %get-tuple-element.290), channel_id=1, source_target_pairs={{0,8},{4,12},{8,16},{12,20},{16,24},{20,28},{24,0},{28,4},{1,9},{5... | collective-permute-start | bytes 786440 | tf_op jit(solution)/shard_map/ppermute | solution.py:49
  389.9 38.3 %collective-permute-start.32 = (bf16[128,1024]{1,0:T(8,128)(2,1)}, bf16[128,1024]{1,0:T(8,128)(2,1)}, u32[]{:S(2)}, u32[]{:S(2)}) collective-permute-start(bf16[128,1024]{1,0:T(8,128)(2,1)} %get-tuple-element.292), channel_id=1, source_target_pairs={{0,16},{4,20},{8,24},{12,28},{16,0},{20,4},{24,8},{28,12},{1,17},{... | collective-permute-start | bytes 786440 | tf_op jit(solution)/shard_map/ppermute | solution.py:49
  392.3 36.6 %collective-permute-start.33 = (bf16[128,1024]{1,0:T(8,128)(2,1)S(1)}, bf16[128,1024]{1,0:T(8,128)(2,1)}, u32[]{:S(2)}, u32[]{:S(2)}) collective-permute-start(bf16[128,1024]{1,0:T(8,128)(2,1)S(1)} %get-tuple-element.291), channel_id=1, source_target_pairs={{0,24},{4,28},{8,0},{12,4},{16,8},{20,12},{24,16},{28,20},{1,25},{... | collective-permute-start | bytes 786440 | tf_op jit(solution)/shard_map/ppermute | solution.py:49
  426.0 11.5 %copy-start.3 = (bf16[384,1024]{1,0:T(8,128)(2,1)S(1)}, bf16[384,1024]{1,0:T(8,128)(2,1)}, u32[]{:S(2)}) copy-start(bf16[384,1024]{1,0:T(8,128)(2,1)} %reduce-scatter.2.cloned.1.call-done) | copy-start | bytes 2359300
  433.3 13.3 %all-to-all-start.2 = ((f32[32,1,128]{2,1,0:T(1,128)}), f32[32,1,128]{2,1,0:T(1,128)S(1)}, u32[]{:S(2)}, u32[]{:S(2)}) async-start(f32[32,1,128]{2,1,0:T(1,128)} %broadcast_in_dim.285), calls=%async_computation.3 | async-start | bytes 32768 | tf_op jit(solution)/shard_map/all_to_all | solution.py:130
  (30 other events, 67.3 us)
Sparse Core Ops, SparseCore 0:
  35.5 108.9 all-gather.1
  260.4 165.4 reduce-scatter.1

commit v5 on v4

--- a/solution.py
+++ b/solution.py
@@ -64,7 +64,7 @@
 def gather(shard, before):
     if lax.axis_size("dp") != 8:
         full = lax.all_gather(shard, "dp", axis=0, tiled=True)
-        return full, full
+        return full, [(full,)] * 4
     d = lax.axis_index("dp")
     rows, width = shard.shape
     place = jnp.where((d & 1) == 0, d >> 1, 7 - (d >> 1))
@@ -75,7 +75,7 @@
         return lax.dynamic_update_slice(full, part, (index * rows, jnp.int32(0)))
 
     full = put(jnp.zeros((8 * rows, width), shard.dtype), shard, 0)
-    ahead = behind = shard
+    ahead, behind, arrived = shard, shard, []
     for step in (1, 2, 3, 4):
         if step > 1:
             ahead, behind = lax.optimization_barrier((ahead, behind) + tuple(before[step - 1]))[:2]
@@ -84,9 +84,8 @@
         if step < 4:
             behind = around(behind, -1)
             full = put(full, behind, step)
-        if step == 3:
-            third = behind
-    return full, third
+        arrived.append((ahead, behind))
+    return full, arrived
 
 
 def chip_groups():
@@ -96,29 +95,14 @@
     ]
 
 
-def scatter_y(*grads):
-    if lax.axis_size("dp") != 8:
-        whole = jnp.concatenate(grads, axis=1)
-        return whole, whole
-    y = lax.axis_index("dp") & 1
-    grads = [g.reshape(4, 2, g.shape[0] // 8, g.shape[1]) for g in grads]
-
-    def rows(index, kind):
-        parts = [lax.dynamic_index_in_dim(g, index, axis=1, keepdims=False).astype(kind) for g in grads]
-        return jnp.concatenate(parts, axis=2)
-
-    sent = rows(1 - y, BF16)
-    return rows(y, F32) + swap(sent, "dp", 1).astype(F32), sent
-
-
-def scatter_z(half, *before_sum):
+def scatter_z(half):
     if lax.axis_size("dp") != 8:
         return lax.psum_scatter(half.astype(F32), "dp", scatter_dimension=0, tiled=True)
     z = lax.axis_index("dp") >> 1
     total = lax.dynamic_index_in_dim(half, z, axis=0, keepdims=False)
     for step in (1, 2, 3):
         part = lax.dynamic_index_in_dim(half, (z + step) & 3, axis=0, keepdims=False)
-        total = total + after(to_z(part.astype(BF16), step), *before_sum).astype(F32)
+        total = total + to_z(part.astype(BF16), step).astype(F32)
     return total
 
 
@@ -232,18 +216,6 @@
     return pl.ds(pl.multiple_of(block * BLOCK, BLOCK), BLOCK)
 
 
-def by_pairs(low, high, visit):
-    def pair(i, carry):
-        visit(low + 2 * i, low + 2 * i + 1)
-        return carry
-
-    lax.fori_loop(0, (high - low) >> 1, pair, 0)
-
-    @pl.when(((high - low) & 1) == 1)
-    def _():
-        visit(high - 1)
-
-
 def split_heads(source_ref, split_ref):
     def one(block, carry):
         split_ref[block] = stack_heads(source_ref[block_at(block), :])
@@ -287,12 +259,13 @@
         vals = jnp.concatenate([vs_ref[block] for block in blocks], axis=0)
         acc_ref[...] += dot(jnp.concatenate(expos, axis=1), vals)
 
-    def off_diagonal(*blocks):
-        visit(blocks, [kpos_ref[0:1, block_at(block)] >= starts for block in blocks])
-
-    by_pairs(low, step, off_diagonal)
-    cols = lax.broadcasted_iota(jnp.int32, (BLOCK, BLOCK), 1) + base
-    visit([step], [((kpos_ref[0:1, block_at(step)] >= starts) & (cols <= rows)) | (cols == rows)])
+    def one(block, carry):
+        cols = lax.broadcasted_iota(jnp.int32, (BLOCK, BLOCK), 1) + block * BLOCK
+        same = kpos_ref[0:1, block_at(block)] >= starts
+        visit([block], [(same & (cols <= rows)) | (cols == rows)])
+        return carry
+
+    lax.fori_loop(low, step + 1, one, 0)
     lane = lax.broadcasted_iota(jnp.int32, (BLOCK, q_ref.shape[1]), 1) // HEAD
     inverse = jnp.zeros((BLOCK, q_ref.shape[1]), F32)
     for h in range(heads):
@@ -421,15 +394,22 @@
         split = jnp.concatenate([ks_ref[block + i] for i in range(count)], axis=0)
         dq_ref[...] += dot(jnp.concatenate(pieces, axis=0), split, 0, 0)
 
-    def off_diagonal(*blocks):
-        keys_at = pl.ds(pl.multiple_of(blocks[0] * BLOCK, BLOCK), len(blocks) * BLOCK)
-        again = jnp.concatenate([starts] * len(blocks), axis=0)
-        visit(blocks[0], len(blocks), wide(kpos_ref[keys_at, :]) >= again)
-
-    by_pairs(low, step, off_diagonal)
-    rows = lax.broadcasted_iota(jnp.int32, (BLOCK, BLOCK), 0) + base
-    key_slots = wide(kpos_ref[block_at(step), :])
-    visit(step, 1, ((key_slots >= starts) & (rows <= cols)) | (rows == cols))
+    pairs = (step - low) >> 1
+
+    def pair(i, carry):
+        block = low + 2 * i
+        keys_at = pl.ds(pl.multiple_of(block * BLOCK, BLOCK), 2 * BLOCK)
+        visit(block, 2, wide(kpos_ref[keys_at, :]) >= jnp.concatenate([starts, starts], axis=0))
+        return carry
+
+    def one(block, carry):
+        rows = lax.broadcasted_iota(jnp.int32, (BLOCK, BLOCK), 0) + block * BLOCK
+        same = wide(kpos_ref[block_at(block), :]) >= starts
+        visit(block, 1, (same & (rows <= cols)) | (rows == cols))
+        return carry
+
+    lax.fori_loop(0, pairs, pair, 0)
+    lax.fori_loop(low + 2 * pairs, step + 1, one, 0)
 
     scale = sqk_ref[0:1, :]
     here = pl.ds(pl.multiple_of(base, BLOCK), BLOCK)
@@ -678,6 +658,95 @@
     )(*lefts, *rights)
 
 
+def attn_grad_body(m_ref, xf_ref, xs_ref, g_ref, out_ref, over_ref, mine_ref, sent_ref, xt_ref, sum_ref):
+    t = pl.program_id(0)
+    rows = xf_ref.shape[0]
+    y = m_ref[1]
+
+    @pl.when(t == 0)
+    def _():
+        def one(block, carry):
+            for start, ref in ((0, xf_ref), (rows, xs_ref)):
+                at = pl.ds(pl.multiple_of(start + block * BLOCK, BLOCK), BLOCK)
+                xt_ref[:, at] = ref[block_at(block), :].T
+            return carry
+
+        lax.fori_loop(0, rows // BLOCK, one, 0)
+
+    @pl.when(t < 3)
+    def _():
+        sum_ref[...] = dot(xt_ref[...], g_ref[...]).reshape(sum_ref.shape)
+
+    @pl.when(t == 3)
+    def _():
+        sum_ref[...] = (out_ref[...] + over_ref[...].astype(F32)).reshape(sum_ref.shape)
+
+    mine_ref[...] = sum_ref[:, y]
+    sent_ref[...] = sum_ref[:, 1 - y].astype(BF16)
+
+
+def attn_grads(place, x_first, x_second, grads, out_sum, over_out):
+    width = out_sum.shape[1]
+    rows = D // lax.axis_size("dp")
+
+    def whole(array):
+        return pl.BlockSpec(array.shape, lambda t, m: (0, 0))
+
+    half = (D // rows // 2, rows, width)
+    out = pl.BlockSpec(half, lambda t, m: (0, 0, t))
+    return pl.pallas_call(
+        attn_grad_body,
+        out_shape=[
+            jax.ShapeDtypeStruct(half[:2] + (4 * width,), F32),
+            jax.ShapeDtypeStruct(half[:2] + (4 * width,), BF16),
+        ],
+        grid_spec=pltpu.PrefetchScalarGridSpec(
+            num_scalar_prefetch=1,
+            grid=(4,),
+            in_specs=[
+                whole(x_first),
+                whole(x_second),
+                pl.BlockSpec((grads.shape[0], width), lambda t, m: (0, jnp.minimum(t, 2))),
+                whole(out_sum),
+                whole(over_out),
+            ],
+            out_specs=[out, out],
+            scratch_shapes=[
+                pltpu.VMEM((D, grads.shape[0]), BF16),
+                pltpu.VMEM((half[0], 2) + half[1:], F32),
+            ],
+        ),
+        cost_estimate=pl.CostEstimate(
+            flops=2 * D * grads.size, bytes_accessed=4 * grads.size, transcendentals=0
+        ),
+        name="attn_grads",
+    )(place, x_first, x_second, grads, out_sum, over_out)
+
+
+def to_tokens(grads, half, weight, kind):
+    rows, width = grads.shape[0] // 2, grads.shape[1]
+    step = rows // 2
+    row = weight.shape[0]
+
+    def body(g_ref, w_ref, out_ref):
+        out_ref[...] = dot(g_ref[...], w_ref[...], 1, 1).astype(kind)
+
+    return pl.pallas_call(
+        body,
+        out_shape=jax.ShapeDtypeStruct((rows, row), kind),
+        grid=(2,),
+        in_specs=[
+            pl.BlockSpec((step, width), lambda i: (2 * half + i, 0)),
+            pl.BlockSpec((row, width), lambda i: (0, 0)),
+        ],
+        out_specs=pl.BlockSpec((step, row), lambda i: (i, 0)),
+        cost_estimate=pl.CostEstimate(
+            flops=2 * rows * width * row, bytes_accessed=6 * rows * row, transcendentals=0
+        ),
+        name="to_tokens",
+    )(grads, weight)
+
+
 def own_call(body, name, rows_in, vectors, wholes, outs, sums, flops):
     count = outs[0][0]
     blocks = count // BLOCK
@@ -731,13 +800,17 @@
     keep_ref[...] = grad_two * (1.0 - alpha)
     gm_ref[...] = normed_back(grad_two * alpha, h_mlp, mlp_factor).astype(BF16)
 
-    sum_ref[0:1, :] = jnp.sum(grad_two * step, axis=0, keepdims=True)
+    @pl.when(pl.program_id(0) == 0)
+    def _():
+        sum_ref[...] = jnp.zeros_like(sum_ref)
+
+    sum_ref[0:1, :] += jnp.sum(grad_two * step, axis=0, keepdims=True)
 
 
 def turn(chunk, own, far, branch, x_rows, cotangent, one, two, previous):
     count = branch.shape[0]
-    rows = pl.BlockSpec((BLOCK, D), lambda i: (chunk, 0))
-    first = pl.BlockSpec((BLOCK, D), lambda i: (0, 0))
+    rows = pl.BlockSpec((BLOCK // 2, D), lambda i: (2 * chunk + i, 0))
+    first = pl.BlockSpec((BLOCK // 2, D), lambda i: (i, 0))
     vector = pl.BlockSpec((1, D), lambda i: (0, 0))
     total = pl.BlockSpec((8, D), lambda i: (0, 0))
     extra = list(previous)
@@ -749,7 +822,7 @@
             jax.ShapeDtypeStruct((BLOCK, D), BF16),
             jax.ShapeDtypeStruct((8, D), F32),
         ],
-        grid=(1,),
+        grid=(2,),
         in_specs=[rows, first, rows, rows, rows, vector, vector]
         + [pl.BlockSpec(memory_space=pl.ANY)] * len(extra),
         out_specs=[rows, rows, first, total],
@@ -832,16 +905,16 @@
     cosine = slot_cos * start_cos + slot_sin * start_sin
     sine = slot_sin * start_cos - slot_cos * start_sin
     x_halves = [swap(tokens[i * local // 2 : (i + 1) * local // 2], "mp", 2) for i in range(2)]
-    x_first = jnp.concatenate([tokens] + x_halves, axis=0)
     vector = jnp.concatenate([s_up, s_gate, s_qk, alpha_attn, alpha_mlp])[None]
     every = to_all(jnp.broadcast_to(vector, (devices, vector.shape[1])))
-    attn, third = gather(
+    attn, arrived = gather(
         jnp.concatenate([w_query, w_key, w_value, w_out.T], axis=1),
         [(), (), (x_halves[0],), (x_halves[1], every)],
     )
+    x_first = jnp.concatenate([tokens, x_halves[0], after(x_halves[1], *arrived[2])], axis=0)
     x_second = swap(x_first, "mp", 1)
     shard = jnp.concatenate([w_up, w_gate, w_down.T], axis=0)
-    shard = with_layout_constraint(after(shard, third), Layout(major_to_minor=(0, 1)))
+    shard = with_layout_constraint(after(shard, *arrived[2]), Layout(major_to_minor=(0, 1)))
     weights = lax.all_gather(
         shard, ("dp", "mp"), axis=0, tiled=True, axis_index_groups=chip_groups()
     ).reshape(-1, 2, 3, shard.shape[0] // 3, part)
@@ -949,18 +1022,21 @@
     core_out = swap(jnp.concatenate([outs[1], outs[3]], axis=1).astype(BF16), "mp", 1)
     core_out, g_att = lax.optimization_barrier((core_out, g_att))
     over_out = swap((outs[2] + core_out[:, width:].astype(F32)).astype(BF16), "mp", 2)
-    grad_out = outs[0] + core_out[:, :width].astype(F32) + over_out.astype(F32)
+    out_sum = outs[0] + core_out[:, :width].astype(F32)
     grads, g_sqk = attend_back(
         meta, queries, qrot, attended, inverse_mass, g_att, keys, vals, krot, kpos_cols, cosine, sine, sqk, docs
     )
-    first, second = grads[: 2 * local], grads[2 * local :]
-    qkv_sum = dot(x_first, first, 0, 0) + dot(x_second, second, 0, 0)
-    half_sum, sent = scatter_y(qkv_sum, grad_out)
+    if lax.axis_size("dp") == 8:
+        both = jnp.stack([m, lax.axis_index("dp").astype(jnp.int32) & 1])
+        half_sum, sent = attn_grads(both, x_first, x_second, grads, out_sum, over_out)
+        half_sum = half_sum + swap(sent, "dp", 1).astype(F32)
+    else:
+        sent = dot(x_first, grads[: 2 * local], 0, 0) + dot(x_second, grads[2 * local :], 0, 0)
+        half_sum = jnp.concatenate([sent, out_sum + over_out.astype(F32)], axis=1)
     mlp_squares = jnp.sum(grad_mlp * grad_mlp)
-    qkv = after(attn, sent)[:, : 3 * width]
-    second_tokens = dot(second, qkv, 1, 1).astype(BF16)
+    second_tokens = to_tokens(after(grads, sent), 1, attn, BF16)
     to_core = swap(second_tokens, "mp", 1)
-    partial = dot(first, after(qkv, second_tokens), 1, 1)
+    partial = to_tokens(after(grads, second_tokens), 0, attn, F32)
     for_x = (partial[local:] + to_core[local:].astype(F32)).astype(BF16)
     to_x = swap(for_x, "mp", 2)
 
@@ -984,10 +1060,10 @@
     def squared(*arrays):
         return sum(jnp.sum(array * array) for array in arrays)
 
-    grad_attn = scatter_z(after(half_sum, for_x), mlp_squares)
+    grad_attn = scatter_z(after(half_sum, for_x))
     squares = mlp_squares + squared(grad_attn, small)
     g_qkv = [grad_attn[:, i * width : (i + 1) * width] for i in range(3)]
-    grad_down, grad_out = turned(grad_down), turned(grad_attn[:, 3 * width :])
+    grad_down, grad_out = turned(after(grad_down, squares)), turned(after(grad_attn, squares)[:, 3 * width :])
     to_x = after(to_x, squares)
     grad_tokens = grad_x + partial[:local] + to_core[:local].astype(F32) + to_x.astype(F32)
     pieces = tuple(g_qkv) + (grad_out, grad_up, grad_gate, grad_down)

time: 457 us -> 451 us (0.987)
  Pallas kernels: 187 us -> 202 us
  matrix products: 20.4 us -> 6.43 us
    pallas_call x0 -> x3, Pallas kernels: none -> 20.3 us  [the longest x1 10.4 us: attn_grads(): pl.pallas_call(attn_grad_body, out_shape=[jax.ShapeDtypeStruct(half[:2] +...]
    reduce_scatter x1, waiting for transfers between devices: 16.1 us -> 0.01 us  [shards(): lax.psum_scatter(grad_mlp.reshape(-1, part), ('dp', 'mp'), scatter_dimens...]
    dot_general x8 -> x4, matrix products: 20.4 us -> 6.43 us  [dot(): lax.dot_general(left, right, (((left_dim,), (right_dim,)), ((), ())), pre...]
    all_gather x1, waiting for transfers between devices: 5.58 us -> 17.2 us  [shards(): lax.all_gather(shard, ('dp', 'mp'), axis=0, tiled=True, axis_index_groups...]
    ppermute x24, waiting for transfers between devices: 35.1 us -> 45.2 us  [swap(): return lax.ppermute(array, axis, [(i, i ^ bit) for i in range(size)])]
    ppermute x7, waiting for transfers between devices: 32.4 us -> 23.8 us  [around(): lax.ppermute(array, 'dp', [(RING[p], RING[(p + step) % 8]) for p in range...]
    ppermute x7, starting transfers between devices: 14.2 us -> 9.09 us  [around(): lax.ppermute(array, 'dp', [(RING[p], RING[(p + step) % 8]) for p in range...]
    unnamed x117 -> x103, local copies, waits for them, and re-layouts: 14.8 us -> 13.9 us
  transfers between devices with their start and end apart: 39 -> 39, of which waited for: 17 -> 16; matrix products, arithmetic and copies ran while one was open for 18% -> 14% of each run, Pallas kernels for 41% -> 45%
where the time goes in v5:
time: 451 us; the launch traced here: 447 us
  Pallas kernels  202 us (45%)
  waiting for transfers between devices  102 us (23%)
  starting transfers between devices  48.6 us (11%)
  local copies, waits for them, and re-layouts  38.4 us (9%)
  other arithmetic  29.1 us (6%)
  between operations  19.9 us (4%)
  matrix products  6.43 us (1%)
    ppermute x24, waiting for transfers between devices, swap(): return lax.ppermute(array, axis, [(i, i ^ bit) for i in range(size)])  45.2 us
    pallas_call x1, Pallas kernels, attend_back(): pl.pallas_call(functools.partial(back_body, docs), out_shape=[jax.ShapeDt...  37.8 us
    pallas_call x3, Pallas kernels, ffn_backward(): pl.pallas_call(functools.partial(backward_body, len(grads)), out_shape=[j...  34.4 us
    pallas_call x3, Pallas kernels, ffn_forward(): pl.pallas_call(forward_body, out_shape=[jax.ShapeDtypeStruct((2, count, h...  32.2 us
    ppermute x7, waiting for transfers between devices, around(): lax.ppermute(array, 'dp', [(RING[p], RING[(p + step) % 8]) for p in range...  23.8 us
    pallas_call x2, Pallas kernels, attend(): pl.pallas_call(functools.partial(attend_body, docs, first), out_shape=[ja...  21.2 us
    pallas_call x1, Pallas kernels, weight_grads(): pl.pallas_call(functools.partial(weight_body, (len(hs), len(ups), len(ms)...  20.5 us
    ppermute x24, starting transfers between devices, swap(): return lax.ppermute(array, axis, [(i, i ^ bit) for i in range(size)])  20.3 us
  transfers between devices with their start and end apart: 39, of which 16 were waited for; matrix products, arithmetic and copies ran while one was open for 14% of the time, Pallas kernels for 45%

profile of v5, /device:TPU:0, one launch (start us, length us, event | category | flops | bytes accessed | tf_op | source)
XLA Modules:
  0.0 446.7 jit_solution(9211539234626899300)
XLA Ops:
  8.7 3.1 collective-permute-start.2
  12.7 1.9 collective-permute-start
  14.6 3.4 collective-permute-done.2
  18.1 1.5 collective-permute-done.3
  19.6 1.6 collective-permute-start.4
  21.6 4.9 %collective-permute-done.4 = bf16[128,1024]{1,0:T(8,128)(2,1)} collective-permute-done((bf16[128,1024]{1,0:T(8,128)(2,1)S(1)}, bf16[128,1024]{1,0:T(8,128)(2,1)}, u32[]{:S(2)}, u32[]{:S(2)}) %collective-permute-start.4) | collective-permute-done | bytes 262176 | tf_op jit(solution)/shard_map/ppermute | solution.py:55
  26.5 1.3 collective-permute-done.5
  27.8 1.6 collective-permute-start.6
  31.0 2.0 pad_maximum_fusion.3
  33.0 1.6 collective-permute-done.6
  34.5 1.6 collective-permute-done.7
  36.2 1.6 collective-permute-start.1
  38.5 2.8 all-to-all-start
  42.9 1.3 iota_compare_fusion
  47.5 1.9 constant_dynamic-update-slice_fusion.x_ref.xf_ref
  49.7 3.1 fusion.5
  55.8 1.9 collective-permute-start.9
  60.7 9.5 %collective-permute-done.9 = bf16[128,1024]{1,0:T(8,128)(2,1)S(1)} collective-permute-done((bf16[128,1024]{1,0:T(8,128)(2,1)}, bf16[128,1024]{1,0:T(8,128)(2,1)S(1)}, u32[]{:S(2)}, u32[]{:S(2)}) %collective-permute-start.9) | collective-permute-done | bytes 262176 | tf_op jit(solution)/shard_map/ppermute | solution.py:55
  70.3 1.5 collective-permute-start.14
  71.8 6.8 %project.2 = (bf16[2048,256]{1,0:T(8,128)(2,1)}, bf16[2048,256]{1,0:T(8,128)(2,1)}, bf16[2048,256]{1,0:T(8,128)(2,1)}, f32[2048,256]{1,0:T(8,128)}, f32[2048,256]{1,0:T(8,128)}) custom-call(s32[1]{0:T(128)} %bitcast.m_ref, bf16[1024,1024]{1,0:T(8,128)(2,1)} %constant_dynamic-update-slice_fusion.x_ref.xf_ref, bf16[1024,1024]{1,0:T(8,128)(2,1)} %copy-done, ...), custom_call_target="tpu_custom_call" | custom-call | flops 1610612736 | bytes 8388608 | tf_op jit(solution)/shard_map/project/pallas_call | solution.py:167
  78.6 7.0 %project.3 = (bf16[2048,256]{1,0:T(8,128)(2,1)}, bf16[2048,256]{1,0:T(8,128)(2,1)}, bf16[2048,256]{1,0:T(8,128)(2,1)}, f32[2048,256]{1,0:T(8,128)}, f32[2048,256]{1,0:T(8,128)}) custom-call(s32[1]{0:T(128)} %bitcast.m_ref, ...), custom_call_target="tpu_custom_call", output_to_operand_aliasing={{0}: (6, {}), {1}: (7, {}), {2}: (8, {}), {3}: (9, {}), {4}... | custom-call | flops 1610612736 | bytes 8388608 | tf_op jit(solution)/shard_map/project/pallas_call | solution.py:167
  85.6 11.2 %attend.2 = (bf16[2048,256]{1,0:T(8,128)(2,1)}, f32[2048,256]{1,0:T(8,128)}) custom-call(s32[5]{0:T(128)} %pad_add_fusion.meta_ref, bf16[2048,256]{1,0:T(8,128)(2,1)} %get-tuple-element.122.q_ref, bf16[2048,256]{1,0:T(8,128)(2,1)} %get-tuple-element.123.k_ref, bf16[2048,256]{1,0:T(8,128)(2,1)} %get-tuple-element.124.v_ref, s32[1,2048]{1,0:T(1,128)} %compare_select_fusion.kpos_ref), custom_call_target="tpu_custom_call" | custom-call | flops 8000000000 | bytes 4194304 | tf_op jit(solution)/shard_map/attend/pallas_call | solution.py:290
  99.6 10.0 %attend.3 = (bf16[2048,256]{1,0:T(8,128)(2,1)}, f32[2048,256]{1,0:T(8,128)}) custom-call(s32[5]{0:T(128)} %pad_add_fusion.meta_ref, bf16[2048,256]{1,0:T(8,128)(2,1)} %get-tuple-element.122.q_ref, bf16[2048,256]{1,0:T(8,128)(2,1)} %get-tuple-element.123.k_ref, ...), custom_call_target="tpu_custom_call", output_to_operand_aliasing={{0}: (5, {}), {1}: (6, {})} | custom-call | flops 8000000000 | bytes 4194304 | tf_op jit(solution)/shard_map/attend/pallas_call | solution.py:290
  109.6 1.7 slice.178
  115.1 5.1 %attn_out.1 = (f32[512,1024]{1,0:T(8,128)}, bf16[512,1024]{1,0:T(8,128)(2,1)}) custom-call(bf16[2048,256]{1,0:T(8,128)(2,1)} %get-tuple-element.128.a0.o_ref, bf16[512,256]{1,0:T(8,128)(2,1)} %copy-done.17, bf16[1024,256]{1,0:T(8,128)(2,1)} %copy-done.4, bf16[1024,256]{1,0:T(8,128)(2,1)} %copy-done.4, bf16[512,1024]{1,0:T(8,128)(2,1)} %x_ref.7, ...), custom_call_target="tpu_custom_call" | custom-call | flops 1073741824 | bytes 10485760 | tf_op jit(solution)/shard_map/attn_out/pallas_call | solution.py:764
  120.2 1.4 fusion.18
  121.5 3.0 collective-permute-start.17
  124.7 17.2 %all-gather.2.cloned.1.call-done = bf16[6144,1024]{1,0:T(8,128)(2,1)} async-done(((bf16[384,1024]{1,0:T(8,128)(2,1)}), bf16[6144,1024]{1,0:T(8,128)(2,1)}) %all-gather.2.cloned.1.call-update) | async-done | bytes 12582928 | tf_op jit(solution)/shard_map/all_gather | solution.py:918
  141.8 13.5 %ffn_forward.3 = (bf16[2,512,1024]{2,1,0:T(8,128)(2,1)}, bf16[2,512,1024]{2,1,0:T(8,128)(2,1)}, bf16[2,512,1024]{2,1,0:T(8,128)(2,1)}, bf16[2,512,1024]{2,1,0:T(8,128)(2,1)}, f32[512,1024]{1,0:T(8,128)}) custom-call(bf16[512,1024]{1,0:T(8,128)(2,1)} %get-tuple-element.129.h_ref.refs_0_, bf16[8,2,3,128,1024]{4,3,2,1,0:T(8,128)(2,1)} %bitcast.106, ...), custom_call_target="tpu_custom_call" | custom-call | flops 6442450944 | bytes 18874368 | tf_op jit(solution)/shard_map/ffn_forward/pallas_call | solution.py:546
  156.2 9.2 %ffn_forward.4 = (bf16[2,256,1024]{2,1,0:T(8,128)(2,1)}, bf16[2,256,1024]{2,1,0:T(8,128)(2,1)}, bf16[2,256,1024]{2,1,0:T(8,128)(2,1)}, bf16[2,256,1024]{2,1,0:T(8,128)(2,1)}, bf16[256,1024]{1,0:T(8,128)(2,1)}) custom-call(bf16[256,1024]{1,0:T(8,128)(2,1)} %copy-done.9, bf16[8,2,3,128,1024]{4,3,2,1,0:T(8,128)(2,1)} %bitcast.107, ...), custom_call_target="tpu_custom_call" | custom-call | flops 3221225472 | bytes 15728640 | tf_op jit(solution)/shard_map/ffn_forward/pallas_call | solution.py:546
  165.5 1.6 collective-permute-start.19
  167.9 9.4 %ffn_forward.5 = (bf16[2,256,1024]{2,1,0:T(8,128)(2,1)}, bf16[2,256,1024]{2,1,0:T(8,128)(2,1)}, bf16[2,256,1024]{2,1,0:T(8,128)(2,1)}, bf16[2,256,1024]{2,1,0:T(8,128)(2,1)}, bf16[256,1024]{1,0:T(8,128)(2,1)}) custom-call(bf16[256,1024]{1,0:T(8,128)(2,1)} %copy-done.10, bf16[8,2,3,128,1024]{4,3,2,1,0:T(8,128)(2,1)} %bitcast.108, ...), custom_call_target="tpu_custom_call" | custom-call | flops 3221225472 | bytes 15728640 | tf_op jit(solution)/shard_map/ffn_forward/pallas_call | solution.py:546
  178.5 1.4 collective-permute-done.19.far_ref
  180.6 4.0 turn.2
  184.6 2.3 collective-permute-start.20
  186.9 5.5 %collective-permute-done.18.far_ref = bf16[256,1024]{1,0:T(8,128)(2,1)S(1)} collective-permute-done((bf16[256,1024]{1,0:T(8,128)(2,1)}, bf16[256,1024]{1,0:T(8,128)(2,1)S(1)}, u32[]{:S(2)}, u32[]{:S(2)}) %collective-permute-start.18) | collective-permute-done | bytes 524320 | tf_op jit(solution)/shard_map/ppermute | solution.py:45
  193.2 4.2 turn.3
  198.4 14.2 %ffn_backward.3 = (bf16[2,512,1024]{2,1,0:T(8,128)(2,1)}, bf16[2,512,1024]{2,1,0:T(8,128)(2,1)}, f32[2,8,1024]{2,1,0:T(8,128)}, f32[2,8,1024]{2,1,0:T(8,128)}, f32[512,1024]{1,0:T(8,128)}) custom-call(bf16[256,1024]{1,0:T(8,128)(2,1)} %get-tuple-element.141.refs_0_.refs_3_, bf16[256,1024]{1,0:T(8,128)(2,1)} %get-tuple-element.142.refs_1_.refs_4_, ...), custom_call_target="tpu_custom_call" | custom-call | flops 6442450944 | bytes 25165824 | tf_op jit(solution)/shard_map/ffn_backward/pallas_call | solution.py:590
  213.4 10.1 %ffn_backward.4 = (bf16[2,256,1024]{2,1,0:T(8,128)(2,1)}, bf16[2,256,1024]{2,1,0:T(8,128)(2,1)}, f32[2,8,1024]{2,1,0:T(8,128)}, f32[2,8,1024]{2,1,0:T(8,128)}, bf16[256,1024]{1,0:T(8,128)(2,1)}) custom-call(bf16[256,1024]{1,0:T(8,128)(2,1)} %copy-done.11, bf16[8,2,3,128,1024]{4,3,2,1,0:T(8,128)(2,1)} %bitcast.110, ...), custom_call_target="tpu_custom_call" | custom-call | flops 3221225472 | bytes 18874368 | tf_op jit(solution)/shard_map/ffn_backward/pallas_call | solution.py:590
  225.5 10.1 %ffn_backward.5 = (bf16[2,256,1024]{2,1,0:T(8,128)(2,1)}, bf16[2,256,1024]{2,1,0:T(8,128)(2,1)}, f32[2,8,1024]{2,1,0:T(8,128)}, f32[2,8,1024]{2,1,0:T(8,128)}, bf16[256,1024]{1,0:T(8,128)(2,1)}) custom-call(bf16[256,1024]{1,0:T(8,128)(2,1)} %copy-done.12, bf16[8,2,3,128,1024]{4,3,2,1,0:T(8,128)(2,1)} %bitcast.111, ...), custom_call_target="tpu_custom_call" | custom-call | flops 3221225472 | bytes 18874368 | tf_op jit(solution)/shard_map/ffn_backward/pallas_call | solution.py:590
  236.6 20.5 %weight_grads.1 = bf16[8,2,3,128,1024]{4,3,2,1,0:T(8,128)(2,1)} custom-call(bf16[512,1024]{1,0:T(8,128)(2,1)} %get-tuple-element.129.h_ref.refs_0_, bf16[256,1024]{1,0:T(8,128)(2,1)} %copy-done.9, bf16[256,1024]{1,0:T(8,128)(2,1)} %copy-done.10, bf16[256,1024]{1,0:T(8,128)(2,1)} %get-tuple-element.141.refs_0_.refs_3_, ...), custom_call_target="tpu_custom_call" | custom-call | flops 12884901888 | bytes 25165824 | tf_op jit(solution)/shard_map/weight_grads/pallas_call | solution.py:645
  258.7 9.0 %attn_back_out.1 = (bf16[512,1024]{1,0:T(8,128)(2,1)}, f32[512,1024]{1,0:T(8,128)}, bf16[512,256]{1,0:T(8,128)(2,1)}, bf16[512,256]{1,0:T(8,128)(2,1)}, bf16[512...) custom-call(f32[512,1024]{1,0:T(8,128)} %get-tuple-element.147.own_ref, ...), custom_call_target="tpu_custom_call" | custom-call | flops 1073741824 | bytes 10485760 | tf_op jit(solution)/shard_map/attn_back_out/pallas_call | solution.py:764
  270.1 1.8 convolution_convert_fusion.1
  272.6 7.7 %collective-permute-done.25 = bf16[1024,256]{1,0:T(8,128)(2,1)S(1)} collective-permute-done((bf16[1024,256]{1,0:T(8,128)(2,1)S(1)}, bf16[1024,256]{1,0:T(8,128)(2,1)S(1)}, u32[]{:S(2)}, u32[]{:S(2)}) %collective-permute-start.25) | collective-permute-done | bytes 524320 | tf_op jit(solution)/shard_map/ppermute | solution.py:45
  284.2 1.5 fusion.3
  286.3 1.3 broadcast_in_dim.258.kpos_ref
  287.6 37.8 %attend_back.1 = (bf16[2048,768]{1,0:T(8,128)(2,1)}, f32[8,256]{1,0:T(8,128)}) custom-call(s32[5]{0:T(128)} %pad_add_fusion.meta_ref, bf16[2048,256]{1,0:T(8,128)(2,1)} %get-tuple-element.122.q_ref, f32[2048,256]{1,0:T(8,128)} %get-tuple-element.170.qr_ref, bf16[2048,256]{1,0:T(8,128)(2,1)} %get-tuple-element.128.a0.o_ref, ...), custom_call_target="tpu_custom_call" | custom-call | flops 40000000000 | bytes 6291456 | tf_op jit(solution)/shard_map/attend_back/pallas_call | solution.py:455
  325.4 2.6 convolution_add_fusion.1.out_ref
  328.8 10.4 %attn_grads.1 = (f32[4,128,1024]{2,1,0:T(8,128)}, bf16[4,128,1024]{2,1,0:T(8,128)(2,1)}) custom-call(s32[2]{0:T(128)} %pad_add_fusion.1.m_ref, bf16[1024,1024]{1,0:T(8,128)(2,1)} %constant_dynamic-update-slice_fusion.x_ref.xf_ref, bf16[1024,1024]{1,0:T(8,128)(2,1)} %collective-permute-done.8.x_ref.xs_ref, bf16[2048,768]{1,0:T(8,128)(2,1)} %get-tuple-element.183.g_ref, ...), custom_call_target="tpu_custom_call" | custom-call | flops 3221225472 | bytes 6291456 | tf_op jit(solution)/shard_map/attn_grads/pallas_call | solution.py:697
  339.2 4.8 %to_tokens.2 = bf16[1024,1024]{1,0:T(8,128)(2,1)} custom-call(bf16[2048,768]{1,0:T(8,128)(2,1)} %get-tuple-element.183.g_ref, bf16[1024,1024]{1,0:T(8,128)(2,1)} %copy-done), custom_call_target="tpu_custom_call" | custom-call | flops 1610612736 | bytes 6291456 | tf_op jit(solution)/shard_map/to_tokens/pallas_call | solution.py:734
  346.3 5.1 %to_tokens.3 = f32[1024,1024]{1,0:T(8,128)} custom-call(bf16[2048,768]{1,0:T(8,128)(2,1)} %get-tuple-element.183.g_ref, bf16[1024,1024]{1,0:T(8,128)(2,1)} %copy-done), custom_call_target="tpu_custom_call" | custom-call | flops 1610612736 | bytes 6291456 | tf_op jit(solution)/shard_map/to_tokens/pallas_call | solution.py:734
  351.4 29.4 %collective-permute-done.30 = bf16[4,128,1024]{2,1,0:T(8,128)(2,1)S(1)} collective-permute-done((bf16[4,128,1024]{2,1,0:T(8,128)(2,1)S(1)}, bf16[4,128,1024]{2,1,0:T(8,128)(2,1)S(1)}, u32[]{:S(2)}, u32[]{:S(2)}) %collective-permute-start.30) | collective-permute-done | bytes 1048608 | tf_op jit(solution)/shard_map/ppermute | solution.py:45
  380.8 2.0 convert_add_fusion
  383.7 2.6 fusion
  386.3 1.5 collective-permute-start.29
  388.4 2.6 all-to-all-start.1
  391.8 1.7 collective-permute-start.31
  393.5 2.5 collective-permute-start.32
  396.0 1.4 collective-permute-start.33
  397.4 14.6 %all-to-all-done.1 = f32[32,1,352]{2,1,0:T(1,128)S(1)} async-done(((f32[32,1,352]{2,1,0:T(1,128)}), f32[32,1,352]{2,1,0:T(1,128)S(1)}, u32[]{:S(2)}, u32[]{:S(2)}) %all-to-all-start.1) | async-done | bytes 45088 | tf_op jit(solution)/shard_map/all_to_all | solution.py:114
  417.7 2.1 multiply_reduce_fusion
  421.1 8.2 %all-to-all-start.2 = ((f32[32,1,128]{2,1,0:T(1,128)}), f32[32,1,128]{2,1,0:T(1,128)S(1)}, u32[]{:S(2)}, u32[]{:S(2)}) async-start(f32[32,1,128]{2,1,0:T(1,128)} %broadcast_in_dim.285), calls=%async_computation.3 | async-start | bytes 32768 | tf_op jit(solution)/shard_map/all_to_all | solution.py:114
  429.3 2.3 fusion.21
  431.5 4.9 %fusion.2 = f32[512,1024]{1,0:T(8,128)} fusion(f32[512,1024]{1,0:T(8,128)} %get-tuple-element.169, f32[1024,1024]{1,0:T(8,128)} %to_tokens.3, bf16[512,1024]{1,0:T(8,128)(2,1)} %collective-permute-done.29, bf16[1024,1024]{1,0:T(8,128)(2,1)} %collective-permute-done.28), kind=kLoop, calls=%fused_computation.4 | loop fusion | flops 2621440 | bytes 8388608 | tf_op jit(solution)/shard_map/add | solution.py:1068
  (239 shorter events, 51.6 us)
Async XLA Ops:
  7.2 134.6 %all-gather.2.cloned.1.call-start = ((), (), s32[]{:S(2)}) async-start(), calls=%async_computation.4 | async-start | bytes 13369344 | tf_op jit(solution)/shard_map/all_gather | solution.py:918
  8.7 29.1 %copy-start.37 = (f32[128]{0:T(128)S(1)}, f32[128]{0:T(128)}, u32[]{:S(2)}) copy-start(f32[128]{0:T(128)} %param.28) | copy-start | bytes 1540
  8.7 29.1 %copy-start.38 = (f32[128]{0:T(128)S(1)}, f32[128]{0:T(128)}, u32[]{:S(2)}) copy-start(f32[128]{0:T(128)} %param.29) | copy-start | bytes 1540
  8.7 29.1 %copy-start.39 = (f32[32]{0:T(128)S(1)}, f32[32]{0:T(128)}, u32[]{:S(2)}) copy-start(f32[32]{0:T(128)} %param.27) | copy-start | bytes 388
  8.7 29.0 %copy-start.40 = (f32[32]{0:T(128)S(1)}, f32[32]{0:T(128)}, u32[]{:S(2)}) copy-start(f32[32]{0:T(128)} %param.30) | copy-start | bytes 388
  8.7 29.0 %copy-start.41 = (f32[32]{0:T(128)S(1)}, f32[32]{0:T(128)}, u32[]{:S(2)}) copy-start(f32[32]{0:T(128)} %param.31) | copy-start | bytes 388
  8.7 9.3 %collective-permute-start.2 = (bf16[128,1024]{1,0:T(8,128)(2,1)S(1)}, bf16[128,1024]{1,0:T(8,128)(2,1)S(1)}, u32[]{:S(2)}, u32[]{:S(2)}) collective-permute-start(bf16[128,1024]{1,0:T(8,128)(2,1)S(1)} %get-tuple-element.298), channel_id=1, source_target_pairs={{0,8},{8,16},{16,24},{24,28},{28,20},{20,12},{12,4},{4,0},{1,9},{9... | collective-permute-start | bytes 786440 | tf_op jit(solution)/shard_map/ppermute | solution.py:55
  11.8 7.8 %collective-permute-start.3 = (bf16[128,1024]{1,0:T(8,128)(2,1)S(1)}, bf16[128,1024]{1,0:T(8,128)(2,1)S(1)}, u32[]{:S(2)}, u32[]{:S(2)}) collective-permute-start(bf16[128,1024]{1,0:T(8,128)(2,1)S(1)} %get-tuple-element.298), channel_id=1, source_target_pairs={{0,4},{8,0},{16,8},{24,16},{28,24},{20,28},{12,20},{4,12},{1,5},{9... | collective-permute-start | bytes 786440 | tf_op jit(solution)/shard_map/ppermute | solution.py:55
  12.7 28.8 %copy-start.42 = (s32[1,4]{1,0:T(1,128)S(1)}, s32[1,4]{1,0:T(1,128)}, u32[]{:S(2)}) copy-start(s32[1,4]{1,0:T(1,128)} %param.18) | copy-start | bytes 52
  12.7 15.2 %collective-permute-start = (bf16[256,1024]{1,0:T(8,128)(2,1)S(1)}, bf16[256,1024]{1,0:T(8,128)(2,1)S(1)}, u32[]{:S(2)}, u32[]{:S(2)}) collective-permute-start(bf16[256,1024]{1,0:T(8,128)(2,1)S(1)} %get-tuple-element.286), channel_id=1, source_target_pairs={{0,2},{1,3},{2,0},{3,1},{4,6},{5,7},{6,4},{7,5},{8,10},{9,11},{10,... | collective-permute-start | bytes 1572872 | tf_op jit(solution)/shard_map/ppermute | solution.py:45
  18.1 11.4 %copy-start.19 = (bf16[128,1024]{1,0:T(8,128)(2,1)}, bf16[128,1024]{1,0:T(8,128)(2,1)S(1)}, u32[]{:S(2)}) copy-start(bf16[128,1024]{1,0:T(8,128)(2,1)S(1)} %collective-permute-done.2) | copy-start | bytes 786436
  19.6 9.8 %copy-start.21 = (bf16[128,1024]{1,0:T(8,128)(2,1)}, bf16[128,1024]{1,0:T(8,128)(2,1)S(1)}, u32[]{:S(2)}) copy-start(bf16[128,1024]{1,0:T(8,128)(2,1)S(1)} %collective-permute-done.3) | copy-start | bytes 786436
  19.6 7.0 %collective-permute-start.4 = (bf16[128,1024]{1,0:T(8,128)(2,1)S(1)}, bf16[128,1024]{1,0:T(8,128)(2,1)}, u32[]{:S(2)}, u32[]{:S(2)}) collective-permute-start(bf16[128,1024]{1,0:T(8,128)(2,1)S(1)} %collective-permute-done.2), channel_id=1, source_target_pairs={{0,8},{8,16},{16,24},{24,28},{28,20},{20,12},{12,4},{4,0},{1,9},{9... | collective-permute-start | bytes 786440 | tf_op jit(solution)/shard_map/ppermute | solution.py:55
  21.2 6.7 %collective-permute-start.5 = (bf16[128,1024]{1,0:T(8,128)(2,1)S(1)}, bf16[128,1024]{1,0:T(8,128)(2,1)}, u32[]{:S(2)}, u32[]{:S(2)}) collective-permute-start(bf16[128,1024]{1,0:T(8,128)(2,1)S(1)} %collective-permute-done.3), channel_id=1, source_target_pairs={{0,4},{8,0},{16,8},{24,16},{28,24},{20,28},{12,20},{4,12},{1,5},{9... | collective-permute-start | bytes 786440 | tf_op jit(solution)/shard_map/ppermute | solution.py:55
  27.8 6.7 %collective-permute-start.6 = (bf16[128,1024]{1,0:T(8,128)(2,1)}, bf16[128,1024]{1,0:T(8,128)(2,1)}, u32[]{:S(2)}, u32[]{:S(2)}) collective-permute-start(bf16[128,1024]{1,0:T(8,128)(2,1)} %collective-permute-done.4), channel_id=1, source_target_pairs={{0,8},{8,16},{16,24},{24,28},{28,20},{20,12},{12,4},{4,0},{1,9},{9... | collective-permute-start | bytes 786440 | tf_op jit(solution)/shard_map/ppermute | solution.py:55
  29.4 6.7 %collective-permute-start.7 = (bf16[128,1024]{1,0:T(8,128)(2,1)}, bf16[128,1024]{1,0:T(8,128)(2,1)}, u32[]{:S(2)}, u32[]{:S(2)}) collective-permute-start(bf16[128,1024]{1,0:T(8,128)(2,1)} %collective-permute-done.5), channel_id=1, source_target_pairs={{0,4},{8,0},{16,8},{24,16},{28,24},{20,28},{12,20},{4,12},{1,5},{9... | collective-permute-start | bytes 786440 | tf_op jit(solution)/shard_map/ppermute | solution.py:55
  36.2 11.3 %collective-permute-start.1 = (bf16[256,1024]{1,0:T(8,128)(2,1)}, bf16[256,1024]{1,0:T(8,128)(2,1)}, u32[]{:S(2)}, u32[]{:S(2)}) collective-permute-start(bf16[256,1024]{1,0:T(8,128)(2,1)} %get-tuple-element.285), channel_id=1, source_target_pairs={{0,2},{1,3},{2,0},{3,1},{4,6},{5,7},{6,4},{7,5},{8,10},{9,11},{10,... | collective-permute-start | bytes 1572872 | tf_op jit(solution)/shard_map/ppermute | solution.py:45
  38.5 14.9 %all-to-all-start = ((f32[32,1,352]{2,1,0:T(1,128)}), f32[32,1,352]{2,1,0:T(1,128)S(1)}, u32[]{:S(2)}, u32[]{:S(2)}) async-start(f32[32,1,352]{2,1,0:T(1,128)} %broadcast_in_dim.235), calls=%async_computation | async-start | bytes 98304 | tf_op jit(solution)/shard_map/all_to_all | solution.py:114
  41.3 376.4 %reduce-scatter.2.cloned.1.call-start = ((), (), s32[]{:S(2)}) async-start(), calls=%async_computation.5 | async-start | bytes 13369344 | tf_op jit(solution)/shard_map/reduce_scatter | solution.py:1003
  49.4 29.2 %collective-permute-start.8 = (bf16[1024,1024]{1,0:T(8,128)(2,1)}, bf16[1024,1024]{1,0:T(8,128)(2,1)}, u32[]{:S(2)}, u32[]{:S(2)}) collective-permute-start(bf16[1024,1024]{1,0:T(8,128)(2,1)} %constant_dynamic-update-slice_fusion.x_ref.xf_ref), channel_id=1, source_target_pairs={{0,1},{1,0},{2,3},{3,2},{4,5},{5,4},{6,7},{7,6},{8,9},{9,8},{10,11... | collective-permute-start | bytes 6291464 | tf_op jit(solution)/shard_map/ppermute | solution.py:45
  49.7 5.1 %copy-start.20 = (bf16[128,1024]{1,0:T(8,128)(2,1)S(1)}, bf16[128,1024]{1,0:T(8,128)(2,1)}, u32[]{:S(2)}) copy-start(bf16[128,1024]{1,0:T(8,128)(2,1)} %copy-done.19) | copy-start | bytes 786436
  49.7 5.2 %copy-start.22 = (bf16[128,1024]{1,0:T(8,128)(2,1)S(1)}, bf16[128,1024]{1,0:T(8,128)(2,1)}, u32[]{:S(2)}) copy-start(bf16[128,1024]{1,0:T(8,128)(2,1)} %copy-done.21) | copy-start | bytes 786436
  55.8 14.3 %collective-permute-start.9 = (bf16[128,1024]{1,0:T(8,128)(2,1)}, bf16[128,1024]{1,0:T(8,128)(2,1)S(1)}, u32[]{:S(2)}, u32[]{:S(2)}) collective-permute-start(bf16[128,1024]{1,0:T(8,128)(2,1)} %collective-permute-done.6), channel_id=1, source_target_pairs={{0,8},{8,16},{16,24},{24,28},{28,20},{20,12},{12,4},{4,0},{1,9},{9... | collective-permute-start | bytes 786440 | tf_op jit(solution)/shard_map/ppermute | solution.py:55
  70.3 27.7 %copy-start.3 = (bf16[1024,256]{1,0:T(8,128)(2,1)}, bf16[1024,256]{1,0:T(8,128)(2,1)S(1)}, u32[]{:S(2)}) copy-start(bf16[1024,256]{1,0:T(8,128)(2,1)S(1)} %slice.218.w0) | copy-start | bytes 1572868
  70.3 28.2 %collective-permute-start.14 = (bf16[1024,256]{1,0:T(8,128)(2,1)S(1)}, bf16[1024,256]{1,0:T(8,128)(2,1)S(1)}, u32[]{:S(2)}, u32[]{:S(2)}) collective-permute-start(bf16[1024,256]{1,0:T(8,128)(2,1)S(1)} %slice.218.w0), channel_id=1, source_target_pairs={{0,2},{1,3},{2,0},{3,1},{4,6},{5,7},{6,4},{7,5},{8,10},{9,11},{10,... | collective-permute-start | bytes 1572872 | tf_op jit(solution)/shard_map/ppermute | solution.py:45
  97.8 1.6 collective-permute-start.10
  97.9 15.3 %collective-permute-start.13 = (bf16[1024,256]{1,0:T(8,128)(2,1)S(1)}, bf16[1024,256]{1,0:T(8,128)(2,1)S(1)}, u32[]{:S(2)}, u32[]{:S(2)}) collective-permute-start(bf16[1024,256]{1,0:T(8,128)(2,1)S(1)} %slice.218.w0), channel_id=1, source_target_pairs={{0,1},{1,0},{2,3},{3,2},{4,5},{5,4},{6,7},{7,6},{8,9},{9,8},{10,11... | collective-permute-start | bytes 1572872 | tf_op jit(solution)/shard_map/ppermute | solution.py:45
  98.4 11.1 %copy-start.6 = (bf16[1024,256]{1,0:T(8,128)(2,1)}, bf16[1024,256]{1,0:T(8,128)(2,1)S(1)}, u32[]{:S(2)}) copy-start(bf16[1024,256]{1,0:T(8,128)(2,1)S(1)} %collective-permute-done.14.w2) | copy-start | bytes 1572868
  98.4 14.8 %collective-permute-start.15 = (bf16[1024,256]{1,0:T(8,128)(2,1)S(1)}, bf16[1024,256]{1,0:T(8,128)(2,1)S(1)}, u32[]{:S(2)}, u32[]{:S(2)}) collective-permute-start(bf16[1024,256]{1,0:T(8,128)(2,1)S(1)} %collective-permute-done.14.w2), channel_id=1, source_target_pairs={{0,1},{1,0},{2,3},{3,2},{4,5},{5,4},{6,7},{7,6},{8,9},{9,8},{10,11... | collective-permute-start | bytes 1572872 | tf_op jit(solution)/shard_map/ppermute | solution.py:45
  99.5 14.0 %collective-permute-start.12 = (bf16[1024,256]{1,0:T(8,128)(2,1)S(1)}, bf16[1024,256]{1,0:T(8,128)(2,1)S(1)}, u32[]{:S(2)}, u32[]{:S(2)}) collective-permute-start(bf16[1024,256]{1,0:T(8,128)(2,1)S(1)} %pad_maximum_fusion.4), channel_id=1, source_target_pairs={{0,2},{1,3},{2,0},{3,1},{4,6},{5,7},{6,4},{7,5},{8,10},{9,11},{10,... | collective-permute-start | bytes 1572872 | tf_op jit(solution)/shard_map/ppermute | solution.py:45
  111.2 2.0 collective-permute-start.11
  121.5 33.9 %collective-permute-start.17 = (bf16[256,1024]{1,0:T(8,128)(2,1)S(1)}, bf16[256,1024]{1,0:T(8,128)(2,1)S(1)}, u32[]{:S(2)}, u32[]{:S(2)}) collective-permute-start(bf16[256,1024]{1,0:T(8,128)(2,1)S(1)} %get-tuple-element.281), channel_id=1, source_target_pairs={{0,2},{1,3},{2,0},{3,1},{4,6},{5,7},{6,4},{7,5},{8,10},{9,11},{10,... | collective-permute-start | bytes 1572872 | tf_op jit(solution)/shard_map/ppermute | solution.py:45
  124.6 42.5 %collective-permute-start.16 = (bf16[256,1024]{1,0:T(8,128)(2,1)S(1)}, bf16[256,1024]{1,0:T(8,128)(2,1)S(1)}, u32[]{:S(2)}, u32[]{:S(2)}) collective-permute-start(bf16[256,1024]{1,0:T(8,128)(2,1)S(1)} %get-tuple-element.282), channel_id=1, source_target_pairs={{0,2},{1,3},{2,0},{3,1},{4,6},{5,7},{6,4},{7,5},{8,10},{9,11},{10,... | collective-permute-start | bytes 1572872 | tf_op jit(solution)/shard_map/ppermute | solution.py:45
  165.5 14.4 %collective-permute-start.19 = (bf16[256,1024]{1,0:T(8,128)(2,1)}, bf16[256,1024]{1,0:T(8,128)(2,1)S(1)}, u32[]{:S(2)}, u32[]{:S(2)}) collective-permute-start(bf16[256,1024]{1,0:T(8,128)(2,1)} %get-tuple-element.133), channel_id=1, source_target_pairs={{0,2},{1,3},{2,0},{3,1},{4,6},{5,7},{6,4},{7,5},{8,10},{9,11},{10,... | collective-permute-start | bytes 1572872 | tf_op jit(solution)/shard_map/ppermute | solution.py:45
  177.3 15.1 %collective-permute-start.18 = (bf16[256,1024]{1,0:T(8,128)(2,1)}, bf16[256,1024]{1,0:T(8,128)(2,1)S(1)}, u32[]{:S(2)}, u32[]{:S(2)}) collective-permute-start(bf16[256,1024]{1,0:T(8,128)(2,1)} %get-tuple-element.135), channel_id=1, source_target_pairs={{0,2},{1,3},{2,0},{3,1},{4,6},{5,7},{6,4},{7,5},{8,10},{9,11},{10,... | collective-permute-start | bytes 1572872 | tf_op jit(solution)/shard_map/ppermute | solution.py:45
  184.6 27.9 %collective-permute-start.20 = (bf16[256,1024]{1,0:T(8,128)(2,1)}, bf16[256,1024]{1,0:T(8,128)(2,1)S(1)}, u32[]{:S(2)}, u32[]{:S(2)}) collective-permute-start(bf16[256,1024]{1,0:T(8,128)(2,1)} %get-tuple-element.141.refs_0_.refs_3_), channel_id=1, source_target_pairs={{0,2},{1,3},{2,0},{3,1},{4,6},{5,7},{6,4},{7,5},{8,10},{9,11},{10,... | collective-permute-start | bytes 1572872 | tf_op jit(solution)/shard_map/ppermute | solution.py:45
  197.4 27.3 %collective-permute-start.21 = (bf16[256,1024]{1,0:T(8,128)(2,1)}, bf16[256,1024]{1,0:T(8,128)(2,1)S(1)}, u32[]{:S(2)}, u32[]{:S(2)}) collective-permute-start(bf16[256,1024]{1,0:T(8,128)(2,1)} %get-tuple-element.142.refs_1_.refs_4_), channel_id=1, source_target_pairs={{0,2},{1,3},{2,0},{3,1},{4,6},{5,7},{6,4},{7,5},{8,10},{9,11},{10,... | collective-permute-start | bytes 1572872 | tf_op jit(solution)/shard_map/ppermute | solution.py:45
  223.5 33.6 %collective-permute-start.22 = (bf16[256,1024]{1,0:T(8,128)(2,1)}, bf16[256,1024]{1,0:T(8,128)(2,1)S(1)}, u32[]{:S(2)}, u32[]{:S(2)}) collective-permute-start(bf16[256,1024]{1,0:T(8,128)(2,1)} %get-tuple-element.155), channel_id=1, source_target_pairs={{0,2},{1,3},{2,0},{3,1},{4,6},{5,7},{6,4},{7,5},{8,10},{9,11},{10,... | collective-permute-start | bytes 1572872 | tf_op jit(solution)/shard_map/ppermute | solution.py:45
  235.6 21.5 %collective-permute-start.23 = (bf16[256,1024]{1,0:T(8,128)(2,1)}, bf16[256,1024]{1,0:T(8,128)(2,1)S(1)}, u32[]{:S(2)}, u32[]{:S(2)}) collective-permute-start(bf16[256,1024]{1,0:T(8,128)(2,1)} %get-tuple-element.165), channel_id=1, source_target_pairs={{0,2},{1,3},{2,0},{3,1},{4,6},{5,7},{6,4},{7,5},{8,10},{9,11},{10,... | collective-permute-start | bytes 1572872 | tf_op jit(solution)/shard_map/ppermute | solution.py:45
  258.7 11.4 %copy-start.18 = (bf16[512,256]{1,0:T(8,128)(2,1)S(1)}, bf16[512,256]{1,0:T(8,128)(2,1)}, u32[]{:S(2)}) copy-start(bf16[512,256]{1,0:T(8,128)(2,1)} %copy-done.17) | copy-start | bytes 786436
  268.9 11.4 %collective-permute-start.25 = (bf16[1024,256]{1,0:T(8,128)(2,1)S(1)}, bf16[1024,256]{1,0:T(8,128)(2,1)S(1)}, u32[]{:S(2)}, u32[]{:S(2)}) collective-permute-start(bf16[1024,256]{1,0:T(8,128)(2,1)S(1)} %pad_maximum_fusion.5), channel_id=1, source_target_pairs={{0,2},{1,3},{2,0},{3,1},{4,6},{5,7},{6,4},{7,5},{8,10},{9,11},{10,... | collective-permute-start | bytes 1572872 | tf_op jit(solution)/shard_map/ppermute | solution.py:45
  272.4 8.0 %copy-start.23 = (bf16[512,256]{1,0:T(8,128)(2,1)S(1)}, bf16[512,256]{1,0:T(8,128)(2,1)}, u32[]{:S(2)}) copy-start(bf16[512,256]{1,0:T(8,128)(2,1)} %get-tuple-element.175) | copy-start | bytes 786436
  272.4 10.6 %copy-start.34 = (f32[8,1024]{1,0:T(8,128)S(1)}, f32[8,1024]{1,0:T(8,128)}, u32[]{:S(2)}) copy-start(f32[8,1024]{1,0:T(8,128)} %get-tuple-element.195) | copy-start | bytes 98308
  272.4 10.6 %copy-start.35 = (f32[8,1024]{1,0:T(8,128)S(1)}, f32[8,1024]{1,0:T(8,128)}, u32[]{:S(2)}) copy-start(f32[8,1024]{1,0:T(8,128)} %get-tuple-element.196) | copy-start | bytes 98308
  272.5 10.6 %copy-start.24 = (bf16[512,256]{1,0:T(8,128)(2,1)S(1)}, bf16[512,256]{1,0:T(8,128)(2,1)}, u32[]{:S(2)}) copy-start(bf16[512,256]{1,0:T(8,128)(2,1)} %get-tuple-element.176) | copy-start | bytes 786436
  272.5 11.6 %collective-permute-start.24 = (bf16[1024,512]{1,0:T(8,128)(2,1)S(1)}, bf16[1024,512]{1,0:T(8,128)(2,1)}, u32[]{:S(2)}, u32[]{:S(2)}) collective-permute-start(bf16[1024,512]{1,0:T(8,128)(2,1)S(1)} %pad_maximum_fusion.1), channel_id=1, source_target_pairs={{0,1},{1,0},{2,3},{3,2},{4,5},{5,4},{6,7},{7,6},{8,9},{9,8},{10,11... | collective-permute-start | bytes 3145736 | tf_op jit(solution)/shard_map/ppermute | solution.py:45
  280.4 2.6 collective-permute-start.26
  285.7 42.3 %collective-permute-start.27 = (bf16[1024,256]{1,0:T(8,128)(2,1)S(1)}, bf16[1024,256]{1,0:T(8,128)(2,1)S(1)}, u32[]{:S(2)}, u32[]{:S(2)}) collective-permute-start(bf16[1024,256]{1,0:T(8,128)(2,1)S(1)} %fusion.3), channel_id=1, source_target_pairs={{0,2},{1,3},{2,0},{3,1},{4,6},{5,7},{6,4},{7,5},{8,10},{9,11},{10,... | collective-permute-start | bytes 1572872 | tf_op jit(solution)/shard_map/ppermute | solution.py:45
  287.6 37.8 %copy-start.45 = (bf16[512,1024]{1,0:T(8,128)(2,1)S(1)}, bf16[512,1024]{1,0:T(8,128)(2,1)}, u32[]{:S(2)}) copy-start(bf16[512,1024]{1,0:T(8,128)(2,1)} %get-tuple-element.172) | copy-start | bytes 3145732
  339.2 4.9 %copy-start.26 = (f32[2,8,1024]{2,1,0:T(8,128)S(1)}, f32[2,8,1024]{2,1,0:T(8,128)}, u32[]{:S(2)}) copy-start(f32[2,8,1024]{2,1,0:T(8,128)} %get-tuple-element.190) | copy-start | bytes 196612
  339.2 4.9 %copy-start.28 = (f32[2,8,1024]{2,1,0:T(8,128)S(1)}, f32[2,8,1024]{2,1,0:T(8,128)}, u32[]{:S(2)}) copy-start(f32[2,8,1024]{2,1,0:T(8,128)} %get-tuple-element.191) | copy-start | bytes 196612
  339.2 4.9 %copy-start.30 = (f32[2,8,1024]{2,1,0:T(8,128)S(1)}, f32[2,8,1024]{2,1,0:T(8,128)}, u32[]{:S(2)}) copy-start(f32[2,8,1024]{2,1,0:T(8,128)} %get-tuple-element.192) | copy-start | bytes 196612
  339.2 5.0 %copy-start.25 = (f32[2,8,1024]{2,1,0:T(8,128)S(1)}, f32[2,8,1024]{2,1,0:T(8,128)}, u32[]{:S(2)}) copy-start(f32[2,8,1024]{2,1,0:T(8,128)} %get-tuple-element.187) | copy-start | bytes 196612
  339.2 5.0 %copy-start.27 = (f32[2,8,1024]{2,1,0:T(8,128)S(1)}, f32[2,8,1024]{2,1,0:T(8,128)}, u32[]{:S(2)}) copy-start(f32[2,8,1024]{2,1,0:T(8,128)} %get-tuple-element.188) | copy-start | bytes 196612
  339.2 5.0 %copy-start.29 = (f32[2,8,1024]{2,1,0:T(8,128)S(1)}, f32[2,8,1024]{2,1,0:T(8,128)}, u32[]{:S(2)}) copy-start(f32[2,8,1024]{2,1,0:T(8,128)} %get-tuple-element.189) | copy-start | bytes 196612
  339.2 5.0 %copy-start.46 = (bf16[4,128,1024]{2,1,0:T(8,128)(2,1)S(1)}, bf16[4,128,1024]{2,1,0:T(8,128)(2,1)}, u32[]{:S(2)}) copy-start(bf16[4,128,1024]{2,1,0:T(8,128)(2,1)} %get-tuple-element.181) | copy-start | bytes 3145732
  344.0 38.8 %collective-permute-start.28 = (bf16[1024,1024]{1,0:T(8,128)(2,1)}, bf16[1024,1024]{1,0:T(8,128)(2,1)}, u32[]{:S(2)}, u32[]{:S(2)}) collective-permute-start(bf16[1024,1024]{1,0:T(8,128)(2,1)} %to_tokens.2), channel_id=1, source_target_pairs={{0,1},{1,0},{2,3},{3,2},{4,5},{5,4},{6,7},{7,6},{8,9},{9,8},{10,11... | collective-permute-start | bytes 6291464 | tf_op jit(solution)/shard_map/ppermute | solution.py:45
  344.2 36.6 %collective-permute-start.30 = (bf16[4,128,1024]{2,1,0:T(8,128)(2,1)S(1)}, bf16[4,128,1024]{2,1,0:T(8,128)(2,1)S(1)}, u32[]{:S(2)}, u32[]{:S(2)}) collective-permute-start(bf16[4,128,1024]{2,1,0:T(8,128)(2,1)S(1)} %copy-done.46), channel_id=1, source_target_pairs={{0,4},{4,0},{8,12},{12,8},{16,20},{20,16},{24,28},{28,24},{1,5},{5... | collective-permute-start | bytes 3145736 | tf_op jit(solution)/shard_map/ppermute | solution.py:45
  386.3 34.2 %collective-permute-start.29 = (bf16[512,1024]{1,0:T(8,128)(2,1)}, bf16[512,1024]{1,0:T(8,128)(2,1)}, u32[]{:S(2)}, u32[]{:S(2)}) collective-permute-start(bf16[512,1024]{1,0:T(8,128)(2,1)} %fusion), channel_id=1, source_target_pairs={{0,2},{1,3},{2,0},{3,1},{4,6},{5,7},{6,4},{7,5},{8,10},{9,11},{10,... | collective-permute-start | bytes 3145736 | tf_op jit(solution)/shard_map/ppermute | solution.py:45
  388.4 23.6 %all-to-all-start.1 = ((f32[32,1,352]{2,1,0:T(1,128)}), f32[32,1,352]{2,1,0:T(1,128)S(1)}, u32[]{:S(2)}, u32[]{:S(2)}) async-start(f32[32,1,352]{2,1,0:T(1,128)} %all_to_all.18), calls=%async_computation.2 | async-start | bytes 98304 | tf_op jit(solution)/shard_map/all_to_all | solution.py:114
  391.8 22.0 %collective-permute-start.31 = (bf16[128,1024]{1,0:T(8,128)(2,1)}, bf16[128,1024]{1,0:T(8,128)(2,1)S(1)}, u32[]{:S(2)}, u32[]{:S(2)}) collective-permute-start(bf16[128,1024]{1,0:T(8,128)(2,1)} %get-tuple-element.278), channel_id=1, source_target_pairs={{0,8},{4,12},{8,16},{12,20},{16,24},{20,28},{24,0},{28,4},{1,9},{5... | collective-permute-start | bytes 786440 | tf_op jit(solution)/shard_map/ppermute | solution.py:49
  393.5 21.3 %collective-permute-start.32 = (bf16[128,1024]{1,0:T(8,128)(2,1)S(1)}, bf16[128,1024]{1,0:T(8,128)(2,1)S(1)}, u32[]{:S(2)}, u32[]{:S(2)}) collective-permute-start(bf16[128,1024]{1,0:T(8,128)(2,1)S(1)} %get-tuple-element.280), channel_id=1, source_target_pairs={{0,16},{4,20},{8,24},{12,28},{16,0},{20,4},{24,8},{28,12},{1,17},{... | collective-permute-start | bytes 786440 | tf_op jit(solution)/shard_map/ppermute | solution.py:49
  396.0 18.8 %collective-permute-start.33 = (bf16[128,1024]{1,0:T(8,128)(2,1)S(1)}, bf16[128,1024]{1,0:T(8,128)(2,1)S(1)}, u32[]{:S(2)}, u32[]{:S(2)}) collective-permute-start(bf16[128,1024]{1,0:T(8,128)(2,1)S(1)} %get-tuple-element.279), channel_id=1, source_target_pairs={{0,24},{4,28},{8,0},{12,4},{16,8},{20,12},{24,16},{28,20},{1,25},{... | collective-permute-start | bytes 786440 | tf_op jit(solution)/shard_map/ppermute | solution.py:49
  421.1 17.2 %all-to-all-start.2 = ((f32[32,1,128]{2,1,0:T(1,128)}), f32[32,1,128]{2,1,0:T(1,128)S(1)}, u32[]{:S(2)}, u32[]{:S(2)}) async-start(f32[32,1,128]{2,1,0:T(1,128)} %broadcast_in_dim.285), calls=%async_computation.3 | async-start | bytes 32768 | tf_op jit(solution)/shard_map/all_to_all | solution.py:114
  (23 other events, 38.5 us)
Sparse Core Ops, SparseCore 0:
  36.3 105.4 all-gather.1
  257.2 153.5 reduce-scatter.1

commit v6 on v5

--- a/solution.py
+++ b/solution.py
@@ -560,18 +560,22 @@
     )(rows, weights, sup, sgate)
 
 
-def backward_body(pieces, *refs):
+def backward_body(pieces, groups, *refs):
     rows = jnp.concatenate([ref[...] for ref in refs[:pieces]], axis=0)
-    w_ref, gate_ref, act_ref, by_up_ref, by_gate_ref, sup_ref, sgate_ref = refs[pieces : pieces + 7]
-    gu_ref, gg_ref, bu_ref, bg_ref, out_ref, acc_ref = refs[pieces + 7 :]
+    w_ref, kept = refs[pieces], refs[pieces + 1 : pieces + 1 + 4 * groups]
+    sup_ref, sgate_ref, gu_ref, gg_ref, bu_ref, bg_ref, out_ref, acc_ref = refs[pieces + 1 + 4 * groups :]
     t = pl.program_id(0)
+
+    def saved(index, part):
+        return jnp.concatenate([kept[4 * g + index][part] for g in range(groups)], axis=0).astype(F32)
+
     lefts, rights = [], []
     for part in range(2):
         g_act = dot(rows, weight_tile(w_ref, part, 2))
-        g_up = (g_act * by_up_ref[part].astype(F32)).astype(BF16)
-        g_gate = g_act * by_gate_ref[part].astype(F32)
-        up_sum = jnp.sum(g_act * act_ref[part].astype(F32), axis=0, keepdims=True)
-        gate_sum = jnp.sum(g_gate * gate_ref[part].astype(F32), axis=0, keepdims=True)
+        g_up = (g_act * saved(2, part)).astype(BF16)
+        g_gate = g_act * saved(3, part)
+        up_sum = jnp.sum(g_act * saved(1, part), axis=0, keepdims=True)
+        gate_sum = jnp.sum(g_gate * saved(0, part), axis=0, keepdims=True)
         g_gate = g_gate.astype(BF16)
         bu_ref[part, 0:1, :] = up_sum / sup_ref[part, 0:1, :]
         bg_ref[part, 0:1, :] = gate_sum / sgate_ref[part, 0:1, :]
@@ -588,14 +592,14 @@
     whole, tile, scale = ffn_specs(count)
     sums = pl.BlockSpec((2, 8, TILE), lambda t: (0, 0, t))
     return pl.pallas_call(
-        functools.partial(backward_body, len(grads)),
+        functools.partial(backward_body, len(grads), len(saved)),
         out_shape=[jax.ShapeDtypeStruct((2, count, hidden), BF16)] * 2
         + [jax.ShapeDtypeStruct((2, 8, hidden), F32)] * 2
         + [jax.ShapeDtypeStruct((count, D), kind)],
         grid=(hidden // TILE,),
         in_specs=[pl.BlockSpec(g.shape, lambda t: (0, 0)) for g in grads]
         + [weight_spec(weights)]
-        + [tile] * 4
+        + [pl.BlockSpec((2, k.shape[1], TILE), lambda t: (0, 0, t)) for group in saved for k in group]
         + [scale, scale],
         out_specs=[tile, tile, sums, sums, whole],
         scratch_shapes=[pltpu.VMEM((count, D), F32)],
@@ -605,15 +609,15 @@
             transcendentals=0,
         ),
         name="ffn_backward",
-    )(*grads, weights, *saved, sup, sgate)
+    )(*grads, weights, *[k for group in saved for k in group], sup, sgate)
 
 
 def weight_body(counts, *refs):
-    h_count, g_count, m_count = counts
+    h_count, m_count, g_count, a_count = counts
     take = iter(refs)
     hs = [next(take) for _ in range(h_count)]
     ms = [next(take) for _ in range(m_count)]
-    ups, gates, acts = [[next(take) for _ in range(g_count)] for _ in range(3)]
+    ups, gates, acts = [[next(take) for _ in range(n)] for n in (g_count, g_count, a_count)]
     out_ref, ht_ref, mt_ref = refs[-3:]
 
     @pl.when(pl.program_id(0) == 0)
@@ -643,7 +647,7 @@
 
     lefts, rights = list(hs) + list(ms), list(ups) + list(gates) + list(acts)
     return pl.pallas_call(
-        functools.partial(weight_body, (len(hs), len(ups), len(ms))),
+        functools.partial(weight_body, (len(hs), len(ms), len(ups), len(acts))),
         out_shape=jax.ShapeDtypeStruct(shape, BF16),
         grid=(hidden // TILE,),
         in_specs=[whole(a) for a in lefts] + [tile(a) for a in rights],
@@ -945,6 +949,7 @@
     kpos = jnp.where(key_mask[0] == 1, slot_ids, -1)
     kpos_rows = kpos[None, :]
     kpos_cols = jnp.broadcast_to(kpos[:, None], (row_len, 128))
+    x_second, kpos_cols = lax.optimization_barrier((x_second, kpos_cols))
 
     half = project(place, x_first, attn, cosine, sine, sqk, None, 0)
     queries, keys, vals, qrot, krot = project(place, x_second, attn, cosine, sine, sqk, half, 1)
@@ -982,14 +987,13 @@
         gm_far.append(swap(gm, "mp", 2))
         by_two = by_two + by
     result, keep_two = done
-    gu, gg, bu, bg, gh_own = ffn_backward(gm_own, weights, saved_own, sup, sgate, F32)
-    gus, ggs, last, gh_over = [gu], [gg], gh_own, []
-    for c in chunks:
-        gu, gg, bu_c, bg_c, last = ffn_backward([after(gm_far[c], last)], weights, saved_far[c], sup, sgate, BF16)
-        gh_over.append(swap(last, "mp", 2))
-        gus.append(gu)
-        ggs.append(gg)
-        bu, bg = bu + bu_c, bg + bg_c
+    gu, gg, bu, bg, gh_own = ffn_backward(
+        [after(gm_own[0], gm_far[0])] + gm_own[1:], weights, [saved_own], sup, sgate, F32
+    )
+    gm_next = [after(gm, gh_own) for gm in gm_far]
+    gu_far, gg_far, bu_far, bg_far, gh_far = ffn_backward(gm_next, weights, saved_far, sup, sgate, BF16)
+    gus, ggs, bu, bg = [gu, gu_far], [gg, gg_far], bu + bu_far, bg + bg_far
+    gh_over = swap(gh_far, "mp", 2)
     grad_mlp = weight_grads(
         [h_own] + h_far,
         gm_own + gm_far,
@@ -998,8 +1002,7 @@
         [saved_own[1]] + [saved[1] for saved in saved_far],
         weights.shape,
     )
-    grad_mlp, *gh_over = lax.optimization_barrier((grad_mlp, *gh_over))
-    gh_over = jnp.concatenate(gh_over)
+    grad_mlp, gh_over = lax.optimization_barrier((grad_mlp, gh_over))
     grad_mlp = lax.psum_scatter(
         grad_mlp.reshape(-1, part), ("dp", "mp"), scatter_dimension=0, tiled=True, axis_index_groups=chip_groups()
     ).astype(F32)

time: 451 us -> 451 us (level)
  waiting for transfers between devices: 102 us -> 110 us
  Pallas kernels: 202 us -> 195 us
    pallas_call x4 -> x3, Pallas kernels: 54.9 us -> 48.7 us  [the longest x2 28.2 us: ffn_backward(): pl.pallas_call(functools.partial(backward_body, len(grads), len(saved)),...]
    ppermute x24 -> x23, waiting for transfers between devices: 45.2 us -> 51.2 us  [swap(): return lax.ppermute(array, axis, [(i, i ^ bit) for i in range(size)])]
    ppermute x3, waiting for transfers between devices: 1 us -> 5.9 us  [to_z(): lax.ppermute(array, 'dp', [(z * 2 + y, (z + step) % 4 * 2 + y) for z in r...]
    ppermute x24 -> x23, starting transfers between devices: 20.3 us -> 21.1 us  [swap(): return lax.ppermute(array, axis, [(i, i ^ bit) for i in range(size)])]
    unnamed x103 -> x97, local copies, waits for them, and re-layouts: 13.9 us -> 14.2 us
  transfers between devices with their start and end apart: 39 -> 38, of which waited for: 16 -> 18; matrix products, arithmetic and copies ran while one was open for 14% -> 14% of each run, Pallas kernels for 45% -> 41%
where the time goes in v6:
time: 451 us; the launch traced here: 448 us
  Pallas kernels  195 us (43%)
  waiting for transfers between devices  110 us (24%)
  starting transfers between devices  50.4 us (11%)
  local copies, waits for them, and re-layouts  38.5 us (9%)
  other arithmetic  28.1 us (6%)
  between operations  19.9 us (4%)
  matrix products  5.22 us (1%)
    ppermute x23, waiting for transfers between devices, swap(): return lax.ppermute(array, axis, [(i, i ^ bit) for i in range(size)])  51.2 us
    pallas_call x1, Pallas kernels, attend_back(): pl.pallas_call(functools.partial(back_body, docs), out_shape=[jax.ShapeDt...  36.8 us
    pallas_call x3, Pallas kernels, ffn_forward(): pl.pallas_call(forward_body, out_shape=[jax.ShapeDtypeStruct((2, count, h...  32.1 us
    pallas_call x2, Pallas kernels, ffn_backward(): pl.pallas_call(functools.partial(backward_body, len(grads), len(saved)),...  28.2 us
    ppermute x7, waiting for transfers between devices, around(): lax.ppermute(array, 'dp', [(RING[p], RING[(p + step) % 8]) for p in range...  23.8 us
    pallas_call x2, Pallas kernels, attend(): pl.pallas_call(functools.partial(attend_body, docs, first), out_shape=[ja...  21.3 us
    ppermute x23, starting transfers between devices, swap(): return lax.ppermute(array, axis, [(i, i ^ bit) for i in range(size)])  21.1 us
    pallas_call x1, Pallas kernels, weight_grads(): pl.pallas_call(functools.partial(weight_body, (len(hs), len(ms), len(ups)...  20.5 us
  transfers between devices with their start and end apart: 38, of which 18 were waited for; matrix products, arithmetic and copies ran while one was open for 14% of the time, Pallas kernels for 41%

profile of v6, /device:TPU:0, one launch (start us, length us, event | category | flops | bytes accessed | tf_op | source)
XLA Modules:
  0.0 447.9 jit_solution(5678540692300747387)
XLA Ops:
  8.7 3.1 collective-permute-start.2
  12.7 1.9 collective-permute-start
  14.6 3.4 collective-permute-done.2
  18.1 1.5 collective-permute-done.3
  19.6 1.6 collective-permute-start.4
  21.6 4.9 %collective-permute-done.4 = bf16[128,1024]{1,0:T(8,128)(2,1)} collective-permute-done((bf16[128,1024]{1,0:T(8,128)(2,1)S(1)}, bf16[128,1024]{1,0:T(8,128)(2,1)}, u32[]{:S(2)}, u32[]{:S(2)}) %collective-permute-start.4) | collective-permute-done | bytes 262176 | tf_op jit(solution)/shard_map/ppermute | solution.py:55
  27.8 1.6 collective-permute-start.6
  31.0 2.0 pad_maximum_fusion.2
  33.0 1.6 collective-permute-done.6
  34.5 1.6 collective-permute-done.7
  36.2 1.6 collective-permute-start.1
  38.5 2.8 all-to-all-start
  47.6 1.9 constant_dynamic-update-slice_fusion.x_ref.xf_ref
  49.7 3.1 fusion.5
  55.8 1.9 collective-permute-start.9
  60.6 9.5 %collective-permute-done.9 = bf16[128,1024]{1,0:T(8,128)(2,1)S(1)} collective-permute-done((bf16[128,1024]{1,0:T(8,128)(2,1)}, bf16[128,1024]{1,0:T(8,128)(2,1)S(1)}, u32[]{:S(2)}, u32[]{:S(2)}) %collective-permute-start.9) | collective-permute-done | bytes 262176 | tf_op jit(solution)/shard_map/ppermute | solution.py:55
  70.2 1.5 collective-permute-start.14
  71.8 6.8 %project.2 = (bf16[2048,256]{1,0:T(8,128)(2,1)}, bf16[2048,256]{1,0:T(8,128)(2,1)}, bf16[2048,256]{1,0:T(8,128)(2,1)}, f32[2048,256]{1,0:T(8,128)}, f32[2048,256]{1,0:T(8,128)}) custom-call(s32[1]{0:T(128)} %bitcast.m_ref, bf16[1024,1024]{1,0:T(8,128)(2,1)} %constant_dynamic-update-slice_fusion.x_ref.xf_ref, bf16[1024,1024]{1,0:T(8,128)(2,1)} %copy-done, ...), custom_call_target="tpu_custom_call" | custom-call | flops 1610612736 | bytes 8388608 | tf_op jit(solution)/shard_map/project/pallas_call | solution.py:167
  78.5 1.3 broadcast_in_dim.235.kpos_ref
  79.8 7.1 %project.3 = (bf16[2048,256]{1,0:T(8,128)(2,1)}, bf16[2048,256]{1,0:T(8,128)(2,1)}, bf16[2048,256]{1,0:T(8,128)(2,1)}, f32[2048,256]{1,0:T(8,128)}, f32[2048,256]{1,0:T(8,128)}) custom-call(s32[1]{0:T(128)} %bitcast.m_ref, ...), custom_call_target="tpu_custom_call", output_to_operand_aliasing={{0}: (6, {}), {1}: (7, {}), {2}: (8, {}), {3}: (9, {}), {4}... | custom-call | flops 1610612736 | bytes 8388608 | tf_op jit(solution)/shard_map/project/pallas_call | solution.py:167
  86.9 10.0 %attend.2 = (bf16[2048,256]{1,0:T(8,128)(2,1)}, f32[2048,256]{1,0:T(8,128)}) custom-call(s32[5]{0:T(128)} %pad_add_fusion.meta_ref, bf16[2048,256]{1,0:T(8,128)(2,1)} %get-tuple-element.120.q_ref, bf16[2048,256]{1,0:T(8,128)(2,1)} %get-tuple-element.121.k_ref, bf16[2048,256]{1,0:T(8,128)(2,1)} %get-tuple-element.122.v_ref, s32[1,2048]{1,0:T(1,128)} %compare_select_fusion.kpos_ref), custom_call_target="tpu_custom_call" | custom-call | flops 8000000000 | bytes 4194304 | tf_op jit(solution)/shard_map/attend/pallas_call | solution.py:290
  99.6 2.4 collective-permute-start.12
  102.0 11.3 %attend.3 = (bf16[2048,256]{1,0:T(8,128)(2,1)}, f32[2048,256]{1,0:T(8,128)}) custom-call(s32[5]{0:T(128)} %pad_add_fusion.meta_ref, bf16[2048,256]{1,0:T(8,128)(2,1)} %get-tuple-element.120.q_ref, bf16[2048,256]{1,0:T(8,128)(2,1)} %get-tuple-element.121.k_ref, ...), custom_call_target="tpu_custom_call", output_to_operand_aliasing={{0}: (5, {}), {1}: (6, {})} | custom-call | flops 8000000000 | bytes 4194304 | tf_op jit(solution)/shard_map/attend/pallas_call | solution.py:290
  113.3 1.7 slice.178
  118.7 5.2 %attn_out.1 = (f32[512,1024]{1,0:T(8,128)}, bf16[512,1024]{1,0:T(8,128)(2,1)}) custom-call(bf16[2048,256]{1,0:T(8,128)(2,1)} %get-tuple-element.126.a0.o_ref, bf16[512,256]{1,0:T(8,128)(2,1)} %copy-done.16, bf16[1024,256]{1,0:T(8,128)(2,1)} %copy-done.5, bf16[1024,256]{1,0:T(8,128)(2,1)} %copy-done.5, bf16[512,1024]{1,0:T(8,128)(2,1)} %x_ref.7, ...), custom_call_target="tpu_custom_call" | custom-call | flops 1073741824 | bytes 10485760 | tf_op jit(solution)/shard_map/attn_out/pallas_call | solution.py:768
  125.3 2.0 collective-permute-start.16
  127.3 14.5 %all-gather.2.cloned.1.call-done = bf16[6144,1024]{1,0:T(8,128)(2,1)} async-done(((bf16[384,1024]{1,0:T(8,128)(2,1)}), bf16[6144,1024]{1,0:T(8,128)(2,1)}) %all-gather.2.cloned.1.call-update) | async-done | bytes 12582928 | tf_op jit(solution)/shard_map/all_gather | solution.py:922
  141.9 13.5 %ffn_forward.3 = (bf16[2,512,1024]{2,1,0:T(8,128)(2,1)}, bf16[2,512,1024]{2,1,0:T(8,128)(2,1)}, bf16[2,512,1024]{2,1,0:T(8,128)(2,1)}, bf16[2,512,1024]{2,1,0:T(8,128)(2,1)}, f32[512,1024]{1,0:T(8,128)}) custom-call(bf16[512,1024]{1,0:T(8,128)(2,1)} %get-tuple-element.127.h_ref.refs_0_, bf16[8,2,3,128,1024]{4,3,2,1,0:T(8,128)(2,1)} %bitcast.106, ...), custom_call_target="tpu_custom_call" | custom-call | flops 6442450944 | bytes 18874368 | tf_op jit(solution)/shard_map/ffn_forward/pallas_call | solution.py:546
  156.1 9.3 %ffn_forward.4 = (bf16[2,256,1024]{2,1,0:T(8,128)(2,1)}, bf16[2,256,1024]{2,1,0:T(8,128)(2,1)}, bf16[2,256,1024]{2,1,0:T(8,128)(2,1)}, bf16[2,256,1024]{2,1,0:T(8,128)(2,1)}, bf16[256,1024]{1,0:T(8,128)(2,1)}) custom-call(bf16[256,1024]{1,0:T(8,128)(2,1)} %copy-done.10, bf16[8,2,3,128,1024]{4,3,2,1,0:T(8,128)(2,1)} %bitcast.107, ...), custom_call_target="tpu_custom_call" | custom-call | flops 3221225472 | bytes 15728640 | tf_op jit(solution)/shard_map/ffn_forward/pallas_call | solution.py:546
  165.4 1.5 collective-permute-start.19
  168.4 9.3 %ffn_forward.5 = (bf16[2,256,1024]{2,1,0:T(8,128)(2,1)}, bf16[2,256,1024]{2,1,0:T(8,128)(2,1)}, bf16[2,256,1024]{2,1,0:T(8,128)(2,1)}, bf16[2,256,1024]{2,1,0:T(8,128)(2,1)}, bf16[256,1024]{1,0:T(8,128)(2,1)}) custom-call(bf16[256,1024]{1,0:T(8,128)(2,1)} %copy-done.11, bf16[8,2,3,128,1024]{4,3,2,1,0:T(8,128)(2,1)} %bitcast.108, ...), custom_call_target="tpu_custom_call" | custom-call | flops 3221225472 | bytes 15728640 | tf_op jit(solution)/shard_map/ffn_forward/pallas_call | solution.py:546
  178.4 1.4 collective-permute-done.19.far_ref
  180.6 4.0 turn.2
  184.5 1.5 collective-permute-start.20
  186.1 6.8 %collective-permute-done.18.far_ref = bf16[256,1024]{1,0:T(8,128)(2,1)S(1)} collective-permute-done((bf16[256,1024]{1,0:T(8,128)(2,1)}, bf16[256,1024]{1,0:T(8,128)(2,1)S(1)}, u32[]{:S(2)}, u32[]{:S(2)}) %collective-permute-start.18) | collective-permute-done | bytes 524320 | tf_op jit(solution)/shard_map/ppermute | solution.py:45
  193.6 4.2 turn.3
  198.5 5.6 %collective-permute-done.20.refs_0_.refs_5_ = bf16[256,1024]{1,0:T(8,128)(2,1)S(1)} collective-permute-done((bf16[256,1024]{1,0:T(8,128)(2,1)}, bf16[256,1024]{1,0:T(8,128)(2,1)S(1)}, u32[]{:S(2)}, u32[]{:S(2)}) %collective-permute-start.20) | collective-permute-done | bytes 524320 | tf_op jit(solution)/shard_map/ppermute | solution.py:45
  204.1 14.4 %ffn_backward.2 = (bf16[2,512,1024]{2,1,0:T(8,128)(2,1)}, bf16[2,512,1024]{2,1,0:T(8,128)(2,1)}, f32[2,8,1024]{2,1,0:T(8,128)}, f32[2,8,1024]{2,1,0:T(8,128)}, f32[512,1024]{1,0:T(8,128)}) custom-call(bf16[256,1024]{1,0:T(8,128)(2,1)} %get-tuple-element.140.refs_0_.refs_3_, bf16[256,1024]{1,0:T(8,128)(2,1)} %get-tuple-element.141.refs_1_.refs_4_, ...), custom_call_target="tpu_custom_call" | custom-call | flops 6442450944 | bytes 25165824 | tf_op jit(solution)/shard_map/ffn_backward/pallas_call | solution.py:594
  219.3 13.8 %ffn_backward.3 = (bf16[2,512,1024]{2,1,0:T(8,128)(2,1)}, bf16[2,512,1024]{2,1,0:T(8,128)(2,1)}, f32[2,8,1024]{2,1,0:T(8,128)}, f32[2,8,1024]{2,1,0:T(8,128)}, bf16[512,1024]{1,0:T(8,128)(2,1)}) custom-call(bf16[256,1024]{1,0:T(8,128)(2,1)} %copy-done.42, bf16[256,1024]{1,0:T(8,128)(2,1)} %copy-done.43, bf16[8,2,3,128,1024]{4,3,2,1,0:T(8,128)(2,1)} %bitcast.110, ...), custom_call_target="tpu_custom_call" | custom-call | flops 6442450944 | bytes 25165824 | tf_op jit(solution)/shard_map/ffn_backward/pallas_call | solution.py:594
  233.7 20.5 %weight_grads.1 = bf16[8,2,3,128,1024]{4,3,2,1,0:T(8,128)(2,1)} custom-call(bf16[512,1024]{1,0:T(8,128)(2,1)} %get-tuple-element.127.h_ref.refs_0_, bf16[256,1024]{1,0:T(8,128)(2,1)} %copy-done.10, bf16[256,1024]{1,0:T(8,128)(2,1)} %copy-done.11, bf16[256,1024]{1,0:T(8,128)(2,1)} %get-tuple-element.140.refs_0_.refs_3_, ...), custom_call_target="tpu_custom_call" | custom-call | flops 12884901888 | bytes 25165824 | tf_op jit(solution)/shard_map/weight_grads/pallas_call | solution.py:649
  254.2 2.4 collective-permute-done.22.far_ref
  257.6 9.1 %attn_back_out.1 = (bf16[512,1024]{1,0:T(8,128)(2,1)}, f32[512,1024]{1,0:T(8,128)}, bf16[512,256]{1,0:T(8,128)(2,1)}, bf16[512,256]{1,0:T(8,128)(2,1)}, bf16[512...) custom-call(f32[512,1024]{1,0:T(8,128)} %get-tuple-element.146.own_ref, ...), custom_call_target="tpu_custom_call" | custom-call | flops 1073741824 | bytes 10485760 | tf_op jit(solution)/shard_map/attn_back_out/pallas_call | solution.py:768
  268.3 1.8 convolution_convert_fusion.1
  270.9 7.8 %collective-permute-done.24 = bf16[1024,256]{1,0:T(8,128)(2,1)S(1)} collective-permute-done((bf16[1024,256]{1,0:T(8,128)(2,1)S(1)}, bf16[1024,256]{1,0:T(8,128)(2,1)S(1)}, u32[]{:S(2)}, u32[]{:S(2)}) %collective-permute-start.24) | collective-permute-done | bytes 524320 | tf_op jit(solution)/shard_map/ppermute | solution.py:45
  283.3 36.8 %attend_back.1 = (bf16[2048,768]{1,0:T(8,128)(2,1)}, f32[8,256]{1,0:T(8,128)}) custom-call(s32[5]{0:T(128)} %pad_add_fusion.meta_ref, bf16[2048,256]{1,0:T(8,128)(2,1)} %get-tuple-element.120.q_ref, f32[2048,256]{1,0:T(8,128)} %get-tuple-element.165.qr_ref, bf16[2048,256]{1,0:T(8,128)(2,1)} %get-tuple-element.126.a0.o_ref, ...), custom_call_target="tpu_custom_call" | custom-call | flops 40000000000 | bytes 6291456 | tf_op jit(solution)/shard_map/attend_back/pallas_call | solution.py:455
  320.0 2.4 convolution_add_fusion.1.out_ref
  323.2 10.4 %attn_grads.1 = (f32[4,128,1024]{2,1,0:T(8,128)}, bf16[4,128,1024]{2,1,0:T(8,128)(2,1)}) custom-call(s32[2]{0:T(128)} %pad_add_fusion.1.m_ref, bf16[1024,1024]{1,0:T(8,128)(2,1)} %constant_dynamic-update-slice_fusion.x_ref.xf_ref, bf16[1024,1024]{1,0:T(8,128)(2,1)} %collective-permute-done.8.x_ref.xs_ref, bf16[2048,768]{1,0:T(8,128)(2,1)} %get-tuple-element.179.g_ref, ...), custom_call_target="tpu_custom_call" | custom-call | flops 3221225472 | bytes 6291456 | tf_op jit(solution)/shard_map/attn_grads/pallas_call | solution.py:701
  333.8 4.8 %to_tokens.2 = bf16[1024,1024]{1,0:T(8,128)(2,1)} custom-call(bf16[2048,768]{1,0:T(8,128)(2,1)} %get-tuple-element.179.g_ref, bf16[1024,1024]{1,0:T(8,128)(2,1)} %copy-done), custom_call_target="tpu_custom_call" | custom-call | flops 1610612736 | bytes 6291456 | tf_op jit(solution)/shard_map/to_tokens/pallas_call | solution.py:738
  341.1 2.9 collective-permute-start.29
  345.9 5.0 %to_tokens.3 = f32[1024,1024]{1,0:T(8,128)} custom-call(bf16[2048,768]{1,0:T(8,128)(2,1)} %get-tuple-element.179.g_ref, bf16[1024,1024]{1,0:T(8,128)(2,1)} %copy-done), custom_call_target="tpu_custom_call" | custom-call | flops 1610612736 | bytes 6291456 | tf_op jit(solution)/shard_map/to_tokens/pallas_call | solution.py:738
  351.0 24.9 %collective-permute-done.29 = bf16[4,128,1024]{2,1,0:T(8,128)(2,1)S(1)} collective-permute-done((bf16[4,128,1024]{2,1,0:T(8,128)(2,1)S(1)}, bf16[4,128,1024]{2,1,0:T(8,128)(2,1)S(1)}, u32[]{:S(2)}, u32[]{:S(2)}) %collective-permute-start.29) | collective-permute-done | bytes 1048608 | tf_op jit(solution)/shard_map/ppermute | solution.py:45
  375.9 2.1 convert_add_fusion
  378.8 2.6 fusion
  381.4 1.5 collective-permute-start.28
  383.5 2.6 all-to-all-start.1
  386.9 1.7 collective-permute-start.30
  388.6 2.5 collective-permute-start.31
  391.1 1.4 collective-permute-start.32
  392.5 14.9 %all-to-all-done.1 = f32[32,1,352]{2,1,0:T(1,128)S(1)} async-done(((f32[32,1,352]{2,1,0:T(1,128)}), f32[32,1,352]{2,1,0:T(1,128)S(1)}, u32[]{:S(2)}, u32[]{:S(2)}) %all-to-all-start.1) | async-done | bytes 45088 | tf_op jit(solution)/shard_map/all_to_all | solution.py:114
  409.1 5.9 %collective-permute-done.31 = bf16[128,1024]{1,0:T(8,128)(2,1)S(1)} collective-permute-done((bf16[128,1024]{1,0:T(8,128)(2,1)S(1)}, bf16[128,1024]{1,0:T(8,128)(2,1)S(1)}, u32[]{:S(2)}, u32[]{:S(2)}) %collective-permute-start.31) | collective-permute-done | bytes 262176 | tf_op jit(solution)/shard_map/ppermute | solution.py:49
  417.8 2.1 multiply_reduce_fusion
  421.2 9.2 %all-to-all-start.2 = ((f32[32,1,128]{2,1,0:T(1,128)}), f32[32,1,128]{2,1,0:T(1,128)S(1)}, u32[]{:S(2)}, u32[]{:S(2)}) async-start(f32[32,1,128]{2,1,0:T(1,128)} %broadcast_in_dim.285), calls=%async_computation.3 | async-start | bytes 32768 | tf_op jit(solution)/shard_map/all_to_all | solution.py:114
  430.4 2.3 fusion.21
  432.7 4.9 %fusion.2 = f32[512,1024]{1,0:T(8,128)} fusion(f32[512,1024]{1,0:T(8,128)} %get-tuple-element.164, f32[1024,1024]{1,0:T(8,128)} %to_tokens.3, bf16[512,1024]{1,0:T(8,128)(2,1)} %collective-permute-done.28, bf16[1024,1024]{1,0:T(8,128)(2,1)} %collective-permute-done.27), kind=kLoop, calls=%fused_computation.4 | loop fusion | flops 2621440 | bytes 8388608 | tf_op jit(solution)/shard_map/add | solution.py:1071
  (229 shorter events, 52.7 us)
Async XLA Ops:
  7.2 4.6 %copy-start.1 = (bf16[512,1024]{1,0:T(8,128)(2,1)S(1)}, bf16[512,1024]{1,0:T(8,128)(2,1)}, u32[]{:S(2)}) copy-start(bf16[512,1024]{1,0:T(8,128)(2,1)} %x_ref.7) | copy-start | bytes 3145732
  7.2 134.6 %all-gather.2.cloned.1.call-start = ((), (), s32[]{:S(2)}) async-start(), calls=%async_computation.4 | async-start | bytes 13369344 | tf_op jit(solution)/shard_map/all_gather | solution.py:922
  8.7 29.1 %copy-start.34 = (f32[128]{0:T(128)S(1)}, f32[128]{0:T(128)}, u32[]{:S(2)}) copy-start(f32[128]{0:T(128)} %param.28) | copy-start | bytes 1540
  8.7 29.1 %copy-start.35 = (f32[128]{0:T(128)S(1)}, f32[128]{0:T(128)}, u32[]{:S(2)}) copy-start(f32[128]{0:T(128)} %param.29) | copy-start | bytes 1540
  8.7 29.1 %copy-start.36 = (f32[32]{0:T(128)S(1)}, f32[32]{0:T(128)}, u32[]{:S(2)}) copy-start(f32[32]{0:T(128)} %param.27) | copy-start | bytes 388
  8.7 29.0 %copy-start.37 = (f32[32]{0:T(128)S(1)}, f32[32]{0:T(128)}, u32[]{:S(2)}) copy-start(f32[32]{0:T(128)} %param.30) | copy-start | bytes 388
  8.7 29.0 %copy-start.38 = (f32[32]{0:T(128)S(1)}, f32[32]{0:T(128)}, u32[]{:S(2)}) copy-start(f32[32]{0:T(128)} %param.31) | copy-start | bytes 388
  8.7 9.3 %collective-permute-start.2 = (bf16[128,1024]{1,0:T(8,128)(2,1)S(1)}, bf16[128,1024]{1,0:T(8,128)(2,1)S(1)}, u32[]{:S(2)}, u32[]{:S(2)}) collective-permute-start(bf16[128,1024]{1,0:T(8,128)(2,1)S(1)} %get-tuple-element.292), channel_id=1, source_target_pairs={{0,8},{8,16},{16,24},{24,28},{28,20},{20,12},{12,4},{4,0},{1,9},{9... | collective-permute-start | bytes 786440 | tf_op jit(solution)/shard_map/ppermute | solution.py:55
  11.8 7.8 %collective-permute-start.3 = (bf16[128,1024]{1,0:T(8,128)(2,1)S(1)}, bf16[128,1024]{1,0:T(8,128)(2,1)S(1)}, u32[]{:S(2)}, u32[]{:S(2)}) collective-permute-start(bf16[128,1024]{1,0:T(8,128)(2,1)S(1)} %get-tuple-element.292), channel_id=1, source_target_pairs={{0,4},{8,0},{16,8},{24,16},{28,24},{20,28},{12,20},{4,12},{1,5},{9... | collective-permute-start | bytes 786440 | tf_op jit(solution)/shard_map/ppermute | solution.py:55
  12.7 28.8 %copy-start.39 = (s32[1,4]{1,0:T(1,128)S(1)}, s32[1,4]{1,0:T(1,128)}, u32[]{:S(2)}) copy-start(s32[1,4]{1,0:T(1,128)} %param.18) | copy-start | bytes 52
  12.7 31.6 %copy-start.33 = (s32[1,2048]{1,0:T(1,128)S(1)}, s32[1,2048]{1,0:T(1,128)}, u32[]{:S(2)}) copy-start(s32[1,2048]{1,0:T(1,128)} %param.19) | copy-start | bytes 24580
  12.7 15.2 %collective-permute-start = (bf16[256,1024]{1,0:T(8,128)(2,1)S(1)}, bf16[256,1024]{1,0:T(8,128)(2,1)S(1)}, u32[]{:S(2)}, u32[]{:S(2)}) collective-permute-start(bf16[256,1024]{1,0:T(8,128)(2,1)S(1)} %get-tuple-element.280), channel_id=1, source_target_pairs={{0,2},{1,3},{2,0},{3,1},{4,6},{5,7},{6,4},{7,5},{8,10},{9,11},{10,... | collective-permute-start | bytes 1572872 | tf_op jit(solution)/shard_map/ppermute | solution.py:45
  18.1 11.4 %copy-start.18 = (bf16[128,1024]{1,0:T(8,128)(2,1)}, bf16[128,1024]{1,0:T(8,128)(2,1)S(1)}, u32[]{:S(2)}) copy-start(bf16[128,1024]{1,0:T(8,128)(2,1)S(1)} %collective-permute-done.2) | copy-start | bytes 786436
  19.6 9.8 %copy-start.20 = (bf16[128,1024]{1,0:T(8,128)(2,1)}, bf16[128,1024]{1,0:T(8,128)(2,1)S(1)}, u32[]{:S(2)}) copy-start(bf16[128,1024]{1,0:T(8,128)(2,1)S(1)} %collective-permute-done.3) | copy-start | bytes 786436
  19.6 7.0 %collective-permute-start.4 = (bf16[128,1024]{1,0:T(8,128)(2,1)S(1)}, bf16[128,1024]{1,0:T(8,128)(2,1)}, u32[]{:S(2)}, u32[]{:S(2)}) collective-permute-start(bf16[128,1024]{1,0:T(8,128)(2,1)S(1)} %collective-permute-done.2), channel_id=1, source_target_pairs={{0,8},{8,16},{16,24},{24,28},{28,20},{20,12},{12,4},{4,0},{1,9},{9... | collective-permute-start | bytes 786440 | tf_op jit(solution)/shard_map/ppermute | solution.py:55
  21.2 6.7 %collective-permute-start.5 = (bf16[128,1024]{1,0:T(8,128)(2,1)S(1)}, bf16[128,1024]{1,0:T(8,128)(2,1)}, u32[]{:S(2)}, u32[]{:S(2)}) collective-permute-start(bf16[128,1024]{1,0:T(8,128)(2,1)S(1)} %collective-permute-done.3), channel_id=1, source_target_pairs={{0,4},{8,0},{16,8},{24,16},{28,24},{20,28},{12,20},{4,12},{1,5},{9... | collective-permute-start | bytes 786440 | tf_op jit(solution)/shard_map/ppermute | solution.py:55
  27.8 6.7 %collective-permute-start.6 = (bf16[128,1024]{1,0:T(8,128)(2,1)}, bf16[128,1024]{1,0:T(8,128)(2,1)}, u32[]{:S(2)}, u32[]{:S(2)}) collective-permute-start(bf16[128,1024]{1,0:T(8,128)(2,1)} %collective-permute-done.4), channel_id=1, source_target_pairs={{0,8},{8,16},{16,24},{24,28},{28,20},{20,12},{12,4},{4,0},{1,9},{9... | collective-permute-start | bytes 786440 | tf_op jit(solution)/shard_map/ppermute | solution.py:55
  29.4 6.7 %collective-permute-start.7 = (bf16[128,1024]{1,0:T(8,128)(2,1)}, bf16[128,1024]{1,0:T(8,128)(2,1)}, u32[]{:S(2)}, u32[]{:S(2)}) collective-permute-start(bf16[128,1024]{1,0:T(8,128)(2,1)} %collective-permute-done.5), channel_id=1, source_target_pairs={{0,4},{8,0},{16,8},{24,16},{28,24},{20,28},{12,20},{4,12},{1,5},{9... | collective-permute-start | bytes 786440 | tf_op jit(solution)/shard_map/ppermute | solution.py:55
  36.2 11.4 %collective-permute-start.1 = (bf16[256,1024]{1,0:T(8,128)(2,1)}, bf16[256,1024]{1,0:T(8,128)(2,1)}, u32[]{:S(2)}, u32[]{:S(2)}) collective-permute-start(bf16[256,1024]{1,0:T(8,128)(2,1)} %get-tuple-element.279), channel_id=1, source_target_pairs={{0,2},{1,3},{2,0},{3,1},{4,6},{5,7},{6,4},{7,5},{8,10},{9,11},{10,... | collective-permute-start | bytes 1572872 | tf_op jit(solution)/shard_map/ppermute | solution.py:45
  38.5 14.9 %all-to-all-start = ((f32[32,1,352]{2,1,0:T(1,128)}), f32[32,1,352]{2,1,0:T(1,128)S(1)}, u32[]{:S(2)}, u32[]{:S(2)}) async-start(f32[32,1,352]{2,1,0:T(1,128)} %broadcast_in_dim.237), calls=%async_computation | async-start | bytes 98304 | tf_op jit(solution)/shard_map/all_to_all | solution.py:114
  41.3 376.5 %reduce-scatter.2.cloned.1.call-start = ((), (), s32[]{:S(2)}) async-start(), calls=%async_computation.5 | async-start | bytes 13369344 | tf_op jit(solution)/shard_map/reduce_scatter | solution.py:1006
  49.4 29.1 %collective-permute-start.8 = (bf16[1024,1024]{1,0:T(8,128)(2,1)}, bf16[1024,1024]{1,0:T(8,128)(2,1)}, u32[]{:S(2)}, u32[]{:S(2)}) collective-permute-start(bf16[1024,1024]{1,0:T(8,128)(2,1)} %constant_dynamic-update-slice_fusion.x_ref.xf_ref), channel_id=1, source_target_pairs={{0,1},{1,0},{2,3},{3,2},{4,5},{5,4},{6,7},{7,6},{8,9},{9,8},{10,11... | collective-permute-start | bytes 6291464 | tf_op jit(solution)/shard_map/ppermute | solution.py:45
  49.7 5.0 %copy-start.19 = (bf16[128,1024]{1,0:T(8,128)(2,1)S(1)}, bf16[128,1024]{1,0:T(8,128)(2,1)}, u32[]{:S(2)}) copy-start(bf16[128,1024]{1,0:T(8,128)(2,1)} %copy-done.18) | copy-start | bytes 786436
  49.7 5.1 %copy-start.21 = (bf16[128,1024]{1,0:T(8,128)(2,1)S(1)}, bf16[128,1024]{1,0:T(8,128)(2,1)}, u32[]{:S(2)}) copy-start(bf16[128,1024]{1,0:T(8,128)(2,1)} %copy-done.20) | copy-start | bytes 786436
  55.8 14.3 %collective-permute-start.9 = (bf16[128,1024]{1,0:T(8,128)(2,1)}, bf16[128,1024]{1,0:T(8,128)(2,1)S(1)}, u32[]{:S(2)}, u32[]{:S(2)}) collective-permute-start(bf16[128,1024]{1,0:T(8,128)(2,1)} %collective-permute-done.6), channel_id=1, source_target_pairs={{0,8},{8,16},{16,24},{24,28},{28,20},{20,12},{12,4},{4,0},{1,9},{9... | collective-permute-start | bytes 786440 | tf_op jit(solution)/shard_map/ppermute | solution.py:55
  70.2 27.9 %copy-start.3 = (bf16[1024,256]{1,0:T(8,128)(2,1)}, bf16[1024,256]{1,0:T(8,128)(2,1)S(1)}, u32[]{:S(2)}) copy-start(bf16[1024,256]{1,0:T(8,128)(2,1)S(1)} %slice.218.w0) | copy-start | bytes 1572868
  70.2 28.3 %collective-permute-start.14 = (bf16[1024,256]{1,0:T(8,128)(2,1)S(1)}, bf16[1024,256]{1,0:T(8,128)(2,1)S(1)}, u32[]{:S(2)}, u32[]{:S(2)}) collective-permute-start(bf16[1024,256]{1,0:T(8,128)(2,1)S(1)} %slice.218.w0), channel_id=1, source_target_pairs={{0,2},{1,3},{2,0},{3,1},{4,6},{5,7},{6,4},{7,5},{8,10},{9,11},{10,... | collective-permute-start | bytes 1572872 | tf_op jit(solution)/shard_map/ppermute | solution.py:45
  98.0 1.6 collective-permute-start.10
  98.1 18.8 %collective-permute-start.13 = (bf16[1024,256]{1,0:T(8,128)(2,1)S(1)}, bf16[1024,256]{1,0:T(8,128)(2,1)S(1)}, u32[]{:S(2)}, u32[]{:S(2)}) collective-permute-start(bf16[1024,256]{1,0:T(8,128)(2,1)S(1)} %slice.218.w0), channel_id=1, source_target_pairs={{0,1},{1,0},{2,3},{3,2},{4,5},{5,4},{6,7},{7,6},{8,9},{9,8},{10,11... | collective-permute-start | bytes 1572872 | tf_op jit(solution)/shard_map/ppermute | solution.py:45
  98.5 14.8 %copy-start.4 = (bf16[1024,256]{1,0:T(8,128)(2,1)}, bf16[1024,256]{1,0:T(8,128)(2,1)S(1)}, u32[]{:S(2)}) copy-start(bf16[1024,256]{1,0:T(8,128)(2,1)S(1)} %collective-permute-done.14.w2) | copy-start | bytes 1572868
  98.6 18.3 %collective-permute-start.15 = (bf16[1024,256]{1,0:T(8,128)(2,1)S(1)}, bf16[1024,256]{1,0:T(8,128)(2,1)S(1)}, u32[]{:S(2)}, u32[]{:S(2)}) collective-permute-start(bf16[1024,256]{1,0:T(8,128)(2,1)S(1)} %collective-permute-done.14.w2), channel_id=1, source_target_pairs={{0,1},{1,0},{2,3},{3,2},{4,5},{5,4},{6,7},{7,6},{8,9},{9,8},{10,11... | collective-permute-start | bytes 1572872 | tf_op jit(solution)/shard_map/ppermute | solution.py:45
  99.6 17.3 %collective-permute-start.12 = (bf16[1024,256]{1,0:T(8,128)(2,1)S(1)}, bf16[1024,256]{1,0:T(8,128)(2,1)S(1)}, u32[]{:S(2)}, u32[]{:S(2)}) collective-permute-start(bf16[1024,256]{1,0:T(8,128)(2,1)S(1)} %pad_maximum_fusion.3), channel_id=1, source_target_pairs={{0,2},{1,3},{2,0},{3,1},{4,6},{5,7},{6,4},{7,5},{8,10},{9,11},{10,... | collective-permute-start | bytes 1572872 | tf_op jit(solution)/shard_map/ppermute | solution.py:45
  115.0 1.9 collective-permute-start.11
  125.2 30.1 %collective-permute-start.17 = (bf16[256,1024]{1,0:T(8,128)(2,1)S(1)}, bf16[256,1024]{1,0:T(8,128)(2,1)S(1)}, u32[]{:S(2)}, u32[]{:S(2)}) collective-permute-start(bf16[256,1024]{1,0:T(8,128)(2,1)S(1)} %get-tuple-element.275), channel_id=1, source_target_pairs={{0,2},{1,3},{2,0},{3,1},{4,6},{5,7},{6,4},{7,5},{8,10},{9,11},{10,... | collective-permute-start | bytes 1572872 | tf_op jit(solution)/shard_map/ppermute | solution.py:45
  125.3 42.3 %collective-permute-start.16 = (bf16[256,1024]{1,0:T(8,128)(2,1)S(1)}, bf16[256,1024]{1,0:T(8,128)(2,1)S(1)}, u32[]{:S(2)}, u32[]{:S(2)}) collective-permute-start(bf16[256,1024]{1,0:T(8,128)(2,1)S(1)} %get-tuple-element.276), channel_id=1, source_target_pairs={{0,2},{1,3},{2,0},{3,1},{4,6},{5,7},{6,4},{7,5},{8,10},{9,11},{10,... | collective-permute-start | bytes 1572872 | tf_op jit(solution)/shard_map/ppermute | solution.py:45
  165.4 14.4 %collective-permute-start.19 = (bf16[256,1024]{1,0:T(8,128)(2,1)}, bf16[256,1024]{1,0:T(8,128)(2,1)S(1)}, u32[]{:S(2)}, u32[]{:S(2)}) collective-permute-start(bf16[256,1024]{1,0:T(8,128)(2,1)} %get-tuple-element.131), channel_id=1, source_target_pairs={{0,2},{1,3},{2,0},{3,1},{4,6},{5,7},{6,4},{7,5},{8,10},{9,11},{10,... | collective-permute-start | bytes 1572872 | tf_op jit(solution)/shard_map/ppermute | solution.py:45
  177.8 15.1 %collective-permute-start.18 = (bf16[256,1024]{1,0:T(8,128)(2,1)}, bf16[256,1024]{1,0:T(8,128)(2,1)S(1)}, u32[]{:S(2)}, u32[]{:S(2)}) collective-permute-start(bf16[256,1024]{1,0:T(8,128)(2,1)} %get-tuple-element.133), channel_id=1, source_target_pairs={{0,2},{1,3},{2,0},{3,1},{4,6},{5,7},{6,4},{7,5},{8,10},{9,11},{10,... | collective-permute-start | bytes 1572872 | tf_op jit(solution)/shard_map/ppermute | solution.py:45
  184.5 19.5 %collective-permute-start.20 = (bf16[256,1024]{1,0:T(8,128)(2,1)}, bf16[256,1024]{1,0:T(8,128)(2,1)S(1)}, u32[]{:S(2)}, u32[]{:S(2)}) collective-permute-start(bf16[256,1024]{1,0:T(8,128)(2,1)} %get-tuple-element.140.refs_0_.refs_3_), channel_id=1, source_target_pairs={{0,2},{1,3},{2,0},{3,1},{4,6},{5,7},{6,4},{7,5},{8,10},{9,11},{10,... | collective-permute-start | bytes 1572872 | tf_op jit(solution)/shard_map/ppermute | solution.py:45
  197.8 20.6 %collective-permute-start.21 = (bf16[256,1024]{1,0:T(8,128)(2,1)}, bf16[256,1024]{1,0:T(8,128)(2,1)S(1)}, u32[]{:S(2)}, u32[]{:S(2)}) collective-permute-start(bf16[256,1024]{1,0:T(8,128)(2,1)} %get-tuple-element.141.refs_1_.refs_4_), channel_id=1, source_target_pairs={{0,2},{1,3},{2,0},{3,1},{4,6},{5,7},{6,4},{7,5},{8,10},{9,11},{10,... | collective-permute-start | bytes 1572872 | tf_op jit(solution)/shard_map/ppermute | solution.py:45
  204.1 14.4 %copy-start.42 = (bf16[256,1024]{1,0:T(8,128)(2,1)}, bf16[256,1024]{1,0:T(8,128)(2,1)S(1)}, u32[]{:S(2)}) copy-start(bf16[256,1024]{1,0:T(8,128)(2,1)S(1)} %collective-permute-done.20.refs_0_.refs_5_) | copy-start | bytes 1572868
  233.1 23.6 %collective-permute-start.22 = (bf16[512,1024]{1,0:T(8,128)(2,1)}, bf16[512,1024]{1,0:T(8,128)(2,1)S(1)}, u32[]{:S(2)}, u32[]{:S(2)}) collective-permute-start(bf16[512,1024]{1,0:T(8,128)(2,1)} %get-tuple-element.161), channel_id=1, source_target_pairs={{0,2},{1,3},{2,0},{3,1},{4,6},{5,7},{6,4},{7,5},{8,10},{9,11},{10,... | collective-permute-start | bytes 3145736 | tf_op jit(solution)/shard_map/ppermute | solution.py:45
  257.6 10.7 %copy-start.17 = (bf16[512,256]{1,0:T(8,128)(2,1)S(1)}, bf16[512,256]{1,0:T(8,128)(2,1)}, u32[]{:S(2)}) copy-start(bf16[512,256]{1,0:T(8,128)(2,1)} %copy-done.16) | copy-start | bytes 786436
  266.7 3.5 copy-start.6
  268.0 10.7 %collective-permute-start.24 = (bf16[1024,256]{1,0:T(8,128)(2,1)S(1)}, bf16[1024,256]{1,0:T(8,128)(2,1)S(1)}, u32[]{:S(2)}, u32[]{:S(2)}) collective-permute-start(bf16[1024,256]{1,0:T(8,128)(2,1)S(1)} %pad_maximum_fusion.4), channel_id=1, source_target_pairs={{0,2},{1,3},{2,0},{3,1},{4,6},{5,7},{6,4},{7,5},{8,10},{9,11},{10,... | collective-permute-start | bytes 1572872 | tf_op jit(solution)/shard_map/ppermute | solution.py:45
  270.7 8.0 %copy-start.22 = (bf16[512,256]{1,0:T(8,128)(2,1)S(1)}, bf16[512,256]{1,0:T(8,128)(2,1)}, u32[]{:S(2)}) copy-start(bf16[512,256]{1,0:T(8,128)(2,1)} %get-tuple-element.170) | copy-start | bytes 786436
  270.8 10.0 %copy-start.23 = (bf16[512,256]{1,0:T(8,128)(2,1)S(1)}, bf16[512,256]{1,0:T(8,128)(2,1)}, u32[]{:S(2)}) copy-start(bf16[512,256]{1,0:T(8,128)(2,1)} %get-tuple-element.171) | copy-start | bytes 786436
  270.8 11.1 %collective-permute-start.23 = (bf16[1024,512]{1,0:T(8,128)(2,1)S(1)}, bf16[1024,512]{1,0:T(8,128)(2,1)S(1)}, u32[]{:S(2)}, u32[]{:S(2)}) collective-permute-start(bf16[1024,512]{1,0:T(8,128)(2,1)S(1)} %pad_maximum_fusion), channel_id=1, source_target_pairs={{0,1},{1,0},{2,3},{3,2},{4,5},{5,4},{6,7},{7,6},{8,9},{9,8},{10,11... | collective-permute-start | bytes 3145736 | tf_op jit(solution)/shard_map/ppermute | solution.py:45
  278.8 2.0 collective-permute-start.25
  282.3 40.1 %collective-permute-start.26 = (bf16[1024,256]{1,0:T(8,128)(2,1)S(1)}, bf16[1024,256]{1,0:T(8,128)(2,1)S(1)}, u32[]{:S(2)}, u32[]{:S(2)}) collective-permute-start(bf16[1024,256]{1,0:T(8,128)(2,1)S(1)} %fusion.3), channel_id=1, source_target_pairs={{0,2},{1,3},{2,0},{3,1},{4,6},{5,7},{6,4},{7,5},{8,10},{9,11},{10,... | collective-permute-start | bytes 1572872 | tf_op jit(solution)/shard_map/ppermute | solution.py:45
  333.7 7.3 %copy-start.31 = (f32[8,1024]{1,0:T(8,128)S(1)}, f32[8,1024]{1,0:T(8,128)}, u32[]{:S(2)}) copy-start(f32[8,1024]{1,0:T(8,128)} %get-tuple-element.189) | copy-start | bytes 98308
  333.7 7.3 %copy-start.32 = (f32[8,1024]{1,0:T(8,128)S(1)}, f32[8,1024]{1,0:T(8,128)}, u32[]{:S(2)}) copy-start(f32[8,1024]{1,0:T(8,128)} %get-tuple-element.190) | copy-start | bytes 98308
  333.7 7.3 %copy-start.25 = (f32[2,8,1024]{2,1,0:T(8,128)S(1)}, f32[2,8,1024]{2,1,0:T(8,128)}, u32[]{:S(2)}) copy-start(f32[2,8,1024]{2,1,0:T(8,128)} %get-tuple-element.185) | copy-start | bytes 196612
  333.7 7.3 %copy-start.27 = (f32[2,8,1024]{2,1,0:T(8,128)S(1)}, f32[2,8,1024]{2,1,0:T(8,128)}, u32[]{:S(2)}) copy-start(f32[2,8,1024]{2,1,0:T(8,128)} %get-tuple-element.186) | copy-start | bytes 196612
  333.7 7.3 %copy-start.24 = (f32[2,8,1024]{2,1,0:T(8,128)S(1)}, f32[2,8,1024]{2,1,0:T(8,128)}, u32[]{:S(2)}) copy-start(f32[2,8,1024]{2,1,0:T(8,128)} %get-tuple-element.183) | copy-start | bytes 196612
  333.7 7.3 %copy-start.26 = (f32[2,8,1024]{2,1,0:T(8,128)S(1)}, f32[2,8,1024]{2,1,0:T(8,128)}, u32[]{:S(2)}) copy-start(f32[2,8,1024]{2,1,0:T(8,128)} %get-tuple-element.184) | copy-start | bytes 196612
  333.7 7.3 %copy-start.40 = (bf16[4,128,1024]{2,1,0:T(8,128)(2,1)S(1)}, bf16[4,128,1024]{2,1,0:T(8,128)(2,1)}, u32[]{:S(2)}) copy-start(bf16[4,128,1024]{2,1,0:T(8,128)(2,1)} %get-tuple-element.177) | copy-start | bytes 3145732
  338.5 39.4 %collective-permute-start.27 = (bf16[1024,1024]{1,0:T(8,128)(2,1)}, bf16[1024,1024]{1,0:T(8,128)(2,1)}, u32[]{:S(2)}, u32[]{:S(2)}) collective-permute-start(bf16[1024,1024]{1,0:T(8,128)(2,1)} %to_tokens.2), channel_id=1, source_target_pairs={{0,1},{1,0},{2,3},{3,2},{4,5},{5,4},{6,7},{7,6},{8,9},{9,8},{10,11... | collective-permute-start | bytes 6291464 | tf_op jit(solution)/shard_map/ppermute | solution.py:45
  341.1 34.8 %collective-permute-start.29 = (bf16[4,128,1024]{2,1,0:T(8,128)(2,1)S(1)}, bf16[4,128,1024]{2,1,0:T(8,128)(2,1)S(1)}, u32[]{:S(2)}, u32[]{:S(2)}) collective-permute-start(bf16[4,128,1024]{2,1,0:T(8,128)(2,1)S(1)} %copy-done.40), channel_id=1, source_target_pairs={{0,4},{4,0},{8,12},{12,8},{16,20},{20,16},{24,28},{28,24},{1,5},{5... | collective-permute-start | bytes 3145736 | tf_op jit(solution)/shard_map/ppermute | solution.py:45
  381.4 39.2 %collective-permute-start.28 = (bf16[512,1024]{1,0:T(8,128)(2,1)}, bf16[512,1024]{1,0:T(8,128)(2,1)}, u32[]{:S(2)}, u32[]{:S(2)}) collective-permute-start(bf16[512,1024]{1,0:T(8,128)(2,1)} %fusion), channel_id=1, source_target_pairs={{0,2},{1,3},{2,0},{3,1},{4,6},{5,7},{6,4},{7,5},{8,10},{9,11},{10,... | collective-permute-start | bytes 3145736 | tf_op jit(solution)/shard_map/ppermute | solution.py:45
  383.5 23.8 %all-to-all-start.1 = ((f32[32,1,352]{2,1,0:T(1,128)}), f32[32,1,352]{2,1,0:T(1,128)S(1)}, u32[]{:S(2)}, u32[]{:S(2)}) async-start(f32[32,1,352]{2,1,0:T(1,128)} %all_to_all.18), calls=%async_computation.2 | async-start | bytes 98304 | tf_op jit(solution)/shard_map/all_to_all | solution.py:114
  386.9 22.2 %collective-permute-start.30 = (bf16[128,1024]{1,0:T(8,128)(2,1)}, bf16[128,1024]{1,0:T(8,128)(2,1)S(1)}, u32[]{:S(2)}, u32[]{:S(2)}) collective-permute-start(bf16[128,1024]{1,0:T(8,128)(2,1)} %get-tuple-element.272), channel_id=1, source_target_pairs={{0,8},{4,12},{8,16},{12,20},{16,24},{20,28},{24,0},{28,4},{1,9},{5... | collective-permute-start | bytes 786440 | tf_op jit(solution)/shard_map/ppermute | solution.py:49
  388.6 26.4 %collective-permute-start.31 = (bf16[128,1024]{1,0:T(8,128)(2,1)S(1)}, bf16[128,1024]{1,0:T(8,128)(2,1)S(1)}, u32[]{:S(2)}, u32[]{:S(2)}) collective-permute-start(bf16[128,1024]{1,0:T(8,128)(2,1)S(1)} %get-tuple-element.274), channel_id=1, source_target_pairs={{0,16},{4,20},{8,24},{12,28},{16,0},{20,4},{24,8},{28,12},{1,17},{... | collective-permute-start | bytes 786440 | tf_op jit(solution)/shard_map/ppermute | solution.py:49
  391.1 23.9 %collective-permute-start.32 = (bf16[128,1024]{1,0:T(8,128)(2,1)S(1)}, bf16[128,1024]{1,0:T(8,128)(2,1)S(1)}, u32[]{:S(2)}, u32[]{:S(2)}) collective-permute-start(bf16[128,1024]{1,0:T(8,128)(2,1)S(1)} %get-tuple-element.273), channel_id=1, source_target_pairs={{0,24},{4,28},{8,0},{12,4},{16,8},{20,12},{24,16},{28,20},{1,25},{... | collective-permute-start | bytes 786440 | tf_op jit(solution)/shard_map/ppermute | solution.py:49
  421.2 18.1 %all-to-all-start.2 = ((f32[32,1,128]{2,1,0:T(1,128)}), f32[32,1,128]{2,1,0:T(1,128)S(1)}, u32[]{:S(2)}, u32[]{:S(2)}) async-start(f32[32,1,128]{2,1,0:T(1,128)} %broadcast_in_dim.285), calls=%async_computation.3 | async-start | bytes 32768 | tf_op jit(solution)/shard_map/all_to_all | solution.py:114
  (19 other events, 25.5 us)
Sparse Core Ops, SparseCore 0:
  36.3 105.5 all-gather.1
  256.8 156.4 reduce-scatter.1

commit v7 on v6

--- a/solution.py
+++ b/solution.py
@@ -913,7 +913,7 @@
     every = to_all(jnp.broadcast_to(vector, (devices, vector.shape[1])))
     attn, arrived = gather(
         jnp.concatenate([w_query, w_key, w_value, w_out.T], axis=1),
-        [(), (), (x_halves[0],), (x_halves[1], every)],
+        [(), (), (), (x_halves[0], x_halves[1], every)],
     )
     x_first = jnp.concatenate([tokens, x_halves[0], after(x_halves[1], *arrived[2])], axis=0)
     x_second = swap(x_first, "mp", 1)

time: 451 us -> 450 us (level)
    all_gather x1, waiting for transfers between devices: 14.5 us -> 6.94 us  [shards(): lax.all_gather(shard, ('dp', 'mp'), axis=0, tiled=True, axis_index_groups...]
    ppermute x23, waiting for transfers between devices: 51.2 us -> 58.6 us  [swap(): return lax.ppermute(array, axis, [(i, i ^ bit) for i in range(size)])]
    unnamed x97 -> x93, local copies, waits for them, and re-layouts: 14.2 us -> 15.1 us
  transfers between devices with their start and end apart: 38 -> 38, of which waited for: 18 -> 20; matrix products, arithmetic and copies ran while one was open for 14% -> 14% of each run, Pallas kernels for 41% -> 41%
where the time goes in v7:
time: 450 us; the launch traced here: 446 us
  Pallas kernels  195 us (43%)
  waiting for transfers between devices  107 us (24%)
  starting transfers between devices  51 us (11%)
  local copies, waits for them, and re-layouts  39.7 us (9%)
  other arithmetic  28 us (6%)
  between operations  19.9 us (4%)
  matrix products  5.29 us (1%)
    ppermute x23, waiting for transfers between devices, swap(): return lax.ppermute(array, axis, [(i, i ^ bit) for i in range(size)])  58.6 us
    pallas_call x1, Pallas kernels, attend_back(): pl.pallas_call(functools.partial(back_body, docs), out_shape=[jax.ShapeDt...  36.8 us
    pallas_call x3, Pallas kernels, ffn_forward(): pl.pallas_call(forward_body, out_shape=[jax.ShapeDtypeStruct((2, count, h...  32.1 us
    pallas_call x2, Pallas kernels, ffn_backward(): pl.pallas_call(functools.partial(backward_body, len(grads), len(saved)),...  28.3 us
    ppermute x23, starting transfers between devices, swap(): return lax.ppermute(array, axis, [(i, i ^ bit) for i in range(size)])  21.9 us
    ppermute x7, waiting for transfers between devices, around(): lax.ppermute(array, 'dp', [(RING[p], RING[(p + step) % 8]) for p in range...  21.5 us
    pallas_call x2, Pallas kernels, attend(): pl.pallas_call(functools.partial(attend_body, docs, first), out_shape=[ja...  21.2 us
    pallas_call x1, Pallas kernels, weight_grads(): pl.pallas_call(functools.partial(weight_body, (len(hs), len(ms), len(ups)...  20.5 us
  transfers between devices with their start and end apart: 38, of which 20 were waited for; matrix products, arithmetic and copies ran while one was open for 14% of the time, Pallas kernels for 41%

profile of v7, /device:TPU:0, one launch (start us, length us, event | category | flops | bytes accessed | tf_op | source)
XLA Modules:
  0.0 446.2 jit_solution(5370874628482819917)
XLA Ops:
  8.6 3.1 collective-permute-start.2
  11.7 6.2 %collective-permute-done.2 = bf16[128,1024]{1,0:T(8,128)(2,1)S(1)} collective-permute-done((bf16[128,1024]{1,0:T(8,128)(2,1)S(1)}, bf16[128,1024]{1,0:T(8,128)(2,1)S(1)}, u32[]{:S(2)}, u32[]{:S(2)}) %collective-permute-start.2) | collective-permute-done | bytes 262176 | tf_op jit(solution)/shard_map/ppermute | solution.py:55
  17.9 1.5 collective-permute-done.3
  19.4 1.6 collective-permute-start.4
  21.4 4.9 %collective-permute-done.4 = bf16[128,1024]{1,0:T(8,128)(2,1)} collective-permute-done((bf16[128,1024]{1,0:T(8,128)(2,1)S(1)}, bf16[128,1024]{1,0:T(8,128)(2,1)}, u32[]{:S(2)}, u32[]{:S(2)}) %collective-permute-start.4) | collective-permute-done | bytes 262176 | tf_op jit(solution)/shard_map/ppermute | solution.py:55
  27.7 1.6 collective-permute-start.6
  30.9 2.0 pad_maximum_fusion.2
  32.9 1.5 collective-permute-done.6
  34.4 1.6 collective-permute-done.7
  37.0 1.5 collective-permute-start
  39.8 2.9 all-to-all-start
  48.2 4.4 collective-permute-done
  52.6 1.9 constant_dynamic-update-slice_fusion.1
  54.5 4.7 %collective-permute-done.1 = bf16[256,1024]{1,0:T(8,128)(2,1)} collective-permute-done((bf16[256,1024]{1,0:T(8,128)(2,1)}, bf16[256,1024]{1,0:T(8,128)(2,1)}, u32[]{:S(2)}, u32[]{:S(2)}) %collective-permute-start.1) | collective-permute-done | bytes 524320 | tf_op jit(solution)/shard_map/ppermute | solution.py:45
  59.2 1.9 constant_dynamic-update-slice_fusion.x_ref.xf_ref
  61.1 3.1 fusion.5
  67.2 1.7 collective-permute-start.9
  71.9 4.5 %collective-permute-done.9 = bf16[128,1024]{1,0:T(8,128)(2,1)S(1)} collective-permute-done((bf16[128,1024]{1,0:T(8,128)(2,1)}, bf16[128,1024]{1,0:T(8,128)(2,1)S(1)}, u32[]{:S(2)}, u32[]{:S(2)}) %collective-permute-start.9) | collective-permute-done | bytes 262176 | tf_op jit(solution)/shard_map/ppermute | solution.py:55
  76.5 1.6 collective-permute-start.14
  78.0 7.0 %project.2 = (bf16[2048,256]{1,0:T(8,128)(2,1)}, bf16[2048,256]{1,0:T(8,128)(2,1)}, bf16[2048,256]{1,0:T(8,128)(2,1)}, f32[2048,256]{1,0:T(8,128)}, f32[2048,256]{1,0:T(8,128)}) custom-call(s32[1]{0:T(128)} %bitcast.m_ref, bf16[1024,1024]{1,0:T(8,128)(2,1)} %constant_dynamic-update-slice_fusion.x_ref.xf_ref, bf16[1024,1024]{1,0:T(8,128)(2,1)} %copy-done, ...), custom_call_target="tpu_custom_call" | custom-call | flops 1610612736 | bytes 8388608 | tf_op jit(solution)/shard_map/project/pallas_call | solution.py:167
  86.4 6.8 %project.3 = (bf16[2048,256]{1,0:T(8,128)(2,1)}, bf16[2048,256]{1,0:T(8,128)(2,1)}, bf16[2048,256]{1,0:T(8,128)(2,1)}, f32[2048,256]{1,0:T(8,128)}, f32[2048,256]{1,0:T(8,128)}) custom-call(s32[1]{0:T(128)} %bitcast.m_ref, ...), custom_call_target="tpu_custom_call", output_to_operand_aliasing={{0}: (6, {}), {1}: (7, {}), {2}: (8, {}), {3}: (9, {}), {4}... | custom-call | flops 1610612736 | bytes 8388608 | tf_op jit(solution)/shard_map/project/pallas_call | solution.py:167
  93.2 10.0 %attend.2 = (bf16[2048,256]{1,0:T(8,128)(2,1)}, f32[2048,256]{1,0:T(8,128)}) custom-call(s32[5]{0:T(128)} %pad_add_fusion.meta_ref, bf16[2048,256]{1,0:T(8,128)(2,1)} %get-tuple-element.120.q_ref, bf16[2048,256]{1,0:T(8,128)(2,1)} %get-tuple-element.121.k_ref, bf16[2048,256]{1,0:T(8,128)(2,1)} %get-tuple-element.122.v_ref, s32[1,2048]{1,0:T(1,128)} %compare_select_fusion.kpos_ref), custom_call_target="tpu_custom_call" | custom-call | flops 8000000000 | bytes 4194304 | tf_op jit(solution)/shard_map/attend/pallas_call | solution.py:290
  105.9 2.4 collective-permute-start.12
  108.3 11.2 %attend.3 = (bf16[2048,256]{1,0:T(8,128)(2,1)}, f32[2048,256]{1,0:T(8,128)}) custom-call(s32[5]{0:T(128)} %pad_add_fusion.meta_ref, bf16[2048,256]{1,0:T(8,128)(2,1)} %get-tuple-element.120.q_ref, bf16[2048,256]{1,0:T(8,128)(2,1)} %get-tuple-element.121.k_ref, ...), custom_call_target="tpu_custom_call", output_to_operand_aliasing={{0}: (5, {}), {1}: (6, {})} | custom-call | flops 8000000000 | bytes 4194304 | tf_op jit(solution)/shard_map/attend/pallas_call | solution.py:290
  119.5 1.7 slice.178
  124.9 5.1 %attn_out.1 = (f32[512,1024]{1,0:T(8,128)}, bf16[512,1024]{1,0:T(8,128)(2,1)}) custom-call(bf16[2048,256]{1,0:T(8,128)(2,1)} %get-tuple-element.126.a0.o_ref, bf16[512,256]{1,0:T(8,128)(2,1)} %copy-done.14, bf16[1024,256]{1,0:T(8,128)(2,1)} %copy-done.5, bf16[1024,256]{1,0:T(8,128)(2,1)} %copy-done.5, bf16[512,1024]{1,0:T(8,128)(2,1)} %x_ref.7, ...), custom_call_target="tpu_custom_call" | custom-call | flops 1073741824 | bytes 10485760 | tf_op jit(solution)/shard_map/attn_out/pallas_call | solution.py:768
  131.4 2.0 collective-permute-start.16
  133.4 6.9 %all-gather.2.cloned.1.call-done = bf16[6144,1024]{1,0:T(8,128)(2,1)} async-done(((bf16[384,1024]{1,0:T(8,128)(2,1)}), bf16[6144,1024]{1,0:T(8,128)(2,1)}) %all-gather.2.cloned.1.call-update) | async-done | bytes 12582928 | tf_op jit(solution)/shard_map/all_gather | solution.py:922
  140.3 13.5 %ffn_forward.3 = (bf16[2,512,1024]{2,1,0:T(8,128)(2,1)}, bf16[2,512,1024]{2,1,0:T(8,128)(2,1)}, bf16[2,512,1024]{2,1,0:T(8,128)(2,1)}, bf16[2,512,1024]{2,1,0:T(8,128)(2,1)}, f32[512,1024]{1,0:T(8,128)}) custom-call(bf16[512,1024]{1,0:T(8,128)(2,1)} %get-tuple-element.127.h_ref.refs_0_, bf16[8,2,3,128,1024]{4,3,2,1,0:T(8,128)(2,1)} %bitcast.106, ...), custom_call_target="tpu_custom_call" | custom-call | flops 6442450944 | bytes 18874368 | tf_op jit(solution)/shard_map/ffn_forward/pallas_call | solution.py:546
  154.6 9.2 %ffn_forward.4 = (bf16[2,256,1024]{2,1,0:T(8,128)(2,1)}, bf16[2,256,1024]{2,1,0:T(8,128)(2,1)}, bf16[2,256,1024]{2,1,0:T(8,128)(2,1)}, bf16[2,256,1024]{2,1,0:T(8,128)(2,1)}, bf16[256,1024]{1,0:T(8,128)(2,1)}) custom-call(bf16[256,1024]{1,0:T(8,128)(2,1)} %copy-done.10, bf16[8,2,3,128,1024]{4,3,2,1,0:T(8,128)(2,1)} %bitcast.107, ...), custom_call_target="tpu_custom_call" | custom-call | flops 3221225472 | bytes 15728640 | tf_op jit(solution)/shard_map/ffn_forward/pallas_call | solution.py:546
  163.9 1.5 collective-permute-start.19
  166.9 9.3 %ffn_forward.5 = (bf16[2,256,1024]{2,1,0:T(8,128)(2,1)}, bf16[2,256,1024]{2,1,0:T(8,128)(2,1)}, bf16[2,256,1024]{2,1,0:T(8,128)(2,1)}, bf16[2,256,1024]{2,1,0:T(8,128)(2,1)}, bf16[256,1024]{1,0:T(8,128)(2,1)}) custom-call(bf16[256,1024]{1,0:T(8,128)(2,1)} %copy-done.11, bf16[8,2,3,128,1024]{4,3,2,1,0:T(8,128)(2,1)} %bitcast.108, ...), custom_call_target="tpu_custom_call" | custom-call | flops 3221225472 | bytes 15728640 | tf_op jit(solution)/shard_map/ffn_forward/pallas_call | solution.py:546
  179.0 4.0 turn.2
  183.0 1.5 collective-permute-start.20
  184.5 6.7 %collective-permute-done.18.far_ref = bf16[256,1024]{1,0:T(8,128)(2,1)S(1)} collective-permute-done((bf16[256,1024]{1,0:T(8,128)(2,1)}, bf16[256,1024]{1,0:T(8,128)(2,1)S(1)}, u32[]{:S(2)}, u32[]{:S(2)}) %collective-permute-start.18) | collective-permute-done | bytes 524320 | tf_op jit(solution)/shard_map/ppermute | solution.py:45
  192.1 4.2 turn.3
  196.9 5.7 %collective-permute-done.20.refs_0_.refs_5_ = bf16[256,1024]{1,0:T(8,128)(2,1)S(1)} collective-permute-done((bf16[256,1024]{1,0:T(8,128)(2,1)}, bf16[256,1024]{1,0:T(8,128)(2,1)S(1)}, u32[]{:S(2)}, u32[]{:S(2)}) %collective-permute-start.20) | collective-permute-done | bytes 524320 | tf_op jit(solution)/shard_map/ppermute | solution.py:45
  202.5 14.4 %ffn_backward.2 = (bf16[2,512,1024]{2,1,0:T(8,128)(2,1)}, bf16[2,512,1024]{2,1,0:T(8,128)(2,1)}, f32[2,8,1024]{2,1,0:T(8,128)}, f32[2,8,1024]{2,1,0:T(8,128)}, f32[512,1024]{1,0:T(8,128)}) custom-call(bf16[256,1024]{1,0:T(8,128)(2,1)} %get-tuple-element.140.refs_0_.refs_3_, bf16[256,1024]{1,0:T(8,128)(2,1)} %get-tuple-element.141.refs_1_.refs_4_, ...), custom_call_target="tpu_custom_call" | custom-call | flops 6442450944 | bytes 25165824 | tf_op jit(solution)/shard_map/ffn_backward/pallas_call | solution.py:594
  217.7 13.9 %ffn_backward.3 = (bf16[2,512,1024]{2,1,0:T(8,128)(2,1)}, bf16[2,512,1024]{2,1,0:T(8,128)(2,1)}, f32[2,8,1024]{2,1,0:T(8,128)}, f32[2,8,1024]{2,1,0:T(8,128)}, bf16[512,1024]{1,0:T(8,128)(2,1)}) custom-call(bf16[256,1024]{1,0:T(8,128)(2,1)} %copy-done.40, bf16[256,1024]{1,0:T(8,128)(2,1)} %copy-done.41, bf16[8,2,3,128,1024]{4,3,2,1,0:T(8,128)(2,1)} %bitcast.110, ...), custom_call_target="tpu_custom_call" | custom-call | flops 6442450944 | bytes 25165824 | tf_op jit(solution)/shard_map/ffn_backward/pallas_call | solution.py:594
  232.2 20.5 %weight_grads.1 = bf16[8,2,3,128,1024]{4,3,2,1,0:T(8,128)(2,1)} custom-call(bf16[512,1024]{1,0:T(8,128)(2,1)} %get-tuple-element.127.h_ref.refs_0_, bf16[256,1024]{1,0:T(8,128)(2,1)} %copy-done.10, bf16[256,1024]{1,0:T(8,128)(2,1)} %copy-done.11, bf16[256,1024]{1,0:T(8,128)(2,1)} %get-tuple-element.140.refs_0_.refs_3_, ...), custom_call_target="tpu_custom_call" | custom-call | flops 12884901888 | bytes 25165824 | tf_op jit(solution)/shard_map/weight_grads/pallas_call | solution.py:649
  252.7 2.4 collective-permute-done.22.far_ref
  256.1 9.1 %attn_back_out.1 = (bf16[512,1024]{1,0:T(8,128)(2,1)}, f32[512,1024]{1,0:T(8,128)}, bf16[512,256]{1,0:T(8,128)(2,1)}, bf16[512,256]{1,0:T(8,128)(2,1)}, bf16[512...) custom-call(f32[512,1024]{1,0:T(8,128)} %get-tuple-element.146.own_ref, ...), custom_call_target="tpu_custom_call" | custom-call | flops 1073741824 | bytes 10485760 | tf_op jit(solution)/shard_map/attn_back_out/pallas_call | solution.py:768
  266.8 1.9 convolution_convert_fusion.1
  269.4 7.7 %collective-permute-done.24 = bf16[1024,256]{1,0:T(8,128)(2,1)S(1)} collective-permute-done((bf16[1024,256]{1,0:T(8,128)(2,1)S(1)}, bf16[1024,256]{1,0:T(8,128)(2,1)S(1)}, u32[]{:S(2)}, u32[]{:S(2)}) %collective-permute-start.24) | collective-permute-done | bytes 524320 | tf_op jit(solution)/shard_map/ppermute | solution.py:45
  281.8 36.8 %attend_back.1 = (bf16[2048,768]{1,0:T(8,128)(2,1)}, f32[8,256]{1,0:T(8,128)}) custom-call(s32[5]{0:T(128)} %pad_add_fusion.meta_ref, bf16[2048,256]{1,0:T(8,128)(2,1)} %get-tuple-element.120.q_ref, f32[2048,256]{1,0:T(8,128)} %get-tuple-element.165.qr_ref, bf16[2048,256]{1,0:T(8,128)(2,1)} %get-tuple-element.126.a0.o_ref, ...), custom_call_target="tpu_custom_call" | custom-call | flops 40000000000 | bytes 6291456 | tf_op jit(solution)/shard_map/attend_back/pallas_call | solution.py:455
  318.5 2.4 convolution_add_fusion.1.out_ref
  321.7 10.5 %attn_grads.1 = (f32[4,128,1024]{2,1,0:T(8,128)}, bf16[4,128,1024]{2,1,0:T(8,128)(2,1)}) custom-call(s32[2]{0:T(128)} %pad_add_fusion.1.m_ref, bf16[1024,1024]{1,0:T(8,128)(2,1)} %constant_dynamic-update-slice_fusion.x_ref.xf_ref, bf16[1024,1024]{1,0:T(8,128)(2,1)} %collective-permute-done.8.x_ref.xs_ref, bf16[2048,768]{1,0:T(8,128)(2,1)} %get-tuple-element.179.g_ref, ...), custom_call_target="tpu_custom_call" | custom-call | flops 3221225472 | bytes 6291456 | tf_op jit(solution)/shard_map/attn_grads/pallas_call | solution.py:701
  332.3 4.8 %to_tokens.2 = bf16[1024,1024]{1,0:T(8,128)(2,1)} custom-call(bf16[2048,768]{1,0:T(8,128)(2,1)} %get-tuple-element.179.g_ref, bf16[1024,1024]{1,0:T(8,128)(2,1)} %copy-done), custom_call_target="tpu_custom_call" | custom-call | flops 1610612736 | bytes 6291456 | tf_op jit(solution)/shard_map/to_tokens/pallas_call | solution.py:738
  339.6 5.1 %collective-permute-start.29 = (bf16[4,128,1024]{2,1,0:T(8,128)(2,1)S(1)}, bf16[4,128,1024]{2,1,0:T(8,128)(2,1)S(1)}, u32[]{:S(2)}, u32[]{:S(2)}) collective-permute-start(bf16[4,128,1024]{2,1,0:T(8,128)(2,1)S(1)} %copy-done.38), channel_id=1, source_target_pairs={{0,4},{4,0},{8,12},{12,8},{16,20},{20,16},{24,28},{28,24},{1,5},{5... | collective-permute-start | bytes 3145736 | tf_op jit(solution)/shard_map/ppermute | solution.py:45
  346.6 5.0 %to_tokens.3 = f32[1024,1024]{1,0:T(8,128)} custom-call(bf16[2048,768]{1,0:T(8,128)(2,1)} %get-tuple-element.179.g_ref, bf16[1024,1024]{1,0:T(8,128)(2,1)} %copy-done), custom_call_target="tpu_custom_call" | custom-call | flops 1610612736 | bytes 6291456 | tf_op jit(solution)/shard_map/to_tokens/pallas_call | solution.py:738
  351.7 23.2 %collective-permute-done.29 = bf16[4,128,1024]{2,1,0:T(8,128)(2,1)S(1)} collective-permute-done((bf16[4,128,1024]{2,1,0:T(8,128)(2,1)S(1)}, bf16[4,128,1024]{2,1,0:T(8,128)(2,1)S(1)}, u32[]{:S(2)}, u32[]{:S(2)}) %collective-permute-start.29) | collective-permute-done | bytes 1048608 | tf_op jit(solution)/shard_map/ppermute | solution.py:45
  374.9 2.0 convert_add_fusion
  377.7 2.6 fusion
  380.3 1.7 collective-permute-start.28
  382.7 2.6 all-to-all-start.1
  386.1 1.7 collective-permute-start.30
  387.8 2.5 collective-permute-start.31
  390.3 1.4 collective-permute-start.32
  391.7 14.6 %all-to-all-done.1 = f32[32,1,352]{2,1,0:T(1,128)S(1)} async-done(((f32[32,1,352]{2,1,0:T(1,128)}), f32[32,1,352]{2,1,0:T(1,128)S(1)}, u32[]{:S(2)}, u32[]{:S(2)}) %all-to-all-start.1) | async-done | bytes 45088 | tf_op jit(solution)/shard_map/all_to_all | solution.py:114
  408.1 5.3 %collective-permute-done.31 = bf16[128,1024]{1,0:T(8,128)(2,1)S(1)} collective-permute-done((bf16[128,1024]{1,0:T(8,128)(2,1)S(1)}, bf16[128,1024]{1,0:T(8,128)(2,1)S(1)}, u32[]{:S(2)}, u32[]{:S(2)}) %collective-permute-start.31) | collective-permute-done | bytes 262176 | tf_op jit(solution)/shard_map/ppermute | solution.py:49
  416.3 2.1 multiply_reduce_fusion
  419.7 9.1 %all-to-all-start.2 = ((f32[32,1,128]{2,1,0:T(1,128)}), f32[32,1,128]{2,1,0:T(1,128)S(1)}, u32[]{:S(2)}, u32[]{:S(2)}) async-start(f32[32,1,128]{2,1,0:T(1,128)} %broadcast_in_dim.285), calls=%async_computation.3 | async-start | bytes 32768 | tf_op jit(solution)/shard_map/all_to_all | solution.py:114
  428.8 2.3 fusion.21
  431.0 4.9 %fusion.2 = f32[512,1024]{1,0:T(8,128)} fusion(f32[512,1024]{1,0:T(8,128)} %get-tuple-element.164, f32[1024,1024]{1,0:T(8,128)} %to_tokens.3, bf16[512,1024]{1,0:T(8,128)(2,1)} %collective-permute-done.28, bf16[1024,1024]{1,0:T(8,128)(2,1)} %collective-permute-done.27), kind=kLoop, calls=%fused_computation.4 | loop fusion | flops 2621440 | bytes 8388608 | tf_op jit(solution)/shard_map/add | solution.py:1071
  (225 shorter events, 54.8 us)
Async XLA Ops:
  7.2 133.1 %all-gather.2.cloned.1.call-start = ((), (), s32[]{:S(2)}) async-start(), calls=%async_computation.4 | async-start | bytes 13369344 | tf_op jit(solution)/shard_map/all_gather | solution.py:922
  8.5 27.5 %copy-start.1 = (bf16[512,1024]{1,0:T(8,128)(2,1)S(1)}, bf16[512,1024]{1,0:T(8,128)(2,1)}, u32[]{:S(2)}) copy-start(bf16[512,1024]{1,0:T(8,128)(2,1)} %x_ref.7) | copy-start | bytes 3145732
  8.6 9.3 %collective-permute-start.2 = (bf16[128,1024]{1,0:T(8,128)(2,1)S(1)}, bf16[128,1024]{1,0:T(8,128)(2,1)S(1)}, u32[]{:S(2)}, u32[]{:S(2)}) collective-permute-start(bf16[128,1024]{1,0:T(8,128)(2,1)S(1)} %get-tuple-element.292), channel_id=1, source_target_pairs={{0,8},{8,16},{16,24},{24,28},{28,20},{20,12},{12,4},{4,0},{1,9},{9... | collective-permute-start | bytes 786440 | tf_op jit(solution)/shard_map/ppermute | solution.py:55
  11.7 7.8 %collective-permute-start.3 = (bf16[128,1024]{1,0:T(8,128)(2,1)S(1)}, bf16[128,1024]{1,0:T(8,128)(2,1)S(1)}, u32[]{:S(2)}, u32[]{:S(2)}) collective-permute-start(bf16[128,1024]{1,0:T(8,128)(2,1)S(1)} %get-tuple-element.292), channel_id=1, source_target_pairs={{0,4},{8,0},{16,8},{24,16},{28,24},{20,28},{12,20},{4,12},{1,5},{9... | collective-permute-start | bytes 786440 | tf_op jit(solution)/shard_map/ppermute | solution.py:55
  17.9 11.4 %copy-start.16 = (bf16[128,1024]{1,0:T(8,128)(2,1)}, bf16[128,1024]{1,0:T(8,128)(2,1)S(1)}, u32[]{:S(2)}) copy-start(bf16[128,1024]{1,0:T(8,128)(2,1)S(1)} %collective-permute-done.2) | copy-start | bytes 786436
  19.4 9.8 %copy-start.18 = (bf16[128,1024]{1,0:T(8,128)(2,1)}, bf16[128,1024]{1,0:T(8,128)(2,1)S(1)}, u32[]{:S(2)}) copy-start(bf16[128,1024]{1,0:T(8,128)(2,1)S(1)} %collective-permute-done.3) | copy-start | bytes 786436
  19.4 7.0 %collective-permute-start.4 = (bf16[128,1024]{1,0:T(8,128)(2,1)S(1)}, bf16[128,1024]{1,0:T(8,128)(2,1)}, u32[]{:S(2)}, u32[]{:S(2)}) collective-permute-start(bf16[128,1024]{1,0:T(8,128)(2,1)S(1)} %collective-permute-done.2), channel_id=1, source_target_pairs={{0,8},{8,16},{16,24},{24,28},{28,20},{20,12},{12,4},{4,0},{1,9},{9... | collective-permute-start | bytes 786440 | tf_op jit(solution)/shard_map/ppermute | solution.py:55
  21.0 6.7 %collective-permute-start.5 = (bf16[128,1024]{1,0:T(8,128)(2,1)S(1)}, bf16[128,1024]{1,0:T(8,128)(2,1)}, u32[]{:S(2)}, u32[]{:S(2)}) collective-permute-start(bf16[128,1024]{1,0:T(8,128)(2,1)S(1)} %collective-permute-done.3), channel_id=1, source_target_pairs={{0,4},{8,0},{16,8},{24,16},{28,24},{20,28},{12,20},{4,12},{1,5},{9... | collective-permute-start | bytes 786440 | tf_op jit(solution)/shard_map/ppermute | solution.py:55
  27.7 6.7 %collective-permute-start.6 = (bf16[128,1024]{1,0:T(8,128)(2,1)}, bf16[128,1024]{1,0:T(8,128)(2,1)}, u32[]{:S(2)}, u32[]{:S(2)}) collective-permute-start(bf16[128,1024]{1,0:T(8,128)(2,1)} %collective-permute-done.4), channel_id=1, source_target_pairs={{0,8},{8,16},{16,24},{24,28},{28,20},{20,12},{12,4},{4,0},{1,9},{9... | collective-permute-start | bytes 786440 | tf_op jit(solution)/shard_map/ppermute | solution.py:55
  29.3 6.7 %collective-permute-start.7 = (bf16[128,1024]{1,0:T(8,128)(2,1)}, bf16[128,1024]{1,0:T(8,128)(2,1)}, u32[]{:S(2)}, u32[]{:S(2)}) collective-permute-start(bf16[128,1024]{1,0:T(8,128)(2,1)} %collective-permute-done.5), channel_id=1, source_target_pairs={{0,4},{8,0},{16,8},{24,16},{28,24},{20,28},{12,20},{4,12},{1,5},{9... | collective-permute-start | bytes 786440 | tf_op jit(solution)/shard_map/ppermute | solution.py:55
  30.8 8.2 %copy-start.32 = (f32[128]{0:T(128)S(1)}, f32[128]{0:T(128)}, u32[]{:S(2)}) copy-start(f32[128]{0:T(128)} %param.28) | copy-start | bytes 1540
  30.8 8.2 %copy-start.33 = (f32[128]{0:T(128)S(1)}, f32[128]{0:T(128)}, u32[]{:S(2)}) copy-start(f32[128]{0:T(128)} %param.29) | copy-start | bytes 1540
  30.8 8.2 %copy-start.34 = (f32[32]{0:T(128)S(1)}, f32[32]{0:T(128)}, u32[]{:S(2)}) copy-start(f32[32]{0:T(128)} %param.27) | copy-start | bytes 388
  30.8 8.2 %copy-start.35 = (f32[32]{0:T(128)S(1)}, f32[32]{0:T(128)}, u32[]{:S(2)}) copy-start(f32[32]{0:T(128)} %param.30) | copy-start | bytes 388
  30.9 8.2 %copy-start.36 = (f32[32]{0:T(128)S(1)}, f32[32]{0:T(128)}, u32[]{:S(2)}) copy-start(f32[32]{0:T(128)} %param.31) | copy-start | bytes 388
  30.9 12.1 %copy-start.37 = (s32[1,4]{1,0:T(1,128)S(1)}, s32[1,4]{1,0:T(1,128)}, u32[]{:S(2)}) copy-start(s32[1,4]{1,0:T(1,128)} %param.18) | copy-start | bytes 52
  30.9 14.1 %copy-start.31 = (s32[1,2048]{1,0:T(1,128)S(1)}, s32[1,2048]{1,0:T(1,128)}, u32[]{:S(2)}) copy-start(s32[1,2048]{1,0:T(1,128)} %param.19) | copy-start | bytes 24580
  37.0 15.6 %collective-permute-start = (bf16[256,1024]{1,0:T(8,128)(2,1)}, bf16[256,1024]{1,0:T(8,128)(2,1)}, u32[]{:S(2)}, u32[]{:S(2)}) collective-permute-start(bf16[256,1024]{1,0:T(8,128)(2,1)} %get-tuple-element.280), channel_id=1, source_target_pairs={{0,2},{1,3},{2,0},{3,1},{4,6},{5,7},{6,4},{7,5},{8,10},{9,11},{10,... | collective-permute-start | bytes 1572872 | tf_op jit(solution)/shard_map/ppermute | solution.py:45
  38.5 20.7 %collective-permute-start.1 = (bf16[256,1024]{1,0:T(8,128)(2,1)}, bf16[256,1024]{1,0:T(8,128)(2,1)}, u32[]{:S(2)}, u32[]{:S(2)}) collective-permute-start(bf16[256,1024]{1,0:T(8,128)(2,1)} %get-tuple-element.279), channel_id=1, source_target_pairs={{0,2},{1,3},{2,0},{3,1},{4,6},{5,7},{6,4},{7,5},{8,10},{9,11},{10,... | collective-permute-start | bytes 1572872 | tf_op jit(solution)/shard_map/ppermute | solution.py:45
  39.8 24.9 %all-to-all-start = ((f32[32,1,352]{2,1,0:T(1,128)}), f32[32,1,352]{2,1,0:T(1,128)S(1)}, u32[]{:S(2)}, u32[]{:S(2)}) async-start(f32[32,1,352]{2,1,0:T(1,128)} %broadcast_in_dim.237), calls=%async_computation | async-start | bytes 98304 | tf_op jit(solution)/shard_map/all_to_all | solution.py:114
  42.7 373.5 %reduce-scatter.2.cloned.1.call-start = ((), (), s32[]{:S(2)}) async-start(), calls=%async_computation.5 | async-start | bytes 13369344 | tf_op jit(solution)/shard_map/reduce_scatter | solution.py:1006
  61.0 24.0 %collective-permute-start.8 = (bf16[1024,1024]{1,0:T(8,128)(2,1)}, bf16[1024,1024]{1,0:T(8,128)(2,1)}, u32[]{:S(2)}, u32[]{:S(2)}) collective-permute-start(bf16[1024,1024]{1,0:T(8,128)(2,1)} %constant_dynamic-update-slice_fusion.x_ref.xf_ref), channel_id=1, source_target_pairs={{0,1},{1,0},{2,3},{3,2},{4,5},{5,4},{6,7},{7,6},{8,9},{9,8},{10,11... | collective-permute-start | bytes 6291464 | tf_op jit(solution)/shard_map/ppermute | solution.py:45
  61.1 5.1 %copy-start.17 = (bf16[128,1024]{1,0:T(8,128)(2,1)S(1)}, bf16[128,1024]{1,0:T(8,128)(2,1)}, u32[]{:S(2)}) copy-start(bf16[128,1024]{1,0:T(8,128)(2,1)} %copy-done.16) | copy-start | bytes 786436
  61.1 5.1 %copy-start.19 = (bf16[128,1024]{1,0:T(8,128)(2,1)S(1)}, bf16[128,1024]{1,0:T(8,128)(2,1)}, u32[]{:S(2)}) copy-start(bf16[128,1024]{1,0:T(8,128)(2,1)} %copy-done.18) | copy-start | bytes 786436
  67.2 9.1 %collective-permute-start.9 = (bf16[128,1024]{1,0:T(8,128)(2,1)}, bf16[128,1024]{1,0:T(8,128)(2,1)S(1)}, u32[]{:S(2)}, u32[]{:S(2)}) collective-permute-start(bf16[128,1024]{1,0:T(8,128)(2,1)} %collective-permute-done.6), channel_id=1, source_target_pairs={{0,8},{8,16},{16,24},{24,28},{28,20},{20,12},{12,4},{4,0},{1,9},{9... | collective-permute-start | bytes 786440 | tf_op jit(solution)/shard_map/ppermute | solution.py:55
  76.4 28.0 %copy-start.3 = (bf16[1024,256]{1,0:T(8,128)(2,1)}, bf16[1024,256]{1,0:T(8,128)(2,1)S(1)}, u32[]{:S(2)}) copy-start(bf16[1024,256]{1,0:T(8,128)(2,1)S(1)} %slice.218.w0) | copy-start | bytes 1572868
  76.5 28.4 %collective-permute-start.14 = (bf16[1024,256]{1,0:T(8,128)(2,1)S(1)}, bf16[1024,256]{1,0:T(8,128)(2,1)S(1)}, u32[]{:S(2)}, u32[]{:S(2)}) collective-permute-start(bf16[1024,256]{1,0:T(8,128)(2,1)S(1)} %slice.218.w0), channel_id=1, source_target_pairs={{0,2},{1,3},{2,0},{3,1},{4,6},{5,7},{6,4},{7,5},{8,10},{9,11},{10,... | collective-permute-start | bytes 1572872 | tf_op jit(solution)/shard_map/ppermute | solution.py:45
  104.3 1.6 collective-permute-start.10
  104.4 18.7 %collective-permute-start.13 = (bf16[1024,256]{1,0:T(8,128)(2,1)S(1)}, bf16[1024,256]{1,0:T(8,128)(2,1)S(1)}, u32[]{:S(2)}, u32[]{:S(2)}) collective-permute-start(bf16[1024,256]{1,0:T(8,128)(2,1)S(1)} %slice.218.w0), channel_id=1, source_target_pairs={{0,1},{1,0},{2,3},{3,2},{4,5},{5,4},{6,7},{7,6},{8,9},{9,8},{10,11... | collective-permute-start | bytes 1572872 | tf_op jit(solution)/shard_map/ppermute | solution.py:45
  104.9 14.6 %copy-start.4 = (bf16[1024,256]{1,0:T(8,128)(2,1)}, bf16[1024,256]{1,0:T(8,128)(2,1)S(1)}, u32[]{:S(2)}) copy-start(bf16[1024,256]{1,0:T(8,128)(2,1)S(1)} %collective-permute-done.14.w2) | copy-start | bytes 1572868
  104.9 18.2 %collective-permute-start.15 = (bf16[1024,256]{1,0:T(8,128)(2,1)S(1)}, bf16[1024,256]{1,0:T(8,128)(2,1)S(1)}, u32[]{:S(2)}, u32[]{:S(2)}) collective-permute-start(bf16[1024,256]{1,0:T(8,128)(2,1)S(1)} %collective-permute-done.14.w2), channel_id=1, source_target_pairs={{0,1},{1,0},{2,3},{3,2},{4,5},{5,4},{6,7},{7,6},{8,9},{9,8},{10,11... | collective-permute-start | bytes 1572872 | tf_op jit(solution)/shard_map/ppermute | solution.py:45
  105.9 17.2 %collective-permute-start.12 = (bf16[1024,256]{1,0:T(8,128)(2,1)S(1)}, bf16[1024,256]{1,0:T(8,128)(2,1)S(1)}, u32[]{:S(2)}, u32[]{:S(2)}) collective-permute-start(bf16[1024,256]{1,0:T(8,128)(2,1)S(1)} %pad_maximum_fusion.3), channel_id=1, source_target_pairs={{0,2},{1,3},{2,0},{3,1},{4,6},{5,7},{6,4},{7,5},{8,10},{9,11},{10,... | collective-permute-start | bytes 1572872 | tf_op jit(solution)/shard_map/ppermute | solution.py:45
  121.2 1.9 collective-permute-start.11
  131.3 22.5 %collective-permute-start.17 = (bf16[256,1024]{1,0:T(8,128)(2,1)S(1)}, bf16[256,1024]{1,0:T(8,128)(2,1)S(1)}, u32[]{:S(2)}, u32[]{:S(2)}) collective-permute-start(bf16[256,1024]{1,0:T(8,128)(2,1)S(1)} %get-tuple-element.275), channel_id=1, source_target_pairs={{0,2},{1,3},{2,0},{3,1},{4,6},{5,7},{6,4},{7,5},{8,10},{9,11},{10,... | collective-permute-start | bytes 1572872 | tf_op jit(solution)/shard_map/ppermute | solution.py:45
  131.4 34.7 %collective-permute-start.16 = (bf16[256,1024]{1,0:T(8,128)(2,1)S(1)}, bf16[256,1024]{1,0:T(8,128)(2,1)S(1)}, u32[]{:S(2)}, u32[]{:S(2)}) collective-permute-start(bf16[256,1024]{1,0:T(8,128)(2,1)S(1)} %get-tuple-element.276), channel_id=1, source_target_pairs={{0,2},{1,3},{2,0},{3,1},{4,6},{5,7},{6,4},{7,5},{8,10},{9,11},{10,... | collective-permute-start | bytes 1572872 | tf_op jit(solution)/shard_map/ppermute | solution.py:45
  163.9 14.4 %collective-permute-start.19 = (bf16[256,1024]{1,0:T(8,128)(2,1)}, bf16[256,1024]{1,0:T(8,128)(2,1)S(1)}, u32[]{:S(2)}, u32[]{:S(2)}) collective-permute-start(bf16[256,1024]{1,0:T(8,128)(2,1)} %get-tuple-element.131), channel_id=1, source_target_pairs={{0,2},{1,3},{2,0},{3,1},{4,6},{5,7},{6,4},{7,5},{8,10},{9,11},{10,... | collective-permute-start | bytes 1572872 | tf_op jit(solution)/shard_map/ppermute | solution.py:45
  176.2 15.1 %collective-permute-start.18 = (bf16[256,1024]{1,0:T(8,128)(2,1)}, bf16[256,1024]{1,0:T(8,128)(2,1)S(1)}, u32[]{:S(2)}, u32[]{:S(2)}) collective-permute-start(bf16[256,1024]{1,0:T(8,128)(2,1)} %get-tuple-element.133), channel_id=1, source_target_pairs={{0,2},{1,3},{2,0},{3,1},{4,6},{5,7},{6,4},{7,5},{8,10},{9,11},{10,... | collective-permute-start | bytes 1572872 | tf_op jit(solution)/shard_map/ppermute | solution.py:45
  183.0 19.5 %collective-permute-start.20 = (bf16[256,1024]{1,0:T(8,128)(2,1)}, bf16[256,1024]{1,0:T(8,128)(2,1)S(1)}, u32[]{:S(2)}, u32[]{:S(2)}) collective-permute-start(bf16[256,1024]{1,0:T(8,128)(2,1)} %get-tuple-element.140.refs_0_.refs_3_), channel_id=1, source_target_pairs={{0,2},{1,3},{2,0},{3,1},{4,6},{5,7},{6,4},{7,5},{8,10},{9,11},{10,... | collective-permute-start | bytes 1572872 | tf_op jit(solution)/shard_map/ppermute | solution.py:45
  196.3 20.7 %collective-permute-start.21 = (bf16[256,1024]{1,0:T(8,128)(2,1)}, bf16[256,1024]{1,0:T(8,128)(2,1)S(1)}, u32[]{:S(2)}, u32[]{:S(2)}) collective-permute-start(bf16[256,1024]{1,0:T(8,128)(2,1)} %get-tuple-element.141.refs_1_.refs_4_), channel_id=1, source_target_pairs={{0,2},{1,3},{2,0},{3,1},{4,6},{5,7},{6,4},{7,5},{8,10},{9,11},{10,... | collective-permute-start | bytes 1572872 | tf_op jit(solution)/shard_map/ppermute | solution.py:45
  202.5 14.4 %copy-start.40 = (bf16[256,1024]{1,0:T(8,128)(2,1)}, bf16[256,1024]{1,0:T(8,128)(2,1)S(1)}, u32[]{:S(2)}) copy-start(bf16[256,1024]{1,0:T(8,128)(2,1)S(1)} %collective-permute-done.20.refs_0_.refs_5_) | copy-start | bytes 1572868
  231.6 23.5 %collective-permute-start.22 = (bf16[512,1024]{1,0:T(8,128)(2,1)}, bf16[512,1024]{1,0:T(8,128)(2,1)S(1)}, u32[]{:S(2)}, u32[]{:S(2)}) collective-permute-start(bf16[512,1024]{1,0:T(8,128)(2,1)} %get-tuple-element.161), channel_id=1, source_target_pairs={{0,2},{1,3},{2,0},{3,1},{4,6},{5,7},{6,4},{7,5},{8,10},{9,11},{10,... | collective-permute-start | bytes 3145736 | tf_op jit(solution)/shard_map/ppermute | solution.py:45
  256.1 10.7 %copy-start.15 = (bf16[512,256]{1,0:T(8,128)(2,1)S(1)}, bf16[512,256]{1,0:T(8,128)(2,1)}, u32[]{:S(2)}) copy-start(bf16[512,256]{1,0:T(8,128)(2,1)} %copy-done.14) | copy-start | bytes 786436
  265.2 3.5 copy-start.6
  266.4 10.7 %collective-permute-start.24 = (bf16[1024,256]{1,0:T(8,128)(2,1)S(1)}, bf16[1024,256]{1,0:T(8,128)(2,1)S(1)}, u32[]{:S(2)}, u32[]{:S(2)}) collective-permute-start(bf16[1024,256]{1,0:T(8,128)(2,1)S(1)} %pad_maximum_fusion.4), channel_id=1, source_target_pairs={{0,2},{1,3},{2,0},{3,1},{4,6},{5,7},{6,4},{7,5},{8,10},{9,11},{10,... | collective-permute-start | bytes 1572872 | tf_op jit(solution)/shard_map/ppermute | solution.py:45
  269.2 8.0 %copy-start.20 = (bf16[512,256]{1,0:T(8,128)(2,1)S(1)}, bf16[512,256]{1,0:T(8,128)(2,1)}, u32[]{:S(2)}) copy-start(bf16[512,256]{1,0:T(8,128)(2,1)} %get-tuple-element.170) | copy-start | bytes 786436
  269.3 9.9 %copy-start.21 = (bf16[512,256]{1,0:T(8,128)(2,1)S(1)}, bf16[512,256]{1,0:T(8,128)(2,1)}, u32[]{:S(2)}) copy-start(bf16[512,256]{1,0:T(8,128)(2,1)} %get-tuple-element.171) | copy-start | bytes 786436
  269.3 11.0 %collective-permute-start.23 = (bf16[1024,512]{1,0:T(8,128)(2,1)S(1)}, bf16[1024,512]{1,0:T(8,128)(2,1)S(1)}, u32[]{:S(2)}, u32[]{:S(2)}) collective-permute-start(bf16[1024,512]{1,0:T(8,128)(2,1)S(1)} %pad_maximum_fusion), channel_id=1, source_target_pairs={{0,1},{1,0},{2,3},{3,2},{4,5},{5,4},{6,7},{7,6},{8,9},{9,8},{10,11... | collective-permute-start | bytes 3145736 | tf_op jit(solution)/shard_map/ppermute | solution.py:45
  277.2 2.0 collective-permute-start.25
  280.8 40.2 %collective-permute-start.26 = (bf16[1024,256]{1,0:T(8,128)(2,1)S(1)}, bf16[1024,256]{1,0:T(8,128)(2,1)S(1)}, u32[]{:S(2)}, u32[]{:S(2)}) collective-permute-start(bf16[1024,256]{1,0:T(8,128)(2,1)S(1)} %fusion.3), channel_id=1, source_target_pairs={{0,2},{1,3},{2,0},{3,1},{4,6},{5,7},{6,4},{7,5},{8,10},{9,11},{10,... | collective-permute-start | bytes 1572872 | tf_op jit(solution)/shard_map/ppermute | solution.py:45
  332.2 7.3 %copy-start.29 = (f32[8,1024]{1,0:T(8,128)S(1)}, f32[8,1024]{1,0:T(8,128)}, u32[]{:S(2)}) copy-start(f32[8,1024]{1,0:T(8,128)} %get-tuple-element.189) | copy-start | bytes 98308
  332.2 7.3 %copy-start.30 = (f32[8,1024]{1,0:T(8,128)S(1)}, f32[8,1024]{1,0:T(8,128)}, u32[]{:S(2)}) copy-start(f32[8,1024]{1,0:T(8,128)} %get-tuple-element.190) | copy-start | bytes 98308
  332.2 7.3 %copy-start.23 = (f32[2,8,1024]{2,1,0:T(8,128)S(1)}, f32[2,8,1024]{2,1,0:T(8,128)}, u32[]{:S(2)}) copy-start(f32[2,8,1024]{2,1,0:T(8,128)} %get-tuple-element.185) | copy-start | bytes 196612
  332.2 7.3 %copy-start.25 = (f32[2,8,1024]{2,1,0:T(8,128)S(1)}, f32[2,8,1024]{2,1,0:T(8,128)}, u32[]{:S(2)}) copy-start(f32[2,8,1024]{2,1,0:T(8,128)} %get-tuple-element.186) | copy-start | bytes 196612
  332.2 7.3 %copy-start.22 = (f32[2,8,1024]{2,1,0:T(8,128)S(1)}, f32[2,8,1024]{2,1,0:T(8,128)}, u32[]{:S(2)}) copy-start(f32[2,8,1024]{2,1,0:T(8,128)} %get-tuple-element.183) | copy-start | bytes 196612
  332.2 7.3 %copy-start.24 = (f32[2,8,1024]{2,1,0:T(8,128)S(1)}, f32[2,8,1024]{2,1,0:T(8,128)}, u32[]{:S(2)}) copy-start(f32[2,8,1024]{2,1,0:T(8,128)} %get-tuple-element.184) | copy-start | bytes 196612
  332.3 7.3 %copy-start.38 = (bf16[4,128,1024]{2,1,0:T(8,128)(2,1)S(1)}, bf16[4,128,1024]{2,1,0:T(8,128)(2,1)}, u32[]{:S(2)}) copy-start(bf16[4,128,1024]{2,1,0:T(8,128)(2,1)} %get-tuple-element.177) | copy-start | bytes 3145732
  337.0 39.9 %collective-permute-start.27 = (bf16[1024,1024]{1,0:T(8,128)(2,1)}, bf16[1024,1024]{1,0:T(8,128)(2,1)}, u32[]{:S(2)}, u32[]{:S(2)}) collective-permute-start(bf16[1024,1024]{1,0:T(8,128)(2,1)} %to_tokens.2), channel_id=1, source_target_pairs={{0,1},{1,0},{2,3},{3,2},{4,5},{5,4},{6,7},{7,6},{8,9},{9,8},{10,11... | collective-permute-start | bytes 6291464 | tf_op jit(solution)/shard_map/ppermute | solution.py:45
  339.6 35.3 %collective-permute-start.29 = (bf16[4,128,1024]{2,1,0:T(8,128)(2,1)S(1)}, bf16[4,128,1024]{2,1,0:T(8,128)(2,1)S(1)}, u32[]{:S(2)}, u32[]{:S(2)}) collective-permute-start(bf16[4,128,1024]{2,1,0:T(8,128)(2,1)S(1)} %copy-done.38), channel_id=1, source_target_pairs={{0,4},{4,0},{8,12},{12,8},{16,20},{20,16},{24,28},{28,24},{1,5},{5... | collective-permute-start | bytes 3145736 | tf_op jit(solution)/shard_map/ppermute | solution.py:45
  380.3 38.7 %collective-permute-start.28 = (bf16[512,1024]{1,0:T(8,128)(2,1)}, bf16[512,1024]{1,0:T(8,128)(2,1)}, u32[]{:S(2)}, u32[]{:S(2)}) collective-permute-start(bf16[512,1024]{1,0:T(8,128)(2,1)} %fusion), channel_id=1, source_target_pairs={{0,2},{1,3},{2,0},{3,1},{4,6},{5,7},{6,4},{7,5},{8,10},{9,11},{10,... | collective-permute-start | bytes 3145736 | tf_op jit(solution)/shard_map/ppermute | solution.py:45
  382.7 23.6 %all-to-all-start.1 = ((f32[32,1,352]{2,1,0:T(1,128)}), f32[32,1,352]{2,1,0:T(1,128)S(1)}, u32[]{:S(2)}, u32[]{:S(2)}) async-start(f32[32,1,352]{2,1,0:T(1,128)} %all_to_all.18), calls=%async_computation.2 | async-start | bytes 98304 | tf_op jit(solution)/shard_map/all_to_all | solution.py:114
  386.1 22.0 %collective-permute-start.30 = (bf16[128,1024]{1,0:T(8,128)(2,1)}, bf16[128,1024]{1,0:T(8,128)(2,1)S(1)}, u32[]{:S(2)}, u32[]{:S(2)}) collective-permute-start(bf16[128,1024]{1,0:T(8,128)(2,1)} %get-tuple-element.272), channel_id=1, source_target_pairs={{0,8},{4,12},{8,16},{12,20},{16,24},{20,28},{24,0},{28,4},{1,9},{5... | collective-permute-start | bytes 786440 | tf_op jit(solution)/shard_map/ppermute | solution.py:49
  387.8 25.6 %collective-permute-start.31 = (bf16[128,1024]{1,0:T(8,128)(2,1)S(1)}, bf16[128,1024]{1,0:T(8,128)(2,1)S(1)}, u32[]{:S(2)}, u32[]{:S(2)}) collective-permute-start(bf16[128,1024]{1,0:T(8,128)(2,1)S(1)} %get-tuple-element.274), channel_id=1, source_target_pairs={{0,16},{4,20},{8,24},{12,28},{16,0},{20,4},{24,8},{28,12},{1,17},{... | collective-permute-start | bytes 786440 | tf_op jit(solution)/shard_map/ppermute | solution.py:49
  390.3 23.1 %collective-permute-start.32 = (bf16[128,1024]{1,0:T(8,128)(2,1)S(1)}, bf16[128,1024]{1,0:T(8,128)(2,1)S(1)}, u32[]{:S(2)}, u32[]{:S(2)}) collective-permute-start(bf16[128,1024]{1,0:T(8,128)(2,1)S(1)} %get-tuple-element.273), channel_id=1, source_target_pairs={{0,24},{4,28},{8,0},{12,4},{16,8},{20,12},{24,16},{28,20},{1,25},{... | collective-permute-start | bytes 786440 | tf_op jit(solution)/shard_map/ppermute | solution.py:49
  419.7 18.1 %all-to-all-start.2 = ((f32[32,1,128]{2,1,0:T(1,128)}), f32[32,1,128]{2,1,0:T(1,128)S(1)}, u32[]{:S(2)}, u32[]{:S(2)}) async-start(f32[32,1,128]{2,1,0:T(1,128)} %broadcast_in_dim.285), calls=%async_computation.3 | async-start | bytes 32768 | tf_op jit(solution)/shard_map/all_to_all | solution.py:114
  (17 other events, 21.2 us)
Sparse Core Ops, SparseCore 0:
  36.1 104.1 all-gather.1
  255.3 156.1 reduce-scatter.1
